TPU v7x, 32 devices: a whole 2x2x4 slice. The times are simulated.
32 devices in a mesh: shard: 4 (over y, x), rep: 8 (over z, core).
Axes of the slice: x: 2, y: 2, z: 4, core: 2. Of those that a mesh axis runs over, the one named last changes fastest.
Arguments:
- tokens: bfloat16 [32768, 1024], P(('shard', 'rep')), may hold values from -6 to 6
- cotangent: bfloat16 [32768, 1024], P(('shard', 'rep')), may hold values from -6 to 6
- segment: int32 [32768], P(('shard', 'rep')), may hold values from -1 to 15, as said below
- attn_gain: bfloat16 [1024], P('shard'), may hold values from 0.5 to 1.5
- w_query: bfloat16 [1024, 1024], P('shard'), may hold values from -0.1875 to 0.1875
- w_key: bfloat16 [1024, 512], P('shard'), may hold values from -0.1875 to 0.1875
- w_value: bfloat16 [1024, 512], P('shard'), may hold values from -0.1875 to 0.1875
- qk_gain: bfloat16 [128], P('shard'), may hold values from 0.099609375 to 1.8984375
- w_out: bfloat16 [1024, 1024], P('shard'), may hold values from -1.5 to 1.5
- ffn_gain: bfloat16 [1024], P('shard'), may hold values from 0.5 to 1.5
- w_gate: bfloat16 [1024, 4608], P('shard'), may hold values from -0.1875 to 0.1875
- w_up: bfloat16 [1024, 4608], P('shard'), may hold values from -0.1875 to 0.1875
- w_down: bfloat16 [4608, 1024], P('shard'), may hold values from -0.09375 to 0.09375
Outputs:
- out: bfloat16 [32768, 1024], P(('shard', 'rep'))
- grad_tokens: bfloat16 [32768, 1024], P(('shard', 'rep'))
- grad_attn_gain: float32 [1024], P('shard')
- grad_w_query: float32 [1024, 1024], P('shard')
- grad_w_key: float32 [1024, 512], P('shard')
- grad_w_value: float32 [1024, 512], P('shard')
- grad_qk_gain: float32 [128], P('shard')
- grad_w_out: float32 [1024, 1024], P('shard')
- grad_ffn_gain: float32 [1024], P('shard')
- grad_w_gate: float32 [1024, 4608], P('shard')
- grad_w_up: float32 [1024, 4608], P('shard')
- grad_w_down: float32 [4608, 1024], P('shard')
Inputs may be any that keep to these rules, and one draw needn't show every extreme that they name: `segment`: within each device's 1024 slots the live tokens come first, 512 to 1024 of them, followed by padding marked -1; live tokens form runs of equal ids 0, 1, 2, ... in rising order, each run one sequence of 1 to 512 tokens, at most 16 of them on a device. Some device has no padding and holds 16 sequences, some has 512 live tokens, and some sequence has exactly 512 tokens.
All inputs are finite; a program needn't handle non-finite values.
Results may differ from a plain program's by a relative error of at most 0.02.
Values may be sent and summed in bfloat16 or wider, within the bound.
No kernel may reach another device: no remote copies, remote signals or barrier semaphores. Data moves between devices by JAX's collectives and lax.ppermute only.
A program may use at most 384 MiB of HBM per device.

v0:
```python
import math

import jax
import jax.numpy as jnp
from jax import lax
from jax.sharding import PartitionSpec as P

HQ = 16
HK = 8
HD = 64


norm_eps = 1e-05
rope_base = 1000000.0


def inv_rms(values):
    return lax.rsqrt(jnp.mean(values * values, axis=-1, keepdims=True) + norm_eps)


def rope_tables(positions):
    half_dim = HD // 2
    freq_index = jnp.arange(half_dim).astype(jnp.float32)
    freq_vals = jnp.power(rope_base, -(2.0 * freq_index) / HD)
    angles = positions[:, None] * freq_vals[None, :]
    return (jnp.cos(angles)[:, None, :], jnp.sin(angles)[:, None, :])


def rotate(values, cosine, sine_table):
    half_dim = HD // 2
    first_half = values[..., :half_dim]
    second_half = values[..., half_dim:]
    return jnp.concatenate(
        [
            first_half * cosine - second_half * sine_table,
            second_half * cosine + first_half * sine_table,
        ],
        axis=-1,
    )


def rotate_back(grad_vals, cosine, sine_table):
    half_dim = HD // 2
    first_half = grad_vals[..., :half_dim]
    second_half = grad_vals[..., half_dim:]
    return jnp.concatenate(
        [
            first_half * cosine + second_half * sine_table,
            second_half * cosine - first_half * sine_table,
        ],
        axis=-1,
    )


def norm_back(grad_out, inputs, scale_inv, gain_vec):
    weighted = grad_out * gain_vec
    row_inner = jnp.mean(weighted * inputs, axis=-1, keepdims=True)
    return scale_inv * weighted - inputs * (scale_inv * scale_inv * scale_inv) * row_inner


def matmul_plain(left_mat, right_mat):
    return jnp.dot(left_mat, right_mat, preferred_element_type=jnp.float32)


def matmul_rows(left_mat, right_mat):
    return lax.dot_general(
        left_mat, right_mat, (((0,), (0,)), ((), ())), preferred_element_type=jnp.float32
    )


def matmul_cols(left_mat, right_mat):
    return lax.dot_general(
        left_mat, right_mat, (((1,), (1,)), ((), ())), preferred_element_type=jnp.float32
    )


def body(
    tokens,
    cotangent,
    segment,
    attn_gain,
    w_query,
    w_key,
    w_value,
    qk_gain,
    w_out,
    ffn_gain,
    w_gate,
    w_up,
    w_down,
):
    row_count = tokens.shape[0]
    group_size = HQ // HK
    score_scale = 1.0 / math.sqrt(HD)
    block_rows = min(512, row_count)
    block_count = row_count // block_rows
    attn_set = (
        lax.all_gather(attn_gain, "shard", axis=0, tiled=True),
        lax.all_gather(w_query, "shard", axis=0, tiled=True),
        lax.all_gather(w_key, "shard", axis=0, tiled=True),
        lax.all_gather(w_value, "shard", axis=0, tiled=True),
        lax.all_gather(qk_gain, "shard", axis=0, tiled=True),
        lax.all_gather(w_out, "shard", axis=0, tiled=True),
    )
    full_attn_gain, full_query, full_key, full_value, full_qk_gain, full_out = attn_set
    inputs = tokens.astype(jnp.float32)
    token_index = jnp.arange(row_count)
    same_seq = segment[:, None] == segment[None, :]
    allowed = same_seq & (token_index[None, :] <= token_index[:, None])
    positions = jnp.sum(
        (same_seq & (token_index[None, :] < token_index[:, None])).astype(jnp.float32), axis=1
    )
    live_rows = (segment >= 0).astype(jnp.float32)[:, None]
    cosine, sine_table = rope_tables(positions)
    scale_one = inv_rms(inputs)
    normed = (inputs * scale_one * full_attn_gain.astype(jnp.float32)).astype(jnp.bfloat16)
    query_lin = matmul_plain(normed, full_query).reshape(row_count, HQ, HD)
    key_lin = matmul_plain(normed, full_key).reshape(row_count, HK, HD)
    value_low = matmul_plain(normed, full_value).astype(jnp.bfloat16).reshape(row_count, HK, HD)
    qk_gains = full_qk_gain.astype(jnp.float32)
    query_scale = inv_rms(query_lin)
    key_scale = inv_rms(key_lin)
    query_rot = (
        rotate(query_lin * query_scale * qk_gains[:HD], cosine, sine_table)
        .astype(jnp.bfloat16)
        .reshape(row_count, HK, group_size, HD)
    )
    key_rot = rotate(key_lin * key_scale * qk_gains[HD:], cosine, sine_table).astype(jnp.bfloat16)

    def block_scores(begin_row):
        query_block = query_rot[begin_row : begin_row + block_rows]
        raw_scores = score_scale * jnp.einsum(
            "qgrd,kgd->grqk", query_block, key_rot, preferred_element_type=jnp.float32
        )
        mask_block = allowed[begin_row : begin_row + block_rows]
        return jnp.where(mask_block[None, None, :, :], raw_scores, -1e30)

    lse_parts = []
    attended_parts = []
    for block_id in range(block_count):
        begin_row = block_id * block_rows
        masked = block_scores(begin_row)
        row_peak = jnp.max(masked, axis=-1, keepdims=True)
        exp_scores = jnp.exp(masked - row_peak)
        row_total = jnp.sum(exp_scores, axis=-1, keepdims=True)
        probs_low = (exp_scores / row_total).astype(jnp.bfloat16)
        lse_parts.append(row_peak + jnp.log(row_total))
        attended_parts.append(
            jnp.einsum("grqk,kgd->qgrd", probs_low, value_low, preferred_element_type=jnp.float32)
        )
    attn_low = (
        jnp.concatenate(attended_parts, axis=0).astype(jnp.bfloat16).reshape(row_count, HQ * HD)
    )
    hidden = inputs + matmul_plain(attn_low, full_out)
    ffn_set = (
        lax.all_gather(ffn_gain, "shard", axis=0, tiled=True),
        lax.all_gather(w_gate, "shard", axis=0, tiled=True),
        lax.all_gather(w_up, "shard", axis=0, tiled=True),
        lax.all_gather(w_down, "shard", axis=0, tiled=True),
    )
    full_ffn_gain, full_gate, full_up, full_down = ffn_set
    scale_two = inv_rms(hidden)
    normed_ffn = (hidden * scale_two * full_ffn_gain.astype(jnp.float32)).astype(jnp.bfloat16)
    gate_proj = matmul_plain(normed_ffn, full_gate)
    up_proj = matmul_plain(normed_ffn, full_up)
    gate_sig = jax.nn.sigmoid(gate_proj)
    gate_act = gate_proj * gate_sig
    mixed_act = (gate_act * up_proj).astype(jnp.bfloat16)
    result = live_rows * (hidden + matmul_plain(mixed_act, full_down))
    back_ffn = (
        lax.all_gather(ffn_gain, "shard", axis=0, tiled=True),
        lax.all_gather(w_gate, "shard", axis=0, tiled=True),
        lax.all_gather(w_up, "shard", axis=0, tiled=True),
        lax.all_gather(w_down, "shard", axis=0, tiled=True),
    )
    back_ffn_gain, back_gate, back_up, back_down = back_ffn
    out_grad = live_rows * cotangent.astype(jnp.float32)
    out_low = out_grad.astype(jnp.bfloat16)
    grad_mixed = matmul_cols(out_low, back_down)
    grad_w_down = matmul_rows(mixed_act, out_low)
    grad_up_low = (grad_mixed * gate_act).astype(jnp.bfloat16)
    grad_gate_low = (grad_mixed * up_proj * gate_sig * (1.0 + gate_proj * (1.0 - gate_sig))).astype(
        jnp.bfloat16
    )
    grad_w_gate = matmul_rows(normed_ffn, grad_gate_low)
    grad_w_up = matmul_rows(normed_ffn, grad_up_low)
    grad_normed_ffn = matmul_cols(grad_gate_low, back_gate) + matmul_cols(grad_up_low, back_up)
    grad_ffn_gain = jnp.sum(grad_normed_ffn * hidden * scale_two, axis=0)
    grad_hidden = out_grad + norm_back(
        grad_normed_ffn, hidden, scale_two, back_ffn_gain.astype(jnp.float32)
    )
    share_fgain, share_gate, share_up, share_down = (
        lax.psum_scatter(
            grad_ffn_gain.astype(jnp.bfloat16), "shard", scatter_dimension=0, tiled=True
        ).astype(jnp.float32),
        lax.psum_scatter(
            grad_w_gate.astype(jnp.bfloat16), "shard", scatter_dimension=0, tiled=True
        ).astype(jnp.float32),
        lax.psum_scatter(
            grad_w_up.astype(jnp.bfloat16), "shard", scatter_dimension=0, tiled=True
        ).astype(jnp.float32),
        lax.psum_scatter(
            grad_w_down.astype(jnp.bfloat16), "shard", scatter_dimension=0, tiled=True
        ).astype(jnp.float32),
    )
    back_attn = (
        lax.all_gather(attn_gain, "shard", axis=0, tiled=True),
        lax.all_gather(w_query, "shard", axis=0, tiled=True),
        lax.all_gather(w_key, "shard", axis=0, tiled=True),
        lax.all_gather(w_value, "shard", axis=0, tiled=True),
        lax.all_gather(qk_gain, "shard", axis=0, tiled=True),
        lax.all_gather(w_out, "shard", axis=0, tiled=True),
    )
    back_attn_gain, back_query, back_key, back_value, back_qk_gain, back_out = back_attn
    hidden_low = grad_hidden.astype(jnp.bfloat16)
    grad_attn_low = (
        matmul_cols(hidden_low, back_out)
        .astype(jnp.bfloat16)
        .reshape(row_count, HK, group_size, HD)
    )
    grad_w_out = matmul_rows(attn_low, hidden_low)
    grad_query_parts = []
    grad_key_rot = jnp.zeros((row_count, HK, HD), jnp.float32)
    grad_value = jnp.zeros((row_count, HK, HD), jnp.float32)
    for block_id in range(block_count):
        begin_row = block_id * block_rows
        masked = block_scores(begin_row)
        attn_probs = jnp.exp(masked - lse_parts[block_id])
        probs_low = attn_probs.astype(jnp.bfloat16)
        grad_block = grad_attn_low[begin_row : begin_row + block_rows]
        query_block = query_rot[begin_row : begin_row + block_rows]
        grad_probs = jnp.einsum(
            "qgrd,kgd->grqk", grad_block, value_low, preferred_element_type=jnp.float32
        )
        row_inner = jnp.sum(attn_probs * grad_probs, axis=-1, keepdims=True)
        grad_scores = (attn_probs * (grad_probs - row_inner)).astype(jnp.bfloat16)
        grad_query_parts.append(
            score_scale
            * jnp.einsum("grqk,kgd->qgrd", grad_scores, key_rot, preferred_element_type=jnp.float32)
        )
        grad_key_rot = grad_key_rot + score_scale * jnp.einsum(
            "grqk,qgrd->kgd", grad_scores, query_block, preferred_element_type=jnp.float32
        )
        grad_value = grad_value + jnp.einsum(
            "grqk,qgrd->kgd", probs_low, grad_block, preferred_element_type=jnp.float32
        )
    grad_query_rot = jnp.concatenate(grad_query_parts, axis=0).reshape(row_count, HQ, HD)
    grad_query_norm = rotate_back(grad_query_rot, cosine, sine_table)
    grad_key_norm = rotate_back(grad_key_rot, cosine, sine_table)
    back_gains = back_qk_gain.astype(jnp.float32)
    grad_qk_gain = jnp.concatenate(
        [
            jnp.sum(grad_query_norm * query_lin * query_scale, axis=(0, 1)),
            jnp.sum(grad_key_norm * key_lin * key_scale, axis=(0, 1)),
        ]
    )
    grad_query_low = (
        norm_back(grad_query_norm, query_lin, query_scale, back_gains[:HD])
        .astype(jnp.bfloat16)
        .reshape(row_count, HQ * HD)
    )
    grad_key_low = (
        norm_back(grad_key_norm, key_lin, key_scale, back_gains[HD:])
        .astype(jnp.bfloat16)
        .reshape(row_count, HK * HD)
    )
    grad_value_low = grad_value.astype(jnp.bfloat16).reshape(row_count, HK * HD)
    grad_w_query = matmul_rows(normed, grad_query_low)
    grad_w_key = matmul_rows(normed, grad_key_low)
    grad_w_value = matmul_rows(normed, grad_value_low)
    grad_normed = (
        matmul_cols(grad_query_low, back_query)
        + matmul_cols(grad_key_low, back_key)
        + matmul_cols(grad_value_low, back_value)
    )
    grad_attn_gain = jnp.sum(grad_normed * inputs * scale_one, axis=0)
    grad_inputs = grad_hidden + norm_back(
        grad_normed, inputs, scale_one, back_attn_gain.astype(jnp.float32)
    )
    share_again, share_query, share_key, share_value, share_qk, share_out = (
        lax.psum_scatter(
            grad_attn_gain.astype(jnp.bfloat16), "shard", scatter_dimension=0, tiled=True
        ).astype(jnp.float32),
        lax.psum_scatter(
            grad_w_query.astype(jnp.bfloat16), "shard", scatter_dimension=0, tiled=True
        ).astype(jnp.float32),
        lax.psum_scatter(
            grad_w_key.astype(jnp.bfloat16), "shard", scatter_dimension=0, tiled=True
        ).astype(jnp.float32),
        lax.psum_scatter(
            grad_w_value.astype(jnp.bfloat16), "shard", scatter_dimension=0, tiled=True
        ).astype(jnp.float32),
        lax.psum_scatter(
            grad_qk_gain.astype(jnp.bfloat16), "shard", scatter_dimension=0, tiled=True
        ).astype(jnp.float32),
        lax.psum_scatter(
            grad_w_out.astype(jnp.bfloat16), "shard", scatter_dimension=0, tiled=True
        ).astype(jnp.float32),
    )
    (
        share_again,
        share_query,
        share_key,
        share_value,
        share_qk,
        share_out,
        share_fgain,
        share_gate,
        share_up,
        share_down,
    ) = (
        lax.psum(share_again.astype(jnp.bfloat16), "rep").astype(jnp.float32),
        lax.psum(share_query.astype(jnp.bfloat16), "rep").astype(jnp.float32),
        lax.psum(share_key.astype(jnp.bfloat16), "rep").astype(jnp.float32),
        lax.psum(share_value.astype(jnp.bfloat16), "rep").astype(jnp.float32),
        lax.psum(share_qk.astype(jnp.bfloat16), "rep").astype(jnp.float32),
        lax.psum(share_out.astype(jnp.bfloat16), "rep").astype(jnp.float32),
        lax.psum(share_fgain.astype(jnp.bfloat16), "rep").astype(jnp.float32),
        lax.psum(share_gate.astype(jnp.bfloat16), "rep").astype(jnp.float32),
        lax.psum(share_up.astype(jnp.bfloat16), "rep").astype(jnp.float32),
        lax.psum(share_down.astype(jnp.bfloat16), "rep").astype(jnp.float32),
    )
    return (
        result.astype(jnp.bfloat16),
        grad_inputs.astype(jnp.bfloat16),
        share_again,
        share_query,
        share_key,
        share_value,
        share_qk,
        share_out,
        share_fgain,
        share_gate,
        share_up,
        share_down,
    )


def solution(mesh):
    return jax.shard_map(
        body,
        mesh=mesh,
        in_specs=(
            P(("shard", "rep"), None),
            P(("shard", "rep"), None),
            P(("shard", "rep")),
            P("shard"),
            P("shard", None),
            P("shard", None),
            P("shard", None),
            P("shard"),
            P("shard", None),
            P("shard"),
            P("shard", None),
            P("shard", None),
            P("shard", None),
        ),
        out_specs=(
            P(("shard", "rep"), None),
            P(("shard", "rep"), None),
            P("shard"),
            P("shard", None),
            P("shard", None),
            P("shard", None),
            P("shard"),
            P("shard", None),
            P("shard"),
            P("shard", None),
            P("shard", None),
            P("shard", None),
        ),
        check_vma=False,
    )
```

profile of v0, /device:TPU:1, one launch (start us, length us, event | category | flops | bytes accessed | tf_op | source)
XLA Modules:
  0.0 1274.4 jit_solution(9859009708675031357)
XLA Ops:
  15.2 8.8 all-reduce
  24.1 5.1 all-gather.1
  29.8 6.7 all-gather
  38.5 3.0 copy.61
  42.8 3.9 copy.65
  47.3 2.7 multiply_reduce_fusion.6
  52.3 14.9 %all-gather.10.cloned.1.call-done = bf16[1024,512]{1,0:T(8,128)(2,1)} async-done(((bf16[256,512]{1,0:T(8,128)(2,1)}), bf16[1024,512]{1,0:T(8,128)(2,1)}) %all-gather.10.cloned.1.call-update) | async-done | bytes 1048592 | tf_op jit(solution)/shard_map/all_gather | solution.py:101
  67.2 3.5 convolution_convert_fusion.8
  70.7 33.6 %all-gather.14.cloned.1.call-done = bf16[1024,1024]{1,0:T(8,128)(2,1)} async-done(((bf16[256,1024]{1,0:T(8,128)(2,1)}), bf16[1024,1024]{1,0:T(8,128)(2,1)}) %all-gather.14.cloned.1.call-update) | async-done | bytes 2097168 | tf_op jit(solution)/shard_map/all_gather | solution.py:99
  104.4 4.2 multiply_reduce_fusion.4
  112.0 13.6 %fusion.63 = (f32[8,2,512]{2,1,0:T(2,128)S(1)}, f32[8,2,512,1024]{2,3,1,0:T(8,128)}) fusion(bf16[512,8,2,64]{0,3,2,1:T(8,128)(2,1)S(1)} %bitcast.196, bf16[1024,8,32]{0,2,1:T(8,128)(2,1)S(1)} %get-tuple-element.81, bf16[1024,8,32]{0,2,1:T(8,128)(2,1)S(1)} %get-tuple-element.80, pred[512,1024]{0,1:T(8,128)(4,1)S(1)} %copy-done.21), kind=kOutput, calls=%fused_computation.153 | convolution fusion | flops 1100996608 | bytes 36208640 | tf_op jit(solution)/shard_map/qgrd,kgd->grqk/dot_general | solution.py:132
  125.6 13.7 %fusion.7 = f32[8,2,512]{2,1,0:T(2,128)S(1)} fusion(f32[8,2,512,1024]{2,3,1,0:T(8,128)} %get-tuple-element.109, f32[8,2,512]{2,1,0:T(2,128)S(1)} %get-tuple-element.108), kind=kLoop, calls=%fused_computation.19 | loop fusion | flops 16769024 | bytes 33619968 | tf_op jit(solution)/shard_map/reduce_sum | solution.py:145
  139.3 14.6 %fusion.44 = bf16[8,64,2,512]{3,1,2,0:T(8,128)(2,1)} fusion(bf16[1024,8,64,1]{0,2,3,1:T(8,128)(2,1)S(1)} %bitcast.200, f32[8,2,512,1024]{2,3,1,0:T(8,128)} %get-tuple-element.109, f32[8,2,512]{2,1,0:T(2,128)S(1)} %fusion.7, f32[8,2,512]{2,1,0:T(2,128)S(1)} %get-tuple-element.108), kind=kOutput, calls=%fused_computation.115 | convolution fusion | flops 1099431936 | bytes 35717120 | tf_op jit(solution)/shard_map/grqk,kgd->qgrd/dot_general | solution.py:149
  153.9 13.5 %fusion.64 = (f32[8,2,512]{2,1,0:T(2,128)S(1)}, f32[8,2,512,1024]{2,3,1,0:T(8,128)}) fusion(bf16[512,8,2,64]{0,3,2,1:T(8,128)(2,1)S(1)} %bitcast.194, bf16[1024,8,32]{0,2,1:T(8,128)(2,1)S(1)} %get-tuple-element.81, bf16[1024,8,32]{0,2,1:T(8,128)(2,1)S(1)} %get-tuple-element.80, pred[512,1024]{0,1:T(8,128)(4,1)S(1)} %copy-done.20), kind=kOutput, calls=%fused_computation.154 | convolution fusion | flops 1100996608 | bytes 36208640 | tf_op jit(solution)/shard_map/qgrd,kgd->grqk/dot_general | solution.py:132
  167.4 13.1 %fusion.6 = f32[8,2,512]{2,1,0:T(2,128)S(1)} fusion(f32[8,2,512,1024]{2,3,1,0:T(8,128)} %get-tuple-element.111, f32[8,2,512]{2,1,0:T(2,128)S(1)} %get-tuple-element.110), kind=kLoop, calls=%fused_computation.18 | loop fusion | flops 16769024 | bytes 33619968 | tf_op jit(solution)/shard_map/reduce_sum | solution.py:145
  180.6 16.7 %fusion.45 = bf16[8,64,2,512]{3,1,2,0:T(8,128)(2,1)} fusion(bf16[1024,8,64,1]{0,2,3,1:T(8,128)(2,1)S(1)} %bitcast.201, f32[8,2,512,1024]{2,3,1,0:T(8,128)} %get-tuple-element.111, f32[8,2,512]{2,1,0:T(2,128)S(1)} %fusion.6, f32[8,2,512]{2,1,0:T(2,128)S(1)} %get-tuple-element.110), kind=kOutput, calls=%fused_computation.116 | convolution fusion | flops 1099431936 | bytes 35717120 | tf_op jit(solution)/shard_map/grqk,kgd->qgrd/dot_general | solution.py:149
  197.3 4.8 multiply_reduce_fusion.3
  204.6 34.9 %all-gather.20.cloned.1.call-done = bf16[1024,4608]{1,0:T(8,128)(2,1)} async-done(((bf16[256,4608]{1,0:T(8,128)(2,1)}), bf16[1024,4608]{1,0:T(8,128)(2,1)}) %all-gather.20.cloned.1.call-update) | async-done | bytes 9437200 | tf_op jit(solution)/shard_map/all_gather | solution.py:158
  239.5 16.4 %fusion.66 = f32[1024,4608]{1,0:T(8,128)} fusion(bf16[1024,1024]{0,1:T(8,128)(2,1)S(1)} %multiply_convert_fusion.4, bf16[1024,4608]{1,0:T(8,128)(2,1)} %all-gather.20.cloned.1.call-done), kind=kOutput, calls=%fused_computation.156 | convolution fusion | flops 9663676416 | bytes 30408704 | tf_op jit(solution)/shard_map/dot_general | solution.py:62
  255.9 81.6 %all-gather.18.cloned.1.call-done = bf16[1024,4608]{1,0:T(8,128)(2,1)} async-done(((bf16[256,4608]{1,0:T(8,128)(2,1)}), bf16[1024,4608]{1,0:T(8,128)(2,1)}) %all-gather.18.cloned.1.call-update) | async-done | bytes 9437200 | tf_op jit(solution)/shard_map/all_gather | solution.py:157
  337.5 17.1 %fusion.65 = f32[1024,4608]{1,0:T(8,128)} fusion(bf16[1024,1024]{0,1:T(8,128)(2,1)} %copy-done.31, bf16[1024,4608]{1,0:T(8,128)(2,1)} %all-gather.18.cloned.1.call-done), kind=kOutput, calls=%fused_computation.155 | convolution fusion | flops 9663676416 | bytes 30408704 | tf_op jit(solution)/shard_map/dot_general | solution.py:62
  354.6 81.1 %all-gather.22.cloned.1.call-done = bf16[4608,1024]{1,0:T(8,128)(2,1)} async-done(((bf16[1152,1024]{1,0:T(8,128)(2,1)}), bf16[4608,1024]{1,0:T(8,128)(2,1)}) %all-gather.22.cloned.1.call-update) | async-done | bytes 9437200 | tf_op jit(solution)/shard_map/all_gather | solution.py:159
  435.8 31.2 %multiply_convert_fusion = (bf16[1024,4608]{1,0:T(8,128)(2,1)}, bf16[1024,4608]{1,0:T(8,128)(2,1)}, bf16[1024,4608]{1,0:T(8,128)(2,1)}) fusion(f32[1024,4608]{1,0:T(8,128)} %fusion.65, f32[1024,4608]{1,0:T(8,128)} %fusion.66, bf16[4608,1024]{1,0:T(8,128)(2,1)} %all-gather.22.cloned.1.call-done, bf16[1024,1024]{0,1:T(8,128)(2,1)S(1)} %copy-done.18, ...), kind=kOutput, calls=%fused_computation.22 | convolution fusion | flops 9737601024 | bytes 77598720 | tf_op jit(solution)/shard_map/dot_general | solution.py:72
  467.0 14.6 %fusion.67 = f32[1024,1024]{0,1:T(8,128)S(1)} fusion(bf16[1024,4608]{1,0:T(8,128)(2,1)} %get-tuple-element.66, bf16[1024,4608]{1,0:T(8,128)(2,1)} %all-gather.18.cloned.1.call-done), kind=kOutput, calls=%fused_computation.157 | convolution fusion | flops 9663676416 | bytes 23068672 | tf_op jit(solution)/shard_map/dot_general | solution.py:72
  481.6 16.5 %multiply_reduce_fusion = (bf16[1024]{0:T(1024)(128)(2,1)}, f32[1024]{0:T(1024)S(1)}, f32[1024,1024]{0,1:T(8,128)S(1)}) fusion(f32[1024,1024]{0,1:T(8,128)S(1)} %copy-done.9, f32[1024]{0:T(1024)S(1)} %get-tuple-element.99, f32[1024]{0:T(1024)S(1)} %bitcast.223, f32[1024,1024]{0,1:T(8,128)S(1)} %fusion.67, bf16[1024,4608]{1,0:T(8,128)(2,1)} %get-tuple-element.65, ...), kind=kOutput, calls=%fused_computation.65 | convolution fusion | flops 9671014400 | bytes 31471616 | tf_op jit(solution)/shard_map/dot_general | solution.py:72
  499.7 2.3 convolution_convert_fusion.3
  502.2 14.7 %fusion.11 = f32[8,64,1024,1]{2,1,3,0:T(8,128)} fusion(bf16[512,8,2,64]{0,3,2,1:T(8,128)(2,1)S(1)} %bitcast.192, f32[8,2,512,1024]{2,3,1,0:T(8,128)} %get-tuple-element.109, f32[8,2,512]{2,1,0:T(2,128)S(1)} %bitcast.204), kind=kOutput, calls=%fused_computation.27 | convolution fusion | flops 1090519040 | bytes 36732928 | tf_op jit(solution)/shard_map/grqk,qgrd->kgd/dot_general | solution.py:244
  516.9 21.8 %fusion = (f32[8,2,512]{2,1,0:T(2,128)S(1)}, f32[8,1024,512,2]{2,1,3,0:T(8,128)}) fusion(f32[8,2,512,1024]{2,3,1,0:T(8,128)} %get-tuple-element.109, f32[8,2,512]{2,1,0:T(2,128)S(1)} %bitcast.205, bf16[1024,8,64,1]{0,2,3,1:T(8,128)(2,1)S(1)} %bitcast.202, bf16[512,8,2,64]{0,3,2,1:T(8,128)(2,1)S(1)} %bitcast.193), kind=kOutput, calls=%fused_computation.2 | convolution fusion | flops 1098899456 | bytes 69271552 | tf_op jit(solution)/shard_map/qgrd,kgd->grqk/dot_general | solution.py:232
  538.7 21.7 %fusion.3 = (f32[8,2,512]{2,1,0:T(2,128)S(1)}, f32[8,1024,512,2]{2,1,3,0:T(8,128)}) fusion(f32[8,2,512,1024]{2,3,1,0:T(8,128)} %get-tuple-element.111, f32[8,2,512]{2,1,0:T(2,128)S(1)} %bitcast.207, bf16[1024,8,64,1]{0,2,3,1:T(8,128)(2,1)S(1)} %bitcast.203, bf16[512,8,2,64]{0,3,2,1:T(8,128)(2,1)S(1)} %bitcast.190), kind=kOutput, calls=%fused_computation.7 | convolution fusion | flops 1098899456 | bytes 69271552 | tf_op jit(solution)/shard_map/qgrd,kgd->grqk/dot_general | solution.py:232
  560.4 15.3 %fusion.36 = bf16[8,64,1024]{2,1,0:T(8,128)(2,1)} fusion(f32[8,64,1024,1]{2,1,3,0:T(8,128)} %fusion.11, bf16[512,8,2,64]{0,3,2,1:T(8,128)(2,1)S(1)} %bitcast.191, f32[8,2,512,1024]{2,3,1,0:T(8,128)} %get-tuple-element.111, f32[8,2,512]{2,1,0:T(2,128)S(1)} %bitcast.208), kind=kOutput, calls=%fused_computation.90 | convolution fusion | flops 1091567616 | bytes 37781504 | tf_op jit(solution)/shard_map/grqk,qgrd->kgd/dot_general | solution.py:244
  575.7 3.5 convolution_convert_fusion.6
  579.4 28.7 %fusion.5 = bf16[8,2,512,1024]{2,3,1,0:T(8,128)(2,1)} fusion(f32[8,1024,512,2]{2,1,3,0:T(8,128)} %get-tuple-element.118, f32[8,2,512,1024]{2,3,1,0:T(8,128)} %get-tuple-element.111, f32[8,2,512]{2,1,0:T(2,128)S(1)} %get-tuple-element.117, f32[8,2,512]{2,1,0:T(2,128)S(1)} %bitcast.209), kind=kLoop, calls=%fused_computation.9 | loop fusion | flops 33554432 | bytes 83951616 | tf_op jit(solution)/shard_map/convert_element_type | solution.py:236
  608.1 12.2 fusion.68
  620.3 27.5 %fusion.2 = bf16[8,2,512,1024]{2,3,1,0:T(8,128)(2,1)} fusion(f32[8,1024,512,2]{2,1,3,0:T(8,128)} %get-tuple-element.116, f32[8,2,512,1024]{2,3,1,0:T(8,128)} %get-tuple-element.109, f32[8,2,512]{2,1,0:T(2,128)S(1)} %get-tuple-element.115, f32[8,2,512]{2,1,0:T(2,128)S(1)} %bitcast.206), kind=kLoop, calls=%fused_computation.4 | loop fusion | flops 33554432 | bytes 83951616 | tf_op jit(solution)/shard_map/convert_element_type | solution.py:236
  647.8 12.9 %fusion.38 = f32[1024,8,64]{0,2,1:T(8,128)} fusion(f32[8,64,1024,1]{2,1,3,0:T(8,128)} %fusion.68, bf16[512,8,2,64]{0,3,2,1:T(8,128)(2,1)S(1)} %bitcast.197, bf16[8,2,512,1024]{2,3,1,0:T(8,128)(2,1)} %fusion.2), kind=kOutput, calls=%fused_computation.97 | convolution fusion | flops 1074790400 | bytes 22020096 | tf_op jit(solution)/shard_map/grqk,qgrd->kgd/dot_general | solution.py:241
  660.6 2.0 multiply_add_fusion.1
  664.4 2.3 convolution_convert_fusion.7
  666.8 6.6 convolution_convert_fusion.4
  673.9 9.0 multiply_bitcast_fusion.1
  683.0 8.7 multiply_bitcast_fusion
  695.7 2.2 fusion.21
  699.2 3.7 convolution_convert_fusion.5
  703.1 16.7 %convolution_convert_fusion.1 = bf16[1024,4608]{1,0:T(8,128)(2,1)} fusion(bf16[1024,1024]{0,1:T(8,128)(2,1)} %copy-done.31, bf16[1024,4608]{1,0:T(8,128)(2,1)} %get-tuple-element.66), kind=kOutput, calls=%fused_computation.34 | convolution fusion | flops 9668395008 | bytes 20971520 | tf_op jit(solution)/shard_map/dot_general | solution.py:66
  719.8 16.3 %convolution_convert_fusion = bf16[1024,4608]{1,0:T(8,128)(2,1)} fusion(bf16[1024,1024]{0,1:T(8,128)(2,1)} %copy-done.31, bf16[1024,4608]{1,0:T(8,128)(2,1)} %get-tuple-element.65), kind=kOutput, calls=%fused_computation.33 | convolution fusion | flops 9668395008 | bytes 20971520 | tf_op jit(solution)/shard_map/dot_general | solution.py:66
  736.8 16.6 %convolution_convert_fusion.2 = bf16[4608,1024]{1,0:T(8,128)(2,1)} fusion(bf16[1024,4608]{1,0:T(8,128)(2,1)} %get-tuple-element.67, bf16[1024,1024]{0,1:T(8,128)(2,1)} %copy.65, f32[1024]{0:T(1024)S(1)} %copy-done.52), kind=kOutput, calls=%fused_computation.35 | convolution fusion | flops 9671540736 | bytes 20975616 | tf_op jit(solution)/shard_map/dot_general | solution.py:66
  755.0 16.5 %reduce-scatter.8.cloned.1.call-done = bf16[256,1024]{1,0:T(8,128)(2,1)} async-done(((bf16[1024,1024]{1,0:T(8,128)(2,1)}), bf16[256,1024]{1,0:T(8,128)(2,1)}) %reduce-scatter.8.cloned.1.call-update) | async-done | bytes 524304 | tf_op jit(solution)/shard_map/reduce_scatter | solution.py:284
  771.5 98.0 %reduce-scatter.16.cloned.1.call-done = bf16[256,4608]{1,0:T(8,128)(2,1)} async-done(((bf16[1024,4608]{1,0:T(8,128)(2,1)}), bf16[256,4608]{1,0:T(8,128)(2,1)}) %reduce-scatter.16.cloned.1.call-update) | async-done | bytes 2359312 | tf_op jit(solution)/shard_map/reduce_scatter | solution.py:196
  869.5 98.2 %reduce-scatter.18.cloned.1.call-done = bf16[256,4608]{1,0:T(8,128)(2,1)} async-done(((bf16[1024,4608]{1,0:T(8,128)(2,1)}), bf16[256,4608]{1,0:T(8,128)(2,1)}) %reduce-scatter.18.cloned.1.call-update) | async-done | bytes 2359312 | tf_op jit(solution)/shard_map/reduce_scatter | solution.py:199
  967.7 98.0 %reduce-scatter.20.cloned.1.call-done = bf16[1152,1024]{1,0:T(8,128)(2,1)} async-done(((bf16[4608,1024]{1,0:T(8,128)(2,1)}), bf16[1152,1024]{1,0:T(8,128)(2,1)}) %reduce-scatter.20.cloned.1.call-update) | async-done | bytes 2359312 | tf_op jit(solution)/shard_map/reduce_scatter | solution.py:202
  1065.7 16.9 %multiply_convert_fusion.3 = bf16[1024,1024]{0,1:T(8,128)(2,1)} fusion(f32[1024,1024]{0,1:T(8,128)} %copy-done.8, f32[1024]{0:T(1024)S(1)} %copy-done.52, bf16[1024,4608]{1,0:T(8,128)(2,1)} %get-tuple-element.67, bf16[4608,1024]{1,0:T(8,128)(2,1)} %all-gather.22.cloned.1.call-done), kind=kOutput, calls=%fused_computation.72 | convolution fusion | flops 9666822144 | bytes 25169920 | tf_op jit(solution)/shard_map/dot_general | solution.py:62
  1082.6 4.0 copy.77
  1086.9 2.6 fusion.70
  1089.6 2.3 fusion.69
  1092.0 3.6 fusion.31
  1095.6 7.2 all-reduce.6
  1103.1 16.5 %all-reduce.4 = (bf16[256]{0:T(256)(128)(2,1)S(1)}, bf16[32]{0:T(256)(128)(2,1)S(1)}, bf16[256]{0:T(256)(128)(2,1)S(1)}) all-reduce(bf16[256]{0:T(256)(128)(2,1)S(1)} %dynamic-slice.2, bf16[32]{0:T(256)(128)(2,1)S(1)} %dynamic-slice.4, bf16[256]{0:T(256)(128)(2,1)S(1)} %dynamic-slice.6), channel_id=1, replica_groups=mesh['shard'=4,'rep'=8] {'rep'}, use_global_device_ids=true, to_apply=%region_17.18 | all-reduce | flops 544 | bytes 2176 | tf_op jit(solution)/shard_map/psum | solution.py:312
  1121.2 5.9 fusion.28
  1127.2 4.0 copy.78
  1131.1 120.2 %all-reduce.9.cloned.1.call-done = (bf16[256,1024]{1,0:T(8,128)(2,1)}, bf16[256,512]{1,0:T(8,128)(2,1)}, bf16[256,512]{1,0:T(8,128)(2,1)}, bf16[256,1024]{1,0:T(...) async-done(((bf16[256,1024]{1,0:T(8,128)(2,1)}, bf16[256,512]{1,0:T(8,128)(2,1)}, bf16[256,512]{1,0:T(8,128)(2,1)}, ...) | async-done | bytes 8650768 | tf_op jit(solution)/shard_map/psum | solution.py:313
  1251.3 2.3 convert_element_type.210
  1257.2 2.3 convert_element_type.217
  1259.4 2.7 convert_element_type.221
  1262.2 2.7 convert_element_type.223
  1264.9 2.7 convert_element_type.225
  (220 shorter events, 36.1 us)
Async XLA Ops:
  7.2 40.1 %all-gather.12.cloned.1.call-start = ((), (), s32[]{:S(2)}) async-start(), calls=%async_computation.8 | async-start | bytes 1310720 | tf_op jit(solution)/shard_map/all_gather | solution.py:100
  7.9 4.1 copy-start.46
  7.9 59.3 %all-gather.10.cloned.1.call-start = ((), (), s32[]{:S(2)}) async-start(), calls=%async_computation.7 | async-start | bytes 1310720 | tf_op jit(solution)/shard_map/all_gather | solution.py:101
  8.7 95.7 %all-gather.14.cloned.1.call-start = ((), (), s32[]{:S(2)}) async-start(), calls=%async_computation.9 | async-start | bytes 2621440 | tf_op jit(solution)/shard_map/all_gather | solution.py:99
  9.4 187.9 %all-gather.16.cloned.1.call-start = ((), (), s32[]{:S(2)}) async-start(), calls=%async_computation.10 | async-start | bytes 2621440 | tf_op jit(solution)/shard_map/all_gather | solution.py:103
  10.0 3.7 copy-start.58
  10.0 5.0 copy-start.62
  10.0 14.1 %copy-start.63 = (bf16[256]{0:T(256)(128)(2,1)S(1)}, bf16[256]{0:T(256)(128)(2,1)}, u32[]{:S(2)}) copy-start(bf16[256]{0:T(256)(128)(2,1)} %param.16) | copy-start | bytes 1540
  10.0 14.1 %copy-start.64 = (bf16[256]{0:T(256)(128)(2,1)S(1)}, bf16[256]{0:T(256)(128)(2,1)}, u32[]{:S(2)}) copy-start(bf16[256]{0:T(256)(128)(2,1)} %param.22) | copy-start | bytes 1540
  10.0 229.5 %all-gather.20.cloned.1.call-start = ((), (), s32[]{:S(2)}) async-start(), calls=%async_computation.12 | async-start | bytes 11796480 | tf_op jit(solution)/shard_map/all_gather | solution.py:158
  10.6 326.9 %all-gather.18.cloned.1.call-start = ((), (), s32[]{:S(2)}) async-start(), calls=%async_computation.11 | async-start | bytes 11796480 | tf_op jit(solution)/shard_map/all_gather | solution.py:157
  11.2 424.6 %all-gather.22.cloned.1.call-start = ((), (), s32[]{:S(2)}) async-start(), calls=%async_computation.13 | async-start | bytes 11796480 | tf_op jit(solution)/shard_map/all_gather | solution.py:159
  11.9 743.0 %reduce-scatter.12.cloned.1.call-start = ((), (), s32[]{:S(2)}) async-start(), calls=%async_computation.16 | async-start | bytes 1310720 | tf_op jit(solution)/shard_map/reduce_scatter | solution.py:290
  24.1 26.6 %copy-start.56 = (f32[64]{0:T(128)}, f32[64]{0:T(128)S(1)}, u32[]{:S(2)}) copy-start(f32[64]{0:T(128)S(1)} %get-tuple-element.102) | copy-start | bytes 772
  24.1 85.2 %copy-start.54 = (f32[64]{0:T(128)}, f32[64]{0:T(128)S(1)}, u32[]{:S(2)}) copy-start(f32[64]{0:T(128)S(1)} %get-tuple-element.103) | copy-start | bytes 772
  36.5 67.9 %copy-start.47 = (f32[4,1,256]{2,1,0:T(1,128)}, f32[4,1,256]{2,1,0:T(1,128)S(1)}, u32[]{:S(2)}) copy-start(f32[4,1,256]{2,1,0:T(1,128)S(1)} %convert_element_type.226) | copy-start | bytes 12292
  41.5 62.9 %copy-start.2 = (bf16[1024,1024]{0,1:T(8,128)(2,1)}, bf16[1024,1024]{0,1:T(8,128)(2,1)S(1)}, u32[]{:S(2)}) copy-start(bf16[1024,1024]{0,1:T(8,128)(2,1)S(1)} %copy.61) | copy-start | bytes 6291460
  42.8 61.6 %copy-start.44 = (f32[1024]{0:T(1024)}, f32[1024]{0:T(1024)S(1)}, u32[]{:S(2)}) copy-start(f32[1024]{0:T(1024)S(1)} %get-tuple-element.97) | copy-start | bytes 12292
  47.3 63.1 %copy-start.24 = (f32[1024,32]{0,1:T(8,128)}, f32[1024,32]{0,1:T(8,128)S(1)}, u32[]{:S(2)}) copy-start(f32[1024,32]{0,1:T(8,128)S(1)} %get-tuple-element.94) | copy-start | bytes 393220
  47.3 63.1 %copy-start.26 = (f32[1024,32]{0,1:T(8,128)}, f32[1024,32]{0,1:T(8,128)S(1)}, u32[]{:S(2)}) copy-start(f32[1024,32]{0,1:T(8,128)S(1)} %get-tuple-element.95) | copy-start | bytes 393220
  52.3 101.6 %copy-start.10 = (bf16[1024,8,32]{0,2,1:T(8,128)(2,1)}, bf16[1024,8,32]{0,2,1:T(8,128)(2,1)S(1)}, u32[]{:S(2)}) copy-start(bf16[1024,8,32]{0,2,1:T(8,128)(2,1)S(1)} %get-tuple-element.80) | copy-start | bytes 1572868
  52.3 101.6 %copy-start.12 = (bf16[1024,8,32]{0,2,1:T(8,128)(2,1)}, bf16[1024,8,32]{0,2,1:T(8,128)(2,1)S(1)}, u32[]{:S(2)}) copy-start(bf16[1024,8,32]{0,2,1:T(8,128)(2,1)S(1)} %get-tuple-element.81) | copy-start | bytes 1572868
  108.6 2.4 copy-start
  111.9 13.6 %copy-start.16 = (bf16[512,16,64]{0,2,1:T(8,128)(2,1)}, bf16[512,16,64]{0,2,1:T(8,128)(2,1)S(1)}, u32[]{:S(2)}) copy-start(bf16[512,16,64]{0,2,1:T(8,128)(2,1)S(1)} %get-tuple-element.87) | copy-start | bytes 3145732
  111.9 42.0 %copy-start.14 = (bf16[512,16,64]{0,2,1:T(8,128)(2,1)}, bf16[512,16,64]{0,2,1:T(8,128)(2,1)S(1)}, u32[]{:S(2)}) copy-start(bf16[512,16,64]{0,2,1:T(8,128)(2,1)S(1)} %get-tuple-element.86) | copy-start | bytes 3145732
  125.6 13.7 %copy-start.22 = (bf16[1024,512]{0,1:T(8,128)(2,1)S(1)}, bf16[1024,512]{0,1:T(8,128)(2,1)}, u32[]{:S(2)}) copy-start(bf16[1024,512]{0,1:T(8,128)(2,1)} %convolution_convert_fusion.8) | copy-start | bytes 3145732
  139.3 14.7 %copy-start.20 = (pred[512,1024]{0,1:T(8,128)(4,1)S(1)}, pred[512,1024]{0,1:T(8,128)(4,1)}, u32[]{:S(2)}) copy-start(pred[512,1024]{0,1:T(8,128)(4,1)} %get-tuple-element.88) | copy-start | bytes 1572868
  180.6 16.7 %copy-start.3 = (bf16[1024,1024]{0,1:T(8,128)(2,1)S(1)}, bf16[1024,1024]{0,1:T(8,128)(2,1)}, u32[]{:S(2)}) copy-start(bf16[1024,1024]{0,1:T(8,128)(2,1)} %copy-done.2) | copy-start | bytes 6291460
  197.3 6.9 copy-start.49
  204.6 34.9 %copy-start.31 = (bf16[1024,1024]{0,1:T(8,128)(2,1)}, bf16[1024,1024]{0,1:T(8,128)(2,1)S(1)}, u32[]{:S(2)}) copy-start(bf16[1024,1024]{0,1:T(8,128)(2,1)S(1)} %multiply_convert_fusion.4) | copy-start | bytes 6291460
  255.9 179.8 %copy-start.18 = (bf16[1024,1024]{0,1:T(8,128)(2,1)S(1)}, bf16[1024,1024]{0,1:T(8,128)(2,1)}, u32[]{:S(2)}) copy-start(bf16[1024,1024]{0,1:T(8,128)(2,1)} %copy.65) | copy-start | bytes 6291460
  255.9 179.8 %copy-start.51 = (f32[1024]{0:T(1024)S(1)}, f32[1024]{0:T(1024)}, u32[]{:S(2)}) copy-start(f32[1024]{0:T(1024)} %compare_convert_fusion) | copy-start | bytes 12292
  467.0 14.6 %copy-start.9 = (f32[1024,1024]{0,1:T(8,128)S(1)}, f32[1024,1024]{0,1:T(8,128)}, u32[]{:S(2)}) copy-start(f32[1024,1024]{0,1:T(8,128)} %copy-done.8) | copy-start | bytes 12582916
  499.7 2.3 copy-start.7
  502.2 14.7 %copy-start.23 = (bf16[1024,512]{0,1:T(8,128)(2,1)S(1)}, bf16[1024,512]{0,1:T(8,128)(2,1)}, u32[]{:S(2)}) copy-start(bf16[1024,512]{0,1:T(8,128)(2,1)} %convolution_convert_fusion.8) | copy-start | bytes 3145732
  516.9 21.8 %copy-start.37 = (f32[2,8,512]{2,1,0:T(8,128)S(1)}, f32[2,8,512]{2,1,0:T(8,128)}, u32[]{:S(2)}) copy-start(f32[2,8,512]{2,1,0:T(8,128)} %log_add_fusion.1) | copy-start | bytes 98308
  560.4 15.3 %copy-start.4 = (bf16[1024,1024]{0,1:T(8,128)(2,1)S(1)}, bf16[1024,1024]{0,1:T(8,128)(2,1)}, u32[]{:S(2)}) copy-start(bf16[1024,1024]{0,1:T(8,128)(2,1)} %copy-done.2) | copy-start | bytes 6291460
  560.4 15.3 %copy-start.45 = (f32[1024]{0:T(1024)S(1)}, f32[1024]{0:T(1024)}, u32[]{:S(2)}) copy-start(f32[1024]{0:T(1024)} %copy-done.44) | copy-start | bytes 12292
  560.4 15.3 %copy-start.48 = (f32[4,1,256]{2,1,0:T(1,128)S(1)}, f32[4,1,256]{2,1,0:T(1,128)}, u32[]{:S(2)}) copy-start(f32[4,1,256]{2,1,0:T(1,128)} %copy-done.47) | copy-start | bytes 12292
  579.3 175.7 %reduce-scatter.10.cloned.1.call-start = ((), (), s32[]{:S(2)}) async-start(), calls=%async_computation.15 | async-start | bytes 1310720 | tf_op jit(solution)/shard_map/reduce_scatter | solution.py:287
  579.4 28.7 %copy-start.15 = (bf16[512,16,64]{0,2,1:T(8,128)(2,1)S(1)}, bf16[512,16,64]{0,2,1:T(8,128)(2,1)}, u32[]{:S(2)}) copy-start(bf16[512,16,64]{0,2,1:T(8,128)(2,1)} %copy-done.14) | copy-start | bytes 3145732
  620.3 27.5 %copy-start.17 = (bf16[512,16,64]{0,2,1:T(8,128)(2,1)S(1)}, bf16[512,16,64]{0,2,1:T(8,128)(2,1)}, u32[]{:S(2)}) copy-start(bf16[512,16,64]{0,2,1:T(8,128)(2,1)} %copy-done.16) | copy-start | bytes 3145732
  647.8 12.9 %copy-start.25 = (f32[1024,32]{0,1:T(8,128)S(1)}, f32[1024,32]{0,1:T(8,128)}, u32[]{:S(2)}) copy-start(f32[1024,32]{0,1:T(8,128)} %copy-done.24) | copy-start | bytes 393220
  647.8 12.9 %copy-start.27 = (f32[1024,32]{0,1:T(8,128)S(1)}, f32[1024,32]{0,1:T(8,128)}, u32[]{:S(2)}) copy-start(f32[1024,32]{0,1:T(8,128)} %copy-done.26) | copy-start | bytes 393220
  664.4 2.3 copy-start.35
  664.4 2.4 copy-start.55
  666.7 88.3 %reduce-scatter.14.cloned.1.call-start = ((), (), s32[]{:S(2)}) async-start(), calls=%async_computation.17 | async-start | bytes 2621440 | tf_op jit(solution)/shard_map/reduce_scatter | solution.py:296
  666.8 7.1 copy-start.11
  666.8 7.1 copy-start.13
  673.5 98.1 %reduce-scatter.8.cloned.1.call-start = ((), (), s32[]{:S(2)}) async-start(), calls=%async_computation.14 | async-start | bytes 2621440 | tf_op jit(solution)/shard_map/reduce_scatter | solution.py:284
  702.9 166.6 %reduce-scatter.16.cloned.1.call-start = ((), (), s32[]{:S(2)}) async-start(), calls=%async_computation.18 | async-start | bytes 11796480 | tf_op jit(solution)/shard_map/reduce_scatter | solution.py:196
  719.8 247.9 %reduce-scatter.18.cloned.1.call-start = ((), (), s32[]{:S(2)}) async-start(), calls=%async_computation.19 | async-start | bytes 11796480 | tf_op jit(solution)/shard_map/reduce_scatter | solution.py:199
  736.1 329.6 %reduce-scatter.20.cloned.1.call-start = ((), (), s32[]{:S(2)}) async-start(), calls=%async_computation.20 | async-start | bytes 11796480 | tf_op jit(solution)/shard_map/reduce_scatter | solution.py:202
  753.4 497.9 %all-reduce.9.cloned.1.call-start = ((), (), s32[]{:S(2)}) async-start(), calls=%async_computation.21 | async-start | bytes 17301504 | tf_op jit(solution)/shard_map/psum | solution.py:313
  1082.6 4.3 copy-start.36
  1086.9 2.6 copy-start.33
  1086.9 2.6 copy-start.60
  1089.6 2.4 copy-start.19
  1089.6 2.4 copy-start.34
  1092.0 3.6 copy-start.59
  1092.0 29.3 %copy-start.50 = (f32[1024]{0:T(1024)S(1)}, f32[1024]{0:T(1024)}, u32[]{:S(2)}) copy-start(f32[1024]{0:T(1024)} %get-tuple-element.96) | copy-start | bytes 12292
  1251.3 8.2 copy-start.30
  1257.2 5.0 copy-start.29
  1262.2 2.7 copy-start.28
  (16 other events, 23.1 us)
Sparse Core Ops, SparseCore 0:
  9.9 28.7 all-gather.11
  40.5 26.6 all-gather.9
  69.0 35.2 all-gather.13
  106.1 35.2 all-gather.15
  143.1 96.3 all-gather.19
  241.2 96.3 all-gather.17
  339.4 96.3 all-gather.21
  579.4 27.7 reduce-scatter.11
  666.8 27.5 reduce-scatter.9
  697.2 35.1 reduce-scatter.13
  736.3 35.1 reduce-scatter.7
  774.5 94.9 reduce-scatter.15
  872.6 95.0 reduce-scatter.17
  970.6 95.0 reduce-scatter.19
  1068.5 182.7 all-reduce.8
where the time goes:
time: 1280 us; the launch traced here: 1270 us
  waiting for transfers between devices  682 us (53%)
  matrix products  379 us (30%)
  other arithmetic  126 us (10%)
  blocking collectives  44.3 us (3%)
  local copies, waits for them, and re-layouts  25.2 us (2%)
  between operations  17.1 us (1%)
    psum x1, waiting for transfers between devices, body(): lax.psum(share_query.astype(jnp.bfloat16), 'rep').astype(jnp.float32)  120 us
    reduce_scatter x1, waiting for transfers between devices, body(): lax.psum_scatter(grad_w_up.astype(jnp.bfloat16), 'shard', scatter_dimensi...  98.2 us
    reduce_scatter x1, waiting for transfers between devices, body(): lax.psum_scatter(grad_w_down.astype(jnp.bfloat16), 'shard', scatter_dimen...  98 us
    reduce_scatter x1, waiting for transfers between devices, body(): lax.psum_scatter(grad_w_gate.astype(jnp.bfloat16), 'shard', scatter_dimen...  98 us
    all_gather x1, waiting for transfers between devices, body(): lax.all_gather(w_gate, 'shard', axis=0, tiled=True)  81.6 us
    all_gather x1, waiting for transfers between devices, body(): lax.all_gather(w_down, 'shard', axis=0, tiled=True)  81.1 us
    dot_general x7, matrix products, matmul_cols(): lax.dot_general(left_mat, right_mat, (((1,), (1,)), ((), ())), preferred_...  73.2 us
    dot_general x7, matrix products, matmul_plain(): return jnp.dot(left_mat, right_mat, preferred_element_type=jnp.float32)  65.6 us
  transfers between devices with their start and end apart: 15, of which 10 were waited for; matrix products, arithmetic and copies ran while one was open for 29% of the time, Pallas kernels for 0%

commit v1 on v0

--- a/solution.py
+++ b/solution.py
@@ -1,3 +1,4 @@
+import functools
 import math
 
 import jax
@@ -74,7 +75,166 @@
     )
 
 
+def make_links(mesh):
+    shard_size, rep_size = mesh.shape["shard"], mesh.shape["rep"]
+    axes = ("shard", "rep")
+
+    def shard_swap(value, bit):
+        pairs = [
+            (s * rep_size + r, (s ^ bit) * rep_size + r)
+            for s in range(shard_size)
+            for r in range(rep_size)
+        ]
+        return lax.ppermute(value, axes, pairs)
+
+    def rep_swap(value, bit):
+        pairs = [
+            (s * rep_size + r, s * rep_size + (r ^ bit))
+            for s in range(shard_size)
+            for r in range(rep_size)
+        ]
+        return lax.ppermute(value, axes, pairs)
+
+    return shard_size, rep_size, shard_swap, rep_swap
+
+
+def add_low(left, right):
+    return (left.astype(jnp.float32) + right.astype(jnp.float32)).astype(jnp.bfloat16)
+
+
+def gather_rows(links, weight):
+    shard_size, rep_size, shard_swap, rep_swap = links
+    me = lax.axis_index("shard")
+    core = lax.rem(lax.axis_index("rep"), 2)
+    half = weight.shape[0] // 2
+    quarter = half // 2
+    mine = lax.dynamic_slice_in_dim(weight, core * half, half, 0)
+    if shard_size == 4:
+        from_x = shard_swap(mine, 1)
+        from_y = shard_swap(mine, 2)
+        corner_a = shard_swap(from_x[:quarter], 2)
+        corner_b = shard_swap(from_y[quarter:], 1)
+        pieces = {1: from_x, 2: from_y, 3: jnp.concatenate([corner_a, corner_b], axis=0)}
+    else:
+        pieces = {0: mine}
+        bit = 1
+        while bit < shard_size:
+            order = sorted(pieces)
+            got = shard_swap(jnp.stack([pieces[d] for d in order]), bit)
+            for at, d in enumerate(order):
+                pieces[d ^ bit] = got[at]
+            bit *= 2
+        del pieces[0]
+    others = {d: rep_swap(piece, 1) for d, piece in pieces.items()}
+    full = jnp.zeros((shard_size, 2, half, weight.shape[1]), weight.dtype)
+    full = lax.dynamic_update_slice(
+        full, weight.reshape((1, 2, half, weight.shape[1])), (me, 0, 0, 0)
+    )
+    for d in pieces:
+        full = lax.dynamic_update_slice(full, pieces[d][None, None], (me ^ d, core, 0, 0))
+        full = lax.dynamic_update_slice(full, others[d][None, None], (me ^ d, 1 - core, 0, 0))
+    return full.reshape(shard_size * weight.shape[0], weight.shape[1])
+
+
+def scatter_sum(links, own, other):
+    shard_size, rep_size, shard_swap, rep_swap = links
+    me = lax.axis_index("shard")
+    rep = lax.axis_index("rep")
+    received = rep_swap(other().astype(jnp.bfloat16), 1)
+    part = (own() + received.astype(jnp.float32)).astype(jnp.bfloat16)
+    rows = part.shape[1] // 2
+
+    def piece(d, at):
+        return lax.dynamic_slice(
+            part, (me ^ d, at * rows, 0), (1, rows, part.shape[2])
+        )[0]
+
+    if shard_size == 4:
+        got_a = shard_swap(jnp.stack([piece(1, 0), piece(3, 0)]), 1)
+        got_b = shard_swap(jnp.stack([piece(2, 1), piece(3, 1)]), 2)
+        pass_a = shard_swap(add_low(piece(2, 0), got_a[1]), 2)
+        pass_b = shard_swap(add_low(piece(1, 1), got_b[1]), 1)
+        sum_a = add_low(piece(0, 0).astype(jnp.float32) + got_a[0].astype(jnp.float32), pass_a)
+        sum_b = add_low(piece(0, 1).astype(jnp.float32) + got_b[0].astype(jnp.float32), pass_b)
+        halves = [sum_a, sum_b]
+    else:
+        held = {d: jnp.stack([piece(d, 0), piece(d, 1)]) for d in range(shard_size)}
+        bit = shard_size // 2
+        while bit:
+            sent = [d for d in sorted(held) if d & bit]
+            got = shard_swap(jnp.stack([held[d] for d in sent]), bit)
+            held = {d ^ bit: add_low(held[d ^ bit], got[at]) for at, d in enumerate(sent)}
+            bit //= 2
+        halves = [held[0][0], held[0][1]]
+    upper = lax.rem(rep // 2, 2) == 1
+    if rep_size >= 8:
+        keep = jnp.where(upper, halves[1], halves[0])
+        send = jnp.where(upper, halves[0], halves[1])
+        keep = add_low(keep, rep_swap(send, 2))
+        bit = 4
+        while bit < rep_size:
+            keep = add_low(keep, rep_swap(keep, bit))
+            bit *= 2
+        back = rep_swap(keep, 2)
+        halves = [jnp.where(upper, back, keep), jnp.where(upper, keep, back)]
+        half = jnp.concatenate(halves, axis=0)
+    else:
+        half = jnp.concatenate(halves, axis=0)
+        bit = 2
+        while bit < rep_size:
+            half = add_low(half, rep_swap(half, bit))
+            bit *= 2
+    return half, rep_swap(half, 1)
+
+
+def join_rows(pair):
+    core = lax.rem(lax.axis_index("rep"), 2)
+    half, other = pair
+    return jnp.where(
+        core == 0,
+        jnp.concatenate([half, other], axis=0),
+        jnp.concatenate([other, half], axis=0),
+    ).astype(jnp.float32)
+
+
+def join_columns(pair):
+    core = lax.rem(lax.axis_index("rep"), 2)
+    half, other = pair
+    return jnp.where(
+        core == 0,
+        jnp.concatenate([half, other], axis=1),
+        jnp.concatenate([other, half], axis=1),
+    ).astype(jnp.float32)
+
+
+def row_halves(links, left_mat, right_mat):
+    shard_size = links[0]
+    core = lax.rem(lax.axis_index("rep"), 2)
+    count, width = left_mat.shape
+    cut = left_mat.reshape(count, shard_size, 2, width // shard_size // 2)
+
+    def half(which):
+        picked = lax.dynamic_slice_in_dim(cut, which, 1, 2)
+        product = matmul_rows(picked.reshape(count, width // 2), right_mat)
+        return product.reshape(shard_size, width // shard_size // 2, right_mat.shape[1])
+
+    return (lambda: half(core)), (lambda: half(1 - core))
+
+
+def column_halves(links, left_mat, right_mat):
+    shard_size = links[0]
+    core = lax.rem(lax.axis_index("rep"), 2)
+    width = right_mat.shape[1] // 2
+
+    def half(which):
+        picked = lax.dynamic_slice_in_dim(right_mat, which * width, width, 1)
+        return matmul_rows(left_mat, picked).reshape(shard_size, -1, width)
+
+    return (lambda: half(core)), (lambda: half(1 - core))
+
+
 def body(
+    links,
     tokens,
     cotangent,
     segment,
@@ -94,15 +254,21 @@
     score_scale = 1.0 / math.sqrt(HD)
     block_rows = min(512, row_count)
     block_count = row_count // block_rows
-    attn_set = (
-        lax.all_gather(attn_gain, "shard", axis=0, tiled=True),
-        lax.all_gather(w_query, "shard", axis=0, tiled=True),
-        lax.all_gather(w_key, "shard", axis=0, tiled=True),
-        lax.all_gather(w_value, "shard", axis=0, tiled=True),
-        lax.all_gather(qk_gain, "shard", axis=0, tiled=True),
-        lax.all_gather(w_out, "shard", axis=0, tiled=True),
-    )
-    full_attn_gain, full_query, full_key, full_value, full_qk_gain, full_out = attn_set
+    packed = jnp.zeros((attn_gain.shape[0], 128), jnp.bfloat16)
+    packed = packed.at[:, 0].set(attn_gain).at[:, 1].set(ffn_gain)
+    packed = packed.at[: qk_gain.shape[0], 2].set(qk_gain)
+    front = gather_rows(links, jnp.concatenate([w_query, w_key, w_value, packed], axis=1))
+    full_out = gather_rows(links, w_out)
+    full_gate = gather_rows(links, w_gate)
+    full_up = gather_rows(links, w_up)
+    full_down = gather_rows(links, w_down)
+    full_query = front[:, : HQ * HD]
+    full_key = front[:, HQ * HD : (HQ + HK) * HD]
+    full_value = front[:, (HQ + HK) * HD : (HQ + 2 * HK) * HD]
+    gains = front[:, (HQ + 2 * HK) * HD :]
+    full_attn_gain = gains[:, 0]
+    full_ffn_gain = gains[:, 1]
+    full_qk_gain = gains.reshape(links[0], -1, 128)[:, : qk_gain.shape[0], 2].reshape(-1)
     inputs = tokens.astype(jnp.float32)
     token_index = jnp.arange(row_count)
     same_seq = segment[:, None] == segment[None, :]
@@ -152,13 +318,6 @@
         jnp.concatenate(attended_parts, axis=0).astype(jnp.bfloat16).reshape(row_count, HQ * HD)
     )
     hidden = inputs + matmul_plain(attn_low, full_out)
-    ffn_set = (
-        lax.all_gather(ffn_gain, "shard", axis=0, tiled=True),
-        lax.all_gather(w_gate, "shard", axis=0, tiled=True),
-        lax.all_gather(w_up, "shard", axis=0, tiled=True),
-        lax.all_gather(w_down, "shard", axis=0, tiled=True),
-    )
-    full_ffn_gain, full_gate, full_up, full_down = ffn_set
     scale_two = inv_rms(hidden)
     normed_ffn = (hidden * scale_two * full_ffn_gain.astype(jnp.float32)).astype(jnp.bfloat16)
     gate_proj = matmul_plain(normed_ffn, full_gate)
@@ -167,58 +326,28 @@
     gate_act = gate_proj * gate_sig
     mixed_act = (gate_act * up_proj).astype(jnp.bfloat16)
     result = live_rows * (hidden + matmul_plain(mixed_act, full_down))
-    back_ffn = (
-        lax.all_gather(ffn_gain, "shard", axis=0, tiled=True),
-        lax.all_gather(w_gate, "shard", axis=0, tiled=True),
-        lax.all_gather(w_up, "shard", axis=0, tiled=True),
-        lax.all_gather(w_down, "shard", axis=0, tiled=True),
-    )
-    back_ffn_gain, back_gate, back_up, back_down = back_ffn
     out_grad = live_rows * cotangent.astype(jnp.float32)
     out_low = out_grad.astype(jnp.bfloat16)
-    grad_mixed = matmul_cols(out_low, back_down)
-    grad_w_down = matmul_rows(mixed_act, out_low)
+    grad_mixed = matmul_cols(out_low, full_down)
+    down_pair = scatter_sum(links, *column_halves(links, mixed_act, out_low))
     grad_up_low = (grad_mixed * gate_act).astype(jnp.bfloat16)
     grad_gate_low = (grad_mixed * up_proj * gate_sig * (1.0 + gate_proj * (1.0 - gate_sig))).astype(
         jnp.bfloat16
     )
-    grad_w_gate = matmul_rows(normed_ffn, grad_gate_low)
-    grad_w_up = matmul_rows(normed_ffn, grad_up_low)
-    grad_normed_ffn = matmul_cols(grad_gate_low, back_gate) + matmul_cols(grad_up_low, back_up)
+    gate_pair = scatter_sum(links, *row_halves(links, normed_ffn, grad_gate_low))
+    up_pair = scatter_sum(links, *row_halves(links, normed_ffn, grad_up_low))
+    grad_normed_ffn = matmul_cols(grad_gate_low, full_gate) + matmul_cols(grad_up_low, full_up)
     grad_ffn_gain = jnp.sum(grad_normed_ffn * hidden * scale_two, axis=0)
     grad_hidden = out_grad + norm_back(
-        grad_normed_ffn, hidden, scale_two, back_ffn_gain.astype(jnp.float32)
-    )
-    share_fgain, share_gate, share_up, share_down = (
-        lax.psum_scatter(
-            grad_ffn_gain.astype(jnp.bfloat16), "shard", scatter_dimension=0, tiled=True
-        ).astype(jnp.float32),
-        lax.psum_scatter(
-            grad_w_gate.astype(jnp.bfloat16), "shard", scatter_dimension=0, tiled=True
-        ).astype(jnp.float32),
-        lax.psum_scatter(
-            grad_w_up.astype(jnp.bfloat16), "shard", scatter_dimension=0, tiled=True
-        ).astype(jnp.float32),
-        lax.psum_scatter(
-            grad_w_down.astype(jnp.bfloat16), "shard", scatter_dimension=0, tiled=True
-        ).astype(jnp.float32),
-    )
-    back_attn = (
-        lax.all_gather(attn_gain, "shard", axis=0, tiled=True),
-        lax.all_gather(w_query, "shard", axis=0, tiled=True),
-        lax.all_gather(w_key, "shard", axis=0, tiled=True),
-        lax.all_gather(w_value, "shard", axis=0, tiled=True),
-        lax.all_gather(qk_gain, "shard", axis=0, tiled=True),
-        lax.all_gather(w_out, "shard", axis=0, tiled=True),
-    )
-    back_attn_gain, back_query, back_key, back_value, back_qk_gain, back_out = back_attn
+        grad_normed_ffn, hidden, scale_two, full_ffn_gain.astype(jnp.float32)
+    )
     hidden_low = grad_hidden.astype(jnp.bfloat16)
     grad_attn_low = (
-        matmul_cols(hidden_low, back_out)
+        matmul_cols(hidden_low, full_out)
         .astype(jnp.bfloat16)
         .reshape(row_count, HK, group_size, HD)
     )
-    grad_w_out = matmul_rows(attn_low, hidden_low)
+    out_pair = scatter_sum(links, *row_halves(links, attn_low, hidden_low))
     grad_query_parts = []
     grad_key_rot = jnp.zeros((row_count, HK, HD), jnp.float32)
     grad_value = jnp.zeros((row_count, HK, HD), jnp.float32)
@@ -247,7 +376,7 @@
     grad_query_rot = jnp.concatenate(grad_query_parts, axis=0).reshape(row_count, HQ, HD)
     grad_query_norm = rotate_back(grad_query_rot, cosine, sine_table)
     grad_key_norm = rotate_back(grad_key_rot, cosine, sine_table)
-    back_gains = back_qk_gain.astype(jnp.float32)
+    back_gains = full_qk_gain.astype(jnp.float32)
     grad_qk_gain = jnp.concatenate(
         [
             jnp.sum(grad_query_norm * query_lin * query_scale, axis=(0, 1)),
@@ -265,61 +394,47 @@
         .reshape(row_count, HK * HD)
     )
     grad_value_low = grad_value.astype(jnp.bfloat16).reshape(row_count, HK * HD)
-    grad_w_query = matmul_rows(normed, grad_query_low)
-    grad_w_key = matmul_rows(normed, grad_key_low)
-    grad_w_value = matmul_rows(normed, grad_value_low)
     grad_normed = (
-        matmul_cols(grad_query_low, back_query)
-        + matmul_cols(grad_key_low, back_key)
-        + matmul_cols(grad_value_low, back_value)
+        matmul_cols(grad_query_low, full_query)
+        + matmul_cols(grad_key_low, full_key)
+        + matmul_cols(grad_value_low, full_value)
     )
     grad_attn_gain = jnp.sum(grad_normed * inputs * scale_one, axis=0)
     grad_inputs = grad_hidden + norm_back(
-        grad_normed, inputs, scale_one, back_attn_gain.astype(jnp.float32)
-    )
-    share_again, share_query, share_key, share_value, share_qk, share_out = (
-        lax.psum_scatter(
-            grad_attn_gain.astype(jnp.bfloat16), "shard", scatter_dimension=0, tiled=True
-        ).astype(jnp.float32),
-        lax.psum_scatter(
-            grad_w_query.astype(jnp.bfloat16), "shard", scatter_dimension=0, tiled=True
-        ).astype(jnp.float32),
-        lax.psum_scatter(
-            grad_w_key.astype(jnp.bfloat16), "shard", scatter_dimension=0, tiled=True
-        ).astype(jnp.float32),
-        lax.psum_scatter(
-            grad_w_value.astype(jnp.bfloat16), "shard", scatter_dimension=0, tiled=True
-        ).astype(jnp.float32),
-        lax.psum_scatter(
-            grad_qk_gain.astype(jnp.bfloat16), "shard", scatter_dimension=0, tiled=True
-        ).astype(jnp.float32),
-        lax.psum_scatter(
-            grad_w_out.astype(jnp.bfloat16), "shard", scatter_dimension=0, tiled=True
-        ).astype(jnp.float32),
-    )
-    (
-        share_again,
-        share_query,
-        share_key,
-        share_value,
-        share_qk,
-        share_out,
-        share_fgain,
-        share_gate,
-        share_up,
-        share_down,
-    ) = (
-        lax.psum(share_again.astype(jnp.bfloat16), "rep").astype(jnp.float32),
-        lax.psum(share_query.astype(jnp.bfloat16), "rep").astype(jnp.float32),
-        lax.psum(share_key.astype(jnp.bfloat16), "rep").astype(jnp.float32),
-        lax.psum(share_value.astype(jnp.bfloat16), "rep").astype(jnp.float32),
-        lax.psum(share_qk.astype(jnp.bfloat16), "rep").astype(jnp.float32),
-        lax.psum(share_out.astype(jnp.bfloat16), "rep").astype(jnp.float32),
-        lax.psum(share_fgain.astype(jnp.bfloat16), "rep").astype(jnp.float32),
-        lax.psum(share_gate.astype(jnp.bfloat16), "rep").astype(jnp.float32),
-        lax.psum(share_up.astype(jnp.bfloat16), "rep").astype(jnp.float32),
-        lax.psum(share_down.astype(jnp.bfloat16), "rep").astype(jnp.float32),
-    )
+        grad_normed, inputs, scale_one, full_attn_gain.astype(jnp.float32)
+    )
+    small = jnp.zeros((links[0], attn_gain.shape[0], 128), jnp.float32)
+    small = small.at[:, :, 0].set(grad_attn_gain.reshape(links[0], -1))
+    small = small.at[:, :, 1].set(grad_ffn_gain.reshape(links[0], -1))
+    small = small.at[:, : qk_gain.shape[0], 2].set(grad_qk_gain.reshape(links[0], -1))
+    small = small.reshape(links[0], 2, -1, 128)
+    core = lax.rem(lax.axis_index("rep"), 2)
+    own_front, other_front = row_halves(
+        links, normed, jnp.concatenate([grad_query_low, grad_key_low, grad_value_low], axis=1)
+    )
+
+    def with_small(product, which):
+        extra = lax.dynamic_slice_in_dim(small, which, 1, 1)[:, 0]
+        return jnp.concatenate([product(), extra], axis=2)
+
+    front_share = join_rows(
+        scatter_sum(
+            links,
+            lambda: with_small(own_front, core),
+            lambda: with_small(other_front, 1 - core),
+        )
+    )
+    share_query = front_share[:, : HQ * HD]
+    share_key = front_share[:, HQ * HD : (HQ + HK) * HD]
+    share_value = front_share[:, (HQ + HK) * HD : (HQ + 2 * HK) * HD]
+    extras = front_share[:, (HQ + 2 * HK) * HD :]
+    share_again = extras[:, 0]
+    share_fgain = extras[:, 1]
+    share_qk = extras[: qk_gain.shape[0], 2]
+    share_out = join_rows(out_pair)
+    share_gate = join_rows(gate_pair)
+    share_up = join_rows(up_pair)
+    share_down = join_columns(down_pair)
     return (
         result.astype(jnp.bfloat16),
         grad_inputs.astype(jnp.bfloat16),
@@ -338,7 +453,7 @@
 
 def solution(mesh):
     return jax.shard_map(
-        body,
+        functools.partial(body, make_links(mesh)),
         mesh=mesh,
         in_specs=(
             P(("shard", "rep"), None),

time: 1280 us -> 1020 us (0.80)
  waiting for transfers between devices: 682 us -> 238 us
  starting transfers between devices: 1.39 us -> 100 us
  local copies, waits for them, and re-layouts: 25.2 us -> 110 us
  blocking collectives: 44.3 us -> 0 us
  other arithmetic: 126 us -> 166 us
  matrix products: 379 us -> 396 us
  between operations: 17.1 us -> 2.74 us
    reduce_scatter x7 -> x0, waiting for transfers between devices: 311 us -> none  [the longest x1 98.2 us: body(): lax.psum_scatter(grad_w_up.astype(jnp.bfloat16), 'shard', scatter_dimensi...]
    all_gather x7 -> x0, waiting for transfers between devices: 246 us -> none  [the longest x1 81.6 us: body(): lax.all_gather(w_gate, 'shard', axis=0, tiled=True)]
    ppermute x0 -> x80, waiting for transfers between devices: none -> 238 us  [the longest x40 145 us: shard_swap(): return lax.ppermute(value, axes, pairs)]
    psum x1 -> x0, waiting for transfers between devices: 120 us -> none  [body(): lax.psum(share_query.astype(jnp.bfloat16), 'rep').astype(jnp.float32)]
    ppermute x0 -> x80, starting transfers between devices: none -> 100 us  [the longest x40 69.8 us: rep_swap(): return lax.ppermute(value, axes, pairs)]
    dynamic_update_slice x0 -> x35, local copies, waits for them, and re-layouts: none -> 34 us  [the longest x15 16.9 us: gather_rows(): lax.dynamic_update_slice(full, pieces[d][None, None], (me ^ d, core, 0, 0))]
    psum x1 -> x0, blocking collectives: 16.5 us -> none  [body(): lax.psum(share_again.astype(jnp.bfloat16), 'rep').astype(jnp.float32)]
    unnamed x2 -> x0, blocking collectives: 16 us -> none
  transfers between devices with their start and end apart: 15 -> 80, of which waited for: 10 -> 26; matrix products, arithmetic and copies ran while one was open for 29% -> 33% of each run, Pallas kernels for 0% -> 0%
where the time goes in v1:
time: 1020 us; the launch traced here: 1010 us
  matrix products  396 us (39%)
  waiting for transfers between devices  238 us (23%)
  other arithmetic  166 us (16%)
  local copies, waits for them, and re-layouts  110 us (11%)
  starting transfers between devices  100 us (10%)
    ppermute x40, waiting for transfers between devices, shard_swap(): return lax.ppermute(value, axes, pairs)  145 us
    ppermute x40, waiting for transfers between devices, rep_swap(): return lax.ppermute(value, axes, pairs)  93.2 us
    dot_general x7, matrix products, matmul_plain(): return jnp.dot(left_mat, right_mat, preferred_element_type=jnp.float32)  80.3 us
    dot_general x10, matrix products, matmul_rows(): lax.dot_general(left_mat, right_mat, (((0,), (0,)), ((), ())), preferred_...  76.1 us
    ppermute x40, starting transfers between devices, rep_swap(): return lax.ppermute(value, axes, pairs)  69.8 us
    dot_general x7, matrix products, matmul_cols(): lax.dot_general(left_mat, right_mat, (((1,), (1,)), ((), ())), preferred_...  66.1 us
    convert_element_type x2, other arithmetic, body(): grad_scores = (attn_probs * (grad_probs - row_inner)).astype(jnp.bfloat16)  55.1 us
    dot_general x2, matrix products, body(): jnp.einsum('qgrd,kgd->grqk', grad_block, value_low, preferred_element_typ...  45.1 us
  transfers between devices with their start and end apart: 80, of which 26 were waited for; matrix products, arithmetic and copies ran while one was open for 33% of the time, Pallas kernels for 0%

profile of v1, /device:TPU:1, one launch (start us, length us, event | category | flops | bytes accessed | tf_op | source)
XLA Modules:
  0.0 1012.6 jit_solution(17695395001464057357)
XLA Ops:
  31.0 4.1 copy.106
  48.2 4.4 broadcast.326.clone.1
  56.6 4.8 broadcast_in_dim.193
  72.9 3.6 collective-permute-start.10
  87.6 16.6 %collective-permute-done.4 = bf16[64,2176]{1,0:T(8,128)(2,1)S(1)} collective-permute-done((bf16[64,2176]{1,0:T(8,128)(2,1)S(1)}, bf16[64,2176]{1,0:T(8,128)(2,1)S(1)}, u32[]{:S(2)}, u32[]{:S(2)}) %collective-permute-start.4) | collective-permute-done | bytes 278560 | tf_op jit(solution)/shard_map/ppermute | solution.py:88
  104.2 5.0 collective-permute-start.1
  120.5 16.6 %collective-permute-done.14 = bf16[128,4608]{1,0:T(8,128)(2,1)S(1)} collective-permute-done((bf16[128,4608]{1,0:T(8,128)(2,1)}, bf16[128,4608]{1,0:T(8,128)(2,1)S(1)}, u32[]{:S(2)}, u32[]{:S(2)}) %collective-permute-start.14) | collective-permute-done | bytes 1179680 | tf_op jit(solution)/shard_map/ppermute | solution.py:88
  142.4 12.3 %collective-permute-done.30 = bf16[576,1024]{1,0:T(8,128)(2,1)S(1)} collective-permute-done((bf16[576,1024]{1,0:T(8,128)(2,1)S(1)}, bf16[576,1024]{1,0:T(8,128)(2,1)S(1)}, u32[]{:S(2)}, u32[]{:S(2)}) %collective-permute-start.30) | collective-permute-done | bytes 1179680 | tf_op jit(solution)/shard_map/ppermute | solution.py:88
  156.4 6.0 collective-permute-done.28
  171.3 4.7 multiply_reduce_fusion.4
  180.9 13.6 %fusion.176 = (f32[8,2,512]{2,1,0:T(2,128)S(1)}, f32[8,2,512,1024]{2,3,1,0:T(8,128)}) fusion(bf16[512,8,2,64]{0,3,2,1:T(8,128)(2,1)S(1)} %bitcast.435, bf16[1024,8,32]{0,2,1:T(8,128)(2,1)S(1)} %get-tuple-element.189, bf16[1024,8,32]{0,2,1:T(8,128)(2,1)S(1)} %get-tuple-element.188, pred[512,1024]{0,1:T(8,128)(4,1)S(1)} %copy-done.33), kind=kOutput, calls=%fused_computation.400 | convolution fusion | flops 1100996608 | bytes 36208640 | tf_op jit(solution)/shard_map/qgrd,kgd->grqk/dot_general | solution.py:298
  194.5 13.1 %fusion.7 = f32[8,2,512]{2,1,0:T(2,128)S(1)} fusion(f32[8,2,512,1024]{2,3,1,0:T(8,128)} %get-tuple-element.241, f32[8,2,512]{2,1,0:T(2,128)S(1)} %get-tuple-element.240), kind=kLoop, calls=%fused_computation.19 | loop fusion | flops 16769024 | bytes 33619968 | tf_op jit(solution)/shard_map/reduce_sum | solution.py:311
  207.6 13.7 %fusion.77 = bf16[8,64,2,512]{3,1,2,0:T(8,128)(2,1)S(1)} fusion(bf16[1024,8,64,1]{0,2,3,1:T(8,128)(2,1)S(1)} %bitcast.463, f32[8,2,512,1024]{2,3,1,0:T(8,128)} %get-tuple-element.241, f32[8,2,512]{2,1,0:T(2,128)S(1)} %fusion.7, f32[8,2,512]{2,1,0:T(2,128)S(1)} %get-tuple-element.240), kind=kOutput, calls=%fused_computation.150 | convolution fusion | flops 1099431936 | bytes 35717120 | tf_op jit(solution)/shard_map/grqk,kgd->qgrd/dot_general | solution.py:315
  221.4 13.9 %fusion.177 = (f32[8,2,512]{2,1,0:T(2,128)S(1)}, f32[8,2,512,1024]{2,3,1,0:T(8,128)}) fusion(bf16[512,8,2,64]{0,3,2,1:T(8,128)(2,1)S(1)} %bitcast.433, bf16[1024,8,32]{0,2,1:T(8,128)(2,1)S(1)} %get-tuple-element.189, bf16[1024,8,32]{0,2,1:T(8,128)(2,1)S(1)} %get-tuple-element.188, pred[512,1024]{0,1:T(8,128)(4,1)S(1)} %copy-done.32), kind=kOutput, calls=%fused_computation.401 | convolution fusion | flops 1100996608 | bytes 36208640 | tf_op jit(solution)/shard_map/qgrd,kgd->grqk/dot_general | solution.py:298
  235.3 13.1 %fusion.6 = f32[8,2,512]{2,1,0:T(2,128)S(1)} fusion(f32[8,2,512,1024]{2,3,1,0:T(8,128)} %get-tuple-element.243, f32[8,2,512]{2,1,0:T(2,128)S(1)} %get-tuple-element.242), kind=kLoop, calls=%fused_computation.18 | loop fusion | flops 16769024 | bytes 33619968 | tf_op jit(solution)/shard_map/reduce_sum | solution.py:311
  248.5 13.8 %fusion.78 = bf16[8,64,2,512]{3,1,2,0:T(8,128)(2,1)S(1)} fusion(bf16[1024,8,64,1]{0,2,3,1:T(8,128)(2,1)S(1)} %bitcast.464, f32[8,2,512,1024]{2,3,1,0:T(8,128)} %get-tuple-element.243, f32[8,2,512]{2,1,0:T(2,128)S(1)} %fusion.6, f32[8,2,512]{2,1,0:T(2,128)S(1)} %get-tuple-element.242), kind=kOutput, calls=%fused_computation.151 | convolution fusion | flops 1099431936 | bytes 35717120 | tf_op jit(solution)/shard_map/grqk,kgd->qgrd/dot_general | solution.py:315
  275.6 7.8 collective-permute-done.32
  300.7 17.0 %fusion.179 = f32[1024,4608]{1,0:T(8,128)} fusion(bf16[1024,1024]{0,1:T(8,128)(2,1)} %fusion.47, bf16[4608,1024]{1,0:T(8,128)(2,1)} %bitcast.61), kind=kOutput, calls=%fused_computation.403 | convolution fusion | flops 9663676416 | bytes 30408704 | tf_op jit(solution)/shard_map/dot_general | solution.py:73
  319.0 16.4 %fusion.178 = f32[1024,4608]{1,0:T(8,128)} fusion(bf16[1024,1024]{0,1:T(8,128)(2,1)} %multiply_convert_fusion.4, bf16[1024,4608]{1,0:T(8,128)(2,1)S(1)} %bitcast.440), kind=kOutput, calls=%fused_computation.402 | convolution fusion | flops 9663676416 | bytes 30408704 | tf_op jit(solution)/shard_map/dot_general | solution.py:63
  337.8 36.7 %multiply_convert_fusion.1 = (bf16[1024,4608]{1,0:T(8,128)(2,1)}, bf16[1024,4608]{1,0:T(8,128)(2,1)}, bf16[1024,4608]{1,0:T(8,128)(2,1)}) fusion(f32[1024,4608]{1,0:T(8,128)} %fusion.179, f32[1024,4608]{1,0:T(8,128)} %fusion.178, bf16[1024,1024]{0,1:T(8,128)(2,1)} %multiply_convert_fusion.4, bf16[1024,4608]{1,0:T(8,128)(2,1)} %bitcast.45), kind=kOutput, calls=%fused_computation.23 | convolution fusion | flops 9734455296 | bytes 77594624 | tf_op jit(solution)/shard_map/dot_general | solution.py:63
  374.5 14.2 %fusion.180 = f32[1024,1024]{0,1:T(8,128)S(1)} fusion(bf16[1024,4608]{1,0:T(8,128)(2,1)} %get-tuple-element.156, bf16[1024,4608]{1,0:T(8,128)(2,1)} %bitcast.441), kind=kOutput, calls=%fused_computation.404 | convolution fusion | flops 9663676416 | bytes 23068672 | tf_op jit(solution)/shard_map/dot_general | solution.py:73
  388.7 17.1 %multiply_reduce_fusion = (f32[1024]{0:T(1024)}, f32[1024]{0:T(1024)S(1)}, f32[1024,1024]{0,1:T(8,128)S(1)}) fusion(f32[1024,1024]{0,1:T(8,128)S(1)} %copy-done.12, f32[1024]{0:T(1024)S(1)} %get-tuple-element.231, f32[1024]{0:T(1024)S(1)} %copy-done.76, f32[1024,1024]{0,1:T(8,128)S(1)} %fusion.180, bf16[1024,4608]{1,0:T(8,128)(2,1)} %get-tuple-element.155, ...), kind=kOutput, calls=%fused_computation.79 | convolution fusion | flops 9671014400 | bytes 31473664 | tf_op jit(solution)/shard_map/dot_general | solution.py:73
  410.9 22.2 %fusion.3 = (f32[8,2,512]{2,1,0:T(2,128)S(1)}, f32[8,1024,512,2]{2,1,3,0:T(8,128)}) fusion(f32[8,2,512,1024]{2,3,1,0:T(8,128)} %get-tuple-element.243, f32[8,2,512]{2,1,0:T(2,128)S(1)} %bitcast.487, bf16[1024,8,64,1]{0,2,3,1:T(8,128)(2,1)S(1)} %bitcast.465, bf16[512,8,2,64]{0,3,2,1:T(8,128)(2,1)S(1)} %bitcast.429), kind=kOutput, calls=%fused_computation.7 | convolution fusion | flops 1098899456 | bytes 69271552 | tf_op jit(solution)/shard_map/qgrd,kgd->grqk/dot_general | solution.py:361
  433.1 27.6 %fusion.5 = bf16[8,2,512,1024]{2,3,1,0:T(8,128)(2,1)} fusion(f32[8,1024,512,2]{2,1,3,0:T(8,128)} %get-tuple-element.250, f32[8,2,512,1024]{2,3,1,0:T(8,128)} %get-tuple-element.243, f32[8,2,512]{2,1,0:T(2,128)S(1)} %get-tuple-element.249, f32[8,2,512]{2,1,0:T(2,128)S(1)} %bitcast.488), kind=kLoop, calls=%fused_computation.9 | loop fusion | flops 33554432 | bytes 83951616 | tf_op jit(solution)/shard_map/convert_element_type | solution.py:365
  460.7 12.3 %fusion.181 = f32[8,64,1024,1]{2,1,3,0:T(8,128)} fusion(bf16[512,8,2,64]{0,3,2,1:T(8,128)(2,1)S(1)} %bitcast.434, bf16[8,2,512,1024]{2,3,1,0:T(8,128)(2,1)} %fusion.5), kind=kOutput, calls=%fused_computation.405 | convolution fusion | flops 1073741824 | bytes 19922944 | tf_op jit(solution)/shard_map/grqk,qgrd->kgd/dot_general | solution.py:370
  473.0 10.1 multiply_bitcast_fusion.1
  483.1 13.6 %fusion.11 = f32[8,64,1024,1]{2,1,3,0:T(8,128)S(1)} fusion(bf16[512,8,2,64]{0,3,2,1:T(8,128)(2,1)} %bitcast.431, f32[8,2,512,1024]{2,3,1,0:T(8,128)} %get-tuple-element.241, f32[8,2,512]{2,1,0:T(2,128)S(1)} %bitcast.484), kind=kOutput, calls=%fused_computation.27 | convolution fusion | flops 1090519040 | bytes 36732928 | tf_op jit(solution)/shard_map/grqk,qgrd->kgd/dot_general | solution.py:373
  496.7 22.9 %fusion = (f32[8,2,512]{2,1,0:T(2,128)S(1)}, f32[8,1024,512,2]{2,1,3,0:T(8,128)}) fusion(f32[8,2,512,1024]{2,3,1,0:T(8,128)} %get-tuple-element.241, f32[8,2,512]{2,1,0:T(2,128)S(1)} %bitcast.485, bf16[1024,8,64,1]{0,2,3,1:T(8,128)(2,1)} %bitcast.466, bf16[512,8,2,64]{0,3,2,1:T(8,128)(2,1)} %bitcast.432), kind=kOutput, calls=%fused_computation.2 | convolution fusion | flops 1098899456 | bytes 69271552 | tf_op jit(solution)/shard_map/qgrd,kgd->grqk/dot_general | solution.py:361
  519.5 14.6 %fusion.63 = bf16[8,64,1024]{2,1,0:T(8,128)(2,1)} fusion(f32[8,64,1024,1]{2,1,3,0:T(8,128)S(1)} %fusion.11, bf16[512,8,2,64]{0,3,2,1:T(8,128)(2,1)} %bitcast.430, f32[8,2,512,1024]{2,3,1,0:T(8,128)} %get-tuple-element.243, f32[8,2,512]{2,1,0:T(2,128)S(1)} %bitcast.489), kind=kOutput, calls=%fused_computation.124 | convolution fusion | flops 1091567616 | bytes 37781504 | tf_op jit(solution)/shard_map/grqk,qgrd->kgd/dot_general | solution.py:373
  534.1 27.5 %fusion.2 = bf16[8,2,512,1024]{2,3,1,0:T(8,128)(2,1)} fusion(f32[8,1024,512,2]{2,1,3,0:T(8,128)} %get-tuple-element.248, f32[8,2,512,1024]{2,3,1,0:T(8,128)} %get-tuple-element.241, f32[8,2,512]{2,1,0:T(2,128)S(1)} %get-tuple-element.247, f32[8,2,512]{2,1,0:T(2,128)S(1)} %bitcast.486), kind=kLoop, calls=%fused_computation.4 | loop fusion | flops 33554432 | bytes 83951616 | tf_op jit(solution)/shard_map/convert_element_type | solution.py:365
  561.7 10.2 %multiply_bitcast_fusion = f32[512,8,2,64]{0,3,2,1:T(8,128)} fusion(bf16[8,2,512,1024]{2,3,1,0:T(8,128)(2,1)} %fusion.2, bf16[1024,8,32]{0,2,1:T(8,128)(2,1)S(1)} %copy-done.17, bf16[1024,8,32]{0,2,1:T(8,128)(2,1)S(1)} %copy-done.15), kind=kOutput, calls=%fused_computation.136 | convolution fusion | flops 1076363264 | bytes 19922944 | tf_op jit(solution)/shard_map/grqk,kgd->qgrd/dot_general | solution.py:368
  571.9 12.5 %fusion.65 = f32[1024,8,64]{0,2,1:T(8,128)} fusion(f32[8,64,1024,1]{2,1,3,0:T(8,128)S(1)} %copy-done.13, bf16[512,8,2,64]{0,3,2,1:T(8,128)(2,1)} %bitcast.436, bf16[8,2,512,1024]{2,3,1,0:T(8,128)(2,1)} %fusion.2), kind=kOutput, calls=%fused_computation.131 | convolution fusion | flops 1074790400 | bytes 22020096 | tf_op jit(solution)/shard_map/grqk,qgrd->kgd/dot_general | solution.py:370
  596.2 6.9 convolution_convert_fusion.1
  603.1 6.8 fusion.51
  609.9 4.3 fusion.68
  617.9 7.8 fusion.46
  629.6 17.1 %multiply_convert_fusion.3 = bf16[1024,1024]{0,1:T(8,128)(2,1)} fusion(f32[1024,1024]{0,1:T(8,128)} %copy-done.11, f32[1024]{0:T(1024)S(1)} %copy-done.79, bf16[1024,4608]{1,0:T(8,128)(2,1)} %get-tuple-element.157, bf16[4608,1024]{1,0:T(8,128)(2,1)} %bitcast.61), kind=kOutput, calls=%fused_computation.86 | convolution fusion | flops 9666822144 | bytes 25169920 | tf_op jit(solution)/shard_map/dot_general | solution.py:63
  646.7 3.8 fusion.74
  651.4 10.7 %convolution_convert_fusion = bf16[4608,512]{1,0:T(8,128)(2,1)} fusion(bf16[1024,4608]{1,0:T(8,128)(2,1)} %get-tuple-element.157, bf16[1024,1024]{0,1:T(8,128)(2,1)S(1)} %copy-done.53, s32[]{:T(128)S(6)} %select_n.332), kind=kOutput, calls=%fused_computation.50 | convolution fusion | flops 4834197504 | bytes 15204356 | tf_op jit(solution)/shard_map/dot_general | solution.py:67
  667.7 12.1 %fusion.112 = f32[4608,512]{1,0:T(8,128)} fusion(bf16[1024,4608]{1,0:T(8,128)(2,1)} %get-tuple-element.157, bf16[1024,1024]{0,1:T(8,128)(2,1)S(1)} %copy-done.53, s32[]{:T(128)S(6)} %select_n.331), kind=kOutput, calls=%fused_computation.220 | convolution fusion | flops 4831838208 | bytes 19922948 | tf_op jit(solution)/shard_map/dot_general | solution.py:67
  686.0 6.7 fusion.27
  694.7 10.3 %fusion.30 = bf16[4,128,4608]{2,1,0:T(8,128)(2,1)} fusion(bf16[1024,4608]{1,0:T(8,128)(2,1)} %get-tuple-element.156, bf16[1024,4,2,128]{0,3,2,1:T(8,128)(2,1)S(1)} %bitcast.476, s32[]{:T(128)S(6)} %select_n.296), kind=kOutput, calls=%fused_computation.52 | convolution fusion | flops 4834197504 | bytes 15204356 | tf_op jit(solution)/shard_map/dot_general | solution.py:67
  710.7 3.9 copy.124
  715.2 7.8 collective-permute-done.50
  723.8 5.2 collective-permute-done.41
  733.3 3.7 collective-permute-done.42
  739.4 4.6 fusion.43
  744.0 3.9 copy.125
  753.9 10.5 %add_convert_fusion.1 = bf16[4,128,4608]{2,1,0:T(8,128)(2,1)S(1)} fusion(bf16[4,128,4608]{2,1,0:T(8,128)(2,1)} %collective-permute-done.62, bf16[1024,4608]{1,0:T(8,128)(2,1)} %get-tuple-element.156, bf16[1024,4,2,128]{0,3,2,1:T(8,128)(2,1)S(1)} %bitcast.477, s32[]{:T(128)S(6)} %select_n.295), kind=kOutput, calls=%fused_computation.42 | convolution fusion | flops 4838916096 | bytes 19922948 | tf_op jit(solution)/shard_map/dot_general | solution.py:67
  767.4 7.0 add_convert_fusion.2
  779.6 6.7 add_convert_fusion
  787.1 6.6 collective-permute-done.63
  797.6 21.3 %collective-permute-done.54 = bf16[2,64,4608]{2,1,0:T(8,128)(2,1)} collective-permute-done((bf16[2,64,4608]{2,1,0:T(8,128)(2,1)}, bf16[2,64,4608]{2,1,0:T(8,128)(2,1)}, u32[]{:S(2)}, u32[]{:S(2)}) %collective-permute-start.54) | collective-permute-done | bytes 1179680 | tf_op jit(solution)/shard_map/ppermute | solution.py:88
  822.9 21.2 %collective-permute-done.72 = bf16[2,576,512]{2,1,0:T(8,128)(2,1)S(1)} collective-permute-done((bf16[2,576,512]{2,1,0:T(8,128)(2,1)S(1)}, bf16[2,576,512]{2,1,0:T(8,128)(2,1)S(1)}, u32[]{:S(2)}, u32[]{:S(2)}) %collective-permute-start.72) | collective-permute-done | bytes 1179680 | tf_op jit(solution)/shard_map/ppermute | solution.py:88
  846.9 9.9 collective-permute-done.66
  860.2 9.2 collective-permute-done.57
  872.9 9.2 collective-permute-done.75
  888.0 24.7 %collective-permute-done.76 = bf16[576,512]{1,0:T(8,128)(2,1)S(1)} collective-permute-done((bf16[576,512]{1,0:T(8,128)(2,1)S(1)}, bf16[576,512]{1,0:T(8,128)(2,1)S(1)}, u32[]{:S(2)}, u32[]{:S(2)}) %collective-permute-start.76) | collective-permute-done | bytes 589856 | tf_op jit(solution)/shard_map/ppermute | solution.py:96
  915.0 35.6 %collective-permute-done.59 = bf16[64,4608]{1,0:T(8,128)(2,1)S(1)} collective-permute-done((bf16[64,4608]{1,0:T(8,128)(2,1)S(1)}, bf16[64,4608]{1,0:T(8,128)(2,1)S(1)}, u32[]{:S(2)}, u32[]{:S(2)}) %collective-permute-start.59) | collective-permute-done | bytes 589856 | tf_op jit(solution)/shard_map/ppermute | solution.py:96
  950.8 12.4 %collective-permute-done.77 = bf16[576,512]{1,0:T(8,128)(2,1)S(1)} collective-permute-done((bf16[576,512]{1,0:T(8,128)(2,1)S(1)}, bf16[576,512]{1,0:T(8,128)(2,1)S(1)}, u32[]{:S(2)}, u32[]{:S(2)}) %collective-permute-start.77) | collective-permute-done | bytes 589856 | tf_op jit(solution)/shard_map/ppermute | solution.py:96
  963.7 14.3 %collective-permute-start.70 = (bf16[128,4608]{1,0:T(8,128)(2,1)S(1)}, bf16[128,4608]{1,0:T(8,128)(2,1)S(1)}, u32[]{:S(2)}, u32[]{:S(2)}) collective-permute-start(bf16[128,4608]{1,0:T(8,128)(2,1)S(1)} %pad_maximum_fusion.9), channel_id=1, source_target_pairs={{0,1},{1,0},{2,3},{3,2},{4,5},{5,4},{6,7},{7,6},{8,9},{9,8},{10,11... | collective-permute-start | bytes 3538952 | tf_op jit(solution)/shard_map/ppermute | solution.py:96
  978.1 12.5 %collective-permute-start.61 = (bf16[128,4608]{1,0:T(8,128)(2,1)S(1)}, bf16[128,4608]{1,0:T(8,128)(2,1)S(1)}, u32[]{:S(2)}, u32[]{:S(2)}) collective-permute-start(bf16[128,4608]{1,0:T(8,128)(2,1)S(1)} %pad_maximum_fusion.6), channel_id=1, source_target_pairs={{0,1},{1,0},{2,3},{3,2},{4,5},{5,4},{6,7},{7,6},{8,9},{9,8},{10,11... | collective-permute-start | bytes 3538952 | tf_op jit(solution)/shard_map/ppermute | solution.py:96
  990.8 6.2 collective-permute-start.79
  1001.9 10.5 %fusion.50 = f32[1152,1024]{1,0:T(8,128)} fusion(bf16[1152,512]{1,0:T(8,128)(2,1)S(1)} %collective-permute-done.79, bf16[576,512]{1,0:T(8,128)(2,1)S(1)} %get-tuple-element.205, bf16[576,512]{1,0:T(8,128)(2,1)S(1)} %get-tuple-element.204, pred[]{:T(512)S(6)} %eq.13), kind=kLoop, calls=%fused_computation.106 | loop fusion | flops 16515072 | bytes 7077889 | tf_op jit(solution)/shard_map/convert_element_type | solution.py:207
  (556 shorter events, 234.6 us)
Async XLA Ops:
  2.3 61.2 %collective-permute-start.9 = (bf16[128,1024]{1,0:T(8,128)(2,1)}, bf16[128,1024]{1,0:T(8,128)(2,1)}, u32[]{:S(2)}, u32[]{:S(2)}) collective-permute-start(bf16[128,1024]{1,0:T(8,128)(2,1)} %constant_dynamic-slice_fusion.24), channel_id=1, source_target_pairs={{0,16},{1,17},{2,18},{3,19},{4,20},{5,21},{6,22},{7,23},{8,24},{9,... | collective-permute-start | bytes 786440 | tf_op jit(solution)/shard_map/ppermute | solution.py:88
  4.4 61.6 %collective-permute-start.7 = (bf16[128,1024]{1,0:T(8,128)(2,1)}, bf16[128,1024]{1,0:T(8,128)(2,1)}, u32[]{:S(2)}, u32[]{:S(2)}) collective-permute-start(bf16[128,1024]{1,0:T(8,128)(2,1)} %constant_dynamic-slice_fusion.24), channel_id=1, source_target_pairs={{0,8},{1,9},{2,10},{3,11},{4,12},{5,13},{6,14},{7,15},{8,0},{9,1},... | collective-permute-start | bytes 786440 | tf_op jit(solution)/shard_map/ppermute | solution.py:88
  17.2 66.0 %collective-permute-start.2 = (bf16[128,2176]{1,0:T(8,128)(2,1)}, bf16[128,2176]{1,0:T(8,128)(2,1)}, u32[]{:S(2)}, u32[]{:S(2)}) collective-permute-start(bf16[128,2176]{1,0:T(8,128)(2,1)} %constant_dynamic-slice_fusion.25), channel_id=1, source_target_pairs={{0,16},{1,17},{2,18},{3,19},{4,20},{5,21},{6,22},{7,23},{8,24},{9,... | collective-permute-start | bytes 1671176 | tf_op jit(solution)/shard_map/ppermute | solution.py:88
  17.4 62.8 %collective-permute-start = (bf16[128,2176]{1,0:T(8,128)(2,1)}, bf16[128,2176]{1,0:T(8,128)(2,1)}, u32[]{:S(2)}, u32[]{:S(2)}) collective-permute-start(bf16[128,2176]{1,0:T(8,128)(2,1)} %constant_dynamic-slice_fusion.25), channel_id=1, source_target_pairs={{0,8},{1,9},{2,10},{3,11},{4,12},{5,13},{6,14},{7,15},{8,0},{9,1},... | collective-permute-start | bytes 1671176 | tf_op jit(solution)/shard_map/ppermute | solution.py:88
  72.3 44.7 %collective-permute-start.23 = (bf16[128,4608]{1,0:T(8,128)(2,1)}, bf16[128,4608]{1,0:T(8,128)(2,1)S(1)}, u32[]{:S(2)}, u32[]{:S(2)}) collective-permute-start(bf16[128,4608]{1,0:T(8,128)(2,1)} %constant_dynamic-slice_fusion.22), channel_id=1, source_target_pairs={{0,16},{1,17},{2,18},{3,19},{4,20},{5,21},{6,22},{7,23},{8,24},{9,... | collective-permute-start | bytes 3538952 | tf_op jit(solution)/shard_map/ppermute | solution.py:88
  72.5 46.4 %collective-permute-start.21 = (bf16[128,4608]{1,0:T(8,128)(2,1)}, bf16[128,4608]{1,0:T(8,128)(2,1)S(1)}, u32[]{:S(2)}, u32[]{:S(2)}) collective-permute-start(bf16[128,4608]{1,0:T(8,128)(2,1)} %constant_dynamic-slice_fusion.22), channel_id=1, source_target_pairs={{0,8},{1,9},{2,10},{3,11},{4,12},{5,13},{6,14},{7,15},{8,0},{9,1},... | collective-permute-start | bytes 3538952 | tf_op jit(solution)/shard_map/ppermute | solution.py:88
  81.2 22.9 %collective-permute-start.4 = (bf16[64,2176]{1,0:T(8,128)(2,1)S(1)}, bf16[64,2176]{1,0:T(8,128)(2,1)S(1)}, u32[]{:S(2)}, u32[]{:S(2)}) collective-permute-start(bf16[64,2176]{1,0:T(8,128)(2,1)S(1)} %slice.392), channel_id=1, source_target_pairs={{0,16},{1,17},{2,18},{3,19},{4,20},{5,21},{6,22},{7,23},{8,24},{9,... | collective-permute-start | bytes 835592 | tf_op jit(solution)/shard_map/ppermute | solution.py:88
  83.2 56.9 %collective-permute-start.16 = (bf16[128,4608]{1,0:T(8,128)(2,1)}, bf16[128,4608]{1,0:T(8,128)(2,1)S(1)}, u32[]{:S(2)}, u32[]{:S(2)}) collective-permute-start(bf16[128,4608]{1,0:T(8,128)(2,1)} %constant_dynamic-slice_fusion.23), channel_id=1, source_target_pairs={{0,16},{1,17},{2,18},{3,19},{4,20},{5,21},{6,22},{7,23},{8,24},{9,... | collective-permute-start | bytes 3538952 | tf_op jit(solution)/shard_map/ppermute | solution.py:88
  85.7 23.5 %collective-permute-start.5 = (bf16[64,2176]{1,0:T(8,128)(2,1)S(1)}, bf16[64,2176]{1,0:T(8,128)(2,1)S(1)}, u32[]{:S(2)}, u32[]{:S(2)}) collective-permute-start(bf16[64,2176]{1,0:T(8,128)(2,1)S(1)} %slice.393), channel_id=1, source_target_pairs={{0,8},{1,9},{2,10},{3,11},{4,12},{5,13},{6,14},{7,15},{8,0},{9,1},... | collective-permute-start | bytes 835592 | tf_op jit(solution)/shard_map/ppermute | solution.py:88
  109.2 27.9 %collective-permute-start.14 = (bf16[128,4608]{1,0:T(8,128)(2,1)}, bf16[128,4608]{1,0:T(8,128)(2,1)S(1)}, u32[]{:S(2)}, u32[]{:S(2)}) collective-permute-start(bf16[128,4608]{1,0:T(8,128)(2,1)} %constant_dynamic-slice_fusion.23), channel_id=1, source_target_pairs={{0,8},{1,9},{2,10},{3,11},{4,12},{5,13},{6,14},{7,15},{8,0},{9,1},... | collective-permute-start | bytes 3538952 | tf_op jit(solution)/shard_map/ppermute | solution.py:88
  114.1 40.7 %collective-permute-start.30 = (bf16[576,1024]{1,0:T(8,128)(2,1)S(1)}, bf16[576,1024]{1,0:T(8,128)(2,1)S(1)}, u32[]{:S(2)}, u32[]{:S(2)}) collective-permute-start(bf16[576,1024]{1,0:T(8,128)(2,1)S(1)} %copy-done.62), channel_id=1, source_target_pairs={{0,16},{1,17},{2,18},{3,19},{4,20},{5,21},{6,22},{7,23},{8,24},{9,... | collective-permute-start | bytes 3538952 | tf_op jit(solution)/shard_map/ppermute | solution.py:88
  117.0 45.4 %collective-permute-start.28 = (bf16[576,1024]{1,0:T(8,128)(2,1)S(1)}, bf16[576,1024]{1,0:T(8,128)(2,1)S(1)}, u32[]{:S(2)}, u32[]{:S(2)}) collective-permute-start(bf16[576,1024]{1,0:T(8,128)(2,1)S(1)} %copy-done.62), channel_id=1, source_target_pairs={{0,8},{1,9},{2,10},{3,11},{4,12},{5,13},{6,14},{7,15},{8,0},{9,1},... | collective-permute-start | bytes 3538952 | tf_op jit(solution)/shard_map/ppermute | solution.py:88
  118.9 46.8 %collective-permute-start.6 = (bf16[128,2176]{1,0:T(8,128)(2,1)S(1)}, bf16[128,2176]{1,0:T(8,128)(2,1)S(1)}, u32[]{:S(2)}, u32[]{:S(2)}) collective-permute-start(bf16[128,2176]{1,0:T(8,128)(2,1)S(1)} %constant_dynamic-update-slice_fusion.6), channel_id=1, source_target_pairs={{0,1},{1,0},{2,3},{3,2},{4,5},{5,4},{6,7},{7,6},{8,9},{9,8},{10,11... | collective-permute-start | bytes 1671176 | tf_op jit(solution)/shard_map/ppermute | solution.py:96
  137.1 137.2 %collective-permute-start.26 = (bf16[64,4608]{1,0:T(8,128)(2,1)}, bf16[64,4608]{1,0:T(8,128)(2,1)}, u32[]{:S(2)}, u32[]{:S(2)}) collective-permute-start(bf16[64,4608]{1,0:T(8,128)(2,1)} %slice.414), channel_id=1, source_target_pairs={{0,8},{1,9},{2,10},{3,11},{4,12},{5,13},{6,14},{7,15},{8,0},{9,1},... | collective-permute-start | bytes 1769480 | tf_op jit(solution)/shard_map/ppermute | solution.py:88
  140.1 130.1 %collective-permute-start.25 = (bf16[64,4608]{1,0:T(8,128)(2,1)}, bf16[64,4608]{1,0:T(8,128)(2,1)}, u32[]{:S(2)}, u32[]{:S(2)}) collective-permute-start(bf16[64,4608]{1,0:T(8,128)(2,1)} %slice.413), channel_id=1, source_target_pairs={{0,16},{1,17},{2,18},{3,19},{4,20},{5,21},{6,22},{7,23},{8,24},{9,... | collective-permute-start | bytes 1769480 | tf_op jit(solution)/shard_map/ppermute | solution.py:88
  154.7 131.2 %collective-permute-start.19 = (bf16[64,4608]{1,0:T(8,128)(2,1)}, bf16[64,4608]{1,0:T(8,128)(2,1)}, u32[]{:S(2)}, u32[]{:S(2)}) collective-permute-start(bf16[64,4608]{1,0:T(8,128)(2,1)} %slice.412), channel_id=1, source_target_pairs={{0,8},{1,9},{2,10},{3,11},{4,12},{5,13},{6,14},{7,15},{8,0},{9,1},... | collective-permute-start | bytes 1769480 | tf_op jit(solution)/shard_map/ppermute | solution.py:88
  162.4 108.9 %collective-permute-start.18 = (bf16[64,4608]{1,0:T(8,128)(2,1)}, bf16[64,4608]{1,0:T(8,128)(2,1)}, u32[]{:S(2)}, u32[]{:S(2)}) collective-permute-start(bf16[64,4608]{1,0:T(8,128)(2,1)} %slice.411), channel_id=1, source_target_pairs={{0,16},{1,17},{2,18},{3,19},{4,20},{5,21},{6,22},{7,23},{8,24},{9,... | collective-permute-start | bytes 1769480 | tf_op jit(solution)/shard_map/ppermute | solution.py:88
  165.7 121.5 %collective-permute-start.33 = (bf16[288,1024]{1,0:T(8,128)(2,1)}, bf16[288,1024]{1,0:T(8,128)(2,1)}, u32[]{:S(2)}, u32[]{:S(2)}) collective-permute-start(bf16[288,1024]{1,0:T(8,128)(2,1)} %slice.416), channel_id=1, source_target_pairs={{0,8},{1,9},{2,10},{3,11},{4,12},{5,13},{6,14},{7,15},{8,0},{9,1},... | collective-permute-start | bytes 1769480 | tf_op jit(solution)/shard_map/ppermute | solution.py:88
  270.2 13.2 %collective-permute-start.32 = (bf16[288,1024]{1,0:T(8,128)(2,1)S(1)}, bf16[288,1024]{1,0:T(8,128)(2,1)S(1)}, u32[]{:S(2)}, u32[]{:S(2)}) collective-permute-start(bf16[288,1024]{1,0:T(8,128)(2,1)S(1)} %copy-done.67), channel_id=1, source_target_pairs={{0,16},{1,17},{2,18},{3,19},{4,20},{5,21},{6,22},{7,23},{8,24},{9,... | collective-permute-start | bytes 1769480 | tf_op jit(solution)/shard_map/ppermute | solution.py:88
  271.4 22.9 %collective-permute-start.24 = (bf16[128,4608]{1,0:T(8,128)(2,1)}, bf16[128,4608]{1,0:T(8,128)(2,1)S(1)}, u32[]{:S(2)}, u32[]{:S(2)}) collective-permute-start(bf16[128,4608]{1,0:T(8,128)(2,1)} %copy-done.44), channel_id=1, source_target_pairs={{0,1},{1,0},{2,3},{3,2},{4,5},{5,4},{6,7},{7,6},{8,9},{9,8},{10,11... | collective-permute-start | bytes 3538952 | tf_op jit(solution)/shard_map/ppermute | solution.py:96
  274.3 14.6 %collective-permute-start.29 = (bf16[576,1024]{1,0:T(8,128)(2,1)}, bf16[576,1024]{1,0:T(8,128)(2,1)S(1)}, u32[]{:S(2)}, u32[]{:S(2)}) collective-permute-start(bf16[576,1024]{1,0:T(8,128)(2,1)} %copy-done.52), channel_id=1, source_target_pairs={{0,1},{1,0},{2,3},{3,2},{4,5},{5,4},{6,7},{7,6},{8,9},{9,8},{10,11... | collective-permute-start | bytes 3538952 | tf_op jit(solution)/shard_map/ppermute | solution.py:96
  293.9 23.7 %collective-permute-start.27 = (bf16[128,4608]{1,0:T(8,128)(2,1)S(1)}, bf16[128,4608]{1,0:T(8,128)(2,1)}, u32[]{:S(2)}, u32[]{:S(2)}) collective-permute-start(bf16[128,4608]{1,0:T(8,128)(2,1)S(1)} %constant_dynamic-update-slice_fusion.12), channel_id=1, source_target_pairs={{0,1},{1,0},{2,3},{3,2},{4,5},{5,4},{6,7},{7,6},{8,9},{9,8},{10,11... | collective-permute-start | bytes 3538952 | tf_op jit(solution)/shard_map/ppermute | solution.py:96
  294.3 41.2 %collective-permute-start.20 = (bf16[128,4608]{1,0:T(8,128)(2,1)S(1)}, bf16[128,4608]{1,0:T(8,128)(2,1)}, u32[]{:S(2)}, u32[]{:S(2)}) collective-permute-start(bf16[128,4608]{1,0:T(8,128)(2,1)S(1)} %constant_dynamic-update-slice_fusion.10), channel_id=1, source_target_pairs={{0,1},{1,0},{2,3},{3,2},{4,5},{5,4},{6,7},{7,6},{8,9},{9,8},{10,11... | collective-permute-start | bytes 3538952 | tf_op jit(solution)/shard_map/ppermute | solution.py:96
  650.5 11.6 %collective-permute-start.44 = (bf16[4,128,1024]{2,1,0:T(8,128)(2,1)S(1)}, bf16[4,128,1024]{2,1,0:T(8,128)(2,1)S(1)}, u32[]{:S(2)}, u32[]{:S(2)}) collective-permute-start(bf16[4,128,1024]{2,1,0:T(8,128)(2,1)S(1)} %fusion.74), channel_id=1, source_target_pairs={{0,1},{1,0},{2,3},{3,2},{4,5},{5,4},{6,7},{7,6},{8,9},{9,8},{10,11... | collective-permute-start | bytes 3145736 | tf_op jit(solution)/shard_map/ppermute | solution.py:96
  650.9 14.2 %collective-permute-start.35 = (bf16[4,128,2176]{2,1,0:T(8,128)(2,1)S(1)}, bf16[4,128,2176]{2,1,0:T(8,128)(2,1)S(1)}, u32[]{:S(2)}, u32[]{:S(2)}) collective-permute-start(bf16[4,128,2176]{2,1,0:T(8,128)(2,1)S(1)} %pad_maximum_fusion.2), channel_id=1, source_target_pairs={{0,1},{1,0},{2,3},{3,2},{4,5},{5,4},{6,7},{7,6},{8,9},{9,8},{10,11... | collective-permute-start | bytes 6684680 | tf_op jit(solution)/shard_map/ppermute | solution.py:96
  663.5 16.3 %collective-permute-start.45 = (bf16[2,64,1024]{2,1,0:T(8,128)(2,1)S(1)}, bf16[2,64,1024]{2,1,0:T(8,128)(2,1)S(1)}, u32[]{:S(2)}, u32[]{:S(2)}) collective-permute-start(bf16[2,64,1024]{2,1,0:T(8,128)(2,1)S(1)} %pad_maximum_fusion.18), channel_id=1, source_target_pairs={{0,16},{1,17},{2,18},{3,19},{4,20},{5,21},{6,22},{7,23},{8,24},{9,... | collective-permute-start | bytes 786440 | tf_op jit(solution)/shard_map/ppermute | solution.py:88
  663.7 16.1 %collective-permute-start.47 = (bf16[2,64,1024]{2,1,0:T(8,128)(2,1)S(1)}, bf16[2,64,1024]{2,1,0:T(8,128)(2,1)S(1)}, u32[]{:S(2)}, u32[]{:S(2)}) collective-permute-start(bf16[2,64,1024]{2,1,0:T(8,128)(2,1)S(1)} %pad_maximum_fusion.19), channel_id=1, source_target_pairs={{0,8},{1,9},{2,10},{3,11},{4,12},{5,13},{6,14},{7,15},{8,0},{9,1},... | collective-permute-start | bytes 786440 | tf_op jit(solution)/shard_map/ppermute | solution.py:88
  665.9 17.7 %collective-permute-start.36 = (bf16[2,64,2176]{2,1,0:T(8,128)(2,1)S(1)}, bf16[2,64,2176]{2,1,0:T(8,128)(2,1)S(1)}, u32[]{:S(2)}, u32[]{:S(2)}) collective-permute-start(bf16[2,64,2176]{2,1,0:T(8,128)(2,1)S(1)} %pad_maximum_fusion.15), channel_id=1, source_target_pairs={{0,16},{1,17},{2,18},{3,19},{4,20},{5,21},{6,22},{7,23},{8,24},{9,... | collective-permute-start | bytes 1671176 | tf_op jit(solution)/shard_map/ppermute | solution.py:88
  667.2 16.3 %collective-permute-start.38 = (bf16[2,64,2176]{2,1,0:T(8,128)(2,1)S(1)}, bf16[2,64,2176]{2,1,0:T(8,128)(2,1)S(1)}, u32[]{:S(2)}, u32[]{:S(2)}) collective-permute-start(bf16[2,64,2176]{2,1,0:T(8,128)(2,1)S(1)} %pad_maximum_fusion.16), channel_id=1, source_target_pairs={{0,8},{1,9},{2,10},{3,11},{4,12},{5,13},{6,14},{7,15},{8,0},{9,1},... | collective-permute-start | bytes 1671176 | tf_op jit(solution)/shard_map/ppermute | solution.py:88
  679.9 12.9 %collective-permute-start.48 = (bf16[64,1024]{1,0:T(8,128)(2,1)S(1)}, bf16[64,1024]{1,0:T(8,128)(2,1)S(1)}, u32[]{:S(2)}, u32[]{:S(2)}) collective-permute-start(bf16[64,1024]{1,0:T(8,128)(2,1)S(1)} %get-tuple-element.210), channel_id=1, source_target_pairs={{0,16},{1,17},{2,18},{3,19},{4,20},{5,21},{6,22},{7,23},{8,24},{9,... | collective-permute-start | bytes 393224 | tf_op jit(solution)/shard_map/ppermute | solution.py:88
  680.2 12.5 %collective-permute-start.46 = (bf16[64,1024]{1,0:T(8,128)(2,1)S(1)}, bf16[64,1024]{1,0:T(8,128)(2,1)S(1)}, u32[]{:S(2)}, u32[]{:S(2)}) collective-permute-start(bf16[64,1024]{1,0:T(8,128)(2,1)S(1)} %get-tuple-element.211), channel_id=1, source_target_pairs={{0,8},{1,9},{2,10},{3,11},{4,12},{5,13},{6,14},{7,15},{8,0},{9,1},... | collective-permute-start | bytes 393224 | tf_op jit(solution)/shard_map/ppermute | solution.py:88
  692.9 15.1 %collective-permute-start.49 = (bf16[64,1024]{1,0:T(8,128)(2,1)S(1)}, bf16[64,1024]{1,0:T(8,128)(2,1)S(1)}, u32[]{:S(2)}, u32[]{:S(2)}) collective-permute-start(bf16[64,1024]{1,0:T(8,128)(2,1)S(1)} %get-tuple-element.149), channel_id=1, source_target_pairs={{0,2},{1,3},{2,0},{3,1},{4,6},{5,7},{6,4},{7,5},{8,10},{9,11},{10,... | collective-permute-start | bytes 393224 | tf_op jit(solution)/shard_map/ppermute | solution.py:96
  694.5 15.9 %collective-permute-start.40 = (bf16[64,2176]{1,0:T(8,128)(2,1)S(1)}, bf16[64,2176]{1,0:T(8,128)(2,1)S(1)}, u32[]{:S(2)}, u32[]{:S(2)}) collective-permute-start(bf16[64,2176]{1,0:T(8,128)(2,1)S(1)} %get-tuple-element.152), channel_id=1, source_target_pairs={{0,2},{1,3},{2,0},{3,1},{4,6},{5,7},{6,4},{7,5},{8,10},{9,11},{10,... | collective-permute-start | bytes 835592 | tf_op jit(solution)/shard_map/ppermute | solution.py:96
  705.0 48.9 %collective-permute-start.62 = (bf16[4,128,4608]{2,1,0:T(8,128)(2,1)}, bf16[4,128,4608]{2,1,0:T(8,128)(2,1)}, u32[]{:S(2)}, u32[]{:S(2)}) collective-permute-start(bf16[4,128,4608]{2,1,0:T(8,128)(2,1)} %fusion.30), channel_id=1, source_target_pairs={{0,1},{1,0},{2,3},{3,2},{4,5},{5,4},{6,7},{7,6},{8,9},{9,8},{10,11... | collective-permute-start | bytes 14155784 | tf_op jit(solution)/shard_map/ppermute | solution.py:96
  708.1 14.9 %collective-permute-start.50 = (bf16[64,1024]{1,0:T(8,128)(2,1)S(1)}, bf16[64,1024]{1,0:T(8,128)(2,1)S(1)}, u32[]{:S(2)}, u32[]{:S(2)}) collective-permute-start(bf16[64,1024]{1,0:T(8,128)(2,1)S(1)} %add_convert_fusion.23), channel_id=1, source_target_pairs={{0,4},{1,5},{2,6},{3,7},{4,0},{5,1},{6,2},{7,3},{8,12},{9,13},{10,... | collective-permute-start | bytes 393224 | tf_op jit(solution)/shard_map/ppermute | solution.py:96
  710.5 18.4 %collective-permute-start.41 = (bf16[64,2176]{1,0:T(8,128)(2,1)S(1)}, bf16[64,2176]{1,0:T(8,128)(2,1)S(1)}, u32[]{:S(2)}, u32[]{:S(2)}) collective-permute-start(bf16[64,2176]{1,0:T(8,128)(2,1)S(1)} %add_convert_fusion.19), channel_id=1, source_target_pairs={{0,4},{1,5},{2,6},{3,7},{4,0},{5,1},{6,2},{7,3},{8,12},{9,13},{10,... | collective-permute-start | bytes 835592 | tf_op jit(solution)/shard_map/ppermute | solution.py:96
  714.6 52.8 %collective-permute-start.53 = (bf16[4,128,4608]{2,1,0:T(8,128)(2,1)}, bf16[4,128,4608]{2,1,0:T(8,128)(2,1)}, u32[]{:S(2)}, u32[]{:S(2)}) collective-permute-start(bf16[4,128,4608]{2,1,0:T(8,128)(2,1)} %fusion.27), channel_id=1, source_target_pairs={{0,1},{1,0},{2,3},{3,2},{4,5},{5,4},{6,7},{7,6},{8,9},{9,8},{10,11... | collective-permute-start | bytes 14155784 | tf_op jit(solution)/shard_map/ppermute | solution.py:96
  715.2 64.4 %collective-permute-start.71 = (bf16[4,1152,512]{2,1,0:T(8,128)(2,1)}, bf16[4,1152,512]{2,1,0:T(8,128)(2,1)}, u32[]{:S(2)}, u32[]{:S(2)}) collective-permute-start(bf16[4,1152,512]{2,1,0:T(8,128)(2,1)} %bitcast.495), channel_id=1, source_target_pairs={{0,1},{1,0},{2,3},{3,2},{4,5},{5,4},{6,7},{7,6},{8,9},{9,8},{10,11... | collective-permute-start | bytes 14155784 | tf_op jit(solution)/shard_map/ppermute | solution.py:96
  732.7 15.2 %collective-permute-start.52 = (bf16[128,1024]{1,0:T(8,128)(2,1)}, bf16[128,1024]{1,0:T(8,128)(2,1)}, u32[]{:S(2)}, u32[]{:S(2)}) collective-permute-start(bf16[128,1024]{1,0:T(8,128)(2,1)} %pad_maximum_fusion.20), channel_id=1, source_target_pairs={{0,1},{1,0},{2,3},{3,2},{4,5},{5,4},{6,7},{7,6},{8,9},{9,8},{10,11... | collective-permute-start | bytes 786440 | tf_op jit(solution)/shard_map/ppermute | solution.py:96
  737.9 12.2 %collective-permute-start.43 = (bf16[128,2176]{1,0:T(8,128)(2,1)}, bf16[128,2176]{1,0:T(8,128)(2,1)S(1)}, u32[]{:S(2)}, u32[]{:S(2)}) collective-permute-start(bf16[128,2176]{1,0:T(8,128)(2,1)} %pad_maximum_fusion.17), channel_id=1, source_target_pairs={{0,1},{1,0},{2,3},{3,2},{4,5},{5,4},{6,7},{7,6},{8,9},{9,8},{10,11... | collective-permute-start | bytes 1671176 | tf_op jit(solution)/shard_map/ppermute | solution.py:96
  765.7 27.9 %collective-permute-start.63 = (bf16[2,64,4608]{2,1,0:T(8,128)(2,1)}, bf16[2,64,4608]{2,1,0:T(8,128)(2,1)}, u32[]{:S(2)}, u32[]{:S(2)}) collective-permute-start(bf16[2,64,4608]{2,1,0:T(8,128)(2,1)} %pad_maximum_fusion.7), channel_id=1, source_target_pairs={{0,16},{1,17},{2,18},{3,19},{4,20},{5,21},{6,22},{7,23},{8,24},{9,... | collective-permute-start | bytes 3538952 | tf_op jit(solution)/shard_map/ppermute | solution.py:88
  767.3 27.6 %collective-permute-start.65 = (bf16[2,64,4608]{2,1,0:T(8,128)(2,1)}, bf16[2,64,4608]{2,1,0:T(8,128)(2,1)}, u32[]{:S(2)}, u32[]{:S(2)}) collective-permute-start(bf16[2,64,4608]{2,1,0:T(8,128)(2,1)} %pad_maximum_fusion.8), channel_id=1, source_target_pairs={{0,8},{1,9},{2,10},{3,11},{4,12},{5,13},{6,14},{7,15},{8,0},{9,1},... | collective-permute-start | bytes 3538952 | tf_op jit(solution)/shard_map/ppermute | solution.py:88
  776.0 42.9 %collective-permute-start.54 = (bf16[2,64,4608]{2,1,0:T(8,128)(2,1)}, bf16[2,64,4608]{2,1,0:T(8,128)(2,1)}, u32[]{:S(2)}, u32[]{:S(2)}) collective-permute-start(bf16[2,64,4608]{2,1,0:T(8,128)(2,1)} %pad_maximum_fusion.4), channel_id=1, source_target_pairs={{0,16},{1,17},{2,18},{3,19},{4,20},{5,21},{6,22},{7,23},{8,24},{9,... | collective-permute-start | bytes 3538952 | tf_op jit(solution)/shard_map/ppermute | solution.py:88
  778.4 41.8 %collective-permute-start.56 = (bf16[2,64,4608]{2,1,0:T(8,128)(2,1)}, bf16[2,64,4608]{2,1,0:T(8,128)(2,1)}, u32[]{:S(2)}, u32[]{:S(2)}) collective-permute-start(bf16[2,64,4608]{2,1,0:T(8,128)(2,1)} %pad_maximum_fusion.5), channel_id=1, source_target_pairs={{0,8},{1,9},{2,10},{3,11},{4,12},{5,13},{6,14},{7,15},{8,0},{9,1},... | collective-permute-start | bytes 3538952 | tf_op jit(solution)/shard_map/ppermute | solution.py:88
  786.6 57.5 %collective-permute-start.72 = (bf16[2,576,512]{2,1,0:T(8,128)(2,1)S(1)}, bf16[2,576,512]{2,1,0:T(8,128)(2,1)S(1)}, u32[]{:S(2)}, u32[]{:S(2)}) collective-permute-start(bf16[2,576,512]{2,1,0:T(8,128)(2,1)S(1)} %pad_maximum_fusion.10), channel_id=1, source_target_pairs={{0,16},{1,17},{2,18},{3,19},{4,20},{5,21},{6,22},{7,23},{8,24},{9,... | collective-permute-start | bytes 3538952 | tf_op jit(solution)/shard_map/ppermute | solution.py:88
  793.7 51.7 %collective-permute-start.74 = (bf16[2,576,512]{2,1,0:T(8,128)(2,1)S(1)}, bf16[2,576,512]{2,1,0:T(8,128)(2,1)S(1)}, u32[]{:S(2)}, u32[]{:S(2)}) collective-permute-start(bf16[2,576,512]{2,1,0:T(8,128)(2,1)S(1)} %pad_maximum_fusion.11), channel_id=1, source_target_pairs={{0,8},{1,9},{2,10},{3,11},{4,12},{5,13},{6,14},{7,15},{8,0},{9,1},... | collective-permute-start | bytes 3538952 | tf_op jit(solution)/shard_map/ppermute | solution.py:88
  796.4 60.4 %collective-permute-start.66 = (bf16[64,4608]{1,0:T(8,128)(2,1)S(1)}, bf16[64,4608]{1,0:T(8,128)(2,1)S(1)}, u32[]{:S(2)}, u32[]{:S(2)}) collective-permute-start(bf16[64,4608]{1,0:T(8,128)(2,1)S(1)} %get-tuple-element.166), channel_id=1, source_target_pairs={{0,16},{1,17},{2,18},{3,19},{4,20},{5,21},{6,22},{7,23},{8,24},{9,... | collective-permute-start | bytes 1769480 | tf_op jit(solution)/shard_map/ppermute | solution.py:88
  818.9 39.0 %collective-permute-start.64 = (bf16[64,4608]{1,0:T(8,128)(2,1)S(1)}, bf16[64,4608]{1,0:T(8,128)(2,1)S(1)}, u32[]{:S(2)}, u32[]{:S(2)}) collective-permute-start(bf16[64,4608]{1,0:T(8,128)(2,1)S(1)} %get-tuple-element.167), channel_id=1, source_target_pairs={{0,8},{1,9},{2,10},{3,11},{4,12},{5,13},{6,14},{7,15},{8,0},{9,1},... | collective-permute-start | bytes 1769480 | tf_op jit(solution)/shard_map/ppermute | solution.py:88
  821.7 47.7 %collective-permute-start.57 = (bf16[64,4608]{1,0:T(8,128)(2,1)S(1)}, bf16[64,4608]{1,0:T(8,128)(2,1)S(1)}, u32[]{:S(2)}, u32[]{:S(2)}) collective-permute-start(bf16[64,4608]{1,0:T(8,128)(2,1)S(1)} %get-tuple-element.172), channel_id=1, source_target_pairs={{0,16},{1,17},{2,18},{3,19},{4,20},{5,21},{6,22},{7,23},{8,24},{9,... | collective-permute-start | bytes 1769480 | tf_op jit(solution)/shard_map/ppermute | solution.py:88
  844.1 26.5 %collective-permute-start.55 = (bf16[64,4608]{1,0:T(8,128)(2,1)S(1)}, bf16[64,4608]{1,0:T(8,128)(2,1)S(1)}, u32[]{:S(2)}, u32[]{:S(2)}) collective-permute-start(bf16[64,4608]{1,0:T(8,128)(2,1)S(1)} %get-tuple-element.173), channel_id=1, source_target_pairs={{0,8},{1,9},{2,10},{3,11},{4,12},{5,13},{6,14},{7,15},{8,0},{9,1},... | collective-permute-start | bytes 1769480 | tf_op jit(solution)/shard_map/ppermute | solution.py:88
  845.7 36.4 %collective-permute-start.75 = (bf16[576,512]{1,0:T(8,128)(2,1)S(1)}, bf16[576,512]{1,0:T(8,128)(2,1)S(1)}, u32[]{:S(2)}, u32[]{:S(2)}) collective-permute-start(bf16[576,512]{1,0:T(8,128)(2,1)S(1)} %get-tuple-element.160), channel_id=1, source_target_pairs={{0,16},{1,17},{2,18},{3,19},{4,20},{5,21},{6,22},{7,23},{8,24},{9,... | collective-permute-start | bytes 1769480 | tf_op jit(solution)/shard_map/ppermute | solution.py:88
  856.8 26.5 %collective-permute-start.73 = (bf16[576,512]{1,0:T(8,128)(2,1)S(1)}, bf16[576,512]{1,0:T(8,128)(2,1)S(1)}, u32[]{:S(2)}, u32[]{:S(2)}) collective-permute-start(bf16[576,512]{1,0:T(8,128)(2,1)S(1)} %get-tuple-element.161), channel_id=1, source_target_pairs={{0,8},{1,9},{2,10},{3,11},{4,12},{5,13},{6,14},{7,15},{8,0},{9,1},... | collective-permute-start | bytes 1769480 | tf_op jit(solution)/shard_map/ppermute | solution.py:88
  859.7 24.6 %collective-permute-start.67 = (bf16[64,4608]{1,0:T(8,128)(2,1)S(1)}, bf16[64,4608]{1,0:T(8,128)(2,1)S(1)}, u32[]{:S(2)}, u32[]{:S(2)}) collective-permute-start(bf16[64,4608]{1,0:T(8,128)(2,1)S(1)} %get-tuple-element.143), channel_id=1, source_target_pairs={{0,2},{1,3},{2,0},{3,1},{4,6},{5,7},{6,4},{7,5},{8,10},{9,11},{10,... | collective-permute-start | bytes 1769480 | tf_op jit(solution)/shard_map/ppermute | solution.py:96
  872.4 15.3 %collective-permute-start.58 = (bf16[64,4608]{1,0:T(8,128)(2,1)S(1)}, bf16[64,4608]{1,0:T(8,128)(2,1)S(1)}, u32[]{:S(2)}, u32[]{:S(2)}) collective-permute-start(bf16[64,4608]{1,0:T(8,128)(2,1)S(1)} %get-tuple-element.146), channel_id=1, source_target_pairs={{0,2},{1,3},{2,0},{3,1},{4,6},{5,7},{6,4},{7,5},{8,10},{9,11},{10,... | collective-permute-start | bytes 1769480 | tf_op jit(solution)/shard_map/ppermute | solution.py:96
  883.8 28.8 %collective-permute-start.76 = (bf16[576,512]{1,0:T(8,128)(2,1)S(1)}, bf16[576,512]{1,0:T(8,128)(2,1)S(1)}, u32[]{:S(2)}, u32[]{:S(2)}) collective-permute-start(bf16[576,512]{1,0:T(8,128)(2,1)S(1)} %get-tuple-element.140), channel_id=1, source_target_pairs={{0,2},{1,3},{2,0},{3,1},{4,6},{5,7},{6,4},{7,5},{8,10},{9,11},{10,... | collective-permute-start | bytes 1769480 | tf_op jit(solution)/shard_map/ppermute | solution.py:96
  884.5 28.4 %collective-permute-start.68 = (bf16[64,4608]{1,0:T(8,128)(2,1)S(1)}, bf16[64,4608]{1,0:T(8,128)(2,1)S(1)}, u32[]{:S(2)}, u32[]{:S(2)}) collective-permute-start(bf16[64,4608]{1,0:T(8,128)(2,1)S(1)} %add_convert_fusion.10), channel_id=1, source_target_pairs={{0,4},{1,5},{2,6},{3,7},{4,0},{5,1},{6,2},{7,3},{8,12},{9,13},{10,... | collective-permute-start | bytes 1769480 | tf_op jit(solution)/shard_map/ppermute | solution.py:96
  887.9 62.7 %collective-permute-start.59 = (bf16[64,4608]{1,0:T(8,128)(2,1)S(1)}, bf16[64,4608]{1,0:T(8,128)(2,1)S(1)}, u32[]{:S(2)}, u32[]{:S(2)}) collective-permute-start(bf16[64,4608]{1,0:T(8,128)(2,1)S(1)} %add_convert_fusion.14), channel_id=1, source_target_pairs={{0,4},{1,5},{2,6},{3,7},{4,0},{5,1},{6,2},{7,3},{8,12},{9,13},{10,... | collective-permute-start | bytes 1769480 | tf_op jit(solution)/shard_map/ppermute | solution.py:96
  912.8 50.4 %collective-permute-start.77 = (bf16[576,512]{1,0:T(8,128)(2,1)S(1)}, bf16[576,512]{1,0:T(8,128)(2,1)S(1)}, u32[]{:S(2)}, u32[]{:S(2)}) collective-permute-start(bf16[576,512]{1,0:T(8,128)(2,1)S(1)} %add_convert_fusion.6), channel_id=1, source_target_pairs={{0,4},{1,5},{2,6},{3,7},{4,0},{5,1},{6,2},{7,3},{8,12},{9,13},{10,... | collective-permute-start | bytes 1769480 | tf_op jit(solution)/shard_map/ppermute | solution.py:96
  913.1 50.4 %collective-permute-start.69 = (bf16[64,4608]{1,0:T(8,128)(2,1)S(1)}, bf16[64,4608]{1,0:T(8,128)(2,1)S(1)}, u32[]{:S(2)}, u32[]{:S(2)}) collective-permute-start(bf16[64,4608]{1,0:T(8,128)(2,1)S(1)} %add_convert_fusion.9), channel_id=1, source_target_pairs={{0,2},{1,3},{2,0},{3,1},{4,6},{5,7},{6,4},{7,5},{8,10},{9,11},{10,... | collective-permute-start | bytes 1769480 | tf_op jit(solution)/shard_map/ppermute | solution.py:96
  950.7 27.2 %collective-permute-start.60 = (bf16[64,4608]{1,0:T(8,128)(2,1)S(1)}, bf16[64,4608]{1,0:T(8,128)(2,1)S(1)}, u32[]{:S(2)}, u32[]{:S(2)}) collective-permute-start(bf16[64,4608]{1,0:T(8,128)(2,1)S(1)} %add_convert_fusion.13), channel_id=1, source_target_pairs={{0,2},{1,3},{2,0},{3,1},{4,6},{5,7},{6,4},{7,5},{8,10},{9,11},{10,... | collective-permute-start | bytes 1769480 | tf_op jit(solution)/shard_map/ppermute | solution.py:96
  963.4 27.2 %collective-permute-start.78 = (bf16[576,512]{1,0:T(8,128)(2,1)S(1)}, bf16[576,512]{1,0:T(8,128)(2,1)S(1)}, u32[]{:S(2)}, u32[]{:S(2)}) collective-permute-start(bf16[576,512]{1,0:T(8,128)(2,1)S(1)} %add_convert_fusion.5), channel_id=1, source_target_pairs={{0,2},{1,3},{2,0},{3,1},{4,6},{5,7},{6,4},{7,5},{8,10},{9,11},{10,... | collective-permute-start | bytes 1769480 | tf_op jit(solution)/shard_map/ppermute | solution.py:96
  963.7 33.4 %collective-permute-start.70 = (bf16[128,4608]{1,0:T(8,128)(2,1)S(1)}, bf16[128,4608]{1,0:T(8,128)(2,1)S(1)}, u32[]{:S(2)}, u32[]{:S(2)}) collective-permute-start(bf16[128,4608]{1,0:T(8,128)(2,1)S(1)} %pad_maximum_fusion.9), channel_id=1, source_target_pairs={{0,1},{1,0},{2,3},{3,2},{4,5},{5,4},{6,7},{7,6},{8,9},{9,8},{10,11... | collective-permute-start | bytes 3538952 | tf_op jit(solution)/shard_map/ppermute | solution.py:96
  978.1 21.3 %collective-permute-start.61 = (bf16[128,4608]{1,0:T(8,128)(2,1)S(1)}, bf16[128,4608]{1,0:T(8,128)(2,1)S(1)}, u32[]{:S(2)}, u32[]{:S(2)}) collective-permute-start(bf16[128,4608]{1,0:T(8,128)(2,1)S(1)} %pad_maximum_fusion.6), channel_id=1, source_target_pairs={{0,1},{1,0},{2,3},{3,2},{4,5},{5,4},{6,7},{7,6},{8,9},{9,8},{10,11... | collective-permute-start | bytes 3538952 | tf_op jit(solution)/shard_map/ppermute | solution.py:96
  990.8 11.1 %collective-permute-start.79 = (bf16[1152,512]{1,0:T(8,128)(2,1)S(1)}, bf16[1152,512]{1,0:T(8,128)(2,1)S(1)}, u32[]{:S(2)}, u32[]{:S(2)}) collective-permute-start(bf16[1152,512]{1,0:T(8,128)(2,1)S(1)} %pad_maximum_fusion.12), channel_id=1, source_target_pairs={{0,1},{1,0},{2,3},{3,2},{4,5},{5,4},{6,7},{7,6},{8,9},{9,8},{10,11... | collective-permute-start | bytes 3538952 | tf_op jit(solution)/shard_map/ppermute | solution.py:96
  (122 other events, 2046.5 us)

commit v2 on v1

--- a/solution.py
+++ b/solution.py
@@ -4,6 +4,8 @@
 import jax
 import jax.numpy as jnp
 from jax import lax
+from jax.experimental import pallas as pl
+from jax.experimental.pallas import tpu as pltpu
 from jax.sharding import PartitionSpec as P
 
 HQ = 16
@@ -102,46 +104,85 @@
     return (left.astype(jnp.float32) + right.astype(jnp.float32)).astype(jnp.bfloat16)
 
 
-def gather_rows(links, weight):
+def pin(values, *waits):
+    return lax.optimization_barrier((values, waits))[0]
+
+
+class Flow:
+    def __init__(self, steps):
+        self.steps = steps
+        self.pending = ()
+        self.result = None
+        self.advance()
+
+    def advance(self):
+        try:
+            self.pending = next(self.steps)
+        except StopIteration as stop:
+            self.pending = ()
+            if stop.value is not None:
+                self.result = stop.value
+
+    def finish(self):
+        while self.result is None:
+            self.advance()
+        return self.result
+
+
+def gather_steps(links, mine, whole):
     shard_size, rep_size, shard_swap, rep_swap = links
     me = lax.axis_index("shard")
     core = lax.rem(lax.axis_index("rep"), 2)
-    half = weight.shape[0] // 2
+    half, width = mine.shape
     quarter = half // 2
-    mine = lax.dynamic_slice_in_dim(weight, core * half, half, 0)
+    pieces, others = {}, {}
     if shard_size == 4:
-        from_x = shard_swap(mine, 1)
-        from_y = shard_swap(mine, 2)
-        corner_a = shard_swap(from_x[:quarter], 2)
-        corner_b = shard_swap(from_y[quarter:], 1)
-        pieces = {1: from_x, 2: from_y, 3: jnp.concatenate([corner_a, corner_b], axis=0)}
+        pieces[1] = shard_swap(mine, 1)
+        pieces[2] = shard_swap(mine, 2)
+        yield (pieces[1], pieces[2])
+        corner_a = shard_swap(pieces[1][:quarter], 2)
+        corner_b = shard_swap(pieces[2][quarter:], 1)
+        others[1] = rep_swap(pieces[1], 1)
+        others[2] = rep_swap(pieces[2], 1)
+        yield (corner_a, corner_b, others[1], others[2])
+        pieces[3] = jnp.concatenate([corner_a, corner_b], axis=0)
+        others[3] = rep_swap(pieces[3], 1)
+        yield (others[3],)
     else:
-        pieces = {0: mine}
+        pieces[0] = mine
         bit = 1
         while bit < shard_size:
             order = sorted(pieces)
             got = shard_swap(jnp.stack([pieces[d] for d in order]), bit)
+            yield (got,)
             for at, d in enumerate(order):
                 pieces[d ^ bit] = got[at]
             bit *= 2
         del pieces[0]
-    others = {d: rep_swap(piece, 1) for d, piece in pieces.items()}
-    full = jnp.zeros((shard_size, 2, half, weight.shape[1]), weight.dtype)
-    full = lax.dynamic_update_slice(
-        full, weight.reshape((1, 2, half, weight.shape[1])), (me, 0, 0, 0)
-    )
+        others = {d: rep_swap(piece, 1) for d, piece in pieces.items()}
+    full = jnp.zeros((shard_size, 2, half, width), mine.dtype)
+    full = lax.dynamic_update_slice(full, whole.reshape((1, 2, half, width)), (me, 0, 0, 0))
     for d in pieces:
         full = lax.dynamic_update_slice(full, pieces[d][None, None], (me ^ d, core, 0, 0))
         full = lax.dynamic_update_slice(full, others[d][None, None], (me ^ d, 1 - core, 0, 0))
-    return full.reshape(shard_size * weight.shape[0], weight.shape[1])
-
-
-def scatter_sum(links, own, other):
+    return full.reshape(shard_size * 2 * half, width)
+
+
+def core_half(weight):
+    core = lax.rem(lax.axis_index("rep"), 2)
+    half = weight.shape[0] // 2
+    return lax.dynamic_slice_in_dim(weight, core * half, half, 0)
+
+
+def core_sum(links, own, other):
+    received = links[3](other().astype(jnp.bfloat16), 1)
+    return (own() + received.astype(jnp.float32)).astype(jnp.bfloat16)
+
+
+def scatter_steps(links, part):
     shard_size, rep_size, shard_swap, rep_swap = links
     me = lax.axis_index("shard")
     rep = lax.axis_index("rep")
-    received = rep_swap(other().astype(jnp.bfloat16), 1)
-    part = (own() + received.astype(jnp.float32)).astype(jnp.bfloat16)
     rows = part.shape[1] // 2
 
     def piece(d, at):
@@ -152,8 +193,10 @@
     if shard_size == 4:
         got_a = shard_swap(jnp.stack([piece(1, 0), piece(3, 0)]), 1)
         got_b = shard_swap(jnp.stack([piece(2, 1), piece(3, 1)]), 2)
+        yield (got_a, got_b)
         pass_a = shard_swap(add_low(piece(2, 0), got_a[1]), 2)
         pass_b = shard_swap(add_low(piece(1, 1), got_b[1]), 1)
+        yield (pass_a, pass_b)
         sum_a = add_low(piece(0, 0).astype(jnp.float32) + got_a[0].astype(jnp.float32), pass_a)
         sum_b = add_low(piece(0, 1).astype(jnp.float32) + got_b[0].astype(jnp.float32), pass_b)
         halves = [sum_a, sum_b]
@@ -163,6 +206,7 @@
         while bit:
             sent = [d for d in sorted(held) if d & bit]
             got = shard_swap(jnp.stack([held[d] for d in sent]), bit)
+            yield (got,)
             held = {d ^ bit: add_low(held[d ^ bit], got[at]) for at, d in enumerate(sent)}
             bit //= 2
         halves = [held[0][0], held[0][1]]
@@ -170,12 +214,17 @@
     if rep_size >= 8:
         keep = jnp.where(upper, halves[1], halves[0])
         send = jnp.where(upper, halves[0], halves[1])
-        keep = add_low(keep, rep_swap(send, 2))
+        got = rep_swap(send, 2)
+        yield (got,)
+        keep = add_low(keep, got)
         bit = 4
         while bit < rep_size:
-            keep = add_low(keep, rep_swap(keep, bit))
+            got = rep_swap(keep, bit)
+            yield (got,)
+            keep = add_low(keep, got)
             bit *= 2
         back = rep_swap(keep, 2)
+        yield (back,)
         halves = [jnp.where(upper, back, keep), jnp.where(upper, keep, back)]
         half = jnp.concatenate(halves, axis=0)
     else:
@@ -231,6 +280,210 @@
         return matmul_rows(left_mat, picked).reshape(shard_size, -1, width)
 
     return (lambda: half(core)), (lambda: half(1 - core))
+
+
+BLOCK = 256
+LOOK = 3
+
+
+def nt_dot(left_mat, right_mat):
+    return lax.dot_general(
+        left_mat, right_mat, (((1,), (1,)), ((), ())), preferred_element_type=jnp.float32
+    )
+
+
+def attend_kernel(live_ref, q_ref, k_ref, v_ref, seg_col_ref, seg_row_ref, o_ref, acc_ref):
+    at = pl.program_id(1)
+    acc_ref[...] = jnp.zeros_like(acc_ref)
+    lane = lax.broadcasted_iota(jnp.int32, (BLOCK, 2 * HD), 1)
+    low_lane = lane < HD
+    for back in range(LOOK):
+        key_block = jnp.maximum(at - back, 0)
+
+        @pl.when((at >= back) & (live_ref[at, key_block] > 0))
+        def _():
+            begin = pl.multiple_of(key_block * BLOCK, BLOCK)
+            same = seg_col_ref[...] == seg_row_ref[:, pl.ds(begin, BLOCK)]
+            if back == 0:
+                row = lax.broadcasted_iota(jnp.int32, (BLOCK, BLOCK), 0)
+                col = lax.broadcasted_iota(jnp.int32, (BLOCK, BLOCK), 1)
+                same = same & (col <= row)
+            mask = same.astype(jnp.float32)
+            keys = k_ref[pl.ds(begin, BLOCK), :]
+            values = v_ref[pl.ds(begin, BLOCK), :]
+            swapped = pltpu.roll(values.astype(jnp.float32), HD, 1).astype(jnp.bfloat16)
+            one = jnp.ones_like(values)
+            for head in range(4):
+                group, odd = head // 2, head % 2
+                scores = nt_dot(
+                    q_ref[:, head * HD : (head + 1) * HD], keys[:, group * HD : (group + 1) * HD]
+                )
+                weights = (jnp.exp(scores) * mask).astype(jnp.bfloat16)
+                held = values if group == odd else swapped
+                padded = jnp.where(low_lane, held, one) if odd == 0 else jnp.where(low_lane, one, held)
+                acc_ref[head] += jnp.dot(weights, padded, preferred_element_type=jnp.float32)
+
+    for group in range(2):
+        even, odd = acc_ref[2 * group], acc_ref[2 * group + 1]
+        top = jnp.where(low_lane, even, odd)
+        total = pltpu.roll(jnp.where(low_lane, odd, even), HD, 1)
+        o_ref[:, group * 2 * HD : (group + 1) * 2 * HD] = (top / total).astype(o_ref.dtype)
+
+
+def attend_back_kernel(
+    live_ref, q_ref, do_ref, k_ref, v_ref, seg_col_ref, seg_row_ref,
+    dq_ref, dk_ref, dv_ref, exp_ref, dp_ref, total_ref, inner_ref, dqt_ref,
+):
+    at = pl.program_id(1)
+
+    @pl.when(at == 0)
+    def _():
+        dk_ref[...] = jnp.zeros_like(dk_ref)
+        dv_ref[...] = jnp.zeros_like(dv_ref)
+
+    total_ref[...] = jnp.zeros_like(total_ref)
+    inner_ref[...] = jnp.zeros_like(inner_ref)
+    dqt_ref[...] = jnp.zeros_like(dqt_ref)
+
+    def each_block(run):
+        for back in range(LOOK):
+            key_block = jnp.maximum(at - back, 0)
+
+            @pl.when((at >= back) & (live_ref[at, key_block] > 0))
+            def _():
+                run(back, pl.multiple_of(key_block * BLOCK, BLOCK))
+
+    def first(back, begin):
+        same = seg_col_ref[pl.ds(begin, BLOCK), :] == seg_row_ref[...]
+        if back == 0:
+            row = lax.broadcasted_iota(jnp.int32, (BLOCK, BLOCK), 0)
+            col = lax.broadcasted_iota(jnp.int32, (BLOCK, BLOCK), 1)
+            same = same & (row <= col)
+        mask = same.astype(jnp.float32)
+        keys = k_ref[pl.ds(begin, BLOCK), :]
+        values = v_ref[pl.ds(begin, BLOCK), :]
+        for head in range(4):
+            group = head // 2
+            cols = slice(head * HD, (head + 1) * HD)
+            kept = slice(group * HD, (group + 1) * HD)
+            weights = jnp.exp(nt_dot(keys[:, kept], q_ref[:, cols])) * mask
+            grads = nt_dot(values[:, kept], do_ref[:, cols])
+            exp_ref[head, back] = weights
+            dp_ref[head, back] = grads
+            total_ref[head : head + 1] += jnp.sum(weights, axis=0, keepdims=True)
+            inner_ref[head : head + 1] += jnp.sum(weights * grads, axis=0, keepdims=True)
+
+    def second(back, begin):
+        keys = k_ref[pl.ds(begin, BLOCK), :]
+        dk_parts, dv_parts = [], []
+        for group in range(2):
+            dk_sum, dv_sum = None, None
+            for head in (2 * group, 2 * group + 1):
+                cols = slice(head * HD, (head + 1) * HD)
+                scale = 1.0 / total_ref[head : head + 1]
+                probs = exp_ref[head, back] * scale
+                inner = inner_ref[head : head + 1] * scale
+                low_scores = (probs * (dp_ref[head, back] - inner)).astype(jnp.bfloat16)
+                dv_part = jnp.dot(
+                    probs.astype(jnp.bfloat16), do_ref[:, cols], preferred_element_type=jnp.float32
+                )
+                dk_part = jnp.dot(low_scores, q_ref[:, cols], preferred_element_type=jnp.float32)
+                dqt_ref[cols] += lax.dot_general(
+                    keys[:, group * HD : (group + 1) * HD],
+                    low_scores,
+                    (((0,), (0,)), ((), ())),
+                    preferred_element_type=jnp.float32,
+                )
+                dk_sum = dk_part if dk_sum is None else dk_sum + dk_part
+                dv_sum = dv_part if dv_sum is None else dv_sum + dv_part
+            dk_parts.append(dk_sum)
+            dv_parts.append(dv_sum)
+        dk_ref[pl.ds(begin, BLOCK), :] += jnp.concatenate(dk_parts, axis=1)
+        dv_ref[pl.ds(begin, BLOCK), :] += jnp.concatenate(dv_parts, axis=1)
+
+    each_block(first)
+    each_block(second)
+    dq_ref[...] = dqt_ref[...].T
+
+
+def live_blocks(segment):
+    count = segment.shape[0] // BLOCK
+    blocks = segment.reshape(count, BLOCK)
+    index = jnp.arange(count)
+    return (
+        (blocks[:, :1] == blocks[:, -1][None, :]) | (index[:, None] == index[None, :])
+    ).astype(jnp.int32)
+
+
+def attend(query, key, value, segment):
+    rows = query.shape[0]
+    panels, count = HK // 2, rows // BLOCK
+    return pl.pallas_call(
+        attend_kernel,
+        out_shape=jax.ShapeDtypeStruct((rows, HQ * HD), jnp.bfloat16),
+        grid_spec=pltpu.PrefetchScalarGridSpec(
+            num_scalar_prefetch=1,
+            grid=(panels, count),
+            in_specs=[
+                pl.BlockSpec((BLOCK, 4 * HD), lambda p, i, live: (i, p)),
+                pl.BlockSpec((rows, 2 * HD), lambda p, i, live: (0, p)),
+                pl.BlockSpec((rows, 2 * HD), lambda p, i, live: (0, p)),
+                pl.BlockSpec((BLOCK, 1), lambda p, i, live: (i, 0)),
+                pl.BlockSpec((1, rows), lambda p, i, live: (0, 0)),
+            ],
+            out_specs=pl.BlockSpec((BLOCK, 4 * HD), lambda p, i, live: (i, p)),
+            scratch_shapes=[pltpu.VMEM((4, BLOCK, 2 * HD), jnp.float32)],
+        ),
+        cost_estimate=pl.CostEstimate(
+            flops=24 * rows * BLOCK * LOOK * HQ * HD,
+            bytes_accessed=8 * rows * HQ * HD,
+            transcendentals=rows * BLOCK * LOOK * HQ,
+        ),
+        name="attend",
+    )(live_blocks(segment), query, key, value, segment[:, None], segment[None, :])
+
+
+def attend_back(query, grad_out, key, value, segment, start, panels):
+    rows = query.shape[0]
+    count = rows // BLOCK
+    return pl.pallas_call(
+        attend_back_kernel,
+        out_shape=(
+            jax.ShapeDtypeStruct((rows, panels * 4 * HD), jnp.float32),
+            jax.ShapeDtypeStruct((rows, panels * 2 * HD), jnp.float32),
+            jax.ShapeDtypeStruct((rows, panels * 2 * HD), jnp.float32),
+        ),
+        grid_spec=pltpu.PrefetchScalarGridSpec(
+            num_scalar_prefetch=1,
+            grid=(panels, count),
+            in_specs=[
+                pl.BlockSpec((BLOCK, 4 * HD), lambda p, i, live: (i, start + p)),
+                pl.BlockSpec((BLOCK, 4 * HD), lambda p, i, live: (i, start + p)),
+                pl.BlockSpec((rows, 2 * HD), lambda p, i, live: (0, start + p)),
+                pl.BlockSpec((rows, 2 * HD), lambda p, i, live: (0, start + p)),
+                pl.BlockSpec((rows, 1), lambda p, i, live: (0, 0)),
+                pl.BlockSpec((1, BLOCK), lambda p, i, live: (0, i)),
+            ],
+            out_specs=[
+                pl.BlockSpec((BLOCK, 4 * HD), lambda p, i, live: (i, p)),
+                pl.BlockSpec((rows, 2 * HD), lambda p, i, live: (0, p)),
+                pl.BlockSpec((rows, 2 * HD), lambda p, i, live: (0, p)),
+            ],
+            scratch_shapes=[
+                pltpu.VMEM((4, LOOK, BLOCK, BLOCK), jnp.float32),
+                pltpu.VMEM((4, LOOK, BLOCK, BLOCK), jnp.float32),
+                pltpu.VMEM((8, BLOCK), jnp.float32),
+                pltpu.VMEM((8, BLOCK), jnp.float32),
+                pltpu.VMEM((4 * HD, BLOCK), jnp.float32),
+            ],
+        ),
+        cost_estimate=pl.CostEstimate(
+            flops=160 * rows * BLOCK * LOOK * HD * panels,
+            bytes_accessed=64 * rows * HD * panels,
+            transcendentals=4 * rows * BLOCK * LOOK * panels,
+        ),
+        name="attend_back",
+    )(live_blocks(segment), query, grad_out, key, value, segment[:, None], segment[None, :])
 
 
 def body(
@@ -250,18 +503,23 @@
     w_down,
 ):
     row_count = tokens.shape[0]
-    group_size = HQ // HK
     score_scale = 1.0 / math.sqrt(HD)
-    block_rows = min(512, row_count)
-    block_count = row_count // block_rows
-    packed = jnp.zeros((attn_gain.shape[0], 128), jnp.bfloat16)
-    packed = packed.at[:, 0].set(attn_gain).at[:, 1].set(ffn_gain)
-    packed = packed.at[: qk_gain.shape[0], 2].set(qk_gain)
-    front = gather_rows(links, jnp.concatenate([w_query, w_key, w_value, packed], axis=1))
-    full_out = gather_rows(links, w_out)
-    full_gate = gather_rows(links, w_gate)
-    full_up = gather_rows(links, w_up)
-    full_down = gather_rows(links, w_down)
+    spare = jnp.zeros((attn_gain.shape[0] - qk_gain.shape[0],), jnp.bfloat16)
+    packed = jnp.stack([attn_gain, ffn_gain, jnp.concatenate([qk_gain, spare])], axis=1)
+    packed = jnp.pad(packed, ((0, 0), (0, 125)))
+    attn_weights = (w_query, w_key, w_value, packed)
+    front_flow = Flow(
+        gather_steps(
+            links,
+            jnp.concatenate([core_half(weight) for weight in attn_weights], axis=1),
+            jnp.concatenate(attn_weights, axis=1),
+        )
+    )
+    out_flow = Flow(gather_steps(links, pin(core_half(w_out), front_flow.pending), w_out))
+    front_flow.advance()
+    gate_flow = Flow(gather_steps(links, pin(core_half(w_gate), out_flow.pending), w_gate))
+    out_flow.advance()
+    front = front_flow.finish()
     full_query = front[:, : HQ * HD]
     full_key = front[:, HQ * HD : (HQ + HK) * HD]
     full_value = front[:, (HQ + HK) * HD : (HQ + 2 * HK) * HD]
@@ -289,34 +547,23 @@
     query_rot = (
         rotate(query_lin * query_scale * qk_gains[:HD], cosine, sine_table)
         .astype(jnp.bfloat16)
-        .reshape(row_count, HK, group_size, HD)
     )
     key_rot = rotate(key_lin * key_scale * qk_gains[HD:], cosine, sine_table).astype(jnp.bfloat16)
 
-    def block_scores(begin_row):
-        query_block = query_rot[begin_row : begin_row + block_rows]
-        raw_scores = score_scale * jnp.einsum(
-            "qgrd,kgd->grqk", query_block, key_rot, preferred_element_type=jnp.float32
-        )
-        mask_block = allowed[begin_row : begin_row + block_rows]
-        return jnp.where(mask_block[None, None, :, :], raw_scores, -1e30)
-
-    lse_parts = []
-    attended_parts = []
-    for block_id in range(block_count):
-        begin_row = block_id * block_rows
-        masked = block_scores(begin_row)
-        row_peak = jnp.max(masked, axis=-1, keepdims=True)
-        exp_scores = jnp.exp(masked - row_peak)
-        row_total = jnp.sum(exp_scores, axis=-1, keepdims=True)
-        probs_low = (exp_scores / row_total).astype(jnp.bfloat16)
-        lse_parts.append(row_peak + jnp.log(row_total))
-        attended_parts.append(
-            jnp.einsum("grqk,kgd->qgrd", probs_low, value_low, preferred_element_type=jnp.float32)
-        )
-    attn_low = (
-        jnp.concatenate(attended_parts, axis=0).astype(jnp.bfloat16).reshape(row_count, HQ * HD)
-    )
+    query_rot = (query_rot.astype(jnp.float32) * score_scale).astype(jnp.bfloat16)
+    query_rot = query_rot.reshape(row_count, HQ * HD)
+    key_rot = key_rot.reshape(row_count, HK * HD)
+    value_low = value_low.reshape(row_count, HK * HD)
+    up_flow = Flow(gather_steps(links, pin(core_half(w_up), out_flow.pending), w_up))
+    full_out = out_flow.finish()
+    query_rot, key_rot = pin((query_rot, key_rot), full_out)
+    attn_low = attend(query_rot, key_rot, value_low, segment)
+    attn_low = pin(attn_low, gate_flow.pending)
+    gate_flow.advance()
+    down_flow = Flow(gather_steps(links, pin(core_half(w_down), up_flow.pending), w_down))
+    up_flow.advance()
+    full_gate = gate_flow.finish()
+    full_up = up_flow.finish()
     hidden = inputs + matmul_plain(attn_low, full_out)
     scale_two = inv_rms(hidden)
     normed_ffn = (hidden * scale_two * full_ffn_gain.astype(jnp.float32)).astype(jnp.bfloat16)
@@ -325,55 +572,59 @@
     gate_sig = jax.nn.sigmoid(gate_proj)
     gate_act = gate_proj * gate_sig
     mixed_act = (gate_act * up_proj).astype(jnp.bfloat16)
-    result = live_rows * (hidden + matmul_plain(mixed_act, full_down))
+    slope = (up_proj * gate_sig * (1.0 + gate_proj * (1.0 - gate_sig))).astype(jnp.bfloat16)
+    act_low = gate_act.astype(jnp.bfloat16)
+    mixed_act, slope, act_low = pin((mixed_act, slope, act_low), down_flow.pending)
+    down_flow.advance()
+    full_down = down_flow.finish()
     out_grad = live_rows * cotangent.astype(jnp.float32)
     out_low = out_grad.astype(jnp.bfloat16)
     grad_mixed = matmul_cols(out_low, full_down)
-    down_pair = scatter_sum(links, *column_halves(links, mixed_act, out_low))
-    grad_up_low = (grad_mixed * gate_act).astype(jnp.bfloat16)
-    grad_gate_low = (grad_mixed * up_proj * gate_sig * (1.0 + gate_proj * (1.0 - gate_sig))).astype(
-        jnp.bfloat16
-    )
-    gate_pair = scatter_sum(links, *row_halves(links, normed_ffn, grad_gate_low))
-    up_pair = scatter_sum(links, *row_halves(links, normed_ffn, grad_up_low))
-    grad_normed_ffn = matmul_cols(grad_gate_low, full_gate) + matmul_cols(grad_up_low, full_up)
+    grad_up_low = (grad_mixed * act_low.astype(jnp.float32)).astype(jnp.bfloat16)
+    grad_gate_low = (grad_mixed * slope.astype(jnp.float32)).astype(jnp.bfloat16)
+    grad_up_low, grad_gate_low = pin((grad_up_low, grad_gate_low))
+    down_part = core_sum(links, *column_halves(links, mixed_act, out_low))
+    down_back = Flow(scatter_steps(links, down_part))
+    gate_left = pin(grad_gate_low, down_part)
+    gate_part = core_sum(links, *row_halves(links, normed_ffn, gate_left))
+    up_left = pin(grad_up_low, gate_part)
+    up_part = core_sum(links, *row_halves(links, normed_ffn, up_left))
+    grad_gate_low = pin(grad_gate_low, up_part, down_back.pending)
+    gate_back = Flow(scatter_steps(links, pin(gate_part, down_back.pending)))
+    down_back.advance()
+    from_gate = matmul_cols(grad_gate_low, full_gate)
+    grad_up_low = pin(grad_up_low, from_gate, down_back.pending)
+    down_back.advance()
+    grad_normed_ffn = from_gate + matmul_cols(grad_up_low, full_up)
+    grad_normed_ffn = pin(grad_normed_ffn, gate_back.pending, down_back.pending)
+    up_back = Flow(scatter_steps(links, pin(up_part, gate_back.pending)))
+    gate_back.advance()
+    down_back.advance()
     grad_ffn_gain = jnp.sum(grad_normed_ffn * hidden * scale_two, axis=0)
     grad_hidden = out_grad + norm_back(
         grad_normed_ffn, hidden, scale_two, full_ffn_gain.astype(jnp.float32)
     )
     hidden_low = grad_hidden.astype(jnp.bfloat16)
-    grad_attn_low = (
-        matmul_cols(hidden_low, full_out)
-        .astype(jnp.bfloat16)
-        .reshape(row_count, HK, group_size, HD)
-    )
-    out_pair = scatter_sum(links, *row_halves(links, attn_low, hidden_low))
-    grad_query_parts = []
-    grad_key_rot = jnp.zeros((row_count, HK, HD), jnp.float32)
-    grad_value = jnp.zeros((row_count, HK, HD), jnp.float32)
-    for block_id in range(block_count):
-        begin_row = block_id * block_rows
-        masked = block_scores(begin_row)
-        attn_probs = jnp.exp(masked - lse_parts[block_id])
-        probs_low = attn_probs.astype(jnp.bfloat16)
-        grad_block = grad_attn_low[begin_row : begin_row + block_rows]
-        query_block = query_rot[begin_row : begin_row + block_rows]
-        grad_probs = jnp.einsum(
-            "qgrd,kgd->grqk", grad_block, value_low, preferred_element_type=jnp.float32
-        )
-        row_inner = jnp.sum(attn_probs * grad_probs, axis=-1, keepdims=True)
-        grad_scores = (attn_probs * (grad_probs - row_inner)).astype(jnp.bfloat16)
-        grad_query_parts.append(
-            score_scale
-            * jnp.einsum("grqk,kgd->qgrd", grad_scores, key_rot, preferred_element_type=jnp.float32)
-        )
-        grad_key_rot = grad_key_rot + score_scale * jnp.einsum(
-            "grqk,qgrd->kgd", grad_scores, query_block, preferred_element_type=jnp.float32
-        )
-        grad_value = grad_value + jnp.einsum(
-            "grqk,qgrd->kgd", probs_low, grad_block, preferred_element_type=jnp.float32
-        )
-    grad_query_rot = jnp.concatenate(grad_query_parts, axis=0).reshape(row_count, HQ, HD)
+    grad_attn_low = matmul_cols(hidden_low, full_out).astype(jnp.bfloat16)
+    out_part = core_sum(links, *row_halves(links, attn_low, hidden_low))
+    panels = HK // 4
+    grad_attn_low = pin(grad_attn_low, out_part, down_back.pending)
+    down_back.advance()
+    lower = attend_back(query_rot, grad_attn_low, key_rot, value_low, segment, 0, panels)
+    grad_attn_low = pin(grad_attn_low, lower, gate_back.pending, up_back.pending, down_back.pending)
+    gate_back.advance()
+    up_back.advance()
+    down_back.advance()
+    upper = attend_back(query_rot, grad_attn_low, key_rot, value_low, segment, panels, panels)
+    upper = pin(upper, up_back.pending, gate_back.pending)
+    out_back = Flow(scatter_steps(links, pin(out_part, up_back.pending)))
+    up_back.advance()
+    gate_back.advance()
+    grad_query_rot, grad_key_rot, grad_value = (
+        jnp.concatenate(pair, axis=1) for pair in zip(lower, upper)
+    )
+    grad_query_rot = (score_scale * grad_query_rot).reshape(row_count, HQ, HD)
+    grad_key_rot = grad_key_rot.reshape(row_count, HK, HD)
     grad_query_norm = rotate_back(grad_query_rot, cosine, sine_table)
     grad_key_norm = rotate_back(grad_key_rot, cosine, sine_table)
     back_gains = full_qk_gain.astype(jnp.float32)
@@ -417,13 +668,15 @@
         extra = lax.dynamic_slice_in_dim(small, which, 1, 1)[:, 0]
         return jnp.concatenate([product(), extra], axis=2)
 
-    front_share = join_rows(
-        scatter_sum(
-            links,
-            lambda: with_small(own_front, core),
-            lambda: with_small(other_front, 1 - core),
-        )
-    )
+    front_part = core_sum(
+        links,
+        lambda: with_small(own_front, core),
+        lambda: with_small(other_front, 1 - core),
+    )
+    front_back = Flow(scatter_steps(links, pin(front_part, out_back.pending)))
+    last_act = pin(mixed_act, front_part)
+    result = live_rows * (hidden + matmul_plain(last_act, full_down))
+    front_share = join_rows(front_back.finish())
     share_query = front_share[:, : HQ * HD]
     share_key = front_share[:, HQ * HD : (HQ + HK) * HD]
     share_value = front_share[:, (HQ + HK) * HD : (HQ + 2 * HK) * HD]
@@ -431,10 +684,10 @@
     share_again = extras[:, 0]
     share_fgain = extras[:, 1]
     share_qk = extras[: qk_gain.shape[0], 2]
-    share_out = join_rows(out_pair)
-    share_gate = join_rows(gate_pair)
-    share_up = join_rows(up_pair)
-    share_down = join_columns(down_pair)
+    share_out = join_rows(out_back.finish())
+    share_gate = join_rows(gate_back.finish())
+    share_up = join_rows(up_back.finish())
+    share_down = join_columns(down_back.finish())
     return (
         result.astype(jnp.bfloat16),
         grad_inputs.astype(jnp.bfloat16),

time: 1020 us -> 837 us (0.82)
  matrix products: 396 us -> 212 us
  other arithmetic: 166 us -> 93.1 us
  Pallas kernels: 0 us -> 60.8 us
  local copies, waits for them, and re-layouts: 110 us -> 146 us
  waiting for transfers between devices: 238 us -> 207 us
  starting transfers between devices: 100 us -> 111 us
    dot_general x12 -> x0, matrix products: 173 us -> none  [the longest x2 45.1 us: body(): jnp.einsum('qgrd,kgd->grqk', grad_block, value_low, preferred_element_typ...]
    pallas_call x0 -> x3, Pallas kernels: none -> 60.8 us  [the longest x2 37.6 us: attend_back(): pl.pallas_call(attend_back_kernel, out_shape=(jax.ShapeDtypeStruct((rows,...]
    convert_element_type x4, other arithmetic: 62.4 us -> 11.7 us  [the longest x2 9.17 us: core_sum(): return (own() + received.astype(jnp.float32)).astype(jnp.bfloat16)]
    ppermute x40, waiting for transfers between devices: 145 us -> 100 us  [shard_swap(): return lax.ppermute(value, axes, pairs)]
    reduce_sum x2 -> x1, other arithmetic: 26.3 us -> 1.07 us  [body(): grad_ffn_gain = jnp.sum(grad_normed_ffn * hidden * scale_two, axis=0)]
    ppermute x40, waiting for transfers between devices: 93.2 us -> 107 us  [rep_swap(): return lax.ppermute(value, axes, pairs)]
    dot_general x7, matrix products: 80.3 us -> 70 us  [matmul_plain(): return jnp.dot(left_mat, right_mat, preferred_element_type=jnp.float32)]
    unnamed x222 -> x230, local copies, waits for them, and re-layouts: 30.7 us -> 38.2 us
  transfers between devices with their start and end apart: 80 -> 80, of which waited for: 26 -> 26; matrix products, arithmetic and copies ran while one was open for 33% -> 39% of each run, Pallas kernels for 0% -> 7%
where the time goes in v2:
time: 837 us; the launch traced here: 833 us
  matrix products  212 us (25%)
  waiting for transfers between devices  207 us (25%)
  local copies, waits for them, and re-layouts  146 us (17%)
  starting transfers between devices  111 us (13%)
  other arithmetic  93.1 us (11%)
  Pallas kernels  60.8 us (7%)
    ppermute x40, waiting for transfers between devices, rep_swap(): return lax.ppermute(value, axes, pairs)  107 us
    ppermute x40, waiting for transfers between devices, shard_swap(): return lax.ppermute(value, axes, pairs)  100 us
    dot_general x10, matrix products, matmul_rows(): lax.dot_general(left_mat, right_mat, (((0,), (0,)), ((), ())), preferred_...  72.6 us
    ppermute x40, starting transfers between devices, rep_swap(): return lax.ppermute(value, axes, pairs)  70.9 us
    dot_general x7, matrix products, matmul_plain(): return jnp.dot(left_mat, right_mat, preferred_element_type=jnp.float32)  70 us
    dot_general x7, matrix products, matmul_cols(): lax.dot_general(left_mat, right_mat, (((1,), (1,)), ((), ())), preferred_...  69.2 us
    ppermute x40, starting transfers between devices, shard_swap(): return lax.ppermute(value, axes, pairs)  40.1 us
    unnamed x230, local copies, waits for them, and re-layouts  38.2 us
  transfers between devices with their start and end apart: 80, of which 26 were waited for; matrix products, arithmetic and copies ran while one was open for 39% of the time, Pallas kernels for 7%

profile of v2, /device:TPU:1, one launch (start us, length us, event | category | flops | bytes accessed | tf_op | source)
XLA Modules:
  0.0 833.2 jit_solution(14543277893760925269)
XLA Ops:
  19.3 4.1 copy.130
  30.7 4.4 broadcast.245.clone.1
  43.6 4.8 broadcast_in_dim.170
  66.4 4.2 collective-permute-start.8
  84.8 4.5 multiply_reduce_fusion.4
  103.8 3.9 copy.127.q_ref
  109.1 23.2 %attend.1 = bf16[1024,1024]{1,0:T(8,128)(2,1)} custom-call(s32[4,4]{1,0:T(4,128)} %fusion.126.live_ref, bf16[1024,1024]{1,0:T(8,128)(2,1)} %copy.127.q_ref, bf16[1024,512]{1,0:T(8,128)(2,1)} %copy.128.k_ref, bf16[1024,512]{1,0:T(8,128)(2,1)} %convolution_convert_fusion.3.v_ref, s32[1024,1]{1,0:T(8,128)} %copy.129.seg_col_ref, s32[1,1024]{1,0:T(1,128)} %bitcast.372), custom_call_target="tpu_custom_call" | custom-call | flops 19327352832 | bytes 8388608 | tf_op jit(solution)/shard_map/attend/pallas_call | solution.py:421
  132.4 5.0 multiply_reduce_fusion.3
  144.0 3.7 collective-permute-start.16
  158.1 10.7 %collective-permute-done.25 = bf16[64,4608]{1,0:T(8,128)(2,1)S(1)} collective-permute-done((bf16[64,4608]{1,0:T(8,128)(2,1)S(1)}, bf16[64,4608]{1,0:T(8,128)(2,1)S(1)}, u32[]{:S(2)}, u32[]{:S(2)}) %collective-permute-start.25) | collective-permute-done | bytes 589856 | tf_op jit(solution)/shard_map/ppermute | solution.py:90
  175.4 21.1 %collective-permute-done.28 = bf16[576,1024]{1,0:T(8,128)(2,1)} collective-permute-done((bf16[576,1024]{1,0:T(8,128)(2,1)S(1)}, bf16[576,1024]{1,0:T(8,128)(2,1)}, u32[]{:S(2)}, u32[]{:S(2)}) %collective-permute-start.28) | collective-permute-done | bytes 1179680 | tf_op jit(solution)/shard_map/ppermute | solution.py:90
  206.8 6.9 collective-permute-done.32
  219.5 13.4 %fusion.146 = f32[1024,4608]{1,0:T(8,128)} fusion(bf16[1024,1024]{0,1:T(8,128)(2,1)S(1)} %multiply_convert_fusion.5, bf16[1024,4608]{1,0:T(8,128)(2,1)S(1)} %bitcast.333), kind=kOutput, calls=%fused_computation.355 | convolution fusion | flops 9663676416 | bytes 30408704 | tf_op jit(solution)/shard_map/dot_general | solution.py:65
  232.9 25.6 %multiply_convert_fusion.2 = (bf16[1024,4608]{1,0:T(8,128)(2,1)}, bf16[1024,4608]{1,0:T(8,128)(2,1)}, bf16[1024,4608]{1,0:T(8,128)(2,1)}) fusion(f32[1024,4608]{1,0:T(8,128)} %fusion.146, bf16[1024,1024]{0,1:T(8,128)(2,1)} %copy-done.41, bf16[1024,4608]{1,0:T(8,128)(2,1)S(1)} %bitcast.335), kind=kOutput, calls=%fused_computation.2 | convolution fusion | flops 9725018112 | bytes 58720256 | tf_op jit(solution)/shard_map/dot_general | solution.py:65
  258.5 9.6 %convolution_convert_fusion = bf16[4608,512]{1,0:T(8,128)(2,1)} fusion(bf16[1024,4608]{1,0:T(8,128)(2,1)} %get-tuple-element.111, bf16[1024,1024]{0,1:T(8,128)(2,1)} %fusion.29, s32[]{:T(128)S(6)} %select_n.295), kind=kOutput, calls=%fused_computation.23 | convolution fusion | flops 4834197504 | bytes 15204356 | tf_op jit(solution)/shard_map/dot_general | solution.py:69
  268.1 7.6 fusion.82
  287.7 21.9 %multiply_convert_fusion = (bf16[1024,4608]{1,0:T(8,128)(2,1)}, bf16[1024,4608]{1,0:T(8,128)(2,1)}) fusion(bf16[1024,4608]{1,0:T(8,128)(2,1)} %get-tuple-element.90, bf16[1024,4608]{1,0:T(8,128)(2,1)} %get-tuple-element.89, bf16[1024,1024]{0,1:T(8,128)(2,1)S(1)} %copy-done.36, bf16[4608,1024]{1,0:T(8,128)(2,1)} %bitcast.51), kind=kOutput, calls=%fused_computation | convolution fusion | flops 9691987968 | bytes 49283072 | tf_op jit(solution)/shard_map/dot_general | solution.py:75
  309.6 5.7 add_convert_fusion.2
  315.3 9.6 %fusion.9 = bf16[4,128,4608]{2,1,0:T(8,128)(2,1)S(1)} fusion(bf16[1024,4608]{1,0:T(8,128)(2,1)} %get-tuple-element.95, bf16[1024,4,2,128]{0,3,2,1:T(8,128)(2,1)} %bitcast.364, s32[]{:T(128)S(6)} %select_n.290), kind=kOutput, calls=%fused_computation.24 | convolution fusion | flops 4834197504 | bytes 15204356 | tf_op jit(solution)/shard_map/dot_general | solution.py:69
  327.7 5.3 collective-permute-done.36
  333.0 9.4 %add_convert_fusion.1 = bf16[4,128,4608]{2,1,0:T(8,128)(2,1)S(1)} fusion(bf16[4,128,4608]{2,1,0:T(8,128)(2,1)S(1)} %collective-permute-done.36, bf16[1024,4608]{1,0:T(8,128)(2,1)} %get-tuple-element.95, bf16[1024,4,2,128]{0,3,2,1:T(8,128)(2,1)S(1)} %bitcast.365, s32[]{:T(128)S(6)} %select_n.289), kind=kOutput, calls=%fused_computation.15 | convolution fusion | flops 4838916096 | bytes 19922948 | tf_op jit(solution)/shard_map/dot_general | solution.py:69
  342.4 11.1 %collective-permute-done.38 = bf16[2,576,512]{2,1,0:T(8,128)(2,1)S(1)} collective-permute-done((bf16[2,576,512]{2,1,0:T(8,128)(2,1)S(1)}, bf16[2,576,512]{2,1,0:T(8,128)(2,1)S(1)}, u32[]{:S(2)}, u32[]{:S(2)}) %collective-permute-start.38) | collective-permute-done | bytes 1179680 | tf_op jit(solution)/shard_map/ppermute | solution.py:90
  360.6 34.9 %collective-permute-done.40 = bf16[576,512]{1,0:T(8,128)(2,1)} collective-permute-done((bf16[576,512]{1,0:T(8,128)(2,1)}, bf16[576,512]{1,0:T(8,128)(2,1)}, u32[]{:S(2)}, u32[]{:S(2)}) %collective-permute-start.40) | collective-permute-done | bytes 589856 | tf_op jit(solution)/shard_map/ppermute | solution.py:90
  403.5 7.6 collective-permute-done.44
  411.3 4.2 collective-permute-start.46
  418.9 22.1 %collective-permute-done.46 = bf16[576,512]{1,0:T(8,128)(2,1)S(1)} collective-permute-done((bf16[576,512]{1,0:T(8,128)(2,1)S(1)}, bf16[576,512]{1,0:T(8,128)(2,1)S(1)}, u32[]{:S(2)}, u32[]{:S(2)}) %collective-permute-start.46) | collective-permute-done | bytes 589856 | tf_op jit(solution)/shard_map/ppermute | solution.py:98
  446.1 6.7 fusion.12
  452.8 9.5 %collective-permute-start.37 = (bf16[4,128,4608]{2,1,0:T(8,128)(2,1)}, bf16[4,128,4608]{2,1,0:T(8,128)(2,1)}, u32[]{:S(2)}, u32[]{:S(2)}) collective-permute-start(bf16[4,128,4608]{2,1,0:T(8,128)(2,1)} %fusion.12), channel_id=1, source_target_pairs={{0,1},{1,0},{2,3},{3,2},{4,5},{5,4},{6,7},{7,6},{8,9},{9,8},{10,11... | collective-permute-start | bytes 14155784 | tf_op jit(solution)/shard_map/ppermute | solution.py:98
  462.2 5.3 collective-permute-done.72
  467.7 4.2 collective-permute-start.73
  473.0 5.0 collective-permute-start.79
  478.1 6.3 collective-permute-done.73
  486.4 4.3 collective-permute-start.74
  492.9 3.2 reshape.503
  496.1 6.3 constant_dynamic-slice_fusion.14
  502.4 6.0 copy.173
  508.4 4.4 copy.172
  512.8 11.8 %fusion.34 = f32[1152,1024]{1,0:T(8,128)} fusion(bf16[1152,512]{1,0:T(8,128)(2,1)} %collective-permute-done.79, bf16[576,512]{1,0:T(8,128)(2,1)S(1)} %get-tuple-element.237, bf16[576,512]{1,0:T(8,128)(2,1)S(1)} %get-tuple-element.236, pred[]{:T(512)S(6)} %eq.38), kind=kLoop, calls=%fused_computation.75 | loop fusion | flops 16515072 | bytes 7077889 | tf_op jit(solution)/shard_map/convert_element_type | solution.py:256
  524.7 4.1 fusion.32
  528.8 11.9 %add_convert_fusion = bf16[4,128,4608]{2,1,0:T(8,128)(2,1)} fusion(bf16[4,128,4608]{2,1,0:T(8,128)(2,1)} %collective-permute-done.37, bf16[1024,4608]{1,0:T(8,128)(2,1)} %get-tuple-element.96, bf16[1024,4,2,128]{0,3,2,1:T(8,128)(2,1)S(1)} %bitcast.367, s32[]{:T(128)S(6)} %select_n.289), kind=kOutput, calls=%fused_computation.14 | convolution fusion | flops 4838916096 | bytes 19922948 | tf_op jit(solution)/shard_map/dot_general | solution.py:69
  540.7 11.5 %fusion.147 = f32[1024,1024]{1,0:T(8,128)} fusion(bf16[1024,4608]{1,0:T(8,128)(2,1)S(1)} %bitcast.379, bf16[1024,4608]{1,0:T(8,128)(2,1)S(1)} %bitcast.338), kind=kOutput, calls=%fused_computation.356 | convolution fusion | flops 9663676416 | bytes 23068672 | tf_op jit(solution)/shard_map/dot_general | solution.py:75
  552.2 5.4 copy.131
  557.6 14.3 %fusion.148 = f32[1024,1024]{0,1:T(8,128)S(1)} fusion(bf16[1024,4608]{1,0:T(8,128)(2,1)} %get-tuple-element.96, bf16[1024,4608]{1,0:T(8,128)(2,1)} %bitcast.334), kind=kOutput, calls=%fused_computation.357 | convolution fusion | flops 9663676416 | bytes 23068672 | tf_op jit(solution)/shard_map/dot_general | solution.py:75
  582.0 6.0 convolution_convert_fusion.2.do_ref
  590.4 18.9 %attend_back.2 = (f32[1024,512]{1,0:T(8,128)}, f32[1024,256]{1,0:T(8,128)}, f32[1024,256]{1,0:T(8,128)}) custom-call(s32[4,4]{1,0:T(4,128)} %fusion.126.live_ref, bf16[1024,1024]{1,0:T(8,128)(2,1)} %copy.127.q_ref, bf16[1024,1024]{1,0:T(8,128)(2,1)} %convolution_convert_fusion.2.do_ref, bf16[1024,512]{1,0:T(8,128)(2,1)} %copy.128.k_ref, ...), custom_call_target="tpu_custom_call" | custom-call | flops 16106127360 | bytes 8388608 | tf_op jit(solution)/shard_map/attend_back/pallas_call | solution.py:449
  616.5 3.6 collective-permute-start.52
  621.6 18.7 %attend_back.3 = (f32[1024,512]{1,0:T(8,128)}, f32[1024,256]{1,0:T(8,128)}, f32[1024,256]{1,0:T(8,128)}) custom-call(s32[4,4]{1,0:T(4,128)} %fusion.126.live_ref, bf16[1024,1024]{1,0:T(8,128)(2,1)} %copy.127.q_ref, bf16[1024,1024]{1,0:T(8,128)(2,1)} %convolution_convert_fusion.2.do_ref, bf16[1024,512]{1,0:T(8,128)(2,1)} %copy.128.k_ref, ...), custom_call_target="tpu_custom_call" | custom-call | flops 16106127360 | bytes 8388608 | tf_op jit(solution)/shard_map/attend_back/pallas_call | solution.py:449
  653.3 4.4 fusion.42
  665.4 4.7 fusion.87
  671.1 6.3 fusion.28
  685.3 4.7 convolution_convert_fusion.1
  691.6 6.0 collective-permute-start.55
  704.5 3.8 collective-permute-done.68
  710.9 5.7 collective-permute-done.69
  716.8 8.5 %fusion.46 = f32[4,128,2048]{2,1,0:T(8,128)} fusion(bf16[1024,256]{0,1:T(8,128)(2,1)S(1)} %copy-done.66, bf16[1024,256]{0,1:T(8,128)(2,1)S(1)} %copy-done.65, bf16[1024,512]{0,1:T(8,128)(2,1)S(1)} %copy-done.56, bf16[1024,1024]{0,1:T(8,128)(2,1)S(1)} %copy-done.45, bf16[1024,4,2,128]{0,3,2,1:T(8,128)(2,1)S(1)} %bitcast.363, s32[]{:T(128)S(6)} %select_n.289), kind=kOutput, calls=%fused_computation.103 | convolution fusion | flops 2164260864 | bytes 9437188 | tf_op jit(solution)/shard_map/dot_general | solution.py:69
  732.3 3.5 fusion.15
  737.6 3.7 collective-permute-done.75
  742.8 7.5 collective-permute-done.60
  752.6 17.0 %collective-permute-done.76 = bf16[64,4608]{1,0:T(8,128)(2,1)S(1)} collective-permute-done((bf16[64,4608]{1,0:T(8,128)(2,1)S(1)}, bf16[64,4608]{1,0:T(8,128)(2,1)S(1)}, u32[]{:S(2)}, u32[]{:S(2)}) %collective-permute-start.76) | collective-permute-done | bytes 589856 | tf_op jit(solution)/shard_map/ppermute | solution.py:98
  771.5 11.6 %collective-permute-done.77 = bf16[64,4608]{1,0:T(8,128)(2,1)S(1)} collective-permute-done((bf16[64,4608]{1,0:T(8,128)(2,1)S(1)}, bf16[64,4608]{1,0:T(8,128)(2,1)S(1)}, u32[]{:S(2)}, u32[]{:S(2)}) %collective-permute-start.77) | collective-permute-done | bytes 589856 | tf_op jit(solution)/shard_map/ppermute | solution.py:98
  783.2 5.9 collective-permute-done.62
  793.2 11.5 %collective-permute-done.63 = bf16[64,2176]{1,0:T(8,128)(2,1)S(1)} collective-permute-done((bf16[64,2176]{1,0:T(8,128)(2,1)S(1)}, bf16[64,2176]{1,0:T(8,128)(2,1)S(1)}, u32[]{:S(2)}, u32[]{:S(2)}) %collective-permute-start.63) | collective-permute-done | bytes 278560 | tf_op jit(solution)/shard_map/ppermute | solution.py:98
  804.9 16.3 %multiply_convert_fusion.4 = bf16[1024,1024]{0,1:T(8,128)(2,1)S(1)} fusion(f32[1024,1024]{0,1:T(8,128)} %copy-done.2, f32[1024]{0:T(1024)} %copy-done.80, bf16[1024,4608]{1,0:T(8,128)(2,1)} %get-tuple-element.111, bf16[4608,1024]{1,0:T(8,128)(2,1)} %bitcast.51), kind=kOutput, calls=%fused_computation.50 | convolution fusion | flops 9666822144 | bytes 25169920 | tf_op jit(solution)/shard_map/dot_general | solution.py:65
  825.4 3.7 fusion.33
  (565 shorter events, 253.5 us)
Async XLA Ops:
  5.7 46.9 %collective-permute-start = (bf16[128,2176]{1,0:T(8,128)(2,1)}, bf16[128,2176]{1,0:T(8,128)(2,1)}, u32[]{:S(2)}, u32[]{:S(2)}) collective-permute-start(bf16[128,2176]{1,0:T(8,128)(2,1)} %pad_maximum_fusion.15), channel_id=1, source_target_pairs={{0,8},{1,9},{2,10},{3,11},{4,12},{5,13},{6,14},{7,15},{8,0},{9,1},... | collective-permute-start | bytes 1671176 | tf_op jit(solution)/shard_map/ppermute | solution.py:90
  7.8 44.8 %collective-permute-start.2 = (bf16[128,2176]{1,0:T(8,128)(2,1)}, bf16[128,2176]{1,0:T(8,128)(2,1)}, u32[]{:S(2)}, u32[]{:S(2)}) collective-permute-start(bf16[128,2176]{1,0:T(8,128)(2,1)} %pad_maximum_fusion.15), channel_id=1, source_target_pairs={{0,16},{1,17},{2,18},{3,19},{4,20},{5,21},{6,22},{7,23},{8,24},{9,... | collective-permute-start | bytes 1671176 | tf_op jit(solution)/shard_map/ppermute | solution.py:90
  53.8 11.3 %collective-permute-start.4 = (bf16[64,2176]{1,0:T(8,128)(2,1)S(1)}, bf16[64,2176]{1,0:T(8,128)(2,1)S(1)}, u32[]{:S(2)}, u32[]{:S(2)}) collective-permute-start(bf16[64,2176]{1,0:T(8,128)(2,1)S(1)} %slice.312), channel_id=1, source_target_pairs={{0,16},{1,17},{2,18},{3,19},{4,20},{5,21},{6,22},{7,23},{8,24},{9,... | collective-permute-start | bytes 835592 | tf_op jit(solution)/shard_map/ppermute | solution.py:90
  57.7 19.9 %collective-permute-start.1 = (bf16[128,2176]{1,0:T(8,128)(2,1)}, bf16[128,2176]{1,0:T(8,128)(2,1)S(1)}, u32[]{:S(2)}, u32[]{:S(2)}) collective-permute-start(bf16[128,2176]{1,0:T(8,128)(2,1)} %collective-permute-done), channel_id=1, source_target_pairs={{0,1},{1,0},{2,3},{3,2},{4,5},{5,4},{6,7},{7,6},{8,9},{9,8},{10,11... | collective-permute-start | bytes 1671176 | tf_op jit(solution)/shard_map/ppermute | solution.py:98
  61.9 17.3 %collective-permute-start.3 = (bf16[128,2176]{1,0:T(8,128)(2,1)}, bf16[128,2176]{1,0:T(8,128)(2,1)S(1)}, u32[]{:S(2)}, u32[]{:S(2)}) collective-permute-start(bf16[128,2176]{1,0:T(8,128)(2,1)} %collective-permute-done.2), channel_id=1, source_target_pairs={{0,1},{1,0},{2,3},{3,2},{4,5},{5,4},{6,7},{7,6},{8,9},{9,8},{10,11... | collective-permute-start | bytes 1671176 | tf_op jit(solution)/shard_map/ppermute | solution.py:98
  70.6 61.7 %collective-permute-start.14 = (bf16[128,4608]{1,0:T(8,128)(2,1)}, bf16[128,4608]{1,0:T(8,128)(2,1)}, u32[]{:S(2)}, u32[]{:S(2)}) collective-permute-start(bf16[128,4608]{1,0:T(8,128)(2,1)} %constant_dynamic-slice_fusion.25), channel_id=1, source_target_pairs={{0,8},{1,9},{2,10},{3,11},{4,12},{5,13},{6,14},{7,15},{8,0},{9,1},... | collective-permute-start | bytes 3538952 | tf_op jit(solution)/shard_map/ppermute | solution.py:90
  70.8 61.6 %collective-permute-start.15 = (bf16[128,4608]{1,0:T(8,128)(2,1)}, bf16[128,4608]{1,0:T(8,128)(2,1)}, u32[]{:S(2)}, u32[]{:S(2)}) collective-permute-start(bf16[128,4608]{1,0:T(8,128)(2,1)} %constant_dynamic-slice_fusion.25), channel_id=1, source_target_pairs={{0,16},{1,17},{2,18},{3,19},{4,20},{5,21},{6,22},{7,23},{8,24},{9,... | collective-permute-start | bytes 3538952 | tf_op jit(solution)/shard_map/ppermute | solution.py:90
  79.3 70.9 %collective-permute-start.21 = (bf16[128,4608]{1,0:T(8,128)(2,1)}, bf16[128,4608]{1,0:T(8,128)(2,1)}, u32[]{:S(2)}, u32[]{:S(2)}) collective-permute-start(bf16[128,4608]{1,0:T(8,128)(2,1)} %constant_dynamic-slice_fusion.24), channel_id=1, source_target_pairs={{0,8},{1,9},{2,10},{3,11},{4,12},{5,13},{6,14},{7,15},{8,0},{9,1},... | collective-permute-start | bytes 3538952 | tf_op jit(solution)/shard_map/ppermute | solution.py:90
  81.6 72.2 %collective-permute-start.23 = (bf16[128,4608]{1,0:T(8,128)(2,1)}, bf16[128,4608]{1,0:T(8,128)(2,1)}, u32[]{:S(2)}, u32[]{:S(2)}) collective-permute-start(bf16[128,4608]{1,0:T(8,128)(2,1)} %constant_dynamic-slice_fusion.24), channel_id=1, source_target_pairs={{0,16},{1,17},{2,18},{3,19},{4,20},{5,21},{6,22},{7,23},{8,24},{9,... | collective-permute-start | bytes 3538952 | tf_op jit(solution)/shard_map/ppermute | solution.py:90
  139.7 16.7 %collective-permute-start.18 = (bf16[64,4608]{1,0:T(8,128)(2,1)S(1)}, bf16[64,4608]{1,0:T(8,128)(2,1)S(1)}, u32[]{:S(2)}, u32[]{:S(2)}) collective-permute-start(bf16[64,4608]{1,0:T(8,128)(2,1)S(1)} %slice.327), channel_id=1, source_target_pairs={{0,16},{1,17},{2,18},{3,19},{4,20},{5,21},{6,22},{7,23},{8,24},{9,... | collective-permute-start | bytes 1769480 | tf_op jit(solution)/shard_map/ppermute | solution.py:90
  143.5 13.6 %collective-permute-start.19 = (bf16[64,4608]{1,0:T(8,128)(2,1)S(1)}, bf16[64,4608]{1,0:T(8,128)(2,1)S(1)}, u32[]{:S(2)}, u32[]{:S(2)}) collective-permute-start(bf16[64,4608]{1,0:T(8,128)(2,1)S(1)} %slice.328), channel_id=1, source_target_pairs={{0,8},{1,9},{2,10},{3,11},{4,12},{5,13},{6,14},{7,15},{8,0},{9,1},... | collective-permute-start | bytes 1769480 | tf_op jit(solution)/shard_map/ppermute | solution.py:90
  144.0 28.9 %collective-permute-start.16 = (bf16[128,4608]{1,0:T(8,128)(2,1)}, bf16[128,4608]{1,0:T(8,128)(2,1)S(1)}, u32[]{:S(2)}, u32[]{:S(2)}) collective-permute-start(bf16[128,4608]{1,0:T(8,128)(2,1)} %collective-permute-done.14), channel_id=1, source_target_pairs={{0,1},{1,0},{2,3},{3,2},{4,5},{5,4},{6,7},{7,6},{8,9},{9,8},{10,11... | collective-permute-start | bytes 3538952 | tf_op jit(solution)/shard_map/ppermute | solution.py:98
  150.2 24.4 %collective-permute-start.17 = (bf16[128,4608]{1,0:T(8,128)(2,1)}, bf16[128,4608]{1,0:T(8,128)(2,1)S(1)}, u32[]{:S(2)}, u32[]{:S(2)}) collective-permute-start(bf16[128,4608]{1,0:T(8,128)(2,1)} %collective-permute-done.15), channel_id=1, source_target_pairs={{0,1},{1,0},{2,3},{3,2},{4,5},{5,4},{6,7},{7,6},{8,9},{9,8},{10,11... | collective-permute-start | bytes 3538952 | tf_op jit(solution)/shard_map/ppermute | solution.py:98
  153.8 15.0 %collective-permute-start.25 = (bf16[64,4608]{1,0:T(8,128)(2,1)S(1)}, bf16[64,4608]{1,0:T(8,128)(2,1)S(1)}, u32[]{:S(2)}, u32[]{:S(2)}) collective-permute-start(bf16[64,4608]{1,0:T(8,128)(2,1)S(1)} %slice.329), channel_id=1, source_target_pairs={{0,16},{1,17},{2,18},{3,19},{4,20},{5,21},{6,22},{7,23},{8,24},{9,... | collective-permute-start | bytes 1769480 | tf_op jit(solution)/shard_map/ppermute | solution.py:90
  156.4 14.7 %collective-permute-start.26 = (bf16[64,4608]{1,0:T(8,128)(2,1)S(1)}, bf16[64,4608]{1,0:T(8,128)(2,1)S(1)}, u32[]{:S(2)}, u32[]{:S(2)}) collective-permute-start(bf16[64,4608]{1,0:T(8,128)(2,1)S(1)} %slice.330), channel_id=1, source_target_pairs={{0,8},{1,9},{2,10},{3,11},{4,12},{5,13},{6,14},{7,15},{8,0},{9,1},... | collective-permute-start | bytes 1769480 | tf_op jit(solution)/shard_map/ppermute | solution.py:90
  157.1 39.3 %collective-permute-start.28 = (bf16[576,1024]{1,0:T(8,128)(2,1)S(1)}, bf16[576,1024]{1,0:T(8,128)(2,1)}, u32[]{:S(2)}, u32[]{:S(2)}) collective-permute-start(bf16[576,1024]{1,0:T(8,128)(2,1)S(1)} %copy-done.48), channel_id=1, source_target_pairs={{0,8},{1,9},{2,10},{3,11},{4,12},{5,13},{6,14},{7,15},{8,0},{9,1},... | collective-permute-start | bytes 3538952 | tf_op jit(solution)/shard_map/ppermute | solution.py:90
  168.8 29.9 %collective-permute-start.29 = (bf16[576,1024]{1,0:T(8,128)(2,1)S(1)}, bf16[576,1024]{1,0:T(8,128)(2,1)}, u32[]{:S(2)}, u32[]{:S(2)}) collective-permute-start(bf16[576,1024]{1,0:T(8,128)(2,1)S(1)} %copy-done.48), channel_id=1, source_target_pairs={{0,16},{1,17},{2,18},{3,19},{4,20},{5,21},{6,22},{7,23},{8,24},{9,... | collective-permute-start | bytes 3538952 | tf_op jit(solution)/shard_map/ppermute | solution.py:90
  171.1 31.6 %collective-permute-start.22 = (bf16[128,4608]{1,0:T(8,128)(2,1)}, bf16[128,4608]{1,0:T(8,128)(2,1)S(1)}, u32[]{:S(2)}, u32[]{:S(2)}) collective-permute-start(bf16[128,4608]{1,0:T(8,128)(2,1)} %collective-permute-done.21), channel_id=1, source_target_pairs={{0,1},{1,0},{2,3},{3,2},{4,5},{5,4},{6,7},{7,6},{8,9},{9,8},{10,11... | collective-permute-start | bytes 3538952 | tf_op jit(solution)/shard_map/ppermute | solution.py:98
  173.0 32.7 %collective-permute-start.24 = (bf16[128,4608]{1,0:T(8,128)(2,1)}, bf16[128,4608]{1,0:T(8,128)(2,1)S(1)}, u32[]{:S(2)}, u32[]{:S(2)}) collective-permute-start(bf16[128,4608]{1,0:T(8,128)(2,1)} %collective-permute-done.23), channel_id=1, source_target_pairs={{0,1},{1,0},{2,3},{3,2},{4,5},{5,4},{6,7},{7,6},{8,9},{9,8},{10,11... | collective-permute-start | bytes 3538952 | tf_op jit(solution)/shard_map/ppermute | solution.py:98
  174.6 32.0 %collective-permute-start.20 = (bf16[128,4608]{1,0:T(8,128)(2,1)S(1)}, bf16[128,4608]{1,0:T(8,128)(2,1)S(1)}, u32[]{:S(2)}, u32[]{:S(2)}) collective-permute-start(bf16[128,4608]{1,0:T(8,128)(2,1)S(1)} %constant_dynamic-update-slice_fusion.10), channel_id=1, source_target_pairs={{0,1},{1,0},{2,3},{3,2},{4,5},{5,4},{6,7},{7,6},{8,9},{9,8},{10,11... | collective-permute-start | bytes 3538952 | tf_op jit(solution)/shard_map/ppermute | solution.py:98
  196.5 22.9 %collective-permute-start.27 = (bf16[128,4608]{1,0:T(8,128)(2,1)S(1)}, bf16[128,4608]{1,0:T(8,128)(2,1)S(1)}, u32[]{:S(2)}, u32[]{:S(2)}) collective-permute-start(bf16[128,4608]{1,0:T(8,128)(2,1)S(1)} %constant_dynamic-update-slice_fusion.12), channel_id=1, source_target_pairs={{0,1},{1,0},{2,3},{3,2},{4,5},{5,4},{6,7},{7,6},{8,9},{9,8},{10,11... | collective-permute-start | bytes 3538952 | tf_op jit(solution)/shard_map/ppermute | solution.py:98
  198.7 15.0 %collective-permute-start.32 = (bf16[288,1024]{1,0:T(8,128)(2,1)S(1)}, bf16[288,1024]{1,0:T(8,128)(2,1)S(1)}, u32[]{:S(2)}, u32[]{:S(2)}) collective-permute-start(bf16[288,1024]{1,0:T(8,128)(2,1)S(1)} %slice.331), channel_id=1, source_target_pairs={{0,16},{1,17},{2,18},{3,19},{4,20},{5,21},{6,22},{7,23},{8,24},{9,... | collective-permute-start | bytes 1769480 | tf_op jit(solution)/shard_map/ppermute | solution.py:90
  202.7 14.8 %collective-permute-start.33 = (bf16[288,1024]{1,0:T(8,128)(2,1)S(1)}, bf16[288,1024]{1,0:T(8,128)(2,1)S(1)}, u32[]{:S(2)}, u32[]{:S(2)}) collective-permute-start(bf16[288,1024]{1,0:T(8,128)(2,1)S(1)} %slice.332), channel_id=1, source_target_pairs={{0,8},{1,9},{2,10},{3,11},{4,12},{5,13},{6,14},{7,15},{8,0},{9,1},... | collective-permute-start | bytes 1769480 | tf_op jit(solution)/shard_map/ppermute | solution.py:90
  205.7 70.0 %collective-permute-start.30 = (bf16[576,1024]{1,0:T(8,128)(2,1)}, bf16[576,1024]{1,0:T(8,128)(2,1)}, u32[]{:S(2)}, u32[]{:S(2)}) collective-permute-start(bf16[576,1024]{1,0:T(8,128)(2,1)} %collective-permute-done.28), channel_id=1, source_target_pairs={{0,1},{1,0},{2,3},{3,2},{4,5},{5,4},{6,7},{7,6},{8,9},{9,8},{10,11... | collective-permute-start | bytes 3538952 | tf_op jit(solution)/shard_map/ppermute | solution.py:98
  206.6 73.9 %collective-permute-start.31 = (bf16[576,1024]{1,0:T(8,128)(2,1)}, bf16[576,1024]{1,0:T(8,128)(2,1)}, u32[]{:S(2)}, u32[]{:S(2)}) collective-permute-start(bf16[576,1024]{1,0:T(8,128)(2,1)} %collective-permute-done.29), channel_id=1, source_target_pairs={{0,1},{1,0},{2,3},{3,2},{4,5},{5,4},{6,7},{7,6},{8,9},{9,8},{10,11... | collective-permute-start | bytes 3538952 | tf_op jit(solution)/shard_map/ppermute | solution.py:98
  218.3 67.0 %collective-permute-start.34 = (bf16[576,1024]{1,0:T(8,128)(2,1)}, bf16[576,1024]{1,0:T(8,128)(2,1)}, u32[]{:S(2)}, u32[]{:S(2)}) collective-permute-start(bf16[576,1024]{1,0:T(8,128)(2,1)} %constant_dynamic-update-slice_fusion.14), channel_id=1, source_target_pairs={{0,1},{1,0},{2,3},{3,2},{4,5},{5,4},{6,7},{7,6},{8,9},{9,8},{10,11... | collective-permute-start | bytes 3538952 | tf_op jit(solution)/shard_map/ppermute | solution.py:98
  268.1 41.5 %collective-permute-start.35 = (bf16[4,1152,512]{2,1,0:T(8,128)(2,1)}, bf16[4,1152,512]{2,1,0:T(8,128)(2,1)S(1)}, u32[]{:S(2)}, u32[]{:S(2)}) collective-permute-start(bf16[4,1152,512]{2,1,0:T(8,128)(2,1)} %bitcast.59), channel_id=1, source_target_pairs={{0,1},{1,0},{2,3},{3,2},{4,5},{5,4},{6,7},{7,6},{8,9},{9,8},{10,11... | collective-permute-start | bytes 14155784 | tf_op jit(solution)/shard_map/ppermute | solution.py:98
  325.7 27.8 %collective-permute-start.38 = (bf16[2,576,512]{2,1,0:T(8,128)(2,1)S(1)}, bf16[2,576,512]{2,1,0:T(8,128)(2,1)S(1)}, u32[]{:S(2)}, u32[]{:S(2)}) collective-permute-start(bf16[2,576,512]{2,1,0:T(8,128)(2,1)S(1)} %pad_maximum_fusion.4), channel_id=1, source_target_pairs={{0,8},{1,9},{2,10},{3,11},{4,12},{5,13},{6,14},{7,15},{8,0},{9,1},... | collective-permute-start | bytes 3538952 | tf_op jit(solution)/shard_map/ppermute | solution.py:90
  327.4 27.3 %collective-permute-start.39 = (bf16[2,576,512]{2,1,0:T(8,128)(2,1)S(1)}, bf16[2,576,512]{2,1,0:T(8,128)(2,1)S(1)}, u32[]{:S(2)}, u32[]{:S(2)}) collective-permute-start(bf16[2,576,512]{2,1,0:T(8,128)(2,1)S(1)} %pad_maximum_fusion.5), channel_id=1, source_target_pairs={{0,16},{1,17},{2,18},{3,19},{4,20},{5,21},{6,22},{7,23},{8,24},{9,... | collective-permute-start | bytes 3538952 | tf_op jit(solution)/shard_map/ppermute | solution.py:90
  355.1 44.8 %collective-permute-start.42 = (bf16[2,64,4608]{2,1,0:T(8,128)(2,1)S(1)}, bf16[2,64,4608]{2,1,0:T(8,128)(2,1)}, u32[]{:S(2)}, u32[]{:S(2)}) collective-permute-start(bf16[2,64,4608]{2,1,0:T(8,128)(2,1)S(1)} %pad_maximum_fusion.6), channel_id=1, source_target_pairs={{0,8},{1,9},{2,10},{3,11},{4,12},{5,13},{6,14},{7,15},{8,0},{9,1},... | collective-permute-start | bytes 3538952 | tf_op jit(solution)/shard_map/ppermute | solution.py:90
  356.4 43.4 %collective-permute-start.43 = (bf16[2,64,4608]{2,1,0:T(8,128)(2,1)}, bf16[2,64,4608]{2,1,0:T(8,128)(2,1)}, u32[]{:S(2)}, u32[]{:S(2)}) collective-permute-start(bf16[2,64,4608]{2,1,0:T(8,128)(2,1)} %pad_maximum_fusion.7), channel_id=1, source_target_pairs={{0,16},{1,17},{2,18},{3,19},{4,20},{5,21},{6,22},{7,23},{8,24},{9,... | collective-permute-start | bytes 3538952 | tf_op jit(solution)/shard_map/ppermute | solution.py:90
  358.6 36.9 %collective-permute-start.40 = (bf16[576,512]{1,0:T(8,128)(2,1)}, bf16[576,512]{1,0:T(8,128)(2,1)}, u32[]{:S(2)}, u32[]{:S(2)}) collective-permute-start(bf16[576,512]{1,0:T(8,128)(2,1)} %get-tuple-element.207), channel_id=1, source_target_pairs={{0,16},{1,17},{2,18},{3,19},{4,20},{5,21},{6,22},{7,23},{8,24},{9,... | collective-permute-start | bytes 1769480 | tf_op jit(solution)/shard_map/ppermute | solution.py:90
  359.3 36.3 %collective-permute-start.41 = (bf16[576,512]{1,0:T(8,128)(2,1)}, bf16[576,512]{1,0:T(8,128)(2,1)}, u32[]{:S(2)}, u32[]{:S(2)}) collective-permute-start(bf16[576,512]{1,0:T(8,128)(2,1)} %get-tuple-element.206), channel_id=1, source_target_pairs={{0,8},{1,9},{2,10},{3,11},{4,12},{5,13},{6,14},{7,15},{8,0},{9,1},... | collective-permute-start | bytes 1769480 | tf_op jit(solution)/shard_map/ppermute | solution.py:90
  398.2 12.9 %collective-permute-start.44 = (bf16[576,512]{1,0:T(8,128)(2,1)S(1)}, bf16[576,512]{1,0:T(8,128)(2,1)S(1)}, u32[]{:S(2)}, u32[]{:S(2)}) collective-permute-start(bf16[576,512]{1,0:T(8,128)(2,1)S(1)} %get-tuple-element.184), channel_id=1, source_target_pairs={{0,2},{1,3},{2,0},{3,1},{4,6},{5,7},{6,4},{7,5},{8,10},{9,11},{10,... | collective-permute-start | bytes 1769480 | tf_op jit(solution)/shard_map/ppermute | solution.py:98
  401.7 13.8 %collective-permute-start.47 = (bf16[64,4608]{1,0:T(8,128)(2,1)S(1)}, bf16[64,4608]{1,0:T(8,128)(2,1)S(1)}, u32[]{:S(2)}, u32[]{:S(2)}) collective-permute-start(bf16[64,4608]{1,0:T(8,128)(2,1)S(1)} %get-tuple-element.201), channel_id=1, source_target_pairs={{0,16},{1,17},{2,18},{3,19},{4,20},{5,21},{6,22},{7,23},{8,24},{9,... | collective-permute-start | bytes 1769480 | tf_op jit(solution)/shard_map/ppermute | solution.py:90
  403.2 12.3 %collective-permute-start.48 = (bf16[64,4608]{1,0:T(8,128)(2,1)S(1)}, bf16[64,4608]{1,0:T(8,128)(2,1)S(1)}, u32[]{:S(2)}, u32[]{:S(2)}) collective-permute-start(bf16[64,4608]{1,0:T(8,128)(2,1)S(1)} %get-tuple-element.200), channel_id=1, source_target_pairs={{0,8},{1,9},{2,10},{3,11},{4,12},{5,13},{6,14},{7,15},{8,0},{9,1},... | collective-permute-start | bytes 1769480 | tf_op jit(solution)/shard_map/ppermute | solution.py:90
  411.3 29.7 %collective-permute-start.46 = (bf16[576,512]{1,0:T(8,128)(2,1)S(1)}, bf16[576,512]{1,0:T(8,128)(2,1)S(1)}, u32[]{:S(2)}, u32[]{:S(2)}) collective-permute-start(bf16[576,512]{1,0:T(8,128)(2,1)S(1)} %add_convert_fusion.14), channel_id=1, source_target_pairs={{0,4},{1,5},{2,6},{3,7},{4,0},{5,1},{6,2},{7,3},{8,12},{9,13},{10,... | collective-permute-start | bytes 1769480 | tf_op jit(solution)/shard_map/ppermute | solution.py:98
  417.6 25.0 %collective-permute-start.54 = (bf16[64,4608]{1,0:T(8,128)(2,1)S(1)}, bf16[64,4608]{1,0:T(8,128)(2,1)S(1)}, u32[]{:S(2)}, u32[]{:S(2)}) collective-permute-start(bf16[64,4608]{1,0:T(8,128)(2,1)S(1)} %get-tuple-element.181), channel_id=1, source_target_pairs={{0,2},{1,3},{2,0},{3,1},{4,6},{5,7},{6,4},{7,5},{8,10},{9,11},{10,... | collective-permute-start | bytes 1769480 | tf_op jit(solution)/shard_map/ppermute | solution.py:98
  441.2 30.6 %collective-permute-start.51 = (bf16[576,512]{1,0:T(8,128)(2,1)S(1)}, bf16[576,512]{1,0:T(8,128)(2,1)S(1)}, u32[]{:S(2)}, u32[]{:S(2)}) collective-permute-start(bf16[576,512]{1,0:T(8,128)(2,1)S(1)} %add_convert_fusion.11), channel_id=1, source_target_pairs={{0,2},{1,3},{2,0},{3,1},{4,6},{5,7},{6,4},{7,5},{8,10},{9,11},{10,... | collective-permute-start | bytes 1769480 | tf_op jit(solution)/shard_map/ppermute | solution.py:98
  442.9 24.6 %collective-permute-start.72 = (bf16[64,4608]{1,0:T(8,128)(2,1)S(1)}, bf16[64,4608]{1,0:T(8,128)(2,1)S(1)}, u32[]{:S(2)}, u32[]{:S(2)}) collective-permute-start(bf16[64,4608]{1,0:T(8,128)(2,1)S(1)} %add_convert_fusion.8), channel_id=1, source_target_pairs={{0,4},{1,5},{2,6},{3,7},{4,0},{5,1},{6,2},{7,3},{8,12},{9,13},{10,... | collective-permute-start | bytes 1769480 | tf_op jit(solution)/shard_map/ppermute | solution.py:98
  452.8 76.0 %collective-permute-start.37 = (bf16[4,128,4608]{2,1,0:T(8,128)(2,1)}, bf16[4,128,4608]{2,1,0:T(8,128)(2,1)}, u32[]{:S(2)}, u32[]{:S(2)}) collective-permute-start(bf16[4,128,4608]{2,1,0:T(8,128)(2,1)} %fusion.12), channel_id=1, source_target_pairs={{0,1},{1,0},{2,3},{3,2},{4,5},{5,4},{6,7},{7,6},{8,9},{9,8},{10,11... | collective-permute-start | bytes 14155784 | tf_op jit(solution)/shard_map/ppermute | solution.py:98
  467.7 16.7 %collective-permute-start.73 = (bf16[64,4608]{1,0:T(8,128)(2,1)S(1)}, bf16[64,4608]{1,0:T(8,128)(2,1)S(1)}, u32[]{:S(2)}, u32[]{:S(2)}) collective-permute-start(bf16[64,4608]{1,0:T(8,128)(2,1)S(1)} %add_convert_fusion.7), channel_id=1, source_target_pairs={{0,2},{1,3},{2,0},{3,1},{4,6},{5,7},{6,4},{7,5},{8,10},{9,11},{10,... | collective-permute-start | bytes 1769480 | tf_op jit(solution)/shard_map/ppermute | solution.py:98
  473.0 39.8 %collective-permute-start.79 = (bf16[1152,512]{1,0:T(8,128)(2,1)}, bf16[1152,512]{1,0:T(8,128)(2,1)}, u32[]{:S(2)}, u32[]{:S(2)}) collective-permute-start(bf16[1152,512]{1,0:T(8,128)(2,1)} %pad_maximum_fusion.12), channel_id=1, source_target_pairs={{0,1},{1,0},{2,3},{3,2},{4,5},{5,4},{6,7},{7,6},{8,9},{9,8},{10,11... | collective-permute-start | bytes 3538952 | tf_op jit(solution)/shard_map/ppermute | solution.py:98
  486.4 38.3 %collective-permute-start.74 = (bf16[128,4608]{1,0:T(8,128)(2,1)}, bf16[128,4608]{1,0:T(8,128)(2,1)}, u32[]{:S(2)}, u32[]{:S(2)}) collective-permute-start(bf16[128,4608]{1,0:T(8,128)(2,1)} %pad_maximum_fusion.10), channel_id=1, source_target_pairs={{0,1},{1,0},{2,3},{3,2},{4,5},{5,4},{6,7},{7,6},{8,9},{9,8},{10,11... | collective-permute-start | bytes 3538952 | tf_op jit(solution)/shard_map/ppermute | solution.py:98
  580.9 32.7 %collective-permute-start.49 = (bf16[2,64,4608]{2,1,0:T(8,128)(2,1)}, bf16[2,64,4608]{2,1,0:T(8,128)(2,1)}, u32[]{:S(2)}, u32[]{:S(2)}) collective-permute-start(bf16[2,64,4608]{2,1,0:T(8,128)(2,1)} %pad_maximum_fusion.8), channel_id=1, source_target_pairs={{0,8},{1,9},{2,10},{3,11},{4,12},{5,13},{6,14},{7,15},{8,0},{9,1},... | collective-permute-start | bytes 3538952 | tf_op jit(solution)/shard_map/ppermute | solution.py:90
  582.0 31.6 %collective-permute-start.50 = (bf16[2,64,4608]{2,1,0:T(8,128)(2,1)}, bf16[2,64,4608]{2,1,0:T(8,128)(2,1)}, u32[]{:S(2)}, u32[]{:S(2)}) collective-permute-start(bf16[2,64,4608]{2,1,0:T(8,128)(2,1)} %pad_maximum_fusion.9), channel_id=1, source_target_pairs={{0,16},{1,17},{2,18},{3,19},{4,20},{5,21},{6,22},{7,23},{8,24},{9,... | collective-permute-start | bytes 3538952 | tf_op jit(solution)/shard_map/ppermute | solution.py:90
  616.5 23.7 %collective-permute-start.52 = (bf16[64,4608]{1,0:T(8,128)(2,1)}, bf16[64,4608]{1,0:T(8,128)(2,1)S(1)}, u32[]{:S(2)}, u32[]{:S(2)}) collective-permute-start(bf16[64,4608]{1,0:T(8,128)(2,1)} %get-tuple-element.195), channel_id=1, source_target_pairs={{0,16},{1,17},{2,18},{3,19},{4,20},{5,21},{6,22},{7,23},{8,24},{9,... | collective-permute-start | bytes 1769480 | tf_op jit(solution)/shard_map/ppermute | solution.py:90
  620.1 20.1 %collective-permute-start.53 = (bf16[64,4608]{1,0:T(8,128)(2,1)}, bf16[64,4608]{1,0:T(8,128)(2,1)}, u32[]{:S(2)}, u32[]{:S(2)}) collective-permute-start(bf16[64,4608]{1,0:T(8,128)(2,1)} %get-tuple-element.194), channel_id=1, source_target_pairs={{0,8},{1,9},{2,10},{3,11},{4,12},{5,13},{6,14},{7,15},{8,0},{9,1},... | collective-permute-start | bytes 1769480 | tf_op jit(solution)/shard_map/ppermute | solution.py:90
  682.9 14.7 %collective-permute-start.56 = (bf16[2,64,1024]{2,1,0:T(8,128)(2,1)S(1)}, bf16[2,64,1024]{2,1,0:T(8,128)(2,1)S(1)}, u32[]{:S(2)}, u32[]{:S(2)}) collective-permute-start(bf16[2,64,1024]{2,1,0:T(8,128)(2,1)S(1)} %pad_maximum_fusion.19), channel_id=1, source_target_pairs={{0,8},{1,9},{2,10},{3,11},{4,12},{5,13},{6,14},{7,15},{8,0},{9,1},... | collective-permute-start | bytes 786440 | tf_op jit(solution)/shard_map/ppermute | solution.py:90
  685.2 12.4 %collective-permute-start.57 = (bf16[2,64,1024]{2,1,0:T(8,128)(2,1)S(1)}, bf16[2,64,1024]{2,1,0:T(8,128)(2,1)S(1)}, u32[]{:S(2)}, u32[]{:S(2)}) collective-permute-start(bf16[2,64,1024]{2,1,0:T(8,128)(2,1)S(1)} %pad_maximum_fusion.20), channel_id=1, source_target_pairs={{0,16},{1,17},{2,18},{3,19},{4,20},{5,21},{6,22},{7,23},{8,24},{9,... | collective-permute-start | bytes 786440 | tf_op jit(solution)/shard_map/ppermute | solution.py:90
  691.6 40.7 %collective-permute-start.55 = (bf16[4,128,2176]{2,1,0:T(8,128)(2,1)}, bf16[4,128,2176]{2,1,0:T(8,128)(2,1)}, u32[]{:S(2)}, u32[]{:S(2)}) collective-permute-start(bf16[4,128,2176]{2,1,0:T(8,128)(2,1)} %pad_maximum_fusion.1), channel_id=1, source_target_pairs={{0,1},{1,0},{2,3},{3,2},{4,5},{5,4},{6,7},{7,6},{8,9},{9,8},{10,11... | collective-permute-start | bytes 6684680 | tf_op jit(solution)/shard_map/ppermute | solution.py:98
  716.6 13.5 %collective-permute-start.70 = (bf16[64,1024]{1,0:T(8,128)(2,1)S(1)}, bf16[64,1024]{1,0:T(8,128)(2,1)S(1)}, u32[]{:S(2)}, u32[]{:S(2)}) collective-permute-start(bf16[64,1024]{1,0:T(8,128)(2,1)S(1)} %add_convert_fusion.22), channel_id=1, source_target_pairs={{0,2},{1,3},{2,0},{3,1},{4,6},{5,7},{6,4},{7,5},{8,10},{9,11},{10,... | collective-permute-start | bytes 393224 | tf_op jit(solution)/shard_map/ppermute | solution.py:98
  727.8 13.6 %collective-permute-start.75 = (bf16[64,4608]{1,0:T(8,128)(2,1)}, bf16[64,4608]{1,0:T(8,128)(2,1)S(1)}, u32[]{:S(2)}, u32[]{:S(2)}) collective-permute-start(bf16[64,4608]{1,0:T(8,128)(2,1)} %get-tuple-element.172), channel_id=1, source_target_pairs={{0,2},{1,3},{2,0},{3,1},{4,6},{5,7},{6,4},{7,5},{8,10},{9,11},{10,... | collective-permute-start | bytes 1769480 | tf_op jit(solution)/shard_map/ppermute | solution.py:98
  730.2 11.5 %collective-permute-start.71 = (bf16[128,1024]{1,0:T(8,128)(2,1)S(1)}, bf16[128,1024]{1,0:T(8,128)(2,1)S(1)}, u32[]{:S(2)}, u32[]{:S(2)}) collective-permute-start(bf16[128,1024]{1,0:T(8,128)(2,1)S(1)} %pad_maximum_fusion.21), channel_id=1, source_target_pairs={{0,1},{1,0},{2,3},{3,2},{4,5},{5,4},{6,7},{7,6},{8,9},{9,8},{10,11... | collective-permute-start | bytes 786440 | tf_op jit(solution)/shard_map/ppermute | solution.py:98
  736.0 14.3 %collective-permute-start.60 = (bf16[2,64,2176]{2,1,0:T(8,128)(2,1)S(1)}, bf16[2,64,2176]{2,1,0:T(8,128)(2,1)S(1)}, u32[]{:S(2)}, u32[]{:S(2)}) collective-permute-start(bf16[2,64,2176]{2,1,0:T(8,128)(2,1)S(1)} %pad_maximum_fusion.17), channel_id=1, source_target_pairs={{0,8},{1,9},{2,10},{3,11},{4,12},{5,13},{6,14},{7,15},{8,0},{9,1},... | collective-permute-start | bytes 1671176 | tf_op jit(solution)/shard_map/ppermute | solution.py:90
  736.9 14.0 %collective-permute-start.58 = (bf16[2,64,2176]{2,1,0:T(8,128)(2,1)S(1)}, bf16[2,64,2176]{2,1,0:T(8,128)(2,1)S(1)}, u32[]{:S(2)}, u32[]{:S(2)}) collective-permute-start(bf16[2,64,2176]{2,1,0:T(8,128)(2,1)S(1)} %pad_maximum_fusion.16), channel_id=1, source_target_pairs={{0,16},{1,17},{2,18},{3,19},{4,20},{5,21},{6,22},{7,23},{8,24},{9,... | collective-permute-start | bytes 1671176 | tf_op jit(solution)/shard_map/ppermute | solution.py:90
  741.6 27.9 %collective-permute-start.76 = (bf16[64,4608]{1,0:T(8,128)(2,1)S(1)}, bf16[64,4608]{1,0:T(8,128)(2,1)S(1)}, u32[]{:S(2)}, u32[]{:S(2)}) collective-permute-start(bf16[64,4608]{1,0:T(8,128)(2,1)S(1)} %add_convert_fusion.6), channel_id=1, source_target_pairs={{0,4},{1,5},{2,6},{3,7},{4,0},{5,1},{6,2},{7,3},{8,12},{9,13},{10,... | collective-permute-start | bytes 1769480 | tf_op jit(solution)/shard_map/ppermute | solution.py:98
  751.0 18.7 %collective-permute-start.59 = (bf16[64,2176]{1,0:T(8,128)(2,1)S(1)}, bf16[64,2176]{1,0:T(8,128)(2,1)S(1)}, u32[]{:S(2)}, u32[]{:S(2)}) collective-permute-start(bf16[64,2176]{1,0:T(8,128)(2,1)S(1)} %get-tuple-element.227), channel_id=1, source_target_pairs={{0,8},{1,9},{2,10},{3,11},{4,12},{5,13},{6,14},{7,15},{8,0},{9,1},... | collective-permute-start | bytes 835592 | tf_op jit(solution)/shard_map/ppermute | solution.py:90
  751.7 18.0 %collective-permute-start.61 = (bf16[64,2176]{1,0:T(8,128)(2,1)S(1)}, bf16[64,2176]{1,0:T(8,128)(2,1)S(1)}, u32[]{:S(2)}, u32[]{:S(2)}) collective-permute-start(bf16[64,2176]{1,0:T(8,128)(2,1)S(1)} %get-tuple-element.226), channel_id=1, source_target_pairs={{0,16},{1,17},{2,18},{3,19},{4,20},{5,21},{6,22},{7,23},{8,24},{9,... | collective-permute-start | bytes 835592 | tf_op jit(solution)/shard_map/ppermute | solution.py:90
  769.7 13.5 %collective-permute-start.77 = (bf16[64,4608]{1,0:T(8,128)(2,1)S(1)}, bf16[64,4608]{1,0:T(8,128)(2,1)S(1)}, u32[]{:S(2)}, u32[]{:S(2)}) collective-permute-start(bf16[64,4608]{1,0:T(8,128)(2,1)S(1)} %add_convert_fusion.5), channel_id=1, source_target_pairs={{0,2},{1,3},{2,0},{3,1},{4,6},{5,7},{6,4},{7,5},{8,10},{9,11},{10,... | collective-permute-start | bytes 1769480 | tf_op jit(solution)/shard_map/ppermute | solution.py:98
  770.0 19.1 %collective-permute-start.62 = (bf16[64,2176]{1,0:T(8,128)(2,1)S(1)}, bf16[64,2176]{1,0:T(8,128)(2,1)S(1)}, u32[]{:S(2)}, u32[]{:S(2)}) collective-permute-start(bf16[64,2176]{1,0:T(8,128)(2,1)S(1)} %get-tuple-element.178), channel_id=1, source_target_pairs={{0,2},{1,3},{2,0},{3,1},{4,6},{5,7},{6,4},{7,5},{8,10},{9,11},{10,... | collective-permute-start | bytes 835592 | tf_op jit(solution)/shard_map/ppermute | solution.py:98
  789.2 15.5 %collective-permute-start.63 = (bf16[64,2176]{1,0:T(8,128)(2,1)S(1)}, bf16[64,2176]{1,0:T(8,128)(2,1)S(1)}, u32[]{:S(2)}, u32[]{:S(2)}) collective-permute-start(bf16[64,2176]{1,0:T(8,128)(2,1)S(1)} %add_convert_fusion.19), channel_id=1, source_target_pairs={{0,4},{1,5},{2,6},{3,7},{4,0},{5,1},{6,2},{7,3},{8,12},{9,13},{10,... | collective-permute-start | bytes 835592 | tf_op jit(solution)/shard_map/ppermute | solution.py:98
  791.4 34.0 %collective-permute-start.78 = (bf16[128,4608]{1,0:T(8,128)(2,1)}, bf16[128,4608]{1,0:T(8,128)(2,1)}, u32[]{:S(2)}, u32[]{:S(2)}) collective-permute-start(bf16[128,4608]{1,0:T(8,128)(2,1)} %pad_maximum_fusion.11), channel_id=1, source_target_pairs={{0,1},{1,0},{2,3},{3,2},{4,5},{5,4},{6,7},{7,6},{8,9},{9,8},{10,11... | collective-permute-start | bytes 3538952 | tf_op jit(solution)/shard_map/ppermute | solution.py:98
  804.8 18.9 %collective-permute-start.64 = (bf16[64,2176]{1,0:T(8,128)(2,1)S(1)}, bf16[64,2176]{1,0:T(8,128)(2,1)}, u32[]{:S(2)}, u32[]{:S(2)}) collective-permute-start(bf16[64,2176]{1,0:T(8,128)(2,1)S(1)} %add_convert_fusion.18), channel_id=1, source_target_pairs={{0,2},{1,3},{2,0},{3,1},{4,6},{5,7},{6,4},{7,5},{8,10},{9,11},{10,... | collective-permute-start | bytes 835592 | tf_op jit(solution)/shard_map/ppermute | solution.py:98
  (125 other events, 1487.7 us)

commit v3 on v2

--- a/solution.py
+++ b/solution.py
@@ -111,22 +111,62 @@
 class Flow:
     def __init__(self, steps):
         self.steps = steps
-        self.pending = ()
         self.result = None
-        self.advance()
-
-    def advance(self):
+        self.pending = next(steps)
+
+    def resume(self, arrived):
         try:
-            self.pending = next(self.steps)
+            self.pending = self.steps.send(arrived)
         except StopIteration as stop:
             self.pending = ()
-            if stop.value is not None:
-                self.result = stop.value
+            self.steps = None
+            self.result = stop.value
 
     def finish(self):
-        while self.result is None:
-            self.advance()
+        while self.steps is not None:
+            self.resume(self.pending)
         return self.result
+
+
+def sync(values, *flows):
+    flows = [flow for flow in flows if flow.steps is not None]
+    values, arrived = lax.optimization_barrier((values, [flow.pending for flow in flows]))
+    for flow, got in zip(flows, arrived):
+        flow.resume(got)
+    return values
+
+
+def place_kernel(spots_ref, *refs):
+    del spots_ref
+    out_ref = refs[-1]
+    for at in range(len(refs) - 1):
+
+        @pl.when(pl.program_id(0) == at)
+        def _():
+            out_ref[...] = refs[at][...]
+
+
+def place_blocks(blocks, spots):
+    count = len(blocks)
+    rows, width = blocks[0].shape
+    return pl.pallas_call(
+        place_kernel,
+        out_shape=jax.ShapeDtypeStruct((count * rows, width), blocks[0].dtype),
+        grid_spec=pltpu.PrefetchScalarGridSpec(
+            num_scalar_prefetch=1,
+            grid=(count,),
+            in_specs=[
+                pl.BlockSpec((rows, width), lambda i, spot: (0, 0), pipeline_mode=pl.Buffered(1))
+                for _ in blocks
+            ],
+            out_specs=pl.BlockSpec((rows, width), lambda i, spot: (spot[i], 0)),
+        ),
+        cost_estimate=pl.CostEstimate(
+            flops=0, bytes_accessed=4 * count * rows * width, transcendentals=0
+        ),
+        compiler_params=pltpu.CompilerParams(vmem_limit_bytes=60 << 20),
+        name="place_blocks",
+    )(jnp.stack(spots).astype(jnp.int32), *blocks)
 
 
 def gather_steps(links, mine, whole):
@@ -139,33 +179,34 @@
     if shard_size == 4:
         pieces[1] = shard_swap(mine, 1)
         pieces[2] = shard_swap(mine, 2)
-        yield (pieces[1], pieces[2])
+        pieces[1], pieces[2] = yield (pieces[1], pieces[2])
         corner_a = shard_swap(pieces[1][:quarter], 2)
         corner_b = shard_swap(pieces[2][quarter:], 1)
         others[1] = rep_swap(pieces[1], 1)
         others[2] = rep_swap(pieces[2], 1)
-        yield (corner_a, corner_b, others[1], others[2])
+        corner_a, corner_b, others[1], others[2] = yield (
+            corner_a, corner_b, others[1], others[2]
+        )
         pieces[3] = jnp.concatenate([corner_a, corner_b], axis=0)
         others[3] = rep_swap(pieces[3], 1)
-        yield (others[3],)
+        (others[3],) = yield (others[3],)
     else:
         pieces[0] = mine
         bit = 1
         while bit < shard_size:
             order = sorted(pieces)
             got = shard_swap(jnp.stack([pieces[d] for d in order]), bit)
-            yield (got,)
+            (got,) = yield (got,)
             for at, d in enumerate(order):
                 pieces[d ^ bit] = got[at]
             bit *= 2
         del pieces[0]
         others = {d: rep_swap(piece, 1) for d, piece in pieces.items()}
-    full = jnp.zeros((shard_size, 2, half, width), mine.dtype)
-    full = lax.dynamic_update_slice(full, whole.reshape((1, 2, half, width)), (me, 0, 0, 0))
+    blocks, spots = [whole[:half], whole[half:]], [2 * me, 2 * me + 1]
     for d in pieces:
-        full = lax.dynamic_update_slice(full, pieces[d][None, None], (me ^ d, core, 0, 0))
-        full = lax.dynamic_update_slice(full, others[d][None, None], (me ^ d, 1 - core, 0, 0))
-    return full.reshape(shard_size * 2 * half, width)
+        blocks += [pieces[d], others[d]]
+        spots += [2 * (me ^ d) + core, 2 * (me ^ d) + 1 - core]
+    return place_blocks(blocks, spots)
 
 
 def core_half(weight):
@@ -174,9 +215,28 @@
     return lax.dynamic_slice_in_dim(weight, core * half, half, 0)
 
 
-def core_sum(links, own, other):
-    received = links[3](other().astype(jnp.bfloat16), 1)
-    return (own() + received.astype(jnp.float32)).astype(jnp.bfloat16)
+def pick_columns(links, value):
+    core = lax.rem(lax.axis_index("rep"), 2)
+    width = value.shape[1] // links[0] // 2
+
+    def half(which):
+        return jnp.concatenate(
+            [
+                lax.dynamic_slice_in_dim(value, (2 * d + which) * width, width, 1)
+                for d in range(links[0])
+            ],
+            axis=1,
+        )
+
+    return half(core), half(1 - core)
+
+
+def blocked(links, product):
+    return product.reshape(links[0], -1, product.shape[1])
+
+
+def combine(product, received):
+    return (product + received.astype(jnp.float32)).astype(jnp.bfloat16)
 
 
 def scatter_steps(links, part):
@@ -193,10 +253,10 @@
     if shard_size == 4:
         got_a = shard_swap(jnp.stack([piece(1, 0), piece(3, 0)]), 1)
         got_b = shard_swap(jnp.stack([piece(2, 1), piece(3, 1)]), 2)
-        yield (got_a, got_b)
+        got_a, got_b = yield (got_a, got_b)
         pass_a = shard_swap(add_low(piece(2, 0), got_a[1]), 2)
         pass_b = shard_swap(add_low(piece(1, 1), got_b[1]), 1)
-        yield (pass_a, pass_b)
+        pass_a, pass_b = yield (pass_a, pass_b)
         sum_a = add_low(piece(0, 0).astype(jnp.float32) + got_a[0].astype(jnp.float32), pass_a)
         sum_b = add_low(piece(0, 1).astype(jnp.float32) + got_b[0].astype(jnp.float32), pass_b)
         halves = [sum_a, sum_b]
@@ -206,7 +266,7 @@
         while bit:
             sent = [d for d in sorted(held) if d & bit]
             got = shard_swap(jnp.stack([held[d] for d in sent]), bit)
-            yield (got,)
+            (got,) = yield (got,)
             held = {d ^ bit: add_low(held[d ^ bit], got[at]) for at, d in enumerate(sent)}
             bit //= 2
         halves = [held[0][0], held[0][1]]
@@ -215,16 +275,16 @@
         keep = jnp.where(upper, halves[1], halves[0])
         send = jnp.where(upper, halves[0], halves[1])
         got = rep_swap(send, 2)
-        yield (got,)
+        (got,) = yield (got,)
         keep = add_low(keep, got)
         bit = 4
         while bit < rep_size:
             got = rep_swap(keep, bit)
-            yield (got,)
+            (got,) = yield (got,)
             keep = add_low(keep, got)
             bit *= 2
         back = rep_swap(keep, 2)
-        yield (back,)
+        (back,) = yield (back,)
         halves = [jnp.where(upper, back, keep), jnp.where(upper, keep, back)]
         half = jnp.concatenate(halves, axis=0)
     else:
@@ -233,7 +293,9 @@
         while bit < rep_size:
             half = add_low(half, rep_swap(half, bit))
             bit *= 2
-    return half, rep_swap(half, 1)
+    other = rep_swap(half, 1)
+    (other,) = yield (other,)
+    return half, other
 
 
 def join_rows(pair):
@@ -254,32 +316,6 @@
         jnp.concatenate([half, other], axis=1),
         jnp.concatenate([other, half], axis=1),
     ).astype(jnp.float32)
-
-
-def row_halves(links, left_mat, right_mat):
-    shard_size = links[0]
-    core = lax.rem(lax.axis_index("rep"), 2)
-    count, width = left_mat.shape
-    cut = left_mat.reshape(count, shard_size, 2, width // shard_size // 2)
-
-    def half(which):
-        picked = lax.dynamic_slice_in_dim(cut, which, 1, 2)
-        product = matmul_rows(picked.reshape(count, width // 2), right_mat)
-        return product.reshape(shard_size, width // shard_size // 2, right_mat.shape[1])
-
-    return (lambda: half(core)), (lambda: half(1 - core))
-
-
-def column_halves(links, left_mat, right_mat):
-    shard_size = links[0]
-    core = lax.rem(lax.axis_index("rep"), 2)
-    width = right_mat.shape[1] // 2
-
-    def half(which):
-        picked = lax.dynamic_slice_in_dim(right_mat, which * width, width, 1)
-        return matmul_rows(left_mat, picked).reshape(shard_size, -1, width)
-
-    return (lambda: half(core)), (lambda: half(1 - core))
 
 
 BLOCK = 256
@@ -503,6 +539,8 @@
     w_down,
 ):
     row_count = tokens.shape[0]
+    rep_swap = links[3]
+    core = lax.rem(lax.axis_index("rep"), 2)
     score_scale = 1.0 / math.sqrt(HD)
     spare = jnp.zeros((attn_gain.shape[0] - qk_gain.shape[0],), jnp.bfloat16)
     packed = jnp.stack([attn_gain, ffn_gain, jnp.concatenate([qk_gain, spare])], axis=1)
@@ -515,10 +553,11 @@
             jnp.concatenate(attn_weights, axis=1),
         )
     )
-    out_flow = Flow(gather_steps(links, pin(core_half(w_out), front_flow.pending), w_out))
-    front_flow.advance()
-    gate_flow = Flow(gather_steps(links, pin(core_half(w_gate), out_flow.pending), w_gate))
-    out_flow.advance()
+    w_out, w_gate, w_up, w_down = sync((w_out, w_gate, w_up, w_down), front_flow)
+    out_flow = Flow(gather_steps(links, core_half(w_out), w_out))
+    w_gate, w_up, w_down = sync((w_gate, w_up, w_down), front_flow, out_flow)
+    gate_flow = Flow(gather_steps(links, core_half(w_gate), w_gate))
+    w_up, w_down = sync((w_up, w_down), front_flow)
     front = front_flow.finish()
     full_query = front[:, : HQ * HD]
     full_key = front[:, HQ * HD : (HQ + HK) * HD]
@@ -554,72 +593,88 @@
     query_rot = query_rot.reshape(row_count, HQ * HD)
     key_rot = key_rot.reshape(row_count, HK * HD)
     value_low = value_low.reshape(row_count, HK * HD)
-    up_flow = Flow(gather_steps(links, pin(core_half(w_up), out_flow.pending), w_up))
+    query_rot, key_rot, value_low, w_up, w_down = sync(
+        (query_rot, key_rot, value_low, w_up, w_down), out_flow, gate_flow
+    )
+    up_flow = Flow(gather_steps(links, core_half(w_up), w_up))
+    attn_low = attend(query_rot, key_rot, value_low, segment)
+    attn_low = sync(attn_low, out_flow)
     full_out = out_flow.finish()
-    query_rot, key_rot = pin((query_rot, key_rot), full_out)
-    attn_low = attend(query_rot, key_rot, value_low, segment)
-    attn_low = pin(attn_low, gate_flow.pending)
-    gate_flow.advance()
-    down_flow = Flow(gather_steps(links, pin(core_half(w_down), up_flow.pending), w_down))
-    up_flow.advance()
-    full_gate = gate_flow.finish()
-    full_up = up_flow.finish()
     hidden = inputs + matmul_plain(attn_low, full_out)
     scale_two = inv_rms(hidden)
     normed_ffn = (hidden * scale_two * full_ffn_gain.astype(jnp.float32)).astype(jnp.bfloat16)
+    normed_ffn, hidden, w_down = sync((normed_ffn, hidden, w_down), gate_flow, up_flow)
+    down_flow = Flow(gather_steps(links, core_half(w_down), w_down))
+    normed_ffn = sync(normed_ffn, gate_flow)
+    full_gate = gate_flow.finish()
     gate_proj = matmul_plain(normed_ffn, full_gate)
+    gate_proj, normed_ffn = sync((gate_proj, normed_ffn), up_flow, down_flow)
+    normed_ffn = sync(normed_ffn, up_flow)
+    full_up = up_flow.finish()
     up_proj = matmul_plain(normed_ffn, full_up)
     gate_sig = jax.nn.sigmoid(gate_proj)
     gate_act = gate_proj * gate_sig
     mixed_act = (gate_act * up_proj).astype(jnp.bfloat16)
     slope = (up_proj * gate_sig * (1.0 + gate_proj * (1.0 - gate_sig))).astype(jnp.bfloat16)
     act_low = gate_act.astype(jnp.bfloat16)
-    mixed_act, slope, act_low = pin((mixed_act, slope, act_low), down_flow.pending)
-    down_flow.advance()
+    mixed_act, slope, act_low = sync((mixed_act, slope, act_low), down_flow)
+    mixed_act, slope, act_low = sync((mixed_act, slope, act_low), down_flow)
     full_down = down_flow.finish()
     out_grad = live_rows * cotangent.astype(jnp.float32)
     out_low = out_grad.astype(jnp.bfloat16)
     grad_mixed = matmul_cols(out_low, full_down)
     grad_up_low = (grad_mixed * act_low.astype(jnp.float32)).astype(jnp.bfloat16)
     grad_gate_low = (grad_mixed * slope.astype(jnp.float32)).astype(jnp.bfloat16)
-    grad_up_low, grad_gate_low = pin((grad_up_low, grad_gate_low))
-    down_part = core_sum(links, *column_halves(links, mixed_act, out_low))
+    half = out_low.shape[1] // 2
+    out_own = lax.dynamic_slice_in_dim(out_low, core * half, half, 1)
+    out_other = lax.dynamic_slice_in_dim(out_low, (1 - core) * half, half, 1)
+    normed_own, normed_other = pick_columns(links, normed_ffn)
+    grad_up_low, grad_gate_low, out_own, out_other, mixed_act = pin(
+        (grad_up_low, grad_gate_low, out_own, out_other, mixed_act)
+    )
+
+    def hand(product):
+        return rep_swap(blocked(links, product).astype(jnp.bfloat16), 1)
+
+    down_sent = hand(matmul_rows(mixed_act, out_other))
+    gate_given = matmul_rows(normed_other, pin(grad_gate_low, down_sent)).astype(jnp.bfloat16)
+    gate_sent = hand(gate_given)
+    down_sent, mixed_act, grad_up_low, gate_given = pin(
+        (down_sent, mixed_act, grad_up_low, gate_given)
+    )
+    down_part = combine(blocked(links, matmul_rows(mixed_act, out_own)), down_sent)
     down_back = Flow(scatter_steps(links, down_part))
-    gate_left = pin(grad_gate_low, down_part)
-    gate_part = core_sum(links, *row_halves(links, normed_ffn, gate_left))
-    up_left = pin(grad_up_low, gate_part)
-    up_part = core_sum(links, *row_halves(links, normed_ffn, up_left))
-    grad_gate_low = pin(grad_gate_low, up_part, down_back.pending)
-    gate_back = Flow(scatter_steps(links, pin(gate_part, down_back.pending)))
-    down_back.advance()
-    from_gate = matmul_cols(grad_gate_low, full_gate)
-    grad_up_low = pin(grad_up_low, from_gate, down_back.pending)
-    down_back.advance()
-    grad_normed_ffn = from_gate + matmul_cols(grad_up_low, full_up)
-    grad_normed_ffn = pin(grad_normed_ffn, gate_back.pending, down_back.pending)
-    up_back = Flow(scatter_steps(links, pin(up_part, gate_back.pending)))
-    gate_back.advance()
-    down_back.advance()
+    grad_up_low, grad_gate_low, normed_own, normed_other = pin(
+        (grad_up_low, grad_gate_low, normed_own, normed_other), down_part
+    )
+    up_sent = hand(matmul_rows(normed_other, grad_up_low))
+    gate_part = combine(blocked(links, matmul_rows(normed_own, grad_gate_low)), gate_sent)
+    up_part = combine(blocked(links, matmul_rows(normed_own, grad_up_low)), up_sent)
+    gate_part, up_part, grad_gate_low, grad_up_low = sync(
+        (gate_part, up_part, grad_gate_low, grad_up_low), down_back
+    )
+    gate_back = Flow(scatter_steps(links, gate_part))
+    grad_normed_ffn = matmul_cols(grad_gate_low, full_gate) + matmul_cols(grad_up_low, full_up)
+    grad_normed_ffn, up_part = sync((grad_normed_ffn, up_part), down_back)
     grad_ffn_gain = jnp.sum(grad_normed_ffn * hidden * scale_two, axis=0)
     grad_hidden = out_grad + norm_back(
         grad_normed_ffn, hidden, scale_two, full_ffn_gain.astype(jnp.float32)
     )
     hidden_low = grad_hidden.astype(jnp.bfloat16)
     grad_attn_low = matmul_cols(hidden_low, full_out).astype(jnp.bfloat16)
-    out_part = core_sum(links, *row_halves(links, attn_low, hidden_low))
+    attn_own, attn_other = pick_columns(links, attn_low)
+    out_sent = hand(matmul_rows(attn_other, hidden_low))
+    out_part = combine(blocked(links, matmul_rows(attn_own, hidden_low)), out_sent)
     panels = HK // 4
-    grad_attn_low = pin(grad_attn_low, out_part, down_back.pending)
-    down_back.advance()
+    grad_attn_low, out_part, up_part = sync(
+        (grad_attn_low, out_part, up_part), gate_back, down_back
+    )
+    up_back = Flow(scatter_steps(links, up_part))
     lower = attend_back(query_rot, grad_attn_low, key_rot, value_low, segment, 0, panels)
-    grad_attn_low = pin(grad_attn_low, lower, gate_back.pending, up_back.pending, down_back.pending)
-    gate_back.advance()
-    up_back.advance()
-    down_back.advance()
+    grad_attn_low, lower = pin((grad_attn_low, lower))
     upper = attend_back(query_rot, grad_attn_low, key_rot, value_low, segment, panels, panels)
-    upper = pin(upper, up_back.pending, gate_back.pending)
-    out_back = Flow(scatter_steps(links, pin(out_part, up_back.pending)))
-    up_back.advance()
-    gate_back.advance()
+    lower, upper, out_part = sync((lower, upper, out_part), gate_back, down_back)
+    out_back = Flow(scatter_steps(links, out_part))
     grad_query_rot, grad_key_rot, grad_value = (
         jnp.concatenate(pair, axis=1) for pair in zip(lower, upper)
     )
@@ -645,6 +700,14 @@
         .reshape(row_count, HK * HD)
     )
     grad_value_low = grad_value.astype(jnp.bfloat16).reshape(row_count, HK * HD)
+    normed_own, normed_other = pick_columns(links, normed)
+    grad_front = jnp.concatenate([grad_query_low, grad_key_low, grad_value_low], axis=1)
+    grad_front = sync(grad_front, up_back, gate_back, down_back, out_back)
+    grad_query_low = grad_front[:, : HQ * HD]
+    grad_key_low = grad_front[:, HQ * HD : (HQ + HK) * HD]
+    grad_value_low = grad_front[:, (HQ + HK) * HD :]
+    front_other = blocked(links, matmul_rows(normed_other, grad_front))
+    front_own = blocked(links, matmul_rows(normed_own, grad_front))
     grad_normed = (
         matmul_cols(grad_query_low, full_query)
         + matmul_cols(grad_key_low, full_key)
@@ -659,23 +722,16 @@
     small = small.at[:, :, 1].set(grad_ffn_gain.reshape(links[0], -1))
     small = small.at[:, : qk_gain.shape[0], 2].set(grad_qk_gain.reshape(links[0], -1))
     small = small.reshape(links[0], 2, -1, 128)
-    core = lax.rem(lax.axis_index("rep"), 2)
-    own_front, other_front = row_halves(
-        links, normed, jnp.concatenate([grad_query_low, grad_key_low, grad_value_low], axis=1)
-    )
-
-    def with_small(product, which):
-        extra = lax.dynamic_slice_in_dim(small, which, 1, 1)[:, 0]
-        return jnp.concatenate([product(), extra], axis=2)
-
-    front_part = core_sum(
-        links,
-        lambda: with_small(own_front, core),
-        lambda: with_small(other_front, 1 - core),
-    )
-    front_back = Flow(scatter_steps(links, pin(front_part, out_back.pending)))
-    last_act = pin(mixed_act, front_part)
-    result = live_rows * (hidden + matmul_plain(last_act, full_down))
+    own_front = jnp.concatenate([front_own, lax.dynamic_slice_in_dim(small, core, 1, 1)[:, 0]], axis=2)
+    other_front = jnp.concatenate(
+        [front_other, lax.dynamic_slice_in_dim(small, 1 - core, 1, 1)[:, 0]], axis=2
+    )
+    front_sent = rep_swap(other_front.astype(jnp.bfloat16), 1)
+    front_part = combine(own_front, front_sent)
+    front_part, mixed_act = sync((front_part, mixed_act), out_back, up_back, gate_back)
+    front_back = Flow(scatter_steps(links, front_part))
+    result = live_rows * (hidden + matmul_plain(mixed_act, full_down))
+    grad_inputs, result = sync((grad_inputs, result), up_back, gate_back, out_back, front_back)
     front_share = join_rows(front_back.finish())
     share_query = front_share[:, : HQ * HD]
     share_key = front_share[:, HQ * HD : (HQ + HK) * HD]

time: 837 us -> 780 us (0.932)
  waiting for transfers between devices: 207 us -> 110 us
  other arithmetic: 93.1 us -> 169 us
  Pallas kernels: 60.8 us -> 101 us
  local copies, waits for them, and re-layouts: 146 us -> 108 us
  starting transfers between devices: 111 us -> 83.9 us
  matrix products: 212 us -> 197 us
    ppermute x40, waiting for transfers between devices: 100 us -> 47.9 us  [shard_swap(): return lax.ppermute(value, axes, pairs)]
    ppermute x40, waiting for transfers between devices: 107 us -> 62.3 us  [rep_swap(): return lax.ppermute(value, axes, pairs)]
    pallas_call x0 -> x5, Pallas kernels: none -> 40.6 us  [place_blocks(): pl.pallas_call(place_kernel, out_shape=jax.ShapeDtypeStruct((count * rows...]
    dynamic_update_slice x35 -> x0, local copies, waits for them, and re-layouts: 33.5 us -> none  [the longest x15 19.4 us: gather_steps(): lax.dynamic_update_slice(full, pieces[d][None, None], (me ^ d, core, 0, 0))]
    convert_element_type x3 -> x6, other arithmetic: 11.6 us -> 44.5 us  [the longest x5 25.4 us: combine(): return (product + received.astype(jnp.float32)).astype(jnp.bfloat16)]
    ppermute x40, starting transfers between devices: 70.9 us -> 43.5 us  [rep_swap(): return lax.ppermute(value, axes, pairs)]
    convert_element_type x15, other arithmetic: 7.81 us -> 23.6 us  [add_low(): (left.astype(jnp.float32) + right.astype(jnp.float32)).astype(jnp.bfloat16)]
    dot_general x7, matrix products: 70 us -> 60.5 us  [matmul_plain(): return jnp.dot(left_mat, right_mat, preferred_element_type=jnp.float32)]
  transfers between devices with their start and end apart: 80 -> 80, of which waited for: 26 -> 18; matrix products, arithmetic and copies ran while one was open for 39% -> 47% of each run, Pallas kernels for 7% -> 12%
where the time goes in v3:
time: 780 us; the launch traced here: 773 us
  matrix products  197 us (25%)
  other arithmetic  169 us (22%)
  waiting for transfers between devices  110 us (14%)
  local copies, waits for them, and re-layouts  108 us (14%)
  Pallas kernels  101 us (13%)
  starting transfers between devices  83.9 us (11%)
    dot_general x7, matrix products, matmul_cols(): lax.dot_general(left_mat, right_mat, (((1,), (1,)), ((), ())), preferred_...  69.2 us
    dot_general x10, matrix products, matmul_rows(): lax.dot_general(left_mat, right_mat, (((0,), (0,)), ((), ())), preferred_...  67.7 us
    ppermute x40, waiting for transfers between devices, rep_swap(): return lax.ppermute(value, axes, pairs)  62.3 us
    dot_general x7, matrix products, matmul_plain(): return jnp.dot(left_mat, right_mat, preferred_element_type=jnp.float32)  60.5 us
    ppermute x40, waiting for transfers between devices, shard_swap(): return lax.ppermute(value, axes, pairs)  47.9 us
    ppermute x40, starting transfers between devices, rep_swap(): return lax.ppermute(value, axes, pairs)  43.5 us
    pallas_call x5, Pallas kernels, place_blocks(): pl.pallas_call(place_kernel, out_shape=jax.ShapeDtypeStruct((count * rows...  40.6 us
    ppermute x40, starting transfers between devices, shard_swap(): return lax.ppermute(value, axes, pairs)  40.4 us
  transfers between devices with their start and end apart: 80, of which 18 were waited for; matrix products, arithmetic and copies ran while one was open for 47% of the time, Pallas kernels for 12%

profile of v3, /device:TPU:1, one launch (start us, length us, event | category | flops | bytes accessed | tf_op | source)
XLA Modules:
  0.0 772.6 jit_solution(9190106059843884089)
XLA Ops:
  9.2 2.9 copy.141
  14.6 5.8 collective-permute-done.refs_2_
  34.2 5.2 collective-permute-done.2
  42.7 3.8 fusion.109
  52.8 6.8 place_blocks.5
  65.9 4.5 multiply_reduce_fusion.4
  82.4 4.3 collective-permute-done.9
  92.5 3.9 copy.144.q_ref
  97.8 23.2 %attend.1 = bf16[1024,1024]{1,0:T(8,128)(2,1)} custom-call(s32[4,4]{1,0:T(4,128)} %fusion.90.live_ref, bf16[1024,1024]{1,0:T(8,128)(2,1)} %copy.144.q_ref, bf16[1024,512]{1,0:T(8,128)(2,1)} %copy.145.k_ref, bf16[1024,512]{1,0:T(8,128)(2,1)} %convolution_convert_fusion.6.v_ref, s32[1024,1]{1,0:T(8,128)} %copy.146.seg_col_ref, s32[1,1024]{1,0:T(1,128)} %bitcast.219), custom_call_target="tpu_custom_call" | custom-call | flops 19327352832 | bytes 8388608 | tf_op jit(solution)/shard_map/attend/pallas_call | solution.py:457
  124.9 4.3 collective-permute-start.16
  129.2 5.6 place_blocks.6
  134.8 4.9 multiply_reduce_fusion.3
  139.7 3.4 collective-permute-done.16
  144.4 13.0 %collective-permute-done.17 = bf16[64,4608]{1,0:T(8,128)(2,1)S(1)} collective-permute-done((bf16[64,4608]{1,0:T(8,128)(2,1)S(1)}, bf16[64,4608]{1,0:T(8,128)(2,1)S(1)}, u32[]{:S(2)}, u32[]{:S(2)}) %collective-permute-start.17) | collective-permute-done | bytes 589856 | tf_op jit(solution)/shard_map/ppermute | solution.py:90
  165.3 3.8 constant_dynamic-slice_fusion.49
  172.3 9.2 %place_blocks.7 = bf16[1024,4608]{1,0:T(8,128)(2,1)} custom-call(s32[8]{0:T(128)} %stack.54.spots_ref, bf16[128,4608]{1,0:T(8,128)(2,1)} %get-tuple-element.441.refs_0_, bf16[128,4608]{1,0:T(8,128)(2,1)} %get-tuple-element.440.refs_1_, bf16[128,4608]{1,0:T(8,128)(2,1)} %collective-permute-done.13.refs_2_, bf16[128,4608]{1,0:T(8,128)(2,1)} %copy-done.42, ...), custom_call_target="tpu_custom_call" | custom-call | bytes 18874368 | tf_op jit(solution)/shard_map/place_blocks/pallas_call | solution.py:152
  182.9 16.3 %fusion.115 = f32[1024,4608]{1,0:T(8,128)} fusion(bf16[1024,1024]{0,1:T(8,128)(2,1)S(1)} %multiply_convert_fusion.4, bf16[1024,4608]{1,0:T(8,128)(2,1)} %place_blocks.7), kind=kOutput, calls=%fused_computation.338 | convolution fusion | flops 9663676416 | bytes 30408704 | tf_op jit(solution)/shard_map/dot_general | solution.py:65
  199.2 10.1 %collective-permute-done.24 = bf16[64,4608]{1,0:T(8,128)(2,1)S(1)} collective-permute-done((bf16[64,4608]{1,0:T(8,128)(2,1)}, bf16[64,4608]{1,0:T(8,128)(2,1)S(1)}, u32[]{:S(2)}, u32[]{:S(2)}) %collective-permute-start.24) | collective-permute-done | bytes 589856 | tf_op jit(solution)/shard_map/ppermute | solution.py:90
  216.7 9.4 %place_blocks.8 = bf16[1024,4608]{1,0:T(8,128)(2,1)} custom-call(s32[8]{0:T(128)} %stack.54.spots_ref, bf16[128,4608]{1,0:T(8,128)(2,1)} %get-tuple-element.435.refs_0_, bf16[128,4608]{1,0:T(8,128)(2,1)} %get-tuple-element.434.refs_1_, bf16[128,4608]{1,0:T(8,128)(2,1)} %collective-permute-done.20.refs_2_, bf16[128,4608]{1,0:T(8,128)(2,1)} %collective-permute-done.25.refs_3_, ...), custom_call_target="tpu_custom_call" | custom-call | bytes 18874368 | tf_op jit(solution)/shard_map/place_blocks/pallas_call | solution.py:152
  226.1 13.2 %fusion.116 = f32[1024,4608]{1,0:T(8,128)S(1)} fusion(bf16[1024,1024]{0,1:T(8,128)(2,1)S(1)} %multiply_convert_fusion.4, bf16[1024,4608]{1,0:T(8,128)(2,1)} %place_blocks.8), kind=kOutput, calls=%fused_computation.339 | convolution fusion | flops 9663676416 | bytes 30408704 | tf_op jit(solution)/shard_map/dot_general | solution.py:65
  239.2 19.1 %multiply_convert_fusion.2 = (bf16[1024,4608]{1,0:T(8,128)(2,1)}, bf16[1024,4608]{1,0:T(8,128)(2,1)}, bf16[1024,4608]{1,0:T(8,128)(2,1)}) fusion(f32[1024,4608]{1,0:T(8,128)} %fusion.115, f32[1024,4608]{1,0:T(8,128)S(1)} %fusion.116), kind=kLoop, calls=%fused_computation.2 | loop fusion | flops 61341696 | bytes 66060288 | tf_op jit(solution)/shard_map/convert_element_type | solution.py:618
  261.4 2.9 copy.140
  267.0 9.5 %place_blocks.9 = bf16[4608,1024]{1,0:T(8,128)(2,1)} custom-call(s32[8]{0:T(128)} %stack.54.spots_ref, bf16[576,1024]{1,0:T(8,128)(2,1)} %get-tuple-element.439.refs_0_, bf16[576,1024]{1,0:T(8,128)(2,1)} %get-tuple-element.438.refs_1_, bf16[576,1024]{1,0:T(8,128)(2,1)} %copy-done.29, bf16[576,1024]{1,0:T(8,128)(2,1)} %collective-permute-done.32.refs_3_, ...), custom_call_target="tpu_custom_call" | custom-call | bytes 18874368 | tf_op jit(solution)/shard_map/place_blocks/pallas_call | solution.py:152
  276.5 24.2 %multiply_convert_fusion = (bf16[1024,4608]{1,0:T(8,128)(2,1)}, bf16[1024,4608]{1,0:T(8,128)(2,1)}) fusion(bf16[1024,4608]{1,0:T(8,128)(2,1)} %get-tuple-element.241, bf16[1024,4608]{1,0:T(8,128)(2,1)} %get-tuple-element.240, bf16[1024,1024]{0,1:T(8,128)(2,1)} %copy-done.16, bf16[4608,1024]{1,0:T(8,128)(2,1)} %place_blocks.9), kind=kOutput, calls=%fused_computation | convolution fusion | flops 9691987968 | bytes 49283072 | tf_op jit(solution)/shard_map/dot_general | solution.py:75
  300.7 8.1 %convolution_convert_fusion = bf16[4608,512]{1,0:T(8,128)(2,1)} fusion(bf16[1024,4608]{1,0:T(8,128)(2,1)S(1)} %bitcast.199, bf16[1024,512]{0,1:T(8,128)(2,1)} %get-tuple-element.244), kind=kOutput, calls=%fused_computation.15 | convolution fusion | flops 4834197504 | bytes 15204352 | tf_op jit(solution)/shard_map/dot_general | solution.py:69
  313.1 4.0 collective-permute-done.35
  317.1 11.7 %convolution_convert_fusion.2 = bf16[512,4608]{1,0:T(8,128)(2,1)} fusion(bf16[1024,4608]{1,0:T(8,128)(2,1)} %get-tuple-element.256, bf16[1024,128]{0,1:T(8,128)(2,1)S(1)} %get-tuple-element.475, bf16[1024,128]{0,1:T(8,128)(2,1)S(1)} %get-tuple-element.476, bf16[1024,128]{0,1:T(8,128)(2,1)S(1)} %get-tuple-element.477, ...), kind=kOutput, calls=%fused_computation.17 | convolution fusion | flops 4838391808 | bytes 15204352 | tf_op jit(solution)/shard_map/dot_general | solution.py:69
  328.8 5.5 fusion.117
  334.3 6.5 add_convert_fusion.2
  340.9 9.4 %convolution_convert_fusion.1 = bf16[512,4608]{1,0:T(8,128)(2,1)} fusion(bf16[1024,512]{0,1:T(8,128)(2,1)} %pad_maximum_fusion.16, bf16[1024,4608]{1,0:T(8,128)(2,1)} %get-tuple-element.257), kind=kOutput, calls=%fused_computation.16 | convolution fusion | flops 4834197504 | bytes 15204352 | tf_op jit(solution)/shard_map/dot_general | solution.py:69
  362.6 11.9 %fusion.119 = f32[512,4608]{1,0:T(8,128)} fusion(bf16[1024,512]{0,1:T(8,128)(2,1)S(1)} %copy-done.49, bf16[1024,4608]{1,0:T(8,128)(2,1)} %get-tuple-element.257), kind=kOutput, calls=%fused_computation.342 | convolution fusion | flops 4831838208 | bytes 19922944 | tf_op jit(solution)/shard_map/dot_general | solution.py:69
  374.6 7.5 fusion.118
  382.0 8.6 %add_convert_fusion = bf16[4,128,4608]{2,1,0:T(8,128)(2,1)} fusion(f32[4,128,4608]{2,1,0:T(8,128)} %bitcast.196, bf16[4,128,4608]{2,1,0:T(8,128)(2,1)} %collective-permute-done.37), kind=kLoop, calls=%fused_computation.6 | loop fusion | flops 7077888 | bytes 18874368 | tf_op jit(solution)/shard_map/convert_element_type | solution.py:239
  390.6 6.4 add_convert_fusion.1
  400.0 16.0 %fusion.120 = f32[1024,1024]{0,1:T(8,128)} fusion(bf16[1024,4608]{1,0:T(8,128)(2,1)} %get-tuple-element.257, bf16[1024,4608]{1,0:T(8,128)(2,1)} %place_blocks.8), kind=kOutput, calls=%fused_computation.343 | convolution fusion | flops 9663676416 | bytes 23068672 | tf_op jit(solution)/shard_map/dot_general | solution.py:75
  420.9 14.9 %convolution_add_fusion = f32[1024,1024]{0,1:T(8,128)S(1)} fusion(f32[1024,1024]{0,1:T(8,128)S(1)} %copy-done.103, bf16[1024,4608]{1,0:T(8,128)(2,1)} %get-tuple-element.256, bf16[1024,4608]{1,0:T(8,128)(2,1)} %place_blocks.7), kind=kOutput, calls=%fused_computation.87 | convolution fusion | flops 9664724992 | bytes 27262976 | tf_op jit(solution)/shard_map/dot_general | solution.py:75
  445.5 3.8 collective-permute-start.45
  449.9 6.7 convolution_convert_fusion.4.do_ref
  466.6 2.9 fusion.76
  471.4 18.9 %attend_back.2 = (f32[1024,512]{1,0:T(8,128)}, f32[1024,256]{1,0:T(8,128)}, f32[1024,256]{1,0:T(8,128)}) custom-call(s32[4,4]{1,0:T(4,128)} %fusion.90.live_ref, bf16[1024,1024]{1,0:T(8,128)(2,1)} %copy.144.q_ref, bf16[1024,1024]{1,0:T(8,128)(2,1)} %convolution_convert_fusion.4.do_ref, bf16[1024,512]{1,0:T(8,128)(2,1)} %copy.145.k_ref, ...), custom_call_target="tpu_custom_call" | custom-call | flops 16106127360 | bytes 8388608 | tf_op jit(solution)/shard_map/attend_back/pallas_call | solution.py:485
  490.3 18.6 %attend_back.3 = (f32[1024,512]{1,0:T(8,128)}, f32[1024,256]{1,0:T(8,128)}, f32[1024,256]{1,0:T(8,128)}) custom-call(s32[4,4]{1,0:T(4,128)} %fusion.90.live_ref, bf16[1024,1024]{1,0:T(8,128)(2,1)} %copy.144.q_ref, bf16[1024,1024]{1,0:T(8,128)(2,1)} %convolution_convert_fusion.4.do_ref, bf16[1024,512]{1,0:T(8,128)(2,1)} %copy.145.k_ref, ...), custom_call_target="tpu_custom_call" | custom-call | flops 16106127360 | bytes 8388608 | tf_op jit(solution)/shard_map/attend_back/pallas_call | solution.py:485
  511.8 4.6 collective-permute-start.50
  522.0 4.0 collective-permute-start.52
  526.1 3.1 broadcast_select_fusion.5
  531.1 2.9 copy.156
  544.7 5.5 multiply_reduce_fusion.1
  556.0 5.2 fusion.4
  569.9 3.0 collective-permute-done.53
  585.7 2.9 fusion.78
  589.7 3.8 fusion.13
  596.3 2.7 scatter.14
  603.3 4.9 convolution_convert_fusion.3
  614.8 5.0 fusion.50
  624.0 12.2 %fusion.19 = f32[1152,1024]{1,0:T(8,128)} fusion(bf16[1152,512]{1,0:T(8,128)(2,1)} %collective-permute-done.79, bf16[576,512]{1,0:T(8,128)(2,1)S(1)} %get-tuple-element.482, bf16[576,512]{1,0:T(8,128)(2,1)S(1)} %get-tuple-element.481, pred[]{:T(512)S(6)} %eq.38), kind=kLoop, calls=%fused_computation.66 | loop fusion | flops 16515072 | bytes 7077889 | tf_op jit(solution)/shard_map/convert_element_type | solution.py:318
  648.3 3.4 broadcast_select_fusion.4
  652.8 16.9 %add_multiply_fusion = bf16[1024,1024]{0,1:T(8,128)(2,1)} fusion(f32[1024,1024]{0,1:T(8,128)} %copy-done.2, f32[1024]{0:T(1024)S(1)} %copy-done.85, bf16[1024,4608]{1,0:T(8,128)(2,1)} %get-tuple-element.299, bf16[4608,1024]{1,0:T(8,128)(2,1)} %place_blocks.9), kind=kOutput, calls=%fused_computation.41 | convolution fusion | flops 9666822144 | bytes 25169920 | tf_op jit(solution)/shard_map/dot_general | solution.py:65
  669.7 6.1 collective-permute-done.61
  686.0 26.5 %collective-permute-done.72 = bf16[64,1024]{1,0:T(8,128)(2,1)S(1)} collective-permute-done((bf16[64,1024]{1,0:T(8,128)(2,1)S(1)}, bf16[64,1024]{1,0:T(8,128)(2,1)S(1)}, u32[]{:S(2)}, u32[]{:S(2)}) %collective-permute-start.72) | collective-permute-done | bytes 131104 | tf_op jit(solution)/shard_map/ppermute | solution.py:98
  720.1 2.9 collective-permute-done.68
  727.3 3.9 copy.166
  735.9 3.2 collective-permute-done.69
  743.2 4.8 collective-permute-done.70
  750.5 10.2 %collective-permute-done.77 = bf16[64,4608]{1,0:T(8,128)(2,1)S(1)} collective-permute-done((bf16[64,4608]{1,0:T(8,128)(2,1)S(1)}, bf16[64,4608]{1,0:T(8,128)(2,1)S(1)}, u32[]{:S(2)}, u32[]{:S(2)}) %collective-permute-start.77) | collective-permute-done | bytes 589856 | tf_op jit(solution)/shard_map/ppermute | solution.py:98
  762.2 3.7 fusion.17
  (560 shorter events, 257.5 us)
Async XLA Ops:
  5.8 14.7 %collective-permute-start = (bf16[128,2176]{1,0:T(8,128)(2,1)}, bf16[128,2176]{1,0:T(8,128)(2,1)}, u32[]{:S(2)}, u32[]{:S(2)}) collective-permute-start(bf16[128,2176]{1,0:T(8,128)(2,1)} %pad_maximum_fusion.18), channel_id=1, source_target_pairs={{0,8},{1,9},{2,10},{3,11},{4,12},{5,13},{6,14},{7,15},{8,0},{9,1},... | collective-permute-start | bytes 1671176 | tf_op jit(solution)/shard_map/ppermute | solution.py:90
  7.8 13.5 %collective-permute-start.1 = (bf16[128,2176]{1,0:T(8,128)(2,1)}, bf16[128,2176]{1,0:T(8,128)(2,1)}, u32[]{:S(2)}, u32[]{:S(2)}) collective-permute-start(bf16[128,2176]{1,0:T(8,128)(2,1)} %pad_maximum_fusion.18), channel_id=1, source_target_pairs={{0,16},{1,17},{2,18},{3,19},{4,20},{5,21},{6,22},{7,23},{8,24},{9,... | collective-permute-start | bytes 1671176 | tf_op jit(solution)/shard_map/ppermute | solution.py:90
  23.2 16.2 %collective-permute-start.4 = (bf16[128,2176]{1,0:T(8,128)(2,1)}, bf16[128,2176]{1,0:T(8,128)(2,1)S(1)}, u32[]{:S(2)}, u32[]{:S(2)}) collective-permute-start(bf16[128,2176]{1,0:T(8,128)(2,1)} %collective-permute-done.refs_2_), channel_id=1, source_target_pairs={{0,1},{1,0},{2,3},{3,2},{4,5},{5,4},{6,7},{7,6},{8,9},{9,8},{10,11... | collective-permute-start | bytes 1671176 | tf_op jit(solution)/shard_map/ppermute | solution.py:98
  25.1 14.4 %collective-permute-start.5 = (bf16[128,2176]{1,0:T(8,128)(2,1)}, bf16[128,2176]{1,0:T(8,128)(2,1)}, u32[]{:S(2)}, u32[]{:S(2)}) collective-permute-start(bf16[128,2176]{1,0:T(8,128)(2,1)} %collective-permute-done.1.refs_4_), channel_id=1, source_target_pairs={{0,1},{1,0},{2,3},{3,2},{4,5},{5,4},{6,7},{7,6},{8,9},{9,8},{10,11... | collective-permute-start | bytes 1671176 | tf_op jit(solution)/shard_map/ppermute | solution.py:98
  46.6 40.1 %collective-permute-start.13 = (bf16[128,4608]{1,0:T(8,128)(2,1)}, bf16[128,4608]{1,0:T(8,128)(2,1)}, u32[]{:S(2)}, u32[]{:S(2)}) collective-permute-start(bf16[128,4608]{1,0:T(8,128)(2,1)} %get-tuple-element.442), channel_id=1, source_target_pairs={{0,8},{1,9},{2,10},{3,11},{4,12},{5,13},{6,14},{7,15},{8,0},{9,1},... | collective-permute-start | bytes 3538952 | tf_op jit(solution)/shard_map/ppermute | solution.py:90
  48.0 38.8 %collective-permute-start.14 = (bf16[128,4608]{1,0:T(8,128)(2,1)}, bf16[128,4608]{1,0:T(8,128)(2,1)}, u32[]{:S(2)}, u32[]{:S(2)}) collective-permute-start(bf16[128,4608]{1,0:T(8,128)(2,1)} %get-tuple-element.442), channel_id=1, source_target_pairs={{0,16},{1,17},{2,18},{3,19},{4,20},{5,21},{6,22},{7,23},{8,24},{9,... | collective-permute-start | bytes 3538952 | tf_op jit(solution)/shard_map/ppermute | solution.py:90
  50.2 36.6 %collective-permute-start.12 = (bf16[128,1024]{1,0:T(8,128)(2,1)}, bf16[128,1024]{1,0:T(8,128)(2,1)}, u32[]{:S(2)}, u32[]{:S(2)}) collective-permute-start(bf16[128,1024]{1,0:T(8,128)(2,1)} %collective-permute-done.7.refs_4_), channel_id=1, source_target_pairs={{0,1},{1,0},{2,3},{3,2},{4,5},{5,4},{6,7},{7,6},{8,9},{9,8},{10,11... | collective-permute-start | bytes 786440 | tf_op jit(solution)/shard_map/ppermute | solution.py:98
  50.9 35.8 %collective-permute-start.11 = (bf16[128,1024]{1,0:T(8,128)(2,1)S(1)}, bf16[128,1024]{1,0:T(8,128)(2,1)}, u32[]{:S(2)}, u32[]{:S(2)}) collective-permute-start(bf16[128,1024]{1,0:T(8,128)(2,1)S(1)} %collective-permute-done.6.refs_2_), channel_id=1, source_target_pairs={{0,1},{1,0},{2,3},{3,2},{4,5},{5,4},{6,7},{7,6},{8,9},{9,8},{10,11... | collective-permute-start | bytes 786440 | tf_op jit(solution)/shard_map/ppermute | solution.py:98
  52.5 29.7 %collective-permute-start.10 = (bf16[64,1024]{1,0:T(8,128)(2,1)S(1)}, bf16[64,1024]{1,0:T(8,128)(2,1)S(1)}, u32[]{:S(2)}, u32[]{:S(2)}) collective-permute-start(bf16[64,1024]{1,0:T(8,128)(2,1)S(1)} %slice.311), channel_id=1, source_target_pairs={{0,8},{1,9},{2,10},{3,11},{4,12},{5,13},{6,14},{7,15},{8,0},{9,1},... | collective-permute-start | bytes 393224 | tf_op jit(solution)/shard_map/ppermute | solution.py:90
  88.7 68.7 %collective-permute-start.20 = (bf16[128,4608]{1,0:T(8,128)(2,1)}, bf16[128,4608]{1,0:T(8,128)(2,1)}, u32[]{:S(2)}, u32[]{:S(2)}) collective-permute-start(bf16[128,4608]{1,0:T(8,128)(2,1)} %get-tuple-element.436), channel_id=1, source_target_pairs={{0,8},{1,9},{2,10},{3,11},{4,12},{5,13},{6,14},{7,15},{8,0},{9,1},... | collective-permute-start | bytes 3538952 | tf_op jit(solution)/shard_map/ppermute | solution.py:90
  90.0 67.4 %collective-permute-start.21 = (bf16[128,4608]{1,0:T(8,128)(2,1)}, bf16[128,4608]{1,0:T(8,128)(2,1)}, u32[]{:S(2)}, u32[]{:S(2)}) collective-permute-start(bf16[128,4608]{1,0:T(8,128)(2,1)} %get-tuple-element.436), channel_id=1, source_target_pairs={{0,16},{1,17},{2,18},{3,19},{4,20},{5,21},{6,22},{7,23},{8,24},{9,... | collective-permute-start | bytes 3538952 | tf_op jit(solution)/shard_map/ppermute | solution.py:90
  90.3 34.6 %collective-permute-start.15 = (bf16[128,1024]{1,0:T(8,128)(2,1)S(1)}, bf16[128,1024]{1,0:T(8,128)(2,1)}, u32[]{:S(2)}, u32[]{:S(2)}) collective-permute-start(bf16[128,1024]{1,0:T(8,128)(2,1)S(1)} %constant_dynamic-update-slice_fusion.2.refs_6_), channel_id=1, source_target_pairs={{0,1},{1,0},{2,3},{3,2},{4,5},{5,4},{6,7},{7,6},{8,9},{9,8},{10,11... | collective-permute-start | bytes 786440 | tf_op jit(solution)/shard_map/ppermute | solution.py:98
  97.8 59.7 %collective-permute-start.18 = (bf16[128,4608]{1,0:T(8,128)(2,1)}, bf16[128,4608]{1,0:T(8,128)(2,1)S(1)}, u32[]{:S(2)}, u32[]{:S(2)}) collective-permute-start(bf16[128,4608]{1,0:T(8,128)(2,1)} %collective-permute-done.13.refs_2_), channel_id=1, source_target_pairs={{0,1},{1,0},{2,3},{3,2},{4,5},{5,4},{6,7},{7,6},{8,9},{9,8},{10,11... | collective-permute-start | bytes 3538952 | tf_op jit(solution)/shard_map/ppermute | solution.py:98
  124.9 32.6 %collective-permute-start.19 = (bf16[128,4608]{1,0:T(8,128)(2,1)}, bf16[128,4608]{1,0:T(8,128)(2,1)}, u32[]{:S(2)}, u32[]{:S(2)}) collective-permute-start(bf16[128,4608]{1,0:T(8,128)(2,1)} %collective-permute-done.14.refs_4_), channel_id=1, source_target_pairs={{0,1},{1,0},{2,3},{3,2},{4,5},{5,4},{6,7},{7,6},{8,9},{9,8},{10,11... | collective-permute-start | bytes 3538952 | tf_op jit(solution)/shard_map/ppermute | solution.py:98
  124.9 18.3 %collective-permute-start.16 = (bf16[64,4608]{1,0:T(8,128)(2,1)}, bf16[64,4608]{1,0:T(8,128)(2,1)}, u32[]{:S(2)}, u32[]{:S(2)}) collective-permute-start(bf16[64,4608]{1,0:T(8,128)(2,1)} %slice.315), channel_id=1, source_target_pairs={{0,16},{1,17},{2,18},{3,19},{4,20},{5,21},{6,22},{7,23},{8,24},{9,... | collective-permute-start | bytes 1769480 | tf_op jit(solution)/shard_map/ppermute | solution.py:90
  143.2 14.3 %collective-permute-start.17 = (bf16[64,4608]{1,0:T(8,128)(2,1)S(1)}, bf16[64,4608]{1,0:T(8,128)(2,1)S(1)}, u32[]{:S(2)}, u32[]{:S(2)}) collective-permute-start(bf16[64,4608]{1,0:T(8,128)(2,1)S(1)} %copy-done.60), channel_id=1, source_target_pairs={{0,8},{1,9},{2,10},{3,11},{4,12},{5,13},{6,14},{7,15},{8,0},{9,1},... | collective-permute-start | bytes 1769480 | tf_op jit(solution)/shard_map/ppermute | solution.py:90
  164.1 17.4 %collective-permute-start.23 = (bf16[64,4608]{1,0:T(8,128)(2,1)}, bf16[64,4608]{1,0:T(8,128)(2,1)}, u32[]{:S(2)}, u32[]{:S(2)}) collective-permute-start(bf16[64,4608]{1,0:T(8,128)(2,1)} %slice.321), channel_id=1, source_target_pairs={{0,16},{1,17},{2,18},{3,19},{4,20},{5,21},{6,22},{7,23},{8,24},{9,... | collective-permute-start | bytes 1769480 | tf_op jit(solution)/shard_map/ppermute | solution.py:90
  169.2 40.1 %collective-permute-start.27 = (bf16[576,1024]{1,0:T(8,128)(2,1)}, bf16[576,1024]{1,0:T(8,128)(2,1)S(1)}, u32[]{:S(2)}, u32[]{:S(2)}) collective-permute-start(bf16[576,1024]{1,0:T(8,128)(2,1)} %get-tuple-element.437), channel_id=1, source_target_pairs={{0,8},{1,9},{2,10},{3,11},{4,12},{5,13},{6,14},{7,15},{8,0},{9,1},... | collective-permute-start | bytes 3538952 | tf_op jit(solution)/shard_map/ppermute | solution.py:90
  169.4 39.9 %collective-permute-start.28 = (bf16[576,1024]{1,0:T(8,128)(2,1)}, bf16[576,1024]{1,0:T(8,128)(2,1)}, u32[]{:S(2)}, u32[]{:S(2)}) collective-permute-start(bf16[576,1024]{1,0:T(8,128)(2,1)} %get-tuple-element.437), channel_id=1, source_target_pairs={{0,16},{1,17},{2,18},{3,19},{4,20},{5,21},{6,22},{7,23},{8,24},{9,... | collective-permute-start | bytes 3538952 | tf_op jit(solution)/shard_map/ppermute | solution.py:90
  169.5 39.8 %collective-permute-start.25 = (bf16[128,4608]{1,0:T(8,128)(2,1)}, bf16[128,4608]{1,0:T(8,128)(2,1)}, u32[]{:S(2)}, u32[]{:S(2)}) collective-permute-start(bf16[128,4608]{1,0:T(8,128)(2,1)} %collective-permute-done.20.refs_2_), channel_id=1, source_target_pairs={{0,1},{1,0},{2,3},{3,2},{4,5},{5,4},{6,7},{7,6},{8,9},{9,8},{10,11... | collective-permute-start | bytes 3538952 | tf_op jit(solution)/shard_map/ppermute | solution.py:98
  172.2 37.1 %collective-permute-start.26 = (bf16[128,4608]{1,0:T(8,128)(2,1)}, bf16[128,4608]{1,0:T(8,128)(2,1)}, u32[]{:S(2)}, u32[]{:S(2)}) collective-permute-start(bf16[128,4608]{1,0:T(8,128)(2,1)} %collective-permute-done.21.refs_4_), channel_id=1, source_target_pairs={{0,1},{1,0},{2,3},{3,2},{4,5},{5,4},{6,7},{7,6},{8,9},{9,8},{10,11... | collective-permute-start | bytes 3538952 | tf_op jit(solution)/shard_map/ppermute | solution.py:98
  181.5 27.8 %collective-permute-start.24 = (bf16[64,4608]{1,0:T(8,128)(2,1)}, bf16[64,4608]{1,0:T(8,128)(2,1)S(1)}, u32[]{:S(2)}, u32[]{:S(2)}) collective-permute-start(bf16[64,4608]{1,0:T(8,128)(2,1)} %slice.322), channel_id=1, source_target_pairs={{0,8},{1,9},{2,10},{3,11},{4,12},{5,13},{6,14},{7,15},{8,0},{9,1},... | collective-permute-start | bytes 1769480 | tf_op jit(solution)/shard_map/ppermute | solution.py:90
  212.9 45.5 %collective-permute-start.32 = (bf16[576,1024]{1,0:T(8,128)(2,1)S(1)}, bf16[576,1024]{1,0:T(8,128)(2,1)}, u32[]{:S(2)}, u32[]{:S(2)}) collective-permute-start(bf16[576,1024]{1,0:T(8,128)(2,1)S(1)} %collective-permute-done.27.refs_2_), channel_id=1, source_target_pairs={{0,1},{1,0},{2,3},{3,2},{4,5},{5,4},{6,7},{7,6},{8,9},{9,8},{10,11... | collective-permute-start | bytes 3538952 | tf_op jit(solution)/shard_map/ppermute | solution.py:98
  215.0 43.4 %collective-permute-start.33 = (bf16[576,1024]{1,0:T(8,128)(2,1)}, bf16[576,1024]{1,0:T(8,128)(2,1)}, u32[]{:S(2)}, u32[]{:S(2)}) collective-permute-start(bf16[576,1024]{1,0:T(8,128)(2,1)} %collective-permute-done.28.refs_4_), channel_id=1, source_target_pairs={{0,1},{1,0},{2,3},{3,2},{4,5},{5,4},{6,7},{7,6},{8,9},{9,8},{10,11... | collective-permute-start | bytes 3538952 | tf_op jit(solution)/shard_map/ppermute | solution.py:98
  215.4 43.0 %collective-permute-start.30 = (bf16[288,1024]{1,0:T(8,128)(2,1)}, bf16[288,1024]{1,0:T(8,128)(2,1)}, u32[]{:S(2)}, u32[]{:S(2)}) collective-permute-start(bf16[288,1024]{1,0:T(8,128)(2,1)} %slice.325), channel_id=1, source_target_pairs={{0,16},{1,17},{2,18},{3,19},{4,20},{5,21},{6,22},{7,23},{8,24},{9,... | collective-permute-start | bytes 1769480 | tf_op jit(solution)/shard_map/ppermute | solution.py:90
  215.6 42.8 %collective-permute-start.31 = (bf16[288,1024]{1,0:T(8,128)(2,1)}, bf16[288,1024]{1,0:T(8,128)(2,1)}, u32[]{:S(2)}, u32[]{:S(2)}) collective-permute-start(bf16[288,1024]{1,0:T(8,128)(2,1)} %slice.326), channel_id=1, source_target_pairs={{0,8},{1,9},{2,10},{3,11},{4,12},{5,13},{6,14},{7,15},{8,0},{9,1},... | collective-permute-start | bytes 1769480 | tf_op jit(solution)/shard_map/ppermute | solution.py:90
  350.3 31.7 %collective-permute-start.37 = (bf16[4,128,4608]{2,1,0:T(8,128)(2,1)}, bf16[4,128,4608]{2,1,0:T(8,128)(2,1)}, u32[]{:S(2)}, u32[]{:S(2)}) collective-permute-start(bf16[4,128,4608]{2,1,0:T(8,128)(2,1)} %bitcast.20), channel_id=1, source_target_pairs={{0,1},{1,0},{2,3},{3,2},{4,5},{5,4},{6,7},{7,6},{8,9},{9,8},{10,11... | collective-permute-start | bytes 14155784 | tf_op jit(solution)/shard_map/ppermute | solution.py:98
  353.3 37.3 %collective-permute-start.36 = (bf16[4,128,4608]{2,1,0:T(8,128)(2,1)}, bf16[4,128,4608]{2,1,0:T(8,128)(2,1)}, u32[]{:S(2)}, u32[]{:S(2)}) collective-permute-start(bf16[4,128,4608]{2,1,0:T(8,128)(2,1)} %bitcast.223), channel_id=1, source_target_pairs={{0,1},{1,0},{2,3},{3,2},{4,5},{5,4},{6,7},{7,6},{8,9},{9,8},{10,11... | collective-permute-start | bytes 14155784 | tf_op jit(solution)/shard_map/ppermute | solution.py:98
  358.9 38.1 %collective-permute-start.39 = (bf16[2,576,512]{2,1,0:T(8,128)(2,1)}, bf16[2,576,512]{2,1,0:T(8,128)(2,1)}, u32[]{:S(2)}, u32[]{:S(2)}) collective-permute-start(bf16[2,576,512]{2,1,0:T(8,128)(2,1)} %pad_maximum_fusion.6), channel_id=1, source_target_pairs={{0,16},{1,17},{2,18},{3,19},{4,20},{5,21},{6,22},{7,23},{8,24},{9,... | collective-permute-start | bytes 3538952 | tf_op jit(solution)/shard_map/ppermute | solution.py:90
  361.4 35.6 %collective-permute-start.38 = (bf16[2,576,512]{2,1,0:T(8,128)(2,1)}, bf16[2,576,512]{2,1,0:T(8,128)(2,1)}, u32[]{:S(2)}, u32[]{:S(2)}) collective-permute-start(bf16[2,576,512]{2,1,0:T(8,128)(2,1)} %pad_maximum_fusion.5), channel_id=1, source_target_pairs={{0,8},{1,9},{2,10},{3,11},{4,12},{5,13},{6,14},{7,15},{8,0},{9,1},... | collective-permute-start | bytes 3538952 | tf_op jit(solution)/shard_map/ppermute | solution.py:90
  399.5 36.4 %collective-permute-start.40 = (bf16[576,512]{1,0:T(8,128)(2,1)S(1)}, bf16[576,512]{1,0:T(8,128)(2,1)S(1)}, u32[]{:S(2)}, u32[]{:S(2)}) collective-permute-start(bf16[576,512]{1,0:T(8,128)(2,1)S(1)} %get-tuple-element.419), channel_id=1, source_target_pairs={{0,16},{1,17},{2,18},{3,19},{4,20},{5,21},{6,22},{7,23},{8,24},{9,... | collective-permute-start | bytes 1769480 | tf_op jit(solution)/shard_map/ppermute | solution.py:90
  399.6 36.3 %collective-permute-start.41 = (bf16[576,512]{1,0:T(8,128)(2,1)S(1)}, bf16[576,512]{1,0:T(8,128)(2,1)S(1)}, u32[]{:S(2)}, u32[]{:S(2)}) collective-permute-start(bf16[576,512]{1,0:T(8,128)(2,1)S(1)} %get-tuple-element.418), channel_id=1, source_target_pairs={{0,8},{1,9},{2,10},{3,11},{4,12},{5,13},{6,14},{7,15},{8,0},{9,1},... | collective-permute-start | bytes 1769480 | tf_op jit(solution)/shard_map/ppermute | solution.py:90
  417.2 46.0 %collective-permute-start.44 = (bf16[2,64,4608]{2,1,0:T(8,128)(2,1)}, bf16[2,64,4608]{2,1,0:T(8,128)(2,1)}, u32[]{:S(2)}, u32[]{:S(2)}) collective-permute-start(bf16[2,64,4608]{2,1,0:T(8,128)(2,1)} %pad_maximum_fusion.8), channel_id=1, source_target_pairs={{0,16},{1,17},{2,18},{3,19},{4,20},{5,21},{6,22},{7,23},{8,24},{9,... | collective-permute-start | bytes 3538952 | tf_op jit(solution)/shard_map/ppermute | solution.py:90
  419.8 43.4 %collective-permute-start.43 = (bf16[2,64,4608]{2,1,0:T(8,128)(2,1)}, bf16[2,64,4608]{2,1,0:T(8,128)(2,1)}, u32[]{:S(2)}, u32[]{:S(2)}) collective-permute-start(bf16[2,64,4608]{2,1,0:T(8,128)(2,1)} %pad_maximum_fusion.7), channel_id=1, source_target_pairs={{0,8},{1,9},{2,10},{3,11},{4,12},{5,13},{6,14},{7,15},{8,0},{9,1},... | collective-permute-start | bytes 3538952 | tf_op jit(solution)/shard_map/ppermute | solution.py:90
  441.1 16.8 %collective-permute-start.42 = (bf16[4,128,1024]{2,1,0:T(8,128)(2,1)}, bf16[4,128,1024]{2,1,0:T(8,128)(2,1)S(1)}, u32[]{:S(2)}, u32[]{:S(2)}) collective-permute-start(bf16[4,128,1024]{2,1,0:T(8,128)(2,1)} %bitcast.25), channel_id=1, source_target_pairs={{0,1},{1,0},{2,3},{3,2},{4,5},{5,4},{6,7},{7,6},{8,9},{9,8},{10,11... | collective-permute-start | bytes 3145736 | tf_op jit(solution)/shard_map/ppermute | solution.py:98
  445.5 17.7 %collective-permute-start.45 = (bf16[576,512]{1,0:T(8,128)(2,1)}, bf16[576,512]{1,0:T(8,128)(2,1)S(1)}, u32[]{:S(2)}, u32[]{:S(2)}) collective-permute-start(bf16[576,512]{1,0:T(8,128)(2,1)} %get-tuple-element.396), channel_id=1, source_target_pairs={{0,2},{1,3},{2,0},{3,1},{4,6},{5,7},{6,4},{7,5},{8,10},{9,11},{10,... | collective-permute-start | bytes 1769480 | tf_op jit(solution)/shard_map/ppermute | solution.py:98
  465.3 53.0 %collective-permute-start.48 = (bf16[576,512]{1,0:T(8,128)(2,1)S(1)}, bf16[576,512]{1,0:T(8,128)(2,1)S(1)}, u32[]{:S(2)}, u32[]{:S(2)}) collective-permute-start(bf16[576,512]{1,0:T(8,128)(2,1)S(1)} %add_convert_fusion.12), channel_id=1, source_target_pairs={{0,4},{1,5},{2,6},{3,7},{4,0},{5,1},{6,2},{7,3},{8,12},{9,13},{10,... | collective-permute-start | bytes 1769480 | tf_op jit(solution)/shard_map/ppermute | solution.py:98
  469.5 48.8 %collective-permute-start.46 = (bf16[64,4608]{1,0:T(8,128)(2,1)}, bf16[64,4608]{1,0:T(8,128)(2,1)S(1)}, u32[]{:S(2)}, u32[]{:S(2)}) collective-permute-start(bf16[64,4608]{1,0:T(8,128)(2,1)} %get-tuple-element.413), channel_id=1, source_target_pairs={{0,16},{1,17},{2,18},{3,19},{4,20},{5,21},{6,22},{7,23},{8,24},{9,... | collective-permute-start | bytes 1769480 | tf_op jit(solution)/shard_map/ppermute | solution.py:90
  470.8 47.5 %collective-permute-start.47 = (bf16[64,4608]{1,0:T(8,128)(2,1)}, bf16[64,4608]{1,0:T(8,128)(2,1)S(1)}, u32[]{:S(2)}, u32[]{:S(2)}) collective-permute-start(bf16[64,4608]{1,0:T(8,128)(2,1)} %get-tuple-element.412), channel_id=1, source_target_pairs={{0,8},{1,9},{2,10},{3,11},{4,12},{5,13},{6,14},{7,15},{8,0},{9,1},... | collective-permute-start | bytes 1769480 | tf_op jit(solution)/shard_map/ppermute | solution.py:90
  511.8 61.1 %collective-permute-start.50 = (bf16[2,64,4608]{2,1,0:T(8,128)(2,1)}, bf16[2,64,4608]{2,1,0:T(8,128)(2,1)}, u32[]{:S(2)}, u32[]{:S(2)}) collective-permute-start(bf16[2,64,4608]{2,1,0:T(8,128)(2,1)} %pad_maximum_fusion.10), channel_id=1, source_target_pairs={{0,16},{1,17},{2,18},{3,19},{4,20},{5,21},{6,22},{7,23},{8,24},{9,... | collective-permute-start | bytes 3538952 | tf_op jit(solution)/shard_map/ppermute | solution.py:90
  517.5 56.1 %collective-permute-start.49 = (bf16[2,64,4608]{2,1,0:T(8,128)(2,1)}, bf16[2,64,4608]{2,1,0:T(8,128)(2,1)}, u32[]{:S(2)}, u32[]{:S(2)}) collective-permute-start(bf16[2,64,4608]{2,1,0:T(8,128)(2,1)} %pad_maximum_fusion.9), channel_id=1, source_target_pairs={{0,8},{1,9},{2,10},{3,11},{4,12},{5,13},{6,14},{7,15},{8,0},{9,1},... | collective-permute-start | bytes 3538952 | tf_op jit(solution)/shard_map/ppermute | solution.py:90
  519.8 46.3 %collective-permute-start.54 = (bf16[2,64,1024]{2,1,0:T(8,128)(2,1)}, bf16[2,64,1024]{2,1,0:T(8,128)(2,1)}, u32[]{:S(2)}, u32[]{:S(2)}) collective-permute-start(bf16[2,64,1024]{2,1,0:T(8,128)(2,1)} %pad_maximum_fusion.23), channel_id=1, source_target_pairs={{0,16},{1,17},{2,18},{3,19},{4,20},{5,21},{6,22},{7,23},{8,24},{9,... | collective-permute-start | bytes 786440 | tf_op jit(solution)/shard_map/ppermute | solution.py:90
  522.0 50.9 %collective-permute-start.52 = (bf16[576,512]{1,0:T(8,128)(2,1)}, bf16[576,512]{1,0:T(8,128)(2,1)}, u32[]{:S(2)}, u32[]{:S(2)}) collective-permute-start(bf16[576,512]{1,0:T(8,128)(2,1)} %add_convert_fusion.11), channel_id=1, source_target_pairs={{0,2},{1,3},{2,0},{3,1},{4,6},{5,7},{6,4},{7,5},{8,10},{9,11},{10,... | collective-permute-start | bytes 1769480 | tf_op jit(solution)/shard_map/ppermute | solution.py:98
  529.1 43.8 %collective-permute-start.51 = (bf16[64,4608]{1,0:T(8,128)(2,1)}, bf16[64,4608]{1,0:T(8,128)(2,1)}, u32[]{:S(2)}, u32[]{:S(2)}) collective-permute-start(bf16[64,4608]{1,0:T(8,128)(2,1)} %get-tuple-element.393), channel_id=1, source_target_pairs={{0,2},{1,3},{2,0},{3,1},{4,6},{5,7},{6,4},{7,5},{8,10},{9,11},{10,... | collective-permute-start | bytes 1769480 | tf_op jit(solution)/shard_map/ppermute | solution.py:98
  579.8 42.5 %collective-permute-start.79 = (bf16[1152,512]{1,0:T(8,128)(2,1)}, bf16[1152,512]{1,0:T(8,128)(2,1)}, u32[]{:S(2)}, u32[]{:S(2)}) collective-permute-start(bf16[1152,512]{1,0:T(8,128)(2,1)} %pad_maximum_fusion.13), channel_id=1, source_target_pairs={{0,1},{1,0},{2,3},{3,2},{4,5},{5,4},{6,7},{7,6},{8,9},{9,8},{10,11... | collective-permute-start | bytes 3538952 | tf_op jit(solution)/shard_map/ppermute | solution.py:98
  583.9 57.2 %collective-permute-start.60 = (bf16[64,4608]{1,0:T(8,128)(2,1)}, bf16[64,4608]{1,0:T(8,128)(2,1)}, u32[]{:S(2)}, u32[]{:S(2)}) collective-permute-start(bf16[64,4608]{1,0:T(8,128)(2,1)} %add_convert_fusion.8), channel_id=1, source_target_pairs={{0,4},{1,5},{2,6},{3,7},{4,0},{5,1},{6,2},{7,3},{8,12},{9,13},{10,... | collective-permute-start | bytes 1769480 | tf_op jit(solution)/shard_map/ppermute | solution.py:98
  588.6 52.5 %collective-permute-start.58 = (bf16[64,4608]{1,0:T(8,128)(2,1)}, bf16[64,4608]{1,0:T(8,128)(2,1)}, u32[]{:S(2)}, u32[]{:S(2)}) collective-permute-start(bf16[64,4608]{1,0:T(8,128)(2,1)} %get-tuple-element.407), channel_id=1, source_target_pairs={{0,16},{1,17},{2,18},{3,19},{4,20},{5,21},{6,22},{7,23},{8,24},{9,... | collective-permute-start | bytes 1769480 | tf_op jit(solution)/shard_map/ppermute | solution.py:90
  588.6 52.5 %collective-permute-start.59 = (bf16[64,4608]{1,0:T(8,128)(2,1)}, bf16[64,4608]{1,0:T(8,128)(2,1)}, u32[]{:S(2)}, u32[]{:S(2)}) collective-permute-start(bf16[64,4608]{1,0:T(8,128)(2,1)} %get-tuple-element.406), channel_id=1, source_target_pairs={{0,8},{1,9},{2,10},{3,11},{4,12},{5,13},{6,14},{7,15},{8,0},{9,1},... | collective-permute-start | bytes 1769480 | tf_op jit(solution)/shard_map/ppermute | solution.py:90
  609.8 26.4 %collective-permute-start.55 = (bf16[4,128,2176]{2,1,0:T(8,128)(2,1)}, bf16[4,128,2176]{2,1,0:T(8,128)(2,1)}, u32[]{:S(2)}, u32[]{:S(2)}) collective-permute-start(bf16[4,128,2176]{2,1,0:T(8,128)(2,1)} %pad_maximum_fusion.2), channel_id=1, source_target_pairs={{0,1},{1,0},{2,3},{3,2},{4,5},{5,4},{6,7},{7,6},{8,9},{9,8},{10,11... | collective-permute-start | bytes 6684680 | tf_op jit(solution)/shard_map/ppermute | solution.py:98
  622.3 16.7 %collective-permute-start.56 = (bf16[64,1024]{1,0:T(8,128)(2,1)S(1)}, bf16[64,1024]{1,0:T(8,128)(2,1)S(1)}, u32[]{:S(2)}, u32[]{:S(2)}) collective-permute-start(bf16[64,1024]{1,0:T(8,128)(2,1)S(1)} %copy-done.75), channel_id=1, source_target_pairs={{0,16},{1,17},{2,18},{3,19},{4,20},{5,21},{6,22},{7,23},{8,24},{9,... | collective-permute-start | bytes 393224 | tf_op jit(solution)/shard_map/ppermute | solution.py:90
  642.1 27.6 %collective-permute-start.65 = (bf16[2,64,2176]{2,1,0:T(8,128)(2,1)}, bf16[2,64,2176]{2,1,0:T(8,128)(2,1)}, u32[]{:S(2)}, u32[]{:S(2)}) collective-permute-start(bf16[2,64,2176]{2,1,0:T(8,128)(2,1)} %pad_maximum_fusion.20), channel_id=1, source_target_pairs={{0,16},{1,17},{2,18},{3,19},{4,20},{5,21},{6,22},{7,23},{8,24},{9,... | collective-permute-start | bytes 1671176 | tf_op jit(solution)/shard_map/ppermute | solution.py:90
  643.2 26.4 %collective-permute-start.64 = (bf16[2,64,2176]{2,1,0:T(8,128)(2,1)}, bf16[2,64,2176]{2,1,0:T(8,128)(2,1)}, u32[]{:S(2)}, u32[]{:S(2)}) collective-permute-start(bf16[2,64,2176]{2,1,0:T(8,128)(2,1)} %pad_maximum_fusion.19), channel_id=1, source_target_pairs={{0,8},{1,9},{2,10},{3,11},{4,12},{5,13},{6,14},{7,15},{8,0},{9,1},... | collective-permute-start | bytes 1671176 | tf_op jit(solution)/shard_map/ppermute | solution.py:90
  645.3 24.3 %collective-permute-start.63 = (bf16[64,1024]{1,0:T(8,128)(2,1)}, bf16[64,1024]{1,0:T(8,128)(2,1)}, u32[]{:S(2)}, u32[]{:S(2)}) collective-permute-start(bf16[64,1024]{1,0:T(8,128)(2,1)} %get-tuple-element.387), channel_id=1, source_target_pairs={{0,2},{1,3},{2,0},{3,1},{4,6},{5,7},{6,4},{7,5},{8,10},{9,11},{10,... | collective-permute-start | bytes 393224 | tf_op jit(solution)/shard_map/ppermute | solution.py:98
  647.8 21.9 %collective-permute-start.62 = (bf16[64,4608]{1,0:T(8,128)(2,1)S(1)}, bf16[64,4608]{1,0:T(8,128)(2,1)}, u32[]{:S(2)}, u32[]{:S(2)}) collective-permute-start(bf16[64,4608]{1,0:T(8,128)(2,1)S(1)} %add_convert_fusion.7), channel_id=1, source_target_pairs={{0,2},{1,3},{2,0},{3,1},{4,6},{5,7},{6,4},{7,5},{8,10},{9,11},{10,... | collective-permute-start | bytes 1769480 | tf_op jit(solution)/shard_map/ppermute | solution.py:98
  651.7 24.1 %collective-permute-start.61 = (bf16[64,4608]{1,0:T(8,128)(2,1)}, bf16[64,4608]{1,0:T(8,128)(2,1)}, u32[]{:S(2)}, u32[]{:S(2)}) collective-permute-start(bf16[64,4608]{1,0:T(8,128)(2,1)} %get-tuple-element.390), channel_id=1, source_target_pairs={{0,2},{1,3},{2,0},{3,1},{4,6},{5,7},{6,4},{7,5},{8,10},{9,11},{10,... | collective-permute-start | bytes 1769480 | tf_op jit(solution)/shard_map/ppermute | solution.py:98
  678.2 62.1 %collective-permute-start.76 = (bf16[64,4608]{1,0:T(8,128)(2,1)}, bf16[64,4608]{1,0:T(8,128)(2,1)}, u32[]{:S(2)}, u32[]{:S(2)}) collective-permute-start(bf16[64,4608]{1,0:T(8,128)(2,1)} %add_convert_fusion.6), channel_id=1, source_target_pairs={{0,4},{1,5},{2,6},{3,7},{4,0},{5,1},{6,2},{7,3},{8,12},{9,13},{10,... | collective-permute-start | bytes 1769480 | tf_op jit(solution)/shard_map/ppermute | solution.py:98
  679.7 32.7 %collective-permute-start.72 = (bf16[64,1024]{1,0:T(8,128)(2,1)S(1)}, bf16[64,1024]{1,0:T(8,128)(2,1)S(1)}, u32[]{:S(2)}, u32[]{:S(2)}) collective-permute-start(bf16[64,1024]{1,0:T(8,128)(2,1)S(1)} %add_convert_fusion.23), channel_id=1, source_target_pairs={{0,4},{1,5},{2,6},{3,7},{4,0},{5,1},{6,2},{7,3},{8,12},{9,13},{10,... | collective-permute-start | bytes 393224 | tf_op jit(solution)/shard_map/ppermute | solution.py:98
  682.7 29.8 %collective-permute-start.66 = (bf16[64,2176]{1,0:T(8,128)(2,1)S(1)}, bf16[64,2176]{1,0:T(8,128)(2,1)S(1)}, u32[]{:S(2)}, u32[]{:S(2)}) collective-permute-start(bf16[64,2176]{1,0:T(8,128)(2,1)S(1)} %get-tuple-element.448), channel_id=1, source_target_pairs={{0,8},{1,9},{2,10},{3,11},{4,12},{5,13},{6,14},{7,15},{8,0},{9,1},... | collective-permute-start | bytes 835592 | tf_op jit(solution)/shard_map/ppermute | solution.py:90
  683.8 28.8 %collective-permute-start.67 = (bf16[64,2176]{1,0:T(8,128)(2,1)S(1)}, bf16[64,2176]{1,0:T(8,128)(2,1)S(1)}, u32[]{:S(2)}, u32[]{:S(2)}) collective-permute-start(bf16[64,2176]{1,0:T(8,128)(2,1)S(1)} %get-tuple-element.447), channel_id=1, source_target_pairs={{0,16},{1,17},{2,18},{3,19},{4,20},{5,21},{6,22},{7,23},{8,24},{9,... | collective-permute-start | bytes 835592 | tf_op jit(solution)/shard_map/ppermute | solution.py:90
  717.9 15.9 %collective-permute-start.74 = (bf16[128,1024]{1,0:T(8,128)(2,1)}, bf16[128,1024]{1,0:T(8,128)(2,1)}, u32[]{:S(2)}, u32[]{:S(2)}) collective-permute-start(bf16[128,1024]{1,0:T(8,128)(2,1)} %pad_maximum_fusion.24), channel_id=1, source_target_pairs={{0,1},{1,0},{2,3},{3,2},{4,5},{5,4},{6,7},{7,6},{8,9},{9,8},{10,11... | collective-permute-start | bytes 786440 | tf_op jit(solution)/shard_map/ppermute | solution.py:98
  723.9 15.2 %collective-permute-start.69 = (bf16[64,2176]{1,0:T(8,128)(2,1)}, bf16[64,2176]{1,0:T(8,128)(2,1)}, u32[]{:S(2)}, u32[]{:S(2)}) collective-permute-start(bf16[64,2176]{1,0:T(8,128)(2,1)} %add_convert_fusion.19), channel_id=1, source_target_pairs={{0,4},{1,5},{2,6},{3,7},{4,0},{5,1},{6,2},{7,3},{8,12},{9,13},{10,... | collective-permute-start | bytes 835592 | tf_op jit(solution)/shard_map/ppermute | solution.py:98
  725.3 36.9 %collective-permute-start.75 = (bf16[128,4608]{1,0:T(8,128)(2,1)}, bf16[128,4608]{1,0:T(8,128)(2,1)}, u32[]{:S(2)}, u32[]{:S(2)}) collective-permute-start(bf16[128,4608]{1,0:T(8,128)(2,1)} %pad_maximum_fusion.11), channel_id=1, source_target_pairs={{0,1},{1,0},{2,3},{3,2},{4,5},{5,4},{6,7},{7,6},{8,9},{9,8},{10,11... | collective-permute-start | bytes 3538952 | tf_op jit(solution)/shard_map/ppermute | solution.py:98
  741.7 19.0 %collective-permute-start.77 = (bf16[64,4608]{1,0:T(8,128)(2,1)S(1)}, bf16[64,4608]{1,0:T(8,128)(2,1)S(1)}, u32[]{:S(2)}, u32[]{:S(2)}) collective-permute-start(bf16[64,4608]{1,0:T(8,128)(2,1)S(1)} %add_convert_fusion.5), channel_id=1, source_target_pairs={{0,2},{1,3},{2,0},{3,1},{4,6},{5,7},{6,4},{7,5},{8,10},{9,11},{10,... | collective-permute-start | bytes 1769480 | tf_op jit(solution)/shard_map/ppermute | solution.py:98
  748.1 17.8 %collective-permute-start.71 = (bf16[128,2176]{1,0:T(8,128)(2,1)S(1)}, bf16[128,2176]{1,0:T(8,128)(2,1)S(1)}, u32[]{:S(2)}, u32[]{:S(2)}) collective-permute-start(bf16[128,2176]{1,0:T(8,128)(2,1)S(1)} %pad_maximum_fusion.21), channel_id=1, source_target_pairs={{0,1},{1,0},{2,3},{3,2},{4,5},{5,4},{6,7},{7,6},{8,9},{9,8},{10,11... | collective-permute-start | bytes 1671176 | tf_op jit(solution)/shard_map/ppermute | solution.py:98
  (136 other events, 1363.1 us)

commit v4 on v3

--- a/solution.py
+++ b/solution.py
@@ -146,9 +146,10 @@
             out_ref[...] = refs[at][...]
 
 
-def place_blocks(blocks, spots):
-    count = len(blocks)
-    rows, width = blocks[0].shape
+def place_blocks(gathered):
+    blocks, spots = gathered
+    rows, width = blocks[1].shape
+    count = len(blocks) + 1
     return pl.pallas_call(
         place_kernel,
         out_shape=jax.ShapeDtypeStruct((count * rows, width), blocks[0].dtype),
@@ -156,8 +157,8 @@
             num_scalar_prefetch=1,
             grid=(count,),
             in_specs=[
-                pl.BlockSpec((rows, width), lambda i, spot: (0, 0), pipeline_mode=pl.Buffered(1))
-                for _ in blocks
+                pl.BlockSpec((rows, width), lambda i, spot, at=at: (at, 0))
+                for at in (0, 1) + (0,) * (count - 2)
             ],
             out_specs=pl.BlockSpec((rows, width), lambda i, spot: (spot[i], 0)),
         ),
@@ -166,7 +167,149 @@
         ),
         compiler_params=pltpu.CompilerParams(vmem_limit_bytes=60 << 20),
         name="place_blocks",
-    )(jnp.stack(spots).astype(jnp.int32), *blocks)
+    )(spots, blocks[0], *blocks)
+
+
+FF_TILE = 512
+
+
+def block_specs(count, rows):
+    return [
+        pl.BlockSpec((rows, FF_TILE), lambda i, spot, at=at: (at, i))
+        for at in (0, 1) + (0,) * (count - 2)
+    ]
+
+
+def settle(spots_ref, refs, whole_ref):
+    rows = refs[0].shape[0]
+    for at, ref in enumerate(refs):
+        begin = pl.multiple_of(spots_ref[at] * rows, rows)
+        whole_ref[pl.ds(begin, rows), :] = ref[...]
+
+
+def ffn_forward_kernel(count, spots_ref, a_ref, *refs):
+    gate_refs, up_refs = refs[:count], refs[count : 2 * count]
+    z_ref, act_ref, slope_ref, gate_whole, up_whole = refs[2 * count :]
+    settle(spots_ref, gate_refs, gate_whole)
+    settle(spots_ref, up_refs, up_whole)
+    step = min(256, a_ref.shape[0])
+    for begin in range(0, a_ref.shape[0], step):
+        rows = slice(begin, begin + step)
+        gate = jnp.dot(a_ref[rows], gate_whole[...], preferred_element_type=jnp.float32)
+        up = jnp.dot(a_ref[rows], up_whole[...], preferred_element_type=jnp.float32)
+        sig = jax.nn.sigmoid(gate)
+        act = gate * sig
+        z_ref[rows] = (act * up).astype(jnp.bfloat16)
+        act_ref[rows] = act.astype(jnp.bfloat16)
+        slope_ref[rows] = (up * (sig + act * (1.0 - sig))).astype(jnp.bfloat16)
+
+
+def ffn_forward(normed, gate, up):
+    rows, depth = normed.shape
+    (gate_blocks, spots), (up_blocks, _) = gate, up
+    count = len(gate_blocks) + 1
+    hidden = gate_blocks[0].shape[1]
+    part = gate_blocks[1].shape[0]
+    out = jax.ShapeDtypeStruct((rows, hidden), jnp.bfloat16)
+    return pl.pallas_call(
+        functools.partial(ffn_forward_kernel, count),
+        out_shape=(out, out, out),
+        grid_spec=pltpu.PrefetchScalarGridSpec(
+            num_scalar_prefetch=1,
+            grid=(hidden // FF_TILE,),
+            in_specs=[pl.BlockSpec((rows, depth), lambda i, spot: (0, 0))]
+            + block_specs(count, part) * 2,
+            out_specs=[pl.BlockSpec((rows, FF_TILE), lambda i, spot: (0, i))] * 3,
+            scratch_shapes=[pltpu.VMEM((depth, FF_TILE), jnp.bfloat16)] * 2,
+        ),
+        cost_estimate=pl.CostEstimate(
+            flops=4 * rows * depth * hidden,
+            bytes_accessed=4 * depth * hidden + 6 * rows * hidden,
+            transcendentals=rows * hidden,
+        ),
+        compiler_params=pltpu.CompilerParams(vmem_limit_bytes=60 << 20),
+        name="ffn_forward",
+    )(spots, normed, gate_blocks[0], *gate_blocks, up_blocks[0], *up_blocks)
+
+
+def ffn_inner_kernel(g_ref, down_ref, act_ref, slope_ref, dgate_ref, dup_ref):
+    step = min(256, g_ref.shape[0])
+    for begin in range(0, g_ref.shape[0], step):
+        rows = slice(begin, begin + step)
+        mixed = nt_dot(g_ref[rows], down_ref[...])
+        dgate_ref[rows] = (mixed * slope_ref[rows].astype(jnp.float32)).astype(jnp.bfloat16)
+        dup_ref[rows] = (mixed * act_ref[rows].astype(jnp.float32)).astype(jnp.bfloat16)
+
+
+def ffn_inner(grad_low, down, act, slope):
+    rows, depth = grad_low.shape
+    hidden = down.shape[0]
+    out = jax.ShapeDtypeStruct((rows, hidden), jnp.bfloat16)
+    tile = pl.BlockSpec((rows, FF_TILE), lambda i: (0, i))
+    return pl.pallas_call(
+        ffn_inner_kernel,
+        out_shape=(out, out),
+        grid=(hidden // FF_TILE,),
+        in_specs=[
+            pl.BlockSpec((rows, depth), lambda i: (0, 0)),
+            pl.BlockSpec((FF_TILE, depth), lambda i: (i, 0)),
+            tile,
+            tile,
+        ],
+        out_specs=[tile, tile],
+        cost_estimate=pl.CostEstimate(
+            flops=2 * rows * depth * hidden,
+            bytes_accessed=2 * depth * hidden + 8 * rows * hidden,
+            transcendentals=0,
+        ),
+        compiler_params=pltpu.CompilerParams(vmem_limit_bytes=60 << 20),
+        name="ffn_inner",
+    )(grad_low, down, act, slope)
+
+
+def ffn_input_kernel(count, spots_ref, dgate_ref, dup_ref, *refs):
+    gate_refs, up_refs = refs[:count], refs[count : 2 * count]
+    out_ref, gate_whole, up_whole = refs[2 * count :]
+    settle(spots_ref, gate_refs, gate_whole)
+    settle(spots_ref, up_refs, up_whole)
+
+    @pl.when(pl.program_id(0) == 0)
+    def _():
+        out_ref[...] = jnp.zeros_like(out_ref)
+
+    step = min(256, dgate_ref.shape[0])
+    for begin in range(0, dgate_ref.shape[0], step):
+        rows = slice(begin, begin + step)
+        out_ref[rows] += nt_dot(dgate_ref[rows], gate_whole[...]) + nt_dot(
+            dup_ref[rows], up_whole[...]
+        )
+
+
+def ffn_input(grad_gate, grad_up, gate, up):
+    rows, hidden = grad_gate.shape
+    (gate_blocks, spots), (up_blocks, _) = gate, up
+    count = len(gate_blocks) + 1
+    part = gate_blocks[1].shape[0]
+    depth = count * part
+    tile = pl.BlockSpec((rows, FF_TILE), lambda i, spot: (0, i))
+    return pl.pallas_call(
+        functools.partial(ffn_input_kernel, count),
+        out_shape=jax.ShapeDtypeStruct((rows, depth), jnp.float32),
+        grid_spec=pltpu.PrefetchScalarGridSpec(
+            num_scalar_prefetch=1,
+            grid=(hidden // FF_TILE,),
+            in_specs=[tile, tile] + block_specs(count, part) * 2,
+            out_specs=pl.BlockSpec((rows, depth), lambda i, spot: (0, 0)),
+            scratch_shapes=[pltpu.VMEM((depth, FF_TILE), jnp.bfloat16)] * 2,
+        ),
+        cost_estimate=pl.CostEstimate(
+            flops=4 * rows * depth * hidden,
+            bytes_accessed=4 * depth * hidden + 4 * rows * hidden,
+            transcendentals=0,
+        ),
+        compiler_params=pltpu.CompilerParams(vmem_limit_bytes=60 << 20),
+        name="ffn_input",
+    )(spots, grad_gate, grad_up, gate_blocks[0], *gate_blocks, up_blocks[0], *up_blocks)
 
 
 def gather_steps(links, mine, whole):
@@ -202,11 +345,11 @@
             bit *= 2
         del pieces[0]
         others = {d: rep_swap(piece, 1) for d, piece in pieces.items()}
-    blocks, spots = [whole[:half], whole[half:]], [2 * me, 2 * me + 1]
+    blocks, spots = [whole], [2 * me, 2 * me + 1]
     for d in pieces:
         blocks += [pieces[d], others[d]]
         spots += [2 * (me ^ d) + core, 2 * (me ^ d) + 1 - core]
-    return place_blocks(blocks, spots)
+    return blocks, jnp.stack(spots).astype(jnp.int32)
 
 
 def core_half(weight):
@@ -235,20 +378,18 @@
     return product.reshape(links[0], -1, product.shape[1])
 
 
-def combine(product, received):
-    return (product + received.astype(jnp.float32)).astype(jnp.bfloat16)
-
-
-def scatter_steps(links, part):
+def scatter_steps(links, own, received):
     shard_size, rep_size, shard_swap, rep_swap = links
     me = lax.axis_index("shard")
     rep = lax.axis_index("rep")
-    rows = part.shape[1] // 2
+    rows = own.shape[1] // 2
 
     def piece(d, at):
-        return lax.dynamic_slice(
-            part, (me ^ d, at * rows, 0), (1, rows, part.shape[2])
-        )[0]
+        begin, extent = (me ^ d, at * rows, 0), (1, rows, own.shape[2])
+        return add_low(
+            lax.dynamic_slice(own, begin, extent)[0],
+            lax.dynamic_slice(received, begin, extent)[0],
+        )
 
     if shard_size == 4:
         got_a = shard_swap(jnp.stack([piece(1, 0), piece(3, 0)]), 1)
@@ -558,7 +699,8 @@
     w_gate, w_up, w_down = sync((w_gate, w_up, w_down), front_flow, out_flow)
     gate_flow = Flow(gather_steps(links, core_half(w_gate), w_gate))
     w_up, w_down = sync((w_up, w_down), front_flow)
-    front = front_flow.finish()
+    up_flow = Flow(gather_steps(links, core_half(w_up), w_up))
+    front = place_blocks(front_flow.finish())
     full_query = front[:, : HQ * HD]
     full_key = front[:, HQ * HD : (HQ + HK) * HD]
     full_value = front[:, (HQ + HK) * HD : (HQ + 2 * HK) * HD]
@@ -593,38 +735,27 @@
     query_rot = query_rot.reshape(row_count, HQ * HD)
     key_rot = key_rot.reshape(row_count, HK * HD)
     value_low = value_low.reshape(row_count, HK * HD)
-    query_rot, key_rot, value_low, w_up, w_down = sync(
-        (query_rot, key_rot, value_low, w_up, w_down), out_flow, gate_flow
-    )
-    up_flow = Flow(gather_steps(links, core_half(w_up), w_up))
+    query_rot, key_rot, value_low, w_down = sync(
+        (query_rot, key_rot, value_low, w_down), out_flow, gate_flow, up_flow
+    )
+    down_flow = Flow(gather_steps(links, core_half(w_down), w_down))
     attn_low = attend(query_rot, key_rot, value_low, segment)
     attn_low = sync(attn_low, out_flow)
-    full_out = out_flow.finish()
+    full_out = place_blocks(out_flow.finish())
     hidden = inputs + matmul_plain(attn_low, full_out)
     scale_two = inv_rms(hidden)
     normed_ffn = (hidden * scale_two * full_ffn_gain.astype(jnp.float32)).astype(jnp.bfloat16)
-    normed_ffn, hidden, w_down = sync((normed_ffn, hidden, w_down), gate_flow, up_flow)
-    down_flow = Flow(gather_steps(links, core_half(w_down), w_down))
-    normed_ffn = sync(normed_ffn, gate_flow)
+    normed_ffn, hidden = sync((normed_ffn, hidden), gate_flow, up_flow)
+    normed_ffn = sync(normed_ffn, gate_flow, up_flow, down_flow)
     full_gate = gate_flow.finish()
-    gate_proj = matmul_plain(normed_ffn, full_gate)
-    gate_proj, normed_ffn = sync((gate_proj, normed_ffn), up_flow, down_flow)
-    normed_ffn = sync(normed_ffn, up_flow)
     full_up = up_flow.finish()
-    up_proj = matmul_plain(normed_ffn, full_up)
-    gate_sig = jax.nn.sigmoid(gate_proj)
-    gate_act = gate_proj * gate_sig
-    mixed_act = (gate_act * up_proj).astype(jnp.bfloat16)
-    slope = (up_proj * gate_sig * (1.0 + gate_proj * (1.0 - gate_sig))).astype(jnp.bfloat16)
-    act_low = gate_act.astype(jnp.bfloat16)
+    mixed_act, act_low, slope = ffn_forward(normed_ffn, full_gate, full_up)
     mixed_act, slope, act_low = sync((mixed_act, slope, act_low), down_flow)
     mixed_act, slope, act_low = sync((mixed_act, slope, act_low), down_flow)
-    full_down = down_flow.finish()
+    full_down = place_blocks(down_flow.finish())
     out_grad = live_rows * cotangent.astype(jnp.float32)
     out_low = out_grad.astype(jnp.bfloat16)
-    grad_mixed = matmul_cols(out_low, full_down)
-    grad_up_low = (grad_mixed * act_low.astype(jnp.float32)).astype(jnp.bfloat16)
-    grad_gate_low = (grad_mixed * slope.astype(jnp.float32)).astype(jnp.bfloat16)
+    grad_gate_low, grad_up_low = ffn_inner(out_low, full_down, act_low, slope)
     half = out_low.shape[1] // 2
     out_own = lax.dynamic_slice_in_dim(out_low, core * half, half, 1)
     out_other = lax.dynamic_slice_in_dim(out_low, (1 - core) * half, half, 1)
@@ -642,20 +773,20 @@
     down_sent, mixed_act, grad_up_low, gate_given = pin(
         (down_sent, mixed_act, grad_up_low, gate_given)
     )
-    down_part = combine(blocked(links, matmul_rows(mixed_act, out_own)), down_sent)
-    down_back = Flow(scatter_steps(links, down_part))
+    down_given = blocked(links, matmul_rows(mixed_act, out_own).astype(jnp.bfloat16))
+    down_back = Flow(scatter_steps(links, *pin((down_given, down_sent))))
     grad_up_low, grad_gate_low, normed_own, normed_other = pin(
-        (grad_up_low, grad_gate_low, normed_own, normed_other), down_part
+        (grad_up_low, grad_gate_low, normed_own, normed_other), down_given
     )
     up_sent = hand(matmul_rows(normed_other, grad_up_low))
-    gate_part = combine(blocked(links, matmul_rows(normed_own, grad_gate_low)), gate_sent)
-    up_part = combine(blocked(links, matmul_rows(normed_own, grad_up_low)), up_sent)
-    gate_part, up_part, grad_gate_low, grad_up_low = sync(
-        (gate_part, up_part, grad_gate_low, grad_up_low), down_back
-    )
-    gate_back = Flow(scatter_steps(links, gate_part))
-    grad_normed_ffn = matmul_cols(grad_gate_low, full_gate) + matmul_cols(grad_up_low, full_up)
-    grad_normed_ffn, up_part = sync((grad_normed_ffn, up_part), down_back)
+    gate_given = blocked(links, matmul_rows(normed_own, grad_gate_low).astype(jnp.bfloat16))
+    up_given = blocked(links, matmul_rows(normed_own, grad_up_low).astype(jnp.bfloat16))
+    gate_given, gate_sent, up_given, up_sent, grad_gate_low, grad_up_low = sync(
+        (gate_given, gate_sent, up_given, up_sent, grad_gate_low, grad_up_low), down_back
+    )
+    gate_back = Flow(scatter_steps(links, gate_given, gate_sent))
+    grad_normed_ffn = ffn_input(grad_gate_low, grad_up_low, full_gate, full_up)
+    grad_normed_ffn, up_given, up_sent = sync((grad_normed_ffn, up_given, up_sent), down_back)
     grad_ffn_gain = jnp.sum(grad_normed_ffn * hidden * scale_two, axis=0)
     grad_hidden = out_grad + norm_back(
         grad_normed_ffn, hidden, scale_two, full_ffn_gain.astype(jnp.float32)
@@ -664,17 +795,19 @@
     grad_attn_low = matmul_cols(hidden_low, full_out).astype(jnp.bfloat16)
     attn_own, attn_other = pick_columns(links, attn_low)
     out_sent = hand(matmul_rows(attn_other, hidden_low))
-    out_part = combine(blocked(links, matmul_rows(attn_own, hidden_low)), out_sent)
+    out_given = blocked(links, matmul_rows(attn_own, hidden_low).astype(jnp.bfloat16))
     panels = HK // 4
-    grad_attn_low, out_part, up_part = sync(
-        (grad_attn_low, out_part, up_part), gate_back, down_back
-    )
-    up_back = Flow(scatter_steps(links, up_part))
+    grad_attn_low, out_given, out_sent, up_given, up_sent = sync(
+        (grad_attn_low, out_given, out_sent, up_given, up_sent), gate_back, down_back
+    )
+    up_back = Flow(scatter_steps(links, up_given, up_sent))
     lower = attend_back(query_rot, grad_attn_low, key_rot, value_low, segment, 0, panels)
     grad_attn_low, lower = pin((grad_attn_low, lower))
     upper = attend_back(query_rot, grad_attn_low, key_rot, value_low, segment, panels, panels)
-    lower, upper, out_part = sync((lower, upper, out_part), gate_back, down_back)
-    out_back = Flow(scatter_steps(links, out_part))
+    lower, upper, out_given, out_sent = sync(
+        (lower, upper, out_given, out_sent), gate_back, down_back
+    )
+    out_back = Flow(scatter_steps(links, out_given, out_sent))
     grad_query_rot, grad_key_rot, grad_value = (
         jnp.concatenate(pair, axis=1) for pair in zip(lower, upper)
     )
@@ -717,19 +850,23 @@
     grad_inputs = grad_hidden + norm_back(
         grad_normed, inputs, scale_one, full_attn_gain.astype(jnp.float32)
     )
-    small = jnp.zeros((links[0], attn_gain.shape[0], 128), jnp.float32)
-    small = small.at[:, :, 0].set(grad_attn_gain.reshape(links[0], -1))
-    small = small.at[:, :, 1].set(grad_ffn_gain.reshape(links[0], -1))
-    small = small.at[:, : qk_gain.shape[0], 2].set(grad_qk_gain.reshape(links[0], -1))
+    qk_part = jnp.pad(
+        grad_qk_gain.reshape(links[0], -1),
+        ((0, 0), (0, attn_gain.shape[0] - qk_gain.shape[0])),
+    )
+    small = jnp.stack([grad_attn_gain, grad_ffn_gain, qk_part.reshape(-1)], axis=1)
+    small = jnp.pad(small, ((0, 0), (0, 125)))
     small = small.reshape(links[0], 2, -1, 128)
     own_front = jnp.concatenate([front_own, lax.dynamic_slice_in_dim(small, core, 1, 1)[:, 0]], axis=2)
     other_front = jnp.concatenate(
         [front_other, lax.dynamic_slice_in_dim(small, 1 - core, 1, 1)[:, 0]], axis=2
     )
     front_sent = rep_swap(other_front.astype(jnp.bfloat16), 1)
-    front_part = combine(own_front, front_sent)
-    front_part, mixed_act = sync((front_part, mixed_act), out_back, up_back, gate_back)
-    front_back = Flow(scatter_steps(links, front_part))
+    own_front = own_front.astype(jnp.bfloat16)
+    own_front, front_sent, mixed_act = sync(
+        (own_front, front_sent, mixed_act), out_back, up_back, gate_back
+    )
+    front_back = Flow(scatter_steps(links, own_front, front_sent))
     result = live_rows * (hidden + matmul_plain(mixed_act, full_down))
     grad_inputs, result = sync((grad_inputs, result), up_back, gate_back, out_back, front_back)
     front_share = join_rows(front_back.finish())

time: 780 us -> 761 us (0.976)
  waiting for transfers between devices: 110 us -> 204 us
  matrix products: 197 us -> 105 us
  Pallas kernels: 101 us -> 164 us
  other arithmetic: 169 us -> 117 us
  local copies, waits for them, and re-layouts: 108 us -> 66.9 us
  starting transfers between devices: 83.9 us -> 94.6 us
    pallas_call x0 -> x3, Pallas kernels: none -> 81.7 us  [the longest x1 28.7 us: ffn_forward(): pl.pallas_call(functools.partial(ffn_forward_kernel, count), out_shape=(o...]
    dot_general x7 -> x4, matrix products: 69.2 us -> 13 us  [matmul_cols(): lax.dot_general(left_mat, right_mat, (((1,), (1,)), ((), ())), preferred_...]
    ppermute x40, waiting for transfers between devices: 62.3 us -> 117 us  [rep_swap(): return lax.ppermute(value, axes, pairs)]
    convert_element_type x6 -> x0, other arithmetic: 44.5 us -> none  [the longest x5 25.4 us: combine(): return (product + received.astype(jnp.float32)).astype(jnp.bfloat16)]
    ppermute x40, waiting for transfers between devices: 47.9 us -> 87.1 us  [shard_swap(): return lax.ppermute(value, axes, pairs)]
    dot_general x7 -> x5, matrix products: 60.5 us -> 28 us  [matmul_plain(): return jnp.dot(left_mat, right_mat, preferred_element_type=jnp.float32)]
    unnamed x249 -> x266, local copies, waits for them, and re-layouts: 32.1 us -> 6.43 us
    pallas_call x5 -> x3, Pallas kernels: 40.6 us -> 21.6 us  [place_blocks(): pl.pallas_call(place_kernel, out_shape=jax.ShapeDtypeStruct((count * rows...]
  transfers between devices with their start and end apart: 80 -> 80, of which waited for: 18 -> 27; matrix products, arithmetic and copies ran while one was open for 47% -> 29% of each run, Pallas kernels for 12% -> 12%
where the time goes in v4:
time: 761 us; the launch traced here: 754 us
  waiting for transfers between devices  204 us (27%)
  Pallas kernels  164 us (22%)
  other arithmetic  117 us (15%)
  matrix products  105 us (14%)
  starting transfers between devices  94.6 us (12%)
  local copies, waits for them, and re-layouts  66.9 us (9%)
    ppermute x40, waiting for transfers between devices, rep_swap(): return lax.ppermute(value, axes, pairs)  117 us
    ppermute x40, waiting for transfers between devices, shard_swap(): return lax.ppermute(value, axes, pairs)  87.1 us
    dot_general x10, matrix products, matmul_rows(): lax.dot_general(left_mat, right_mat, (((0,), (0,)), ((), ())), preferred_...  63.9 us
    ppermute x40, starting transfers between devices, rep_swap(): return lax.ppermute(value, axes, pairs)  52.1 us
    ppermute x40, starting transfers between devices, shard_swap(): return lax.ppermute(value, axes, pairs)  42.5 us
    pallas_call x2, Pallas kernels, attend_back(): pl.pallas_call(attend_back_kernel, out_shape=(jax.ShapeDtypeStruct((rows,...  37.5 us
    pallas_call x1, Pallas kernels, ffn_forward(): pl.pallas_call(functools.partial(ffn_forward_kernel, count), out_shape=(o...  28.7 us
    pallas_call x1, Pallas kernels, ffn_input(): pl.pallas_call(functools.partial(ffn_input_kernel, count), out_shape=jax....  28.3 us
  transfers between devices with their start and end apart: 80, of which 27 were waited for; matrix products, arithmetic and copies ran while one was open for 29% of the time, Pallas kernels for 12%

profile of v4, /device:TPU:1, one launch (start us, length us, event | category | flops | bytes accessed | tf_op | source)
XLA Modules:
  0.0 754.0 jit_solution(8482248313113049173)
XLA Ops:
  12.2 8.4 %collective-permute-done.refs_2_ = bf16[128,2176]{1,0:T(8,128)(2,1)S(1)} collective-permute-done((bf16[128,2176]{1,0:T(8,128)(2,1)}, bf16[128,2176]{1,0:T(8,128)(2,1)S(1)}, u32[]{:S(2)}, u32[]{:S(2)}) %collective-permute-start) | collective-permute-done | bytes 557088 | tf_op jit(solution)/shard_map/ppermute | solution.py:90
  35.7 6.0 collective-permute-done.2
  52.5 6.9 place_blocks.3
  61.9 4.4 multiply_reduce_fusion.4
  66.3 3.3 multiply_reduce_fusion.6
  75.3 3.2 multiply_multiply_fusion
  84.9 17.6 %collective-permute-done.10 = bf16[64,1024]{1,0:T(8,128)(2,1)S(1)} collective-permute-done((bf16[64,1024]{1,0:T(8,128)(2,1)}, bf16[64,1024]{1,0:T(8,128)(2,1)S(1)}, u32[]{:S(2)}, u32[]{:S(2)}) %collective-permute-start.10) | collective-permute-done | bytes 131104 | tf_op jit(solution)/shard_map/ppermute | solution.py:90
  114.0 3.9 copy.101.q_ref
  122.0 23.5 %attend.1 = bf16[1024,1024]{1,0:T(8,128)(2,1)} custom-call(s32[4,4]{1,0:T(4,128)} %fusion.87.live_ref, bf16[1024,1024]{1,0:T(8,128)(2,1)} %copy.101.q_ref, bf16[1024,512]{1,0:T(8,128)(2,1)} %copy.102.k_ref, bf16[1024,512]{1,0:T(8,128)(2,1)} %convolution_convert_fusion.11.v_ref, s32[1024,1]{1,0:T(8,128)} %copy.103.seg_col_ref, s32[1,1024]{1,0:T(1,128)} %bitcast.214), custom_call_target="tpu_custom_call" | custom-call | flops 19327352832 | bytes 8388608 | tf_op jit(solution)/shard_map/attend/pallas_call | solution.py:598
  151.8 5.3 place_blocks.4
  157.7 3.3 collective-permute-start.22
  160.9 4.7 multiply_reduce_fusion.3
  165.6 8.8 %collective-permute-done.22 = bf16[64,4608]{1,0:T(8,128)(2,1)S(1)} collective-permute-done((bf16[64,4608]{1,0:T(8,128)(2,1)}, bf16[64,4608]{1,0:T(8,128)(2,1)S(1)}, u32[]{:S(2)}, u32[]{:S(2)}) %collective-permute-start.22) | collective-permute-done | bytes 589856 | tf_op jit(solution)/shard_map/ppermute | solution.py:90
  174.5 3.0 collective-permute-start.23
  179.8 10.4 %collective-permute-done.23 = bf16[64,4608]{1,0:T(8,128)(2,1)S(1)} collective-permute-done((bf16[64,4608]{1,0:T(8,128)(2,1)S(1)}, bf16[64,4608]{1,0:T(8,128)(2,1)S(1)}, u32[]{:S(2)}, u32[]{:S(2)}) %collective-permute-start.23) | collective-permute-done | bytes 589856 | tf_op jit(solution)/shard_map/ppermute | solution.py:90
  196.0 20.3 %collective-permute-done.28.refs_2_ = bf16[576,1024]{1,0:T(8,128)(2,1)S(1)} collective-permute-done((bf16[576,1024]{1,0:T(8,128)(2,1)S(1)}, bf16[576,1024]{1,0:T(8,128)(2,1)S(1)}, u32[]{:S(2)}, u32[]{:S(2)}) %collective-permute-start.28) | collective-permute-done | bytes 1179680 | tf_op jit(solution)/shard_map/ppermute | solution.py:90
  217.8 3.0 collective-permute-start.32
  223.9 28.7 %ffn_forward.1 = (bf16[1024,4608]{1,0:T(8,128)(2,1)}, bf16[1024,4608]{1,0:T(8,128)(2,1)}, bf16[1024,4608]{1,0:T(8,128)(2,1)}) custom-call(s32[8]{0:T(128)} %stack.60.spots_ref, bf16[1024,1024]{1,0:T(8,128)(2,1)} %multiply_convert_fusion.a_ref, bf16[256,4608]{1,0:T(8,128)(2,1)} %refs_1_.3, bf16[256,4608]{1,0:T(8,128)(2,1)} %refs_1_.3, ...), custom_call_target="tpu_custom_call" | custom-call | flops 19327352832 | bytes 47185920 | tf_op jit(solution)/shard_map/ffn_forward/pallas_call | solution.py:214
  258.7 9.4 %place_blocks.5.down_ref = bf16[4608,1024]{1,0:T(8,128)(2,1)} custom-call(s32[8]{0:T(128)} %stack.60.spots_ref, bf16[1152,1024]{1,0:T(8,128)(2,1)} %refs_1_.2, bf16[1152,1024]{1,0:T(8,128)(2,1)} %refs_1_.2, bf16[576,1024]{1,0:T(8,128)(2,1)} %copy-done.27, bf16[576,1024]{1,0:T(8,128)(2,1)} %collective-permute-done.32.refs_3_, ...), custom_call_target="tpu_custom_call" | custom-call | bytes 18874368 | tf_op jit(solution)/shard_map/place_blocks/pallas_call | solution.py:153
  268.1 24.8 %ffn_inner.1 = (bf16[1024,4608]{1,0:T(8,128)(2,1)}, bf16[1024,4608]{1,0:T(8,128)(2,1)}) custom-call(bf16[1024,1024]{1,0:T(8,128)(2,1)} %copy-done.14, bf16[4608,1024]{1,0:T(8,128)(2,1)} %place_blocks.5.down_ref, bf16[1024,4608]{1,0:T(8,128)(2,1)} %get-tuple-element.211.act_ref, bf16[1024,4608]{1,0:T(8,128)(2,1)} %get-tuple-element.212.slope_ref), custom_call_target="tpu_custom_call" | custom-call | flops 9663676416 | bytes 47185920 | tf_op jit(solution)/shard_map/ffn_inner/pallas_call | solution.py:249
  292.9 10.9 %convolution_convert_fusion.1 = bf16[4608,512]{1,0:T(8,128)(2,1)} fusion(bf16[1024,4608]{1,0:T(8,128)(2,1)} %get-tuple-element.280, bf16[1024,512]{1,0:T(8,128)(2,1)S(1)} %copy-done.46), kind=kOutput, calls=%fused_computation.7 | convolution fusion | flops 4834197504 | bytes 15204352 | tf_op jit(solution)/shard_map/dot_general | solution.py:69
  306.2 5.9 collective-permute-done.35
  312.1 10.9 %convolution_convert_fusion.5 = bf16[512,4608]{1,0:T(8,128)(2,1)} fusion(bf16[1024,4608]{1,0:T(8,128)(2,1)} %get-tuple-element.231.dgate_ref, bf16[1024,128]{1,0:T(8,128)(2,1)S(1)} %get-tuple-element.389, bf16[1024,128]{1,0:T(8,128)(2,1)S(1)} %get-tuple-element.390, bf16[1024,128]{1,0:T(8,128)(2,1)S(1)} %get-tuple-element.391, ...), kind=kOutput, calls=%fused_computation.11 | convolution fusion | flops 4838391808 | bytes 15204352 | tf_op jit(solution)/shard_map/dot_general | solution.py:69
  323.0 7.0 convolution_convert_fusion
  330.4 7.0 convolution_convert_fusion.2
  338.3 3.0 constant_dynamic-slice_fusion
  348.5 10.8 %convolution_convert_fusion.3 = bf16[512,4608]{1,0:T(8,128)(2,1)} fusion(bf16[1024,512]{1,0:T(8,128)(2,1)S(1)} %pad_maximum_fusion.18, bf16[1024,4608]{1,0:T(8,128)(2,1)} %get-tuple-element.232.dup_ref), kind=kOutput, calls=%fused_computation.9 | convolution fusion | flops 4834197504 | bytes 15204352 | tf_op jit(solution)/shard_map/dot_general | solution.py:69
  359.3 5.4 convolution_convert_fusion.4
  364.8 8.9 %collective-permute-done.38 = bf16[2,576,512]{2,1,0:T(8,128)(2,1)S(1)} collective-permute-done((bf16[2,576,512]{2,1,0:T(8,128)(2,1)S(1)}, bf16[2,576,512]{2,1,0:T(8,128)(2,1)S(1)}, u32[]{:S(2)}, u32[]{:S(2)}) %collective-permute-start.38) | collective-permute-done | bytes 1179680 | tf_op jit(solution)/shard_map/ppermute | solution.py:90
  374.7 3.2 fusion.69
  385.2 28.3 %ffn_input.1 = f32[1024,1024]{1,0:T(8,128)} custom-call(s32[8]{0:T(128)} %stack.60.spots_ref, bf16[1024,4608]{1,0:T(8,128)(2,1)} %get-tuple-element.231.dgate_ref, bf16[1024,4608]{1,0:T(8,128)(2,1)} %get-tuple-element.232.dup_ref, bf16[256,4608]{1,0:T(8,128)(2,1)} %refs_1_.3, bf16[256,4608]{1,0:T(8,128)(2,1)} %refs_1_.3, ...), custom_call_target="tpu_custom_call" | custom-call | flops 19327352832 | bytes 37748736 | tf_op jit(solution)/shard_map/ffn_input/pallas_call | solution.py:295
  413.5 5.2 multiply_reduce_fusion
  431.9 3.7 convolution_convert_fusion.8.do_ref
  435.6 5.9 collective-permute-done.45
  441.5 18.5 %attend_back.2 = (f32[1024,512]{1,0:T(8,128)}, f32[1024,256]{1,0:T(8,128)}, f32[1024,256]{1,0:T(8,128)}) custom-call(s32[4,4]{1,0:T(4,128)} %fusion.87.live_ref, bf16[1024,1024]{1,0:T(8,128)(2,1)} %copy.101.q_ref, bf16[1024,1024]{1,0:T(8,128)(2,1)} %convolution_convert_fusion.8.do_ref, bf16[1024,512]{1,0:T(8,128)(2,1)} %copy.102.k_ref, ...), custom_call_target="tpu_custom_call" | custom-call | flops 16106127360 | bytes 8388608 | tf_op jit(solution)/shard_map/attend_back/pallas_call | solution.py:626
  460.1 19.0 %attend_back.3 = (f32[1024,512]{1,0:T(8,128)}, f32[1024,256]{1,0:T(8,128)}, f32[1024,256]{1,0:T(8,128)}) custom-call(s32[4,4]{1,0:T(4,128)} %fusion.87.live_ref, bf16[1024,1024]{1,0:T(8,128)(2,1)} %copy.101.q_ref, bf16[1024,1024]{1,0:T(8,128)(2,1)} %convolution_convert_fusion.8.do_ref, bf16[1024,512]{1,0:T(8,128)(2,1)} %copy.102.k_ref, ...), custom_call_target="tpu_custom_call" | custom-call | flops 16106127360 | bytes 8388608 | tf_op jit(solution)/shard_map/attend_back/pallas_call | solution.py:626
  481.3 5.7 collective-permute-start.46
  490.3 2.9 add_convert_fusion.19
  498.3 14.0 %collective-permute-done.48 = bf16[576,512]{1,0:T(8,128)(2,1)S(1)} collective-permute-done((bf16[576,512]{1,0:T(8,128)(2,1)S(1)}, bf16[576,512]{1,0:T(8,128)(2,1)S(1)}, u32[]{:S(2)}, u32[]{:S(2)}) %collective-permute-start.48) | collective-permute-done | bytes 589856 | tf_op jit(solution)/shard_map/ppermute | solution.py:98
  522.8 2.9 copy.112
  525.6 3.0 copy.111
  533.0 3.6 broadcast_select_fusion.5
  536.6 4.9 collective-permute-start.51
  544.4 3.1 multiply_reduce_fusion.1
  550.7 4.4 fusion.2
  556.1 6.9 pad_maximum_fusion.1
  563.0 3.6 collective-permute-done.52
  566.6 4.0 fusion.20
  572.3 4.0 fusion.11
  576.6 4.6 convolution_convert_fusion.6
  594.4 3.8 convolution_convert_fusion.7
  602.3 3.1 collective-permute-start.60
  605.4 10.3 %fusion.16 = f32[1152,1024]{1,0:T(8,128)} fusion(bf16[1152,512]{1,0:T(8,128)(2,1)S(1)} %collective-permute-done.79, bf16[576,512]{1,0:T(8,128)(2,1)S(1)} %get-tuple-element.396, bf16[576,512]{1,0:T(8,128)(2,1)S(1)} %get-tuple-element.395, pred[]{:T(512)S(6)} %eq.38), kind=kLoop, calls=%fused_computation.58 | loop fusion | flops 16515072 | bytes 7077889 | tf_op jit(solution)/shard_map/convert_element_type | solution.py:459
  615.7 15.2 %collective-permute-done.60 = bf16[64,4608]{1,0:T(8,128)(2,1)S(1)} collective-permute-done((bf16[64,4608]{1,0:T(8,128)(2,1)S(1)}, bf16[64,4608]{1,0:T(8,128)(2,1)S(1)}, u32[]{:S(2)}, u32[]{:S(2)}) %collective-permute-start.60) | collective-permute-done | bytes 589856 | tf_op jit(solution)/shard_map/ppermute | solution.py:98
  640.1 13.4 %add_multiply_fusion = bf16[1024,1024]{1,0:T(8,128)(2,1)} fusion(f32[1024,1024]{1,0:T(8,128)S(1)} %copy-done.2, f32[1024]{0:T(1024)S(1)} %compare_convert_fusion, bf16[1024,4608]{1,0:T(8,128)(2,1)} %get-tuple-element.280, bf16[4608,1024]{1,0:T(8,128)(2,1)S(1)} %bitcast.190), kind=kOutput, calls=%fused_computation.33 | convolution fusion | flops 9666822144 | bytes 25169920 | tf_op jit(solution)/shard_map/dot_general | solution.py:65
  653.5 9.4 %collective-permute-done.63 = bf16[64,1024]{1,0:T(8,128)(2,1)S(1)} collective-permute-done((bf16[64,1024]{1,0:T(8,128)(2,1)}, bf16[64,1024]{1,0:T(8,128)(2,1)S(1)}, u32[]{:S(2)}, u32[]{:S(2)}) %collective-permute-start.63) | collective-permute-done | bytes 131104 | tf_op jit(solution)/shard_map/ppermute | solution.py:98
  664.1 4.1 collective-permute-start.72
  670.3 3.7 collective-permute-done.72
  678.0 4.1 collective-permute-start.74
  683.8 3.2 collective-permute-start.69
  688.4 23.8 %collective-permute-done.69 = bf16[64,2176]{1,0:T(8,128)(2,1)S(1)} collective-permute-done((bf16[64,2176]{1,0:T(8,128)(2,1)S(1)}, bf16[64,2176]{1,0:T(8,128)(2,1)S(1)}, u32[]{:S(2)}, u32[]{:S(2)}) %collective-permute-start.69) | collective-permute-done | bytes 278560 | tf_op jit(solution)/shard_map/ppermute | solution.py:98
  712.4 12.5 %collective-permute-done.76 = bf16[64,4608]{1,0:T(8,128)(2,1)S(1)} collective-permute-done((bf16[64,4608]{1,0:T(8,128)(2,1)S(1)}, bf16[64,4608]{1,0:T(8,128)(2,1)S(1)}, u32[]{:S(2)}, u32[]{:S(2)}) %collective-permute-start.76) | collective-permute-done | bytes 589856 | tf_op jit(solution)/shard_map/ppermute | solution.py:98
  725.1 6.2 collective-permute-done.70
  732.1 11.9 %collective-permute-done.77 = bf16[64,4608]{1,0:T(8,128)(2,1)S(1)} collective-permute-done((bf16[64,4608]{1,0:T(8,128)(2,1)S(1)}, bf16[64,4608]{1,0:T(8,128)(2,1)S(1)}, u32[]{:S(2)}, u32[]{:S(2)}) %collective-permute-start.77) | collective-permute-done | bytes 589856 | tf_op jit(solution)/shard_map/ppermute | solution.py:98
  (557 shorter events, 206.4 us)
Async XLA Ops:
  5.9 14.7 %collective-permute-start = (bf16[128,2176]{1,0:T(8,128)(2,1)}, bf16[128,2176]{1,0:T(8,128)(2,1)S(1)}, u32[]{:S(2)}, u32[]{:S(2)}) collective-permute-start(bf16[128,2176]{1,0:T(8,128)(2,1)} %pad_maximum_fusion.19), channel_id=1, source_target_pairs={{0,8},{1,9},{2,10},{3,11},{4,12},{5,13},{6,14},{7,15},{8,0},{9,1},... | collective-permute-start | bytes 1671176 | tf_op jit(solution)/shard_map/ppermute | solution.py:90
  8.0 13.5 %collective-permute-start.1 = (bf16[128,2176]{1,0:T(8,128)(2,1)}, bf16[128,2176]{1,0:T(8,128)(2,1)}, u32[]{:S(2)}, u32[]{:S(2)}) collective-permute-start(bf16[128,2176]{1,0:T(8,128)(2,1)} %pad_maximum_fusion.19), channel_id=1, source_target_pairs={{0,16},{1,17},{2,18},{3,19},{4,20},{5,21},{6,22},{7,23},{8,24},{9,... | collective-permute-start | bytes 1671176 | tf_op jit(solution)/shard_map/ppermute | solution.py:90
  23.3 18.4 %collective-permute-start.4 = (bf16[128,2176]{1,0:T(8,128)(2,1)S(1)}, bf16[128,2176]{1,0:T(8,128)(2,1)}, u32[]{:S(2)}, u32[]{:S(2)}) collective-permute-start(bf16[128,2176]{1,0:T(8,128)(2,1)S(1)} %collective-permute-done.refs_2_), channel_id=1, source_target_pairs={{0,1},{1,0},{2,3},{3,2},{4,5},{5,4},{6,7},{7,6},{8,9},{9,8},{10,11... | collective-permute-start | bytes 1671176 | tf_op jit(solution)/shard_map/ppermute | solution.py:98
  25.0 16.6 %collective-permute-start.5 = (bf16[128,2176]{1,0:T(8,128)(2,1)}, bf16[128,2176]{1,0:T(8,128)(2,1)}, u32[]{:S(2)}, u32[]{:S(2)}) collective-permute-start(bf16[128,2176]{1,0:T(8,128)(2,1)} %collective-permute-done.1.refs_4_), channel_id=1, source_target_pairs={{0,1},{1,0},{2,3},{3,2},{4,5},{5,4},{6,7},{7,6},{8,9},{9,8},{10,11... | collective-permute-start | bytes 1671176 | tf_op jit(solution)/shard_map/ppermute | solution.py:98
  29.4 12.2 %collective-permute-start.2 = (bf16[64,2176]{1,0:T(8,128)(2,1)}, bf16[64,2176]{1,0:T(8,128)(2,1)}, u32[]{:S(2)}, u32[]{:S(2)}) collective-permute-start(bf16[64,2176]{1,0:T(8,128)(2,1)} %slice.194), channel_id=1, source_target_pairs={{0,16},{1,17},{2,18},{3,19},{4,20},{5,21},{6,22},{7,23},{8,24},{9,... | collective-permute-start | bytes 835592 | tf_op jit(solution)/shard_map/ppermute | solution.py:90
  29.5 12.2 %collective-permute-start.3 = (bf16[64,2176]{1,0:T(8,128)(2,1)}, bf16[64,2176]{1,0:T(8,128)(2,1)}, u32[]{:S(2)}, u32[]{:S(2)}) collective-permute-start(bf16[64,2176]{1,0:T(8,128)(2,1)} %slice.195), channel_id=1, source_target_pairs={{0,8},{1,9},{2,10},{3,11},{4,12},{5,13},{6,14},{7,15},{8,0},{9,1},... | collective-permute-start | bytes 835592 | tf_op jit(solution)/shard_map/ppermute | solution.py:90
  47.4 62.1 %collective-permute-start.13 = (bf16[128,4608]{1,0:T(8,128)(2,1)}, bf16[128,4608]{1,0:T(8,128)(2,1)}, u32[]{:S(2)}, u32[]{:S(2)}) collective-permute-start(bf16[128,4608]{1,0:T(8,128)(2,1)} %constant_dynamic-slice_fusion.28), channel_id=1, source_target_pairs={{0,8},{1,9},{2,10},{3,11},{4,12},{5,13},{6,14},{7,15},{8,0},{9,1},... | collective-permute-start | bytes 3538952 | tf_op jit(solution)/shard_map/ppermute | solution.py:90
  48.8 60.7 %collective-permute-start.14 = (bf16[128,4608]{1,0:T(8,128)(2,1)}, bf16[128,4608]{1,0:T(8,128)(2,1)}, u32[]{:S(2)}, u32[]{:S(2)}) collective-permute-start(bf16[128,4608]{1,0:T(8,128)(2,1)} %constant_dynamic-slice_fusion.28), channel_id=1, source_target_pairs={{0,16},{1,17},{2,18},{3,19},{4,20},{5,21},{6,22},{7,23},{8,24},{9,... | collective-permute-start | bytes 3538952 | tf_op jit(solution)/shard_map/ppermute | solution.py:90
  50.7 30.9 %collective-permute-start.9 = (bf16[64,1024]{1,0:T(8,128)(2,1)}, bf16[64,1024]{1,0:T(8,128)(2,1)S(1)}, u32[]{:S(2)}, u32[]{:S(2)}) collective-permute-start(bf16[64,1024]{1,0:T(8,128)(2,1)} %slice.210), channel_id=1, source_target_pairs={{0,16},{1,17},{2,18},{3,19},{4,20},{5,21},{6,22},{7,23},{8,24},{9,... | collective-permute-start | bytes 393224 | tf_op jit(solution)/shard_map/ppermute | solution.py:90
  72.9 36.6 %collective-permute-start.15 = (bf16[128,4608]{1,0:T(8,128)(2,1)}, bf16[128,4608]{1,0:T(8,128)(2,1)}, u32[]{:S(2)}, u32[]{:S(2)}) collective-permute-start(bf16[128,4608]{1,0:T(8,128)(2,1)} %constant_dynamic-slice_fusion.27), channel_id=1, source_target_pairs={{0,8},{1,9},{2,10},{3,11},{4,12},{5,13},{6,14},{7,15},{8,0},{9,1},... | collective-permute-start | bytes 3538952 | tf_op jit(solution)/shard_map/ppermute | solution.py:90
  73.0 36.6 %collective-permute-start.16 = (bf16[128,4608]{1,0:T(8,128)(2,1)}, bf16[128,4608]{1,0:T(8,128)(2,1)}, u32[]{:S(2)}, u32[]{:S(2)}) collective-permute-start(bf16[128,4608]{1,0:T(8,128)(2,1)} %constant_dynamic-slice_fusion.27), channel_id=1, source_target_pairs={{0,16},{1,17},{2,18},{3,19},{4,20},{5,21},{6,22},{7,23},{8,24},{9,... | collective-permute-start | bytes 3538952 | tf_op jit(solution)/shard_map/ppermute | solution.py:90
  81.7 20.9 %collective-permute-start.10 = (bf16[64,1024]{1,0:T(8,128)(2,1)}, bf16[64,1024]{1,0:T(8,128)(2,1)S(1)}, u32[]{:S(2)}, u32[]{:S(2)}) collective-permute-start(bf16[64,1024]{1,0:T(8,128)(2,1)} %slice.211), channel_id=1, source_target_pairs={{0,8},{1,9},{2,10},{3,11},{4,12},{5,13},{6,14},{7,15},{8,0},{9,1},... | collective-permute-start | bytes 393224 | tf_op jit(solution)/shard_map/ppermute | solution.py:90
  111.5 79.9 %collective-permute-start.20 = (bf16[128,4608]{1,0:T(8,128)(2,1)}, bf16[128,4608]{1,0:T(8,128)(2,1)}, u32[]{:S(2)}, u32[]{:S(2)}) collective-permute-start(bf16[128,4608]{1,0:T(8,128)(2,1)} %collective-permute-done.13.refs_2_), channel_id=1, source_target_pairs={{0,1},{1,0},{2,3},{3,2},{4,5},{5,4},{6,7},{7,6},{8,9},{9,8},{10,11... | collective-permute-start | bytes 3538952 | tf_op jit(solution)/shard_map/ppermute | solution.py:98
  113.6 78.6 %collective-permute-start.21 = (bf16[128,4608]{1,0:T(8,128)(2,1)}, bf16[128,4608]{1,0:T(8,128)(2,1)}, u32[]{:S(2)}, u32[]{:S(2)}) collective-permute-start(bf16[128,4608]{1,0:T(8,128)(2,1)} %collective-permute-done.14.refs_4_), channel_id=1, source_target_pairs={{0,1},{1,0},{2,3},{3,2},{4,5},{5,4},{6,7},{7,6},{8,9},{9,8},{10,11... | collective-permute-start | bytes 3538952 | tf_op jit(solution)/shard_map/ppermute | solution.py:98
  119.3 32.5 %collective-permute-start.17 = (bf16[128,1024]{1,0:T(8,128)(2,1)S(1)}, bf16[128,1024]{1,0:T(8,128)(2,1)}, u32[]{:S(2)}, u32[]{:S(2)}) collective-permute-start(bf16[128,1024]{1,0:T(8,128)(2,1)S(1)} %constant_dynamic-update-slice_fusion.2.refs_6_), channel_id=1, source_target_pairs={{0,1},{1,0},{2,3},{3,2},{4,5},{5,4},{6,7},{7,6},{8,9},{9,8},{10,11... | collective-permute-start | bytes 786440 | tf_op jit(solution)/shard_map/ppermute | solution.py:98
  119.5 37.5 %collective-permute-start.18 = (bf16[64,4608]{1,0:T(8,128)(2,1)}, bf16[64,4608]{1,0:T(8,128)(2,1)S(1)}, u32[]{:S(2)}, u32[]{:S(2)}) collective-permute-start(bf16[64,4608]{1,0:T(8,128)(2,1)} %slice.213), channel_id=1, source_target_pairs={{0,16},{1,17},{2,18},{3,19},{4,20},{5,21},{6,22},{7,23},{8,24},{9,... | collective-permute-start | bytes 1769480 | tf_op jit(solution)/shard_map/ppermute | solution.py:90
  120.8 36.9 %collective-permute-start.19 = (bf16[64,4608]{1,0:T(8,128)(2,1)}, bf16[64,4608]{1,0:T(8,128)(2,1)S(1)}, u32[]{:S(2)}, u32[]{:S(2)}) collective-permute-start(bf16[64,4608]{1,0:T(8,128)(2,1)} %slice.214), channel_id=1, source_target_pairs={{0,8},{1,9},{2,10},{3,11},{4,12},{5,13},{6,14},{7,15},{8,0},{9,1},... | collective-permute-start | bytes 1769480 | tf_op jit(solution)/shard_map/ppermute | solution.py:90
  151.8 40.4 %collective-permute-start.24 = (bf16[128,4608]{1,0:T(8,128)(2,1)}, bf16[128,4608]{1,0:T(8,128)(2,1)}, u32[]{:S(2)}, u32[]{:S(2)}) collective-permute-start(bf16[128,4608]{1,0:T(8,128)(2,1)} %collective-permute-done.15.refs_10_), channel_id=1, source_target_pairs={{0,1},{1,0},{2,3},{3,2},{4,5},{5,4},{6,7},{7,6},{8,9},{9,8},{10,11... | collective-permute-start | bytes 3538952 | tf_op jit(solution)/shard_map/ppermute | solution.py:98
  157.1 35.1 %collective-permute-start.25 = (bf16[128,4608]{1,0:T(8,128)(2,1)}, bf16[128,4608]{1,0:T(8,128)(2,1)S(1)}, u32[]{:S(2)}, u32[]{:S(2)}) collective-permute-start(bf16[128,4608]{1,0:T(8,128)(2,1)} %collective-permute-done.16.refs_12_), channel_id=1, source_target_pairs={{0,1},{1,0},{2,3},{3,2},{4,5},{5,4},{6,7},{7,6},{8,9},{9,8},{10,11... | collective-permute-start | bytes 3538952 | tf_op jit(solution)/shard_map/ppermute | solution.py:98
  157.7 16.8 %collective-permute-start.22 = (bf16[64,4608]{1,0:T(8,128)(2,1)}, bf16[64,4608]{1,0:T(8,128)(2,1)S(1)}, u32[]{:S(2)}, u32[]{:S(2)}) collective-permute-start(bf16[64,4608]{1,0:T(8,128)(2,1)} %slice.215), channel_id=1, source_target_pairs={{0,16},{1,17},{2,18},{3,19},{4,20},{5,21},{6,22},{7,23},{8,24},{9,... | collective-permute-start | bytes 1769480 | tf_op jit(solution)/shard_map/ppermute | solution.py:90
  174.5 15.7 %collective-permute-start.23 = (bf16[64,4608]{1,0:T(8,128)(2,1)S(1)}, bf16[64,4608]{1,0:T(8,128)(2,1)S(1)}, u32[]{:S(2)}, u32[]{:S(2)}) collective-permute-start(bf16[64,4608]{1,0:T(8,128)(2,1)S(1)} %copy-done.61), channel_id=1, source_target_pairs={{0,8},{1,9},{2,10},{3,11},{4,12},{5,13},{6,14},{7,15},{8,0},{9,1},... | collective-permute-start | bytes 1769480 | tf_op jit(solution)/shard_map/ppermute | solution.py:90
  190.2 26.0 %collective-permute-start.28 = (bf16[576,1024]{1,0:T(8,128)(2,1)S(1)}, bf16[576,1024]{1,0:T(8,128)(2,1)S(1)}, u32[]{:S(2)}, u32[]{:S(2)}) collective-permute-start(bf16[576,1024]{1,0:T(8,128)(2,1)S(1)} %copy-done.42), channel_id=1, source_target_pairs={{0,8},{1,9},{2,10},{3,11},{4,12},{5,13},{6,14},{7,15},{8,0},{9,1},... | collective-permute-start | bytes 3538952 | tf_op jit(solution)/shard_map/ppermute | solution.py:90
  191.4 25.4 %collective-permute-start.29 = (bf16[576,1024]{1,0:T(8,128)(2,1)S(1)}, bf16[576,1024]{1,0:T(8,128)(2,1)}, u32[]{:S(2)}, u32[]{:S(2)}) collective-permute-start(bf16[576,1024]{1,0:T(8,128)(2,1)S(1)} %copy-done.42), channel_id=1, source_target_pairs={{0,16},{1,17},{2,18},{3,19},{4,20},{5,21},{6,22},{7,23},{8,24},{9,... | collective-permute-start | bytes 3538952 | tf_op jit(solution)/shard_map/ppermute | solution.py:90
  192.3 24.5 %collective-permute-start.26 = (bf16[128,4608]{1,0:T(8,128)(2,1)S(1)}, bf16[128,4608]{1,0:T(8,128)(2,1)S(1)}, u32[]{:S(2)}, u32[]{:S(2)}) collective-permute-start(bf16[128,4608]{1,0:T(8,128)(2,1)S(1)} %constant_dynamic-update-slice_fusion.4.refs_6_), channel_id=1, source_target_pairs={{0,1},{1,0},{2,3},{3,2},{4,5},{5,4},{6,7},{7,6},{8,9},{9,8},{10,11... | collective-permute-start | bytes 3538952 | tf_op jit(solution)/shard_map/ppermute | solution.py:98
  195.2 21.6 %collective-permute-start.27 = (bf16[128,4608]{1,0:T(8,128)(2,1)S(1)}, bf16[128,4608]{1,0:T(8,128)(2,1)S(1)}, u32[]{:S(2)}, u32[]{:S(2)}) collective-permute-start(bf16[128,4608]{1,0:T(8,128)(2,1)S(1)} %constant_dynamic-update-slice_fusion.6.refs_14_), channel_id=1, source_target_pairs={{0,1},{1,0},{2,3},{3,2},{4,5},{5,4},{6,7},{7,6},{8,9},{9,8},{10,11... | collective-permute-start | bytes 3538952 | tf_op jit(solution)/shard_map/ppermute | solution.py:98
  217.8 34.9 %collective-permute-start.32 = (bf16[576,1024]{1,0:T(8,128)(2,1)S(1)}, bf16[576,1024]{1,0:T(8,128)(2,1)}, u32[]{:S(2)}, u32[]{:S(2)}) collective-permute-start(bf16[576,1024]{1,0:T(8,128)(2,1)S(1)} %collective-permute-done.28.refs_2_), channel_id=1, source_target_pairs={{0,1},{1,0},{2,3},{3,2},{4,5},{5,4},{6,7},{7,6},{8,9},{9,8},{10,11... | collective-permute-start | bytes 3538952 | tf_op jit(solution)/shard_map/ppermute | solution.py:98
  222.7 29.9 %collective-permute-start.33 = (bf16[576,1024]{1,0:T(8,128)(2,1)}, bf16[576,1024]{1,0:T(8,128)(2,1)}, u32[]{:S(2)}, u32[]{:S(2)}) collective-permute-start(bf16[576,1024]{1,0:T(8,128)(2,1)} %collective-permute-done.29.refs_4_), channel_id=1, source_target_pairs={{0,1},{1,0},{2,3},{3,2},{4,5},{5,4},{6,7},{7,6},{8,9},{9,8},{10,11... | collective-permute-start | bytes 3538952 | tf_op jit(solution)/shard_map/ppermute | solution.py:98
  222.8 29.8 %collective-permute-start.30 = (bf16[288,1024]{1,0:T(8,128)(2,1)}, bf16[288,1024]{1,0:T(8,128)(2,1)}, u32[]{:S(2)}, u32[]{:S(2)}) collective-permute-start(bf16[288,1024]{1,0:T(8,128)(2,1)} %slice.217), channel_id=1, source_target_pairs={{0,16},{1,17},{2,18},{3,19},{4,20},{5,21},{6,22},{7,23},{8,24},{9,... | collective-permute-start | bytes 1769480 | tf_op jit(solution)/shard_map/ppermute | solution.py:90
  223.6 29.0 %collective-permute-start.31 = (bf16[288,1024]{1,0:T(8,128)(2,1)}, bf16[288,1024]{1,0:T(8,128)(2,1)}, u32[]{:S(2)}, u32[]{:S(2)}) collective-permute-start(bf16[288,1024]{1,0:T(8,128)(2,1)} %slice.218), channel_id=1, source_target_pairs={{0,8},{1,9},{2,10},{3,11},{4,12},{5,13},{6,14},{7,15},{8,0},{9,1},... | collective-permute-start | bytes 1769480 | tf_op jit(solution)/shard_map/ppermute | solution.py:90
  330.0 44.7 %collective-permute-start.36 = (bf16[4,128,4608]{2,1,0:T(8,128)(2,1)}, bf16[4,128,4608]{2,1,0:T(8,128)(2,1)}, u32[]{:S(2)}, u32[]{:S(2)}) collective-permute-start(bf16[4,128,4608]{2,1,0:T(8,128)(2,1)} %bitcast.18), channel_id=1, source_target_pairs={{0,1},{1,0},{2,3},{3,2},{4,5},{5,4},{6,7},{7,6},{8,9},{9,8},{10,11... | collective-permute-start | bytes 14155784 | tf_op jit(solution)/shard_map/ppermute | solution.py:98
  337.4 37.3 %collective-permute-start.37 = (bf16[4,128,4608]{2,1,0:T(8,128)(2,1)}, bf16[4,128,4608]{2,1,0:T(8,128)(2,1)}, u32[]{:S(2)}, u32[]{:S(2)}) collective-permute-start(bf16[4,128,4608]{2,1,0:T(8,128)(2,1)} %bitcast.20), channel_id=1, source_target_pairs={{0,1},{1,0},{2,3},{3,2},{4,5},{5,4},{6,7},{7,6},{8,9},{9,8},{10,11... | collective-permute-start | bytes 14155784 | tf_op jit(solution)/shard_map/ppermute | solution.py:98
  346.4 27.2 %collective-permute-start.38 = (bf16[2,576,512]{2,1,0:T(8,128)(2,1)S(1)}, bf16[2,576,512]{2,1,0:T(8,128)(2,1)S(1)}, u32[]{:S(2)}, u32[]{:S(2)}) collective-permute-start(bf16[2,576,512]{2,1,0:T(8,128)(2,1)S(1)} %pad_maximum_fusion.6), channel_id=1, source_target_pairs={{0,8},{1,9},{2,10},{3,11},{4,12},{5,13},{6,14},{7,15},{8,0},{9,1},... | collective-permute-start | bytes 3538952 | tf_op jit(solution)/shard_map/ppermute | solution.py:90
  347.8 26.9 %collective-permute-start.39 = (bf16[2,576,512]{2,1,0:T(8,128)(2,1)S(1)}, bf16[2,576,512]{2,1,0:T(8,128)(2,1)S(1)}, u32[]{:S(2)}, u32[]{:S(2)}) collective-permute-start(bf16[2,576,512]{2,1,0:T(8,128)(2,1)S(1)} %pad_maximum_fusion.7), channel_id=1, source_target_pairs={{0,16},{1,17},{2,18},{3,19},{4,20},{5,21},{6,22},{7,23},{8,24},{9,... | collective-permute-start | bytes 3538952 | tf_op jit(solution)/shard_map/ppermute | solution.py:90
  377.9 35.6 %collective-permute-start.40 = (bf16[576,512]{1,0:T(8,128)(2,1)}, bf16[576,512]{1,0:T(8,128)(2,1)}, u32[]{:S(2)}, u32[]{:S(2)}) collective-permute-start(bf16[576,512]{1,0:T(8,128)(2,1)} %get-tuple-element.334), channel_id=1, source_target_pairs={{0,16},{1,17},{2,18},{3,19},{4,20},{5,21},{6,22},{7,23},{8,24},{9,... | collective-permute-start | bytes 1769480 | tf_op jit(solution)/shard_map/ppermute | solution.py:90
  378.6 34.9 %collective-permute-start.41 = (bf16[576,512]{1,0:T(8,128)(2,1)}, bf16[576,512]{1,0:T(8,128)(2,1)}, u32[]{:S(2)}, u32[]{:S(2)}) collective-permute-start(bf16[576,512]{1,0:T(8,128)(2,1)} %get-tuple-element.333), channel_id=1, source_target_pairs={{0,8},{1,9},{2,10},{3,11},{4,12},{5,13},{6,14},{7,15},{8,0},{9,1},... | collective-permute-start | bytes 1769480 | tf_op jit(solution)/shard_map/ppermute | solution.py:90
  382.4 59.1 %collective-permute-start.43 = (bf16[2,64,4608]{2,1,0:T(8,128)(2,1)}, bf16[2,64,4608]{2,1,0:T(8,128)(2,1)S(1)}, u32[]{:S(2)}, u32[]{:S(2)}) collective-permute-start(bf16[2,64,4608]{2,1,0:T(8,128)(2,1)} %pad_maximum_fusion.8), channel_id=1, source_target_pairs={{0,8},{1,9},{2,10},{3,11},{4,12},{5,13},{6,14},{7,15},{8,0},{9,1},... | collective-permute-start | bytes 3538952 | tf_op jit(solution)/shard_map/ppermute | solution.py:90
  384.5 57.0 %collective-permute-start.44 = (bf16[2,64,4608]{2,1,0:T(8,128)(2,1)}, bf16[2,64,4608]{2,1,0:T(8,128)(2,1)}, u32[]{:S(2)}, u32[]{:S(2)}) collective-permute-start(bf16[2,64,4608]{2,1,0:T(8,128)(2,1)} %pad_maximum_fusion.9), channel_id=1, source_target_pairs={{0,16},{1,17},{2,18},{3,19},{4,20},{5,21},{6,22},{7,23},{8,24},{9,... | collective-permute-start | bytes 3538952 | tf_op jit(solution)/shard_map/ppermute | solution.py:90
  422.6 19.0 %collective-permute-start.42 = (bf16[4,128,1024]{2,1,0:T(8,128)(2,1)S(1)}, bf16[4,128,1024]{2,1,0:T(8,128)(2,1)}, u32[]{:S(2)}, u32[]{:S(2)}) collective-permute-start(bf16[4,128,1024]{2,1,0:T(8,128)(2,1)S(1)} %bitcast.221), channel_id=1, source_target_pairs={{0,1},{1,0},{2,3},{3,2},{4,5},{5,4},{6,7},{7,6},{8,9},{9,8},{10,11... | collective-permute-start | bytes 3145736 | tf_op jit(solution)/shard_map/ppermute | solution.py:98
  427.9 13.6 %collective-permute-start.45 = (bf16[576,512]{1,0:T(8,128)(2,1)S(1)}, bf16[576,512]{1,0:T(8,128)(2,1)S(1)}, u32[]{:S(2)}, u32[]{:S(2)}) collective-permute-start(bf16[576,512]{1,0:T(8,128)(2,1)S(1)} %get-tuple-element.318), channel_id=1, source_target_pairs={{0,2},{1,3},{2,0},{3,1},{4,6},{5,7},{6,4},{7,5},{8,10},{9,11},{10,... | collective-permute-start | bytes 1769480 | tf_op jit(solution)/shard_map/ppermute | solution.py:98
  481.3 17.0 %collective-permute-start.46 = (bf16[64,4608]{1,0:T(8,128)(2,1)S(1)}, bf16[64,4608]{1,0:T(8,128)(2,1)S(1)}, u32[]{:S(2)}, u32[]{:S(2)}) collective-permute-start(bf16[64,4608]{1,0:T(8,128)(2,1)S(1)} %get-tuple-element.328), channel_id=1, source_target_pairs={{0,16},{1,17},{2,18},{3,19},{4,20},{5,21},{6,22},{7,23},{8,24},{9,... | collective-permute-start | bytes 1769480 | tf_op jit(solution)/shard_map/ppermute | solution.py:90
  488.4 23.9 %collective-permute-start.48 = (bf16[576,512]{1,0:T(8,128)(2,1)S(1)}, bf16[576,512]{1,0:T(8,128)(2,1)S(1)}, u32[]{:S(2)}, u32[]{:S(2)}) collective-permute-start(bf16[576,512]{1,0:T(8,128)(2,1)S(1)} %add_convert_fusion.22), channel_id=1, source_target_pairs={{0,4},{1,5},{2,6},{3,7},{4,0},{5,1},{6,2},{7,3},{8,12},{9,13},{10,... | collective-permute-start | bytes 1769480 | tf_op jit(solution)/shard_map/ppermute | solution.py:98
  494.4 72.3 %collective-permute-start.49 = (bf16[2,64,4608]{2,1,0:T(8,128)(2,1)}, bf16[2,64,4608]{2,1,0:T(8,128)(2,1)}, u32[]{:S(2)}, u32[]{:S(2)}) collective-permute-start(bf16[2,64,4608]{2,1,0:T(8,128)(2,1)} %pad_maximum_fusion.10), channel_id=1, source_target_pairs={{0,8},{1,9},{2,10},{3,11},{4,12},{5,13},{6,14},{7,15},{8,0},{9,1},... | collective-permute-start | bytes 3538952 | tf_op jit(solution)/shard_map/ppermute | solution.py:90
  496.2 70.4 %collective-permute-start.50 = (bf16[2,64,4608]{2,1,0:T(8,128)(2,1)}, bf16[2,64,4608]{2,1,0:T(8,128)(2,1)}, u32[]{:S(2)}, u32[]{:S(2)}) collective-permute-start(bf16[2,64,4608]{2,1,0:T(8,128)(2,1)} %pad_maximum_fusion.11), channel_id=1, source_target_pairs={{0,16},{1,17},{2,18},{3,19},{4,20},{5,21},{6,22},{7,23},{8,24},{9,... | collective-permute-start | bytes 3538952 | tf_op jit(solution)/shard_map/ppermute | solution.py:90
  536.6 26.5 %collective-permute-start.51 = (bf16[64,4608]{1,0:T(8,128)(2,1)}, bf16[64,4608]{1,0:T(8,128)(2,1)}, u32[]{:S(2)}, u32[]{:S(2)}) collective-permute-start(bf16[64,4608]{1,0:T(8,128)(2,1)} %get-tuple-element.315), channel_id=1, source_target_pairs={{0,2},{1,3},{2,0},{3,1},{4,6},{5,7},{6,4},{7,5},{8,10},{9,11},{10,... | collective-permute-start | bytes 1769480 | tf_op jit(solution)/shard_map/ppermute | solution.py:98
  549.2 17.4 %collective-permute-start.52 = (bf16[576,512]{1,0:T(8,128)(2,1)}, bf16[576,512]{1,0:T(8,128)(2,1)}, u32[]{:S(2)}, u32[]{:S(2)}) collective-permute-start(bf16[576,512]{1,0:T(8,128)(2,1)} %add_convert_fusion.15), channel_id=1, source_target_pairs={{0,2},{1,3},{2,0},{3,1},{4,6},{5,7},{6,4},{7,5},{8,10},{9,11},{10,... | collective-permute-start | bytes 1769480 | tf_op jit(solution)/shard_map/ppermute | solution.py:98
  582.8 48.1 %collective-permute-start.55 = (bf16[4,128,2176]{2,1,0:T(8,128)(2,1)}, bf16[4,128,2176]{2,1,0:T(8,128)(2,1)S(1)}, u32[]{:S(2)}, u32[]{:S(2)}) collective-permute-start(bf16[4,128,2176]{2,1,0:T(8,128)(2,1)} %pad_maximum_fusion.3), channel_id=1, source_target_pairs={{0,1},{1,0},{2,3},{3,2},{4,5},{5,4},{6,7},{7,6},{8,9},{9,8},{10,11... | collective-permute-start | bytes 6684680 | tf_op jit(solution)/shard_map/ppermute | solution.py:98
  586.0 15.0 %collective-permute-start.56 = (bf16[64,1024]{1,0:T(8,128)(2,1)S(1)}, bf16[64,1024]{1,0:T(8,128)(2,1)S(1)}, u32[]{:S(2)}, u32[]{:S(2)}) collective-permute-start(bf16[64,1024]{1,0:T(8,128)(2,1)S(1)} %get-tuple-element.362), channel_id=1, source_target_pairs={{0,16},{1,17},{2,18},{3,19},{4,20},{5,21},{6,22},{7,23},{8,24},{9,... | collective-permute-start | bytes 393224 | tf_op jit(solution)/shard_map/ppermute | solution.py:90
  586.9 28.9 %collective-permute-start.57 = (bf16[64,1024]{1,0:T(8,128)(2,1)S(1)}, bf16[64,1024]{1,0:T(8,128)(2,1)S(1)}, u32[]{:S(2)}, u32[]{:S(2)}) collective-permute-start(bf16[64,1024]{1,0:T(8,128)(2,1)S(1)} %get-tuple-element.361), channel_id=1, source_target_pairs={{0,8},{1,9},{2,10},{3,11},{4,12},{5,13},{6,14},{7,15},{8,0},{9,1},... | collective-permute-start | bytes 393224 | tf_op jit(solution)/shard_map/ppermute | solution.py:90
  589.7 26.1 %collective-permute-start.58 = (bf16[64,4608]{1,0:T(8,128)(2,1)S(1)}, bf16[64,4608]{1,0:T(8,128)(2,1)}, u32[]{:S(2)}, u32[]{:S(2)}) collective-permute-start(bf16[64,4608]{1,0:T(8,128)(2,1)S(1)} %get-tuple-element.322), channel_id=1, source_target_pairs={{0,16},{1,17},{2,18},{3,19},{4,20},{5,21},{6,22},{7,23},{8,24},{9,... | collective-permute-start | bytes 1769480 | tf_op jit(solution)/shard_map/ppermute | solution.py:90
  601.0 14.7 %collective-permute-start.59 = (bf16[64,4608]{1,0:T(8,128)(2,1)S(1)}, bf16[64,4608]{1,0:T(8,128)(2,1)S(1)}, u32[]{:S(2)}, u32[]{:S(2)}) collective-permute-start(bf16[64,4608]{1,0:T(8,128)(2,1)S(1)} %get-tuple-element.321), channel_id=1, source_target_pairs={{0,8},{1,9},{2,10},{3,11},{4,12},{5,13},{6,14},{7,15},{8,0},{9,1},... | collective-permute-start | bytes 1769480 | tf_op jit(solution)/shard_map/ppermute | solution.py:90
  602.3 28.6 %collective-permute-start.60 = (bf16[64,4608]{1,0:T(8,128)(2,1)S(1)}, bf16[64,4608]{1,0:T(8,128)(2,1)S(1)}, u32[]{:S(2)}, u32[]{:S(2)}) collective-permute-start(bf16[64,4608]{1,0:T(8,128)(2,1)S(1)} %add_convert_fusion.12), channel_id=1, source_target_pairs={{0,4},{1,5},{2,6},{3,7},{4,0},{5,1},{6,2},{7,3},{8,12},{9,13},{10,... | collective-permute-start | bytes 1769480 | tf_op jit(solution)/shard_map/ppermute | solution.py:98
  633.7 29.2 %collective-permute-start.61 = (bf16[64,4608]{1,0:T(8,128)(2,1)S(1)}, bf16[64,4608]{1,0:T(8,128)(2,1)S(1)}, u32[]{:S(2)}, u32[]{:S(2)}) collective-permute-start(bf16[64,4608]{1,0:T(8,128)(2,1)S(1)} %get-tuple-element.312), channel_id=1, source_target_pairs={{0,2},{1,3},{2,0},{3,1},{4,6},{5,7},{6,4},{7,5},{8,10},{9,11},{10,... | collective-permute-start | bytes 1769480 | tf_op jit(solution)/shard_map/ppermute | solution.py:98
  635.3 27.6 %collective-permute-start.62 = (bf16[64,4608]{1,0:T(8,128)(2,1)S(1)}, bf16[64,4608]{1,0:T(8,128)(2,1)S(1)}, u32[]{:S(2)}, u32[]{:S(2)}) collective-permute-start(bf16[64,4608]{1,0:T(8,128)(2,1)S(1)} %add_convert_fusion.9), channel_id=1, source_target_pairs={{0,2},{1,3},{2,0},{3,1},{4,6},{5,7},{6,4},{7,5},{8,10},{9,11},{10,... | collective-permute-start | bytes 1769480 | tf_op jit(solution)/shard_map/ppermute | solution.py:98
  637.3 25.6 %collective-permute-start.63 = (bf16[64,1024]{1,0:T(8,128)(2,1)}, bf16[64,1024]{1,0:T(8,128)(2,1)S(1)}, u32[]{:S(2)}, u32[]{:S(2)}) collective-permute-start(bf16[64,1024]{1,0:T(8,128)(2,1)} %get-tuple-element.309), channel_id=1, source_target_pairs={{0,2},{1,3},{2,0},{3,1},{4,6},{5,7},{6,4},{7,5},{8,10},{9,11},{10,... | collective-permute-start | bytes 393224 | tf_op jit(solution)/shard_map/ppermute | solution.py:98
  639.0 23.9 %collective-permute-start.64 = (bf16[2,64,2176]{2,1,0:T(8,128)(2,1)S(1)}, bf16[2,64,2176]{2,1,0:T(8,128)(2,1)S(1)}, u32[]{:S(2)}, u32[]{:S(2)}) collective-permute-start(bf16[2,64,2176]{2,1,0:T(8,128)(2,1)S(1)} %pad_maximum_fusion.20), channel_id=1, source_target_pairs={{0,8},{1,9},{2,10},{3,11},{4,12},{5,13},{6,14},{7,15},{8,0},{9,1},... | collective-permute-start | bytes 1671176 | tf_op jit(solution)/shard_map/ppermute | solution.py:90
  639.3 23.6 %collective-permute-start.65 = (bf16[2,64,2176]{2,1,0:T(8,128)(2,1)S(1)}, bf16[2,64,2176]{2,1,0:T(8,128)(2,1)S(1)}, u32[]{:S(2)}, u32[]{:S(2)}) collective-permute-start(bf16[2,64,2176]{2,1,0:T(8,128)(2,1)S(1)} %pad_maximum_fusion.21), channel_id=1, source_target_pairs={{0,16},{1,17},{2,18},{3,19},{4,20},{5,21},{6,22},{7,23},{8,24},{9,... | collective-permute-start | bytes 1671176 | tf_op jit(solution)/shard_map/ppermute | solution.py:90
  663.1 11.6 %collective-permute-start.66 = (bf16[64,2176]{1,0:T(8,128)(2,1)S(1)}, bf16[64,2176]{1,0:T(8,128)(2,1)S(1)}, u32[]{:S(2)}, u32[]{:S(2)}) collective-permute-start(bf16[64,2176]{1,0:T(8,128)(2,1)S(1)} %get-tuple-element.342), channel_id=1, source_target_pairs={{0,8},{1,9},{2,10},{3,11},{4,12},{5,13},{6,14},{7,15},{8,0},{9,1},... | collective-permute-start | bytes 835592 | tf_op jit(solution)/shard_map/ppermute | solution.py:90
  663.4 11.4 %collective-permute-start.67 = (bf16[64,2176]{1,0:T(8,128)(2,1)S(1)}, bf16[64,2176]{1,0:T(8,128)(2,1)S(1)}, u32[]{:S(2)}, u32[]{:S(2)}) collective-permute-start(bf16[64,2176]{1,0:T(8,128)(2,1)S(1)} %get-tuple-element.341), channel_id=1, source_target_pairs={{0,16},{1,17},{2,18},{3,19},{4,20},{5,21},{6,22},{7,23},{8,24},{9,... | collective-permute-start | bytes 835592 | tf_op jit(solution)/shard_map/ppermute | solution.py:90
  668.4 76.4 %collective-permute-start.75 = (bf16[128,4608]{1,0:T(8,128)(2,1)S(1)}, bf16[128,4608]{1,0:T(8,128)(2,1)S(1)}, u32[]{:S(2)}, u32[]{:S(2)}) collective-permute-start(bf16[128,4608]{1,0:T(8,128)(2,1)S(1)} %pad_maximum_fusion.12), channel_id=1, source_target_pairs={{0,1},{1,0},{2,3},{3,2},{4,5},{5,4},{6,7},{7,6},{8,9},{9,8},{10,11... | collective-permute-start | bytes 3538952 | tf_op jit(solution)/shard_map/ppermute | solution.py:98
  683.8 28.4 %collective-permute-start.69 = (bf16[64,2176]{1,0:T(8,128)(2,1)S(1)}, bf16[64,2176]{1,0:T(8,128)(2,1)S(1)}, u32[]{:S(2)}, u32[]{:S(2)}) collective-permute-start(bf16[64,2176]{1,0:T(8,128)(2,1)S(1)} %add_convert_fusion.41), channel_id=1, source_target_pairs={{0,4},{1,5},{2,6},{3,7},{4,0},{5,1},{6,2},{7,3},{8,12},{9,13},{10,... | collective-permute-start | bytes 835592 | tf_op jit(solution)/shard_map/ppermute | solution.py:98
  687.2 37.7 %collective-permute-start.76 = (bf16[64,4608]{1,0:T(8,128)(2,1)S(1)}, bf16[64,4608]{1,0:T(8,128)(2,1)S(1)}, u32[]{:S(2)}, u32[]{:S(2)}) collective-permute-start(bf16[64,4608]{1,0:T(8,128)(2,1)S(1)} %add_convert_fusion.8), channel_id=1, source_target_pairs={{0,4},{1,5},{2,6},{3,7},{4,0},{5,1},{6,2},{7,3},{8,12},{9,13},{10,... | collective-permute-start | bytes 1769480 | tf_op jit(solution)/shard_map/ppermute | solution.py:98
  712.3 19.1 %collective-permute-start.70 = (bf16[64,2176]{1,0:T(8,128)(2,1)S(1)}, bf16[64,2176]{1,0:T(8,128)(2,1)S(1)}, u32[]{:S(2)}, u32[]{:S(2)}) collective-permute-start(bf16[64,2176]{1,0:T(8,128)(2,1)S(1)} %add_convert_fusion.40), channel_id=1, source_target_pairs={{0,2},{1,3},{2,0},{3,1},{4,6},{5,7},{6,4},{7,5},{8,10},{9,11},{10,... | collective-permute-start | bytes 835592 | tf_op jit(solution)/shard_map/ppermute | solution.py:98
  725.1 18.9 %collective-permute-start.77 = (bf16[64,4608]{1,0:T(8,128)(2,1)S(1)}, bf16[64,4608]{1,0:T(8,128)(2,1)S(1)}, u32[]{:S(2)}, u32[]{:S(2)}) collective-permute-start(bf16[64,4608]{1,0:T(8,128)(2,1)S(1)} %add_convert_fusion.7), channel_id=1, source_target_pairs={{0,2},{1,3},{2,0},{3,1},{4,6},{5,7},{6,4},{7,5},{8,10},{9,11},{10,... | collective-permute-start | bytes 1769480 | tf_op jit(solution)/shard_map/ppermute | solution.py:98
  731.5 15.7 %collective-permute-start.71 = (bf16[128,2176]{1,0:T(8,128)(2,1)S(1)}, bf16[128,2176]{1,0:T(8,128)(2,1)S(1)}, u32[]{:S(2)}, u32[]{:S(2)}) collective-permute-start(bf16[128,2176]{1,0:T(8,128)(2,1)S(1)} %pad_maximum_fusion.22), channel_id=1, source_target_pairs={{0,1},{1,0},{2,3},{3,2},{4,5},{5,4},{6,7},{7,6},{8,9},{9,8},{10,11... | collective-permute-start | bytes 1671176 | tf_op jit(solution)/shard_map/ppermute | solution.py:98
  (146 other events, 1413.1 us)

commit v5 on v4

--- a/solution.py
+++ b/solution.py
@@ -14,6 +14,7 @@
 
 
 norm_eps = 1e-05
+TINY = pl.CostEstimate(flops=1, bytes_accessed=1, transcendentals=0)
 rope_base = 1000000.0
 
 
@@ -162,9 +163,7 @@
             ],
             out_specs=pl.BlockSpec((rows, width), lambda i, spot: (spot[i], 0)),
         ),
-        cost_estimate=pl.CostEstimate(
-            flops=0, bytes_accessed=4 * count * rows * width, transcendentals=0
-        ),
+        cost_estimate=TINY,
         compiler_params=pltpu.CompilerParams(vmem_limit_bytes=60 << 20),
         name="place_blocks",
     )(spots, blocks[0], *blocks)
@@ -173,11 +172,13 @@
 FF_TILE = 512
 
 
-def block_specs(count, rows):
-    return [
-        pl.BlockSpec((rows, FF_TILE), lambda i, spot, at=at: (at, i))
-        for at in (0, 1) + (0,) * (count - 2)
+def block_specs(count, rows, tiles):
+    own = [
+        pl.BlockSpec((rows, FF_TILE), lambda i, spot, at=at: (at, i)) for at in (0, 1)
     ]
+    gate = [pl.BlockSpec((rows, FF_TILE), lambda i, spot: (0, i))] * (count - 2)
+    up = [pl.BlockSpec((rows, FF_TILE), lambda i, spot: (0, i + tiles))] * (count - 2)
+    return own + gate + own + up
 
 
 def settle(spots_ref, refs, whole_ref):
@@ -204,12 +205,12 @@
         slope_ref[rows] = (up * (sig + act * (1.0 - sig))).astype(jnp.bfloat16)
 
 
-def ffn_forward(normed, gate, up):
+def ffn_forward(normed, gate, up, gathered):
     rows, depth = normed.shape
-    (gate_blocks, spots), (up_blocks, _) = gate, up
-    count = len(gate_blocks) + 1
-    hidden = gate_blocks[0].shape[1]
-    part = gate_blocks[1].shape[0]
+    blocks, spots = gathered
+    count = len(blocks) + 2
+    hidden = gate.shape[1]
+    part = gate.shape[0] // 2
     out = jax.ShapeDtypeStruct((rows, hidden), jnp.bfloat16)
     return pl.pallas_call(
         functools.partial(ffn_forward_kernel, count),
@@ -218,18 +219,14 @@
             num_scalar_prefetch=1,
             grid=(hidden // FF_TILE,),
             in_specs=[pl.BlockSpec((rows, depth), lambda i, spot: (0, 0))]
-            + block_specs(count, part) * 2,
+            + block_specs(count, part, hidden // FF_TILE),
             out_specs=[pl.BlockSpec((rows, FF_TILE), lambda i, spot: (0, i))] * 3,
             scratch_shapes=[pltpu.VMEM((depth, FF_TILE), jnp.bfloat16)] * 2,
         ),
-        cost_estimate=pl.CostEstimate(
-            flops=4 * rows * depth * hidden,
-            bytes_accessed=4 * depth * hidden + 6 * rows * hidden,
-            transcendentals=rows * hidden,
-        ),
+        cost_estimate=TINY,
         compiler_params=pltpu.CompilerParams(vmem_limit_bytes=60 << 20),
         name="ffn_forward",
-    )(spots, normed, gate_blocks[0], *gate_blocks, up_blocks[0], *up_blocks)
+    )(spots, normed, gate, gate, *blocks, up, up, *blocks)
 
 
 def ffn_inner_kernel(g_ref, down_ref, act_ref, slope_ref, dgate_ref, dup_ref):
@@ -257,11 +254,7 @@
             tile,
         ],
         out_specs=[tile, tile],
-        cost_estimate=pl.CostEstimate(
-            flops=2 * rows * depth * hidden,
-            bytes_accessed=2 * depth * hidden + 8 * rows * hidden,
-            transcendentals=0,
-        ),
+        cost_estimate=TINY,
         compiler_params=pltpu.CompilerParams(vmem_limit_bytes=60 << 20),
         name="ffn_inner",
     )(grad_low, down, act, slope)
@@ -285,11 +278,11 @@
         )
 
 
-def ffn_input(grad_gate, grad_up, gate, up):
+def ffn_input(grad_gate, grad_up, gate, up, gathered):
     rows, hidden = grad_gate.shape
-    (gate_blocks, spots), (up_blocks, _) = gate, up
-    count = len(gate_blocks) + 1
-    part = gate_blocks[1].shape[0]
+    blocks, spots = gathered
+    count = len(blocks) + 2
+    part = gate.shape[0] // 2
     depth = count * part
     tile = pl.BlockSpec((rows, FF_TILE), lambda i, spot: (0, i))
     return pl.pallas_call(
@@ -298,21 +291,17 @@
         grid_spec=pltpu.PrefetchScalarGridSpec(
             num_scalar_prefetch=1,
             grid=(hidden // FF_TILE,),
-            in_specs=[tile, tile] + block_specs(count, part) * 2,
+            in_specs=[tile, tile] + block_specs(count, part, hidden // FF_TILE),
             out_specs=pl.BlockSpec((rows, depth), lambda i, spot: (0, 0)),
             scratch_shapes=[pltpu.VMEM((depth, FF_TILE), jnp.bfloat16)] * 2,
         ),
-        cost_estimate=pl.CostEstimate(
-            flops=4 * rows * depth * hidden,
-            bytes_accessed=4 * depth * hidden + 4 * rows * hidden,
-            transcendentals=0,
-        ),
+        cost_estimate=TINY,
         compiler_params=pltpu.CompilerParams(vmem_limit_bytes=60 << 20),
         name="ffn_input",
-    )(spots, grad_gate, grad_up, gate_blocks[0], *gate_blocks, up_blocks[0], *up_blocks)
-
-
-def gather_steps(links, mine, whole):
+    )(spots, grad_gate, grad_up, gate, gate, *blocks, up, up, *blocks)
+
+
+def gather_steps(links, mine, whole, late=False):
     shard_size, rep_size, shard_swap, rep_swap = links
     me = lax.axis_index("shard")
     core = lax.rem(lax.axis_index("rep"), 2)
@@ -325,14 +314,17 @@
         pieces[1], pieces[2] = yield (pieces[1], pieces[2])
         corner_a = shard_swap(pieces[1][:quarter], 2)
         corner_b = shard_swap(pieces[2][quarter:], 1)
-        others[1] = rep_swap(pieces[1], 1)
-        others[2] = rep_swap(pieces[2], 1)
-        corner_a, corner_b, others[1], others[2] = yield (
-            corner_a, corner_b, others[1], others[2]
-        )
+        if late:
+            early, waiting = (), (1, 2, 3)
+            corner_a, corner_b, pieces[1], pieces[2] = yield (
+                corner_a, corner_b, pieces[1], pieces[2]
+            )
+        else:
+            early, waiting = (rep_swap(pieces[1], 1), rep_swap(pieces[2], 1)), (3,)
+            corner_a, corner_b, *early = yield (corner_a, corner_b, *early)
         pieces[3] = jnp.concatenate([corner_a, corner_b], axis=0)
-        others[3] = rep_swap(pieces[3], 1)
-        (others[3],) = yield (others[3],)
+        rest = yield tuple(rep_swap(pieces[d], 1) for d in waiting)
+        others = dict(zip((1, 2, 3), (*early, *rest)))
     else:
         pieces[0] = mine
         bit = 1
@@ -345,7 +337,7 @@
             bit *= 2
         del pieces[0]
         others = {d: rep_swap(piece, 1) for d, piece in pieces.items()}
-    blocks, spots = [whole], [2 * me, 2 * me + 1]
+    blocks, spots = [whole] if whole is not None else [], [2 * me, 2 * me + 1]
     for d in pieces:
         blocks += [pieces[d], others[d]]
         spots += [2 * (me ^ d) + core, 2 * (me ^ d) + 1 - core]
@@ -611,11 +603,7 @@
             out_specs=pl.BlockSpec((BLOCK, 4 * HD), lambda p, i, live: (i, p)),
             scratch_shapes=[pltpu.VMEM((4, BLOCK, 2 * HD), jnp.float32)],
         ),
-        cost_estimate=pl.CostEstimate(
-            flops=24 * rows * BLOCK * LOOK * HQ * HD,
-            bytes_accessed=8 * rows * HQ * HD,
-            transcendentals=rows * BLOCK * LOOK * HQ,
-        ),
+        cost_estimate=TINY,
         name="attend",
     )(live_blocks(segment), query, key, value, segment[:, None], segment[None, :])
 
@@ -654,11 +642,7 @@
                 pltpu.VMEM((4 * HD, BLOCK), jnp.float32),
             ],
         ),
-        cost_estimate=pl.CostEstimate(
-            flops=160 * rows * BLOCK * LOOK * HD * panels,
-            bytes_accessed=64 * rows * HD * panels,
-            transcendentals=4 * rows * BLOCK * LOOK * panels,
-        ),
+        cost_estimate=TINY,
         name="attend_back",
     )(live_blocks(segment), query, grad_out, key, value, segment[:, None], segment[None, :])
 
@@ -697,9 +681,9 @@
     w_out, w_gate, w_up, w_down = sync((w_out, w_gate, w_up, w_down), front_flow)
     out_flow = Flow(gather_steps(links, core_half(w_out), w_out))
     w_gate, w_up, w_down = sync((w_gate, w_up, w_down), front_flow, out_flow)
-    gate_flow = Flow(gather_steps(links, core_half(w_gate), w_gate))
-    w_up, w_down = sync((w_up, w_down), front_flow)
-    up_flow = Flow(gather_steps(links, core_half(w_up), w_up))
+    pair = jnp.concatenate([core_half(w_gate), core_half(w_up)], axis=1)
+    pair_flow = Flow(gather_steps(links, pair, None, late=True))
+    w_down = sync(w_down, front_flow)
     front = place_blocks(front_flow.finish())
     full_query = front[:, : HQ * HD]
     full_key = front[:, HQ * HD : (HQ + HK) * HD]
@@ -736,7 +720,7 @@
     key_rot = key_rot.reshape(row_count, HK * HD)
     value_low = value_low.reshape(row_count, HK * HD)
     query_rot, key_rot, value_low, w_down = sync(
-        (query_rot, key_rot, value_low, w_down), out_flow, gate_flow, up_flow
+        (query_rot, key_rot, value_low, w_down), out_flow, pair_flow
     )
     down_flow = Flow(gather_steps(links, core_half(w_down), w_down))
     attn_low = attend(query_rot, key_rot, value_low, segment)
@@ -745,11 +729,10 @@
     hidden = inputs + matmul_plain(attn_low, full_out)
     scale_two = inv_rms(hidden)
     normed_ffn = (hidden * scale_two * full_ffn_gain.astype(jnp.float32)).astype(jnp.bfloat16)
-    normed_ffn, hidden = sync((normed_ffn, hidden), gate_flow, up_flow)
-    normed_ffn = sync(normed_ffn, gate_flow, up_flow, down_flow)
-    full_gate = gate_flow.finish()
-    full_up = up_flow.finish()
-    mixed_act, act_low, slope = ffn_forward(normed_ffn, full_gate, full_up)
+    normed_ffn, hidden = sync((normed_ffn, hidden), pair_flow)
+    normed_ffn = sync(normed_ffn, pair_flow, down_flow)
+    pair = pair_flow.finish()
+    mixed_act, act_low, slope = ffn_forward(normed_ffn, w_gate, w_up, pair)
     mixed_act, slope, act_low = sync((mixed_act, slope, act_low), down_flow)
     mixed_act, slope, act_low = sync((mixed_act, slope, act_low), down_flow)
     full_down = place_blocks(down_flow.finish())
@@ -767,8 +750,9 @@
     def hand(product):
         return rep_swap(blocked(links, product).astype(jnp.bfloat16), 1)
 
-    down_sent = hand(matmul_rows(mixed_act, out_other))
-    gate_given = matmul_rows(normed_other, pin(grad_gate_low, down_sent)).astype(jnp.bfloat16)
+    down_given = matmul_rows(mixed_act, out_other).astype(jnp.bfloat16)
+    down_sent = hand(down_given)
+    gate_given = matmul_rows(normed_other, pin(grad_gate_low, down_given)).astype(jnp.bfloat16)
     gate_sent = hand(gate_given)
     down_sent, mixed_act, grad_up_low, gate_given = pin(
         (down_sent, mixed_act, grad_up_low, gate_given)
@@ -785,7 +769,7 @@
         (gate_given, gate_sent, up_given, up_sent, grad_gate_low, grad_up_low), down_back
     )
     gate_back = Flow(scatter_steps(links, gate_given, gate_sent))
-    grad_normed_ffn = ffn_input(grad_gate_low, grad_up_low, full_gate, full_up)
+    grad_normed_ffn = ffn_input(grad_gate_low, grad_up_low, w_gate, w_up, pair)
     grad_normed_ffn, up_given, up_sent = sync((grad_normed_ffn, up_given, up_sent), down_back)
     grad_ffn_gain = jnp.sum(grad_normed_ffn * hidden * scale_two, axis=0)
     grad_hidden = out_grad + norm_back(
@@ -805,7 +789,7 @@
     grad_attn_low, lower = pin((grad_attn_low, lower))
     upper = attend_back(query_rot, grad_attn_low, key_rot, value_low, segment, panels, panels)
     lower, upper, out_given, out_sent = sync(
-        (lower, upper, out_given, out_sent), gate_back, down_back
+        (lower, upper, out_given, out_sent), gate_back, down_back, up_back
     )
     out_back = Flow(scatter_steps(links, out_given, out_sent))
     grad_query_rot, grad_key_rot, grad_value = (

time: 761 us -> 705 us (0.926)
  waiting for transfers between devices: 204 us -> 159 us
  starting transfers between devices: 94.6 us -> 82.5 us
    ppermute x40 -> x37, waiting for transfers between devices: 117 us -> 71.5 us  [rep_swap(): return lax.ppermute(value, axes, pairs)]
    ppermute x40 -> x37, starting transfers between devices: 52.1 us -> 37.5 us  [rep_swap(): return lax.ppermute(value, axes, pairs)]
    unnamed x266 -> x247, local copies, waits for them, and re-layouts: 6.43 us -> 14.9 us
    ppermute x40 -> x36, starting transfers between devices: 42.5 us -> 45 us  [shard_swap(): return lax.ppermute(value, axes, pairs)]
    ppermute x40 -> x36, waiting for transfers between devices: 87.1 us -> 87.5 us  [shard_swap(): return lax.ppermute(value, axes, pairs)]
  transfers between devices with their start and end apart: 80 -> 73, of which waited for: 27 -> 20; matrix products, arithmetic and copies ran while one was open for 29% -> 30% of each run, Pallas kernels for 12% -> 19%
where the time goes in v5:
time: 705 us; the launch traced here: 701 us
  Pallas kernels  165 us (23%)
  waiting for transfers between devices  159 us (23%)
  other arithmetic  119 us (17%)
  matrix products  104 us (15%)
  starting transfers between devices  82.5 us (12%)
  local copies, waits for them, and re-layouts  69.1 us (10%)
    ppermute x36, waiting for transfers between devices, shard_swap(): return lax.ppermute(value, axes, pairs)  87.5 us
    ppermute x37, waiting for transfers between devices, rep_swap(): return lax.ppermute(value, axes, pairs)  71.5 us
    dot_general x10, matrix products, matmul_rows(): lax.dot_general(left_mat, right_mat, (((0,), (0,)), ((), ())), preferred_...  63 us
    ppermute x36, starting transfers between devices, shard_swap(): return lax.ppermute(value, axes, pairs)  45 us
    pallas_call x2, Pallas kernels, attend_back(): pl.pallas_call(attend_back_kernel, out_shape=(jax.ShapeDtypeStruct((rows,...  37.5 us
    ppermute x37, starting transfers between devices, rep_swap(): return lax.ppermute(value, axes, pairs)  37.5 us
    pallas_call x1, Pallas kernels, ffn_forward(): pl.pallas_call(functools.partial(ffn_forward_kernel, count), out_shape=(o...  28.8 us
    pallas_call x1, Pallas kernels, ffn_input(): pl.pallas_call(functools.partial(ffn_input_kernel, count), out_shape=jax....  28.5 us
  transfers between devices with their start and end apart: 73, of which 20 were waited for; matrix products, arithmetic and copies ran while one was open for 30% of the time, Pallas kernels for 19%

profile of v5, /device:TPU:1, one launch (start us, length us, event | category | flops | bytes accessed | tf_op | source)
XLA Modules:
  0.0 701.3 jit_solution(2002700492094073414)
XLA Ops:
  11.0 9.6 %collective-permute-done.refs_2_ = bf16[128,2176]{1,0:T(8,128)(2,1)S(1)} collective-permute-done((bf16[128,2176]{1,0:T(8,128)(2,1)S(1)}, bf16[128,2176]{1,0:T(8,128)(2,1)S(1)}, u32[]{:S(2)}, u32[]{:S(2)}) %collective-permute-start) | collective-permute-done | bytes 557088 | tf_op jit(solution)/shard_map/ppermute | solution.py:91
  31.3 3.4 collective-permute-done.7.refs_4_
  34.7 6.0 collective-permute-done.2
  54.5 6.9 place_blocks.3
  65.1 4.4 multiply_reduce_fusion.4
  69.5 2.7 multiply_reduce_fusion.6
  83.6 24.0 %collective-permute-done.9 = bf16[64,1024]{1,0:T(8,128)(2,1)S(1)} collective-permute-done((bf16[64,1024]{1,0:T(8,128)(2,1)}, bf16[64,1024]{1,0:T(8,128)(2,1)S(1)}, u32[]{:S(2)}, u32[]{:S(2)}) %collective-permute-start.9) | collective-permute-done | bytes 131104 | tf_op jit(solution)/shard_map/ppermute | solution.py:91
  108.4 3.1 collective-permute-done.10
  113.0 2.4 collective-permute-start.15
  118.4 3.9 copy.101.q_ref
  128.6 23.2 %attend.1 = bf16[1024,1024]{1,0:T(8,128)(2,1)} custom-call(s32[4,4]{1,0:T(4,128)} %fusion.87.live_ref, bf16[1024,1024]{1,0:T(8,128)(2,1)} %copy.101.q_ref, bf16[1024,512]{1,0:T(8,128)(2,1)} %copy.102.k_ref, bf16[1024,512]{1,0:T(8,128)(2,1)} %convolution_convert_fusion.11.v_ref, s32[1024,1]{1,0:T(8,128)} %copy.103.seg_col_ref, s32[1,1024]{1,0:T(1,128)} %bitcast.222), custom_call_target="tpu_custom_call" | custom-call | flops 1 | bytes 1 | tf_op jit(solution)/shard_map/attend/pallas_call | solution.py:590
  151.8 5.5 place_blocks.4
  157.4 5.3 multiply_reduce_fusion.3
  172.2 7.1 %collective-permute-start.21 = (bf16[576,1024]{1,0:T(8,128)(2,1)S(1)}, bf16[576,1024]{1,0:T(8,128)(2,1)}, u32[]{:S(2)}, u32[]{:S(2)}) collective-permute-start(bf16[576,1024]{1,0:T(8,128)(2,1)S(1)} %constant_dynamic-slice_fusion.26), channel_id=1, source_target_pairs={{0,8},{1,9},{2,10},{3,11},{4,12},{5,13},{6,14},{7,15},{8,0},{9,1},... | collective-permute-start | bytes 3538952 | tf_op jit(solution)/shard_map/ppermute | solution.py:91
  179.3 26.4 %collective-permute-done.21.refs_2_ = bf16[576,1024]{1,0:T(8,128)(2,1)} collective-permute-done((bf16[576,1024]{1,0:T(8,128)(2,1)S(1)}, bf16[576,1024]{1,0:T(8,128)(2,1)}, u32[]{:S(2)}, u32[]{:S(2)}) %collective-permute-start.21) | collective-permute-done | bytes 1179680 | tf_op jit(solution)/shard_map/ppermute | solution.py:91
  211.9 28.8 %ffn_forward.1 = (bf16[1024,4608]{1,0:T(8,128)(2,1)}, bf16[1024,4608]{1,0:T(8,128)(2,1)}, bf16[1024,4608]{1,0:T(8,128)(2,1)}) custom-call(s32[8]{0:T(128)} %stack.60.spots_ref, bf16[1024,1024]{1,0:T(8,128)(2,1)} %multiply_convert_fusion.a_ref, bf16[256,4608]{1,0:T(8,128)(2,1)} %refs_1_.3, bf16[256,4608]{1,0:T(8,128)(2,1)} %refs_1_.3, ...), custom_call_target="tpu_custom_call" | custom-call | flops 1 | bytes 1 | tf_op jit(solution)/shard_map/ffn_forward/pallas_call | solution.py:215
  248.1 9.3 %place_blocks.5.down_ref = bf16[4608,1024]{1,0:T(8,128)(2,1)} custom-call(s32[8]{0:T(128)} %stack.60.spots_ref, bf16[1152,1024]{1,0:T(8,128)(2,1)} %refs_1_.2, bf16[1152,1024]{1,0:T(8,128)(2,1)} %refs_1_.2, bf16[576,1024]{1,0:T(8,128)(2,1)} %collective-permute-done.21.refs_2_, bf16[576,1024]{1,0:T(8,128)(2,1)} %copy-done.35, ...), custom_call_target="tpu_custom_call" | custom-call | flops 1 | bytes 1 | tf_op jit(solution)/shard_map/place_blocks/pallas_call | solution.py:154
  257.5 24.8 %ffn_inner.1 = (bf16[1024,4608]{1,0:T(8,128)(2,1)}, bf16[1024,4608]{1,0:T(8,128)(2,1)}) custom-call(bf16[1024,1024]{1,0:T(8,128)(2,1)} %copy-done.11, bf16[4608,1024]{1,0:T(8,128)(2,1)} %place_blocks.5.down_ref, bf16[1024,4608]{1,0:T(8,128)(2,1)} %get-tuple-element.200.act_ref, bf16[1024,4608]{1,0:T(8,128)(2,1)} %get-tuple-element.201.slope_ref), custom_call_target="tpu_custom_call" | custom-call | flops 1 | bytes 1 | tf_op jit(solution)/shard_map/ffn_inner/pallas_call | solution.py:246
  282.3 11.0 %convolution_convert_fusion.1 = bf16[4608,512]{1,0:T(8,128)(2,1)} fusion(bf16[1024,4608]{1,0:T(8,128)(2,1)} %get-tuple-element.271, bf16[1024,512]{1,0:T(8,128)(2,1)S(1)} %copy-done.48), kind=kOutput, calls=%fused_computation.7 | convolution fusion | flops 4834197504 | bytes 15204352 | tf_op jit(solution)/shard_map/dot_general | solution.py:70
  294.6 10.9 %convolution_convert_fusion.5 = bf16[512,4608]{1,0:T(8,128)(2,1)} fusion(bf16[1024,4608]{1,0:T(8,128)(2,1)} %get-tuple-element.220.dgate_ref, bf16[1024,128]{1,0:T(8,128)(2,1)S(1)} %get-tuple-element.379, bf16[1024,128]{1,0:T(8,128)(2,1)S(1)} %get-tuple-element.380, bf16[1024,128]{1,0:T(8,128)(2,1)S(1)} %get-tuple-element.381, ...), kind=kOutput, calls=%fused_computation.11 | convolution fusion | flops 4838391808 | bytes 15204352 | tf_op jit(solution)/shard_map/dot_general | solution.py:70
  305.7 6.9 convolution_convert_fusion
  312.6 6.9 convolution_convert_fusion.2
  321.5 3.0 add_convert_fusion.34
  327.7 11.3 %convolution_convert_fusion.3 = bf16[512,4608]{1,0:T(8,128)(2,1)} fusion(bf16[1024,512]{1,0:T(8,128)(2,1)S(1)} %pad_maximum_fusion.19, bf16[1024,4608]{1,0:T(8,128)(2,1)} %get-tuple-element.221.dup_ref), kind=kOutput, calls=%fused_computation.9 | convolution fusion | flops 4834197504 | bytes 15204352 | tf_op jit(solution)/shard_map/dot_general | solution.py:70
  339.0 5.4 convolution_convert_fusion.4
  344.5 7.8 %collective-permute-done.31 = bf16[2,576,512]{2,1,0:T(8,128)(2,1)S(1)} collective-permute-done((bf16[2,576,512]{2,1,0:T(8,128)(2,1)S(1)}, bf16[2,576,512]{2,1,0:T(8,128)(2,1)S(1)}, u32[]{:S(2)}, u32[]{:S(2)}) %collective-permute-start.31) | collective-permute-done | bytes 1179680 | tf_op jit(solution)/shard_map/ppermute | solution.py:91
  353.5 3.4 fusion.69
  364.2 28.5 %ffn_input.1 = f32[1024,1024]{1,0:T(8,128)} custom-call(s32[8]{0:T(128)} %stack.60.spots_ref, bf16[1024,4608]{1,0:T(8,128)(2,1)} %get-tuple-element.220.dgate_ref, bf16[1024,4608]{1,0:T(8,128)(2,1)} %get-tuple-element.221.dup_ref, bf16[256,4608]{1,0:T(8,128)(2,1)} %refs_1_.3, bf16[256,4608]{1,0:T(8,128)(2,1)} %refs_1_.3, bf16[128,9216]{1,0:T(8,128)(2,1)} %copy-done.1, ...), custom_call_target="tpu_custom_call" | custom-call | flops 1 | bytes 1 | tf_op jit(solution)/shard_map/ffn_input/pallas_call | solution.py:288
  392.7 5.2 multiply_reduce_fusion
  404.3 2.7 broadcast_select_fusion.8
  410.6 3.7 convolution_convert_fusion.8.do_ref
  414.3 5.8 collective-permute-done.38
  420.2 2.9 add_convert_fusion.19
  426.9 3.3 fusion.71
  432.0 2.6 collective-permute-start.41
  436.9 18.5 %attend_back.2 = (f32[1024,512]{1,0:T(8,128)}, f32[1024,256]{1,0:T(8,128)}, f32[1024,256]{1,0:T(8,128)}) custom-call(s32[4,4]{1,0:T(4,128)} %fusion.87.live_ref, bf16[1024,1024]{1,0:T(8,128)(2,1)} %copy.101.q_ref, bf16[1024,1024]{1,0:T(8,128)(2,1)} %convolution_convert_fusion.8.do_ref, bf16[1024,512]{1,0:T(8,128)(2,1)} %copy.102.k_ref, ...), custom_call_target="tpu_custom_call" | custom-call | flops 1 | bytes 1 | tf_op jit(solution)/shard_map/attend_back/pallas_call | solution.py:614
  455.4 19.0 %attend_back.3 = (f32[1024,512]{1,0:T(8,128)}, f32[1024,256]{1,0:T(8,128)}, f32[1024,256]{1,0:T(8,128)}) custom-call(s32[4,4]{1,0:T(4,128)} %fusion.87.live_ref, bf16[1024,1024]{1,0:T(8,128)(2,1)} %copy.101.q_ref, bf16[1024,1024]{1,0:T(8,128)(2,1)} %convolution_convert_fusion.8.do_ref, bf16[1024,512]{1,0:T(8,128)(2,1)} %copy.102.k_ref, ...), custom_call_target="tpu_custom_call" | custom-call | flops 1 | bytes 1 | tf_op jit(solution)/shard_map/attend_back/pallas_call | solution.py:614
  487.0 2.9 copy.112
  489.9 2.9 copy.111
  492.8 2.7 maximum_multiply_fusion
  497.7 3.1 multiply_reduce_fusion.1
  501.4 3.5 fusion.73
  504.9 9.8 %collective-permute-start.44 = (bf16[64,4608]{1,0:T(8,128)(2,1)}, bf16[64,4608]{1,0:T(8,128)(2,1)}, u32[]{:S(2)}, u32[]{:S(2)}) collective-permute-start(bf16[64,4608]{1,0:T(8,128)(2,1)} %get-tuple-element.312), channel_id=1, source_target_pairs={{0,16},{1,17},{2,18},{3,19},{4,20},{5,21},{6,22},{7,23},{8,24},{9,... | collective-permute-start | bytes 1769480 | tf_op jit(solution)/shard_map/ppermute | solution.py:91
  514.7 3.9 broadcast_select_fusion.5
  525.1 4.6 fusion.2
  529.9 4.2 collective-permute-done.48
  534.1 6.7 pad_maximum_fusion.1
  543.2 4.0 fusion.20
  548.9 4.2 fusion.11
  554.0 4.6 convolution_convert_fusion.6
  558.9 4.3 collective-permute-start.50
  566.5 3.1 broadcast_select_fusion.4
  576.1 2.4 convolution_convert_fusion.7
  582.4 10.5 %fusion.16 = f32[1152,1024]{1,0:T(8,128)} fusion(bf16[1152,512]{1,0:T(8,128)(2,1)S(1)} %collective-permute-done.72, bf16[576,512]{1,0:T(8,128)(2,1)S(1)} %get-tuple-element.386, bf16[576,512]{1,0:T(8,128)(2,1)S(1)} %get-tuple-element.385, pred[]{:T(512)S(6)} %eq.38), kind=kLoop, calls=%fused_computation.59 | loop fusion | flops 16515072 | bytes 7077889 | tf_op jit(solution)/shard_map/convert_element_type | solution.py:451
  593.0 16.0 %collective-permute-done.54 = bf16[64,4608]{1,0:T(8,128)(2,1)S(1)} collective-permute-done((bf16[64,4608]{1,0:T(8,128)(2,1)S(1)}, bf16[64,4608]{1,0:T(8,128)(2,1)S(1)}, u32[]{:S(2)}, u32[]{:S(2)}) %collective-permute-start.54) | collective-permute-done | bytes 589856 | tf_op jit(solution)/shard_map/ppermute | solution.py:99
  615.1 13.1 %add_multiply_fusion = bf16[1024,1024]{1,0:T(8,128)(2,1)} fusion(f32[1024,1024]{1,0:T(8,128)S(1)} %copy-done.5, f32[1024]{0:T(1024)S(1)} %compare_convert_fusion, bf16[1024,4608]{1,0:T(8,128)(2,1)} %get-tuple-element.271, bf16[4608,1024]{1,0:T(8,128)(2,1)S(1)} %bitcast.190), kind=kOutput, calls=%fused_computation.33 | convolution fusion | flops 9666822144 | bytes 25169920 | tf_op jit(solution)/shard_map/dot_general | solution.py:66
  628.2 10.2 %collective-permute-done.57 = bf16[64,1024]{1,0:T(8,128)(2,1)S(1)} collective-permute-done((bf16[64,1024]{1,0:T(8,128)(2,1)S(1)}, bf16[64,1024]{1,0:T(8,128)(2,1)S(1)}, u32[]{:S(2)}, u32[]{:S(2)}) %collective-permute-start.57) | collective-permute-done | bytes 131104 | tf_op jit(solution)/shard_map/ppermute | solution.py:99
  642.2 6.6 collective-permute-done.66
  652.8 2.8 collective-permute-start.68
  658.7 5.5 collective-permute-done.62
  665.1 17.8 %collective-permute-done.70 = bf16[64,4608]{1,0:T(8,128)(2,1)S(1)} collective-permute-done((bf16[64,4608]{1,0:T(8,128)(2,1)S(1)}, bf16[64,4608]{1,0:T(8,128)(2,1)S(1)}, u32[]{:S(2)}, u32[]{:S(2)}) %collective-permute-start.70) | collective-permute-done | bytes 589856 | tf_op jit(solution)/shard_map/ppermute | solution.py:99
  684.7 5.8 collective-permute-done.64
  692.3 2.4 fusion.14
  698.6 2.4 fusion.15
  (524 shorter events, 182.8 us)
Async XLA Ops:
  6.0 14.6 %collective-permute-start = (bf16[128,2176]{1,0:T(8,128)(2,1)S(1)}, bf16[128,2176]{1,0:T(8,128)(2,1)S(1)}, u32[]{:S(2)}, u32[]{:S(2)}) collective-permute-start(bf16[128,2176]{1,0:T(8,128)(2,1)S(1)} %pad_maximum_fusion.20), channel_id=1, source_target_pairs={{0,8},{1,9},{2,10},{3,11},{4,12},{5,13},{6,14},{7,15},{8,0},{9,1},... | collective-permute-start | bytes 1671176 | tf_op jit(solution)/shard_map/ppermute | solution.py:91
  8.1 13.3 %collective-permute-start.1 = (bf16[128,2176]{1,0:T(8,128)(2,1)S(1)}, bf16[128,2176]{1,0:T(8,128)(2,1)}, u32[]{:S(2)}, u32[]{:S(2)}) collective-permute-start(bf16[128,2176]{1,0:T(8,128)(2,1)S(1)} %pad_maximum_fusion.20), channel_id=1, source_target_pairs={{0,16},{1,17},{2,18},{3,19},{4,20},{5,21},{6,22},{7,23},{8,24},{9,... | collective-permute-start | bytes 1671176 | tf_op jit(solution)/shard_map/ppermute | solution.py:91
  22.5 18.2 %collective-permute-start.4 = (bf16[128,2176]{1,0:T(8,128)(2,1)S(1)}, bf16[128,2176]{1,0:T(8,128)(2,1)}, u32[]{:S(2)}, u32[]{:S(2)}) collective-permute-start(bf16[128,2176]{1,0:T(8,128)(2,1)S(1)} %collective-permute-done.refs_2_), channel_id=1, source_target_pairs={{0,1},{1,0},{2,3},{3,2},{4,5},{5,4},{6,7},{7,6},{8,9},{9,8},{10,11... | collective-permute-start | bytes 1671176 | tf_op jit(solution)/shard_map/ppermute | solution.py:99
  24.3 16.4 %collective-permute-start.5 = (bf16[128,2176]{1,0:T(8,128)(2,1)}, bf16[128,2176]{1,0:T(8,128)(2,1)}, u32[]{:S(2)}, u32[]{:S(2)}) collective-permute-start(bf16[128,2176]{1,0:T(8,128)(2,1)} %collective-permute-done.1.refs_4_), channel_id=1, source_target_pairs={{0,1},{1,0},{2,3},{3,2},{4,5},{5,4},{6,7},{7,6},{8,9},{9,8},{10,11... | collective-permute-start | bytes 1671176 | tf_op jit(solution)/shard_map/ppermute | solution.py:99
  27.3 7.5 %collective-permute-start.7 = (bf16[128,1024]{1,0:T(8,128)(2,1)S(1)}, bf16[128,1024]{1,0:T(8,128)(2,1)}, u32[]{:S(2)}, u32[]{:S(2)}) collective-permute-start(bf16[128,1024]{1,0:T(8,128)(2,1)S(1)} %constant_dynamic-slice_fusion.29), channel_id=1, source_target_pairs={{0,16},{1,17},{2,18},{3,19},{4,20},{5,21},{6,22},{7,23},{8,24},{9,... | collective-permute-start | bytes 786440 | tf_op jit(solution)/shard_map/ppermute | solution.py:91
  28.7 12.0 %collective-permute-start.2 = (bf16[64,2176]{1,0:T(8,128)(2,1)}, bf16[64,2176]{1,0:T(8,128)(2,1)}, u32[]{:S(2)}, u32[]{:S(2)}) collective-permute-start(bf16[64,2176]{1,0:T(8,128)(2,1)} %slice.188), channel_id=1, source_target_pairs={{0,16},{1,17},{2,18},{3,19},{4,20},{5,21},{6,22},{7,23},{8,24},{9,... | collective-permute-start | bytes 835592 | tf_op jit(solution)/shard_map/ppermute | solution.py:91
  28.7 12.0 %collective-permute-start.3 = (bf16[64,2176]{1,0:T(8,128)(2,1)}, bf16[64,2176]{1,0:T(8,128)(2,1)}, u32[]{:S(2)}, u32[]{:S(2)}) collective-permute-start(bf16[64,2176]{1,0:T(8,128)(2,1)} %slice.189), channel_id=1, source_target_pairs={{0,8},{1,9},{2,10},{3,11},{4,12},{5,13},{6,14},{7,15},{8,0},{9,1},... | collective-permute-start | bytes 835592 | tf_op jit(solution)/shard_map/ppermute | solution.py:91
  42.3 69.2 %collective-permute-start.11 = (bf16[128,1024]{1,0:T(8,128)(2,1)}, bf16[128,1024]{1,0:T(8,128)(2,1)}, u32[]{:S(2)}, u32[]{:S(2)}) collective-permute-start(bf16[128,1024]{1,0:T(8,128)(2,1)} %collective-permute-done.6.refs_2_), channel_id=1, source_target_pairs={{0,1},{1,0},{2,3},{3,2},{4,5},{5,4},{6,7},{7,6},{8,9},{9,8},{10,11... | collective-permute-start | bytes 786440 | tf_op jit(solution)/shard_map/ppermute | solution.py:99
  45.2 66.3 %collective-permute-start.12 = (bf16[128,1024]{1,0:T(8,128)(2,1)}, bf16[128,1024]{1,0:T(8,128)(2,1)}, u32[]{:S(2)}, u32[]{:S(2)}) collective-permute-start(bf16[128,1024]{1,0:T(8,128)(2,1)} %collective-permute-done.7.refs_4_), channel_id=1, source_target_pairs={{0,1},{1,0},{2,3},{3,2},{4,5},{5,4},{6,7},{7,6},{8,9},{9,8},{10,11... | collective-permute-start | bytes 786440 | tf_op jit(solution)/shard_map/ppermute | solution.py:99
  50.9 60.6 %collective-permute-start.13 = (bf16[128,9216]{1,0:T(8,128)(2,1)}, bf16[128,9216]{1,0:T(8,128)(2,1)S(1)}, u32[]{:S(2)}, u32[]{:S(2)}) collective-permute-start(bf16[128,9216]{1,0:T(8,128)(2,1)} %pad_maximum_fusion.2), channel_id=1, source_target_pairs={{0,8},{1,9},{2,10},{3,11},{4,12},{5,13},{6,14},{7,15},{8,0},{9,1},... | collective-permute-start | bytes 7077896 | tf_op jit(solution)/shard_map/ppermute | solution.py:91
  52.2 59.3 %collective-permute-start.14 = (bf16[128,9216]{1,0:T(8,128)(2,1)}, bf16[128,9216]{1,0:T(8,128)(2,1)}, u32[]{:S(2)}, u32[]{:S(2)}) collective-permute-start(bf16[128,9216]{1,0:T(8,128)(2,1)} %pad_maximum_fusion.2), channel_id=1, source_target_pairs={{0,16},{1,17},{2,18},{3,19},{4,20},{5,21},{6,22},{7,23},{8,24},{9,... | collective-permute-start | bytes 7077896 | tf_op jit(solution)/shard_map/ppermute | solution.py:91
  54.3 53.4 %collective-permute-start.9 = (bf16[64,1024]{1,0:T(8,128)(2,1)}, bf16[64,1024]{1,0:T(8,128)(2,1)S(1)}, u32[]{:S(2)}, u32[]{:S(2)}) collective-permute-start(bf16[64,1024]{1,0:T(8,128)(2,1)} %slice.204), channel_id=1, source_target_pairs={{0,16},{1,17},{2,18},{3,19},{4,20},{5,21},{6,22},{7,23},{8,24},{9,... | collective-permute-start | bytes 393224 | tf_op jit(solution)/shard_map/ppermute | solution.py:91
  113.0 38.9 %collective-permute-start.15 = (bf16[128,1024]{1,0:T(8,128)(2,1)}, bf16[128,1024]{1,0:T(8,128)(2,1)}, u32[]{:S(2)}, u32[]{:S(2)}) collective-permute-start(bf16[128,1024]{1,0:T(8,128)(2,1)} %constant_dynamic-update-slice_fusion.2.refs_6_), channel_id=1, source_target_pairs={{0,1},{1,0},{2,3},{3,2},{4,5},{5,4},{6,7},{7,6},{8,9},{9,8},{10,11... | collective-permute-start | bytes 786440 | tf_op jit(solution)/shard_map/ppermute | solution.py:99
  124.7 40.7 %collective-permute-start.16 = (bf16[64,9216]{1,0:T(8,128)(2,1)}, bf16[64,9216]{1,0:T(8,128)(2,1)}, u32[]{:S(2)}, u32[]{:S(2)}) collective-permute-start(bf16[64,9216]{1,0:T(8,128)(2,1)} %slice.207), channel_id=1, source_target_pairs={{0,16},{1,17},{2,18},{3,19},{4,20},{5,21},{6,22},{7,23},{8,24},{9,... | collective-permute-start | bytes 3538952 | tf_op jit(solution)/shard_map/ppermute | solution.py:91
  128.3 37.1 %collective-permute-start.17 = (bf16[64,9216]{1,0:T(8,128)(2,1)}, bf16[64,9216]{1,0:T(8,128)(2,1)}, u32[]{:S(2)}, u32[]{:S(2)}) collective-permute-start(bf16[64,9216]{1,0:T(8,128)(2,1)} %slice.208), channel_id=1, source_target_pairs={{0,8},{1,9},{2,10},{3,11},{4,12},{5,13},{6,14},{7,15},{8,0},{9,1},... | collective-permute-start | bytes 3538952 | tf_op jit(solution)/shard_map/ppermute | solution.py:91
  165.4 41.2 %collective-permute-start.18 = (bf16[128,9216]{1,0:T(8,128)(2,1)S(1)}, bf16[128,9216]{1,0:T(8,128)(2,1)}, u32[]{:S(2)}, u32[]{:S(2)}) collective-permute-start(bf16[128,9216]{1,0:T(8,128)(2,1)S(1)} %collective-permute-done.13.refs_2_.refs_10_), channel_id=1, source_target_pairs={{0,1},{1,0},{2,3},{3,2},{4,5},{5,4},{6,7},{7,6},{8,9},{9,8},{10,11... | collective-permute-start | bytes 7077896 | tf_op jit(solution)/shard_map/ppermute | solution.py:99
  165.5 41.1 %collective-permute-start.19 = (bf16[128,9216]{1,0:T(8,128)(2,1)}, bf16[128,9216]{1,0:T(8,128)(2,1)}, u32[]{:S(2)}, u32[]{:S(2)}) collective-permute-start(bf16[128,9216]{1,0:T(8,128)(2,1)} %collective-permute-done.14.refs_4_.refs_12_), channel_id=1, source_target_pairs={{0,1},{1,0},{2,3},{3,2},{4,5},{5,4},{6,7},{7,6},{8,9},{9,8},{10,11... | collective-permute-start | bytes 7077896 | tf_op jit(solution)/shard_map/ppermute | solution.py:99
  170.8 35.8 %collective-permute-start.20 = (bf16[128,9216]{1,0:T(8,128)(2,1)}, bf16[128,9216]{1,0:T(8,128)(2,1)}, u32[]{:S(2)}, u32[]{:S(2)}) collective-permute-start(bf16[128,9216]{1,0:T(8,128)(2,1)} %constant_dynamic-update-slice_fusion.4.refs_6_.refs_14_), channel_id=1, source_target_pairs={{0,1},{1,0},{2,3},{3,2},{4,5},{5,4},{6,7},{7,6},{8,9},{9,8},{10,11... | collective-permute-start | bytes 7077896 | tf_op jit(solution)/shard_map/ppermute | solution.py:99
  172.2 33.4 %collective-permute-start.21 = (bf16[576,1024]{1,0:T(8,128)(2,1)S(1)}, bf16[576,1024]{1,0:T(8,128)(2,1)}, u32[]{:S(2)}, u32[]{:S(2)}) collective-permute-start(bf16[576,1024]{1,0:T(8,128)(2,1)S(1)} %constant_dynamic-slice_fusion.26), channel_id=1, source_target_pairs={{0,8},{1,9},{2,10},{3,11},{4,12},{5,13},{6,14},{7,15},{8,0},{9,1},... | collective-permute-start | bytes 3538952 | tf_op jit(solution)/shard_map/ppermute | solution.py:91
  179.3 27.3 %collective-permute-start.22 = (bf16[576,1024]{1,0:T(8,128)(2,1)S(1)}, bf16[576,1024]{1,0:T(8,128)(2,1)}, u32[]{:S(2)}, u32[]{:S(2)}) collective-permute-start(bf16[576,1024]{1,0:T(8,128)(2,1)S(1)} %constant_dynamic-slice_fusion.26), channel_id=1, source_target_pairs={{0,16},{1,17},{2,18},{3,19},{4,20},{5,21},{6,22},{7,23},{8,24},{9,... | collective-permute-start | bytes 3538952 | tf_op jit(solution)/shard_map/ppermute | solution.py:91
  206.6 34.1 %collective-permute-start.25 = (bf16[576,1024]{1,0:T(8,128)(2,1)}, bf16[576,1024]{1,0:T(8,128)(2,1)S(1)}, u32[]{:S(2)}, u32[]{:S(2)}) collective-permute-start(bf16[576,1024]{1,0:T(8,128)(2,1)} %collective-permute-done.21.refs_2_), channel_id=1, source_target_pairs={{0,1},{1,0},{2,3},{3,2},{4,5},{5,4},{6,7},{7,6},{8,9},{9,8},{10,11... | collective-permute-start | bytes 3538952 | tf_op jit(solution)/shard_map/ppermute | solution.py:99
  207.9 32.8 %collective-permute-start.26 = (bf16[576,1024]{1,0:T(8,128)(2,1)}, bf16[576,1024]{1,0:T(8,128)(2,1)S(1)}, u32[]{:S(2)}, u32[]{:S(2)}) collective-permute-start(bf16[576,1024]{1,0:T(8,128)(2,1)} %collective-permute-done.22.refs_4_), channel_id=1, source_target_pairs={{0,1},{1,0},{2,3},{3,2},{4,5},{5,4},{6,7},{7,6},{8,9},{9,8},{10,11... | collective-permute-start | bytes 3538952 | tf_op jit(solution)/shard_map/ppermute | solution.py:99
  211.8 28.9 %collective-permute-start.23 = (bf16[288,1024]{1,0:T(8,128)(2,1)}, bf16[288,1024]{1,0:T(8,128)(2,1)S(1)}, u32[]{:S(2)}, u32[]{:S(2)}) collective-permute-start(bf16[288,1024]{1,0:T(8,128)(2,1)} %slice.209), channel_id=1, source_target_pairs={{0,16},{1,17},{2,18},{3,19},{4,20},{5,21},{6,22},{7,23},{8,24},{9,... | collective-permute-start | bytes 1769480 | tf_op jit(solution)/shard_map/ppermute | solution.py:91
  211.8 28.9 %collective-permute-start.24 = (bf16[288,1024]{1,0:T(8,128)(2,1)}, bf16[288,1024]{1,0:T(8,128)(2,1)S(1)}, u32[]{:S(2)}, u32[]{:S(2)}) collective-permute-start(bf16[288,1024]{1,0:T(8,128)(2,1)} %slice.210), channel_id=1, source_target_pairs={{0,8},{1,9},{2,10},{3,11},{4,12},{5,13},{6,14},{7,15},{8,0},{9,1},... | collective-permute-start | bytes 1769480 | tf_op jit(solution)/shard_map/ppermute | solution.py:91
  293.3 12.3 %collective-permute-start.28 = (bf16[4,1152,512]{2,1,0:T(8,128)(2,1)}, bf16[4,1152,512]{2,1,0:T(8,128)(2,1)}, u32[]{:S(2)}, u32[]{:S(2)}) collective-permute-start(bf16[4,1152,512]{2,1,0:T(8,128)(2,1)} %bitcast.15), channel_id=1, source_target_pairs={{0,1},{1,0},{2,3},{3,2},{4,5},{5,4},{6,7},{7,6},{8,9},{9,8},{10,11... | collective-permute-start | bytes 14155784 | tf_op jit(solution)/shard_map/ppermute | solution.py:99
  305.5 38.9 %collective-permute-start.29 = (bf16[4,128,4608]{2,1,0:T(8,128)(2,1)}, bf16[4,128,4608]{2,1,0:T(8,128)(2,1)}, u32[]{:S(2)}, u32[]{:S(2)}) collective-permute-start(bf16[4,128,4608]{2,1,0:T(8,128)(2,1)} %bitcast.18), channel_id=1, source_target_pairs={{0,1},{1,0},{2,3},{3,2},{4,5},{5,4},{6,7},{7,6},{8,9},{9,8},{10,11... | collective-permute-start | bytes 14155784 | tf_op jit(solution)/shard_map/ppermute | solution.py:99
  319.5 34.0 %collective-permute-start.30 = (bf16[4,128,4608]{2,1,0:T(8,128)(2,1)}, bf16[4,128,4608]{2,1,0:T(8,128)(2,1)}, u32[]{:S(2)}, u32[]{:S(2)}) collective-permute-start(bf16[4,128,4608]{2,1,0:T(8,128)(2,1)} %bitcast.20), channel_id=1, source_target_pairs={{0,1},{1,0},{2,3},{3,2},{4,5},{5,4},{6,7},{7,6},{8,9},{9,8},{10,11... | collective-permute-start | bytes 14155784 | tf_op jit(solution)/shard_map/ppermute | solution.py:99
  324.6 27.6 %collective-permute-start.31 = (bf16[2,576,512]{2,1,0:T(8,128)(2,1)S(1)}, bf16[2,576,512]{2,1,0:T(8,128)(2,1)S(1)}, u32[]{:S(2)}, u32[]{:S(2)}) collective-permute-start(bf16[2,576,512]{2,1,0:T(8,128)(2,1)S(1)} %pad_maximum_fusion.7), channel_id=1, source_target_pairs={{0,8},{1,9},{2,10},{3,11},{4,12},{5,13},{6,14},{7,15},{8,0},{9,1},... | collective-permute-start | bytes 3538952 | tf_op jit(solution)/shard_map/ppermute | solution.py:91
  326.3 27.3 %collective-permute-start.32 = (bf16[2,576,512]{2,1,0:T(8,128)(2,1)S(1)}, bf16[2,576,512]{2,1,0:T(8,128)(2,1)S(1)}, u32[]{:S(2)}, u32[]{:S(2)}) collective-permute-start(bf16[2,576,512]{2,1,0:T(8,128)(2,1)S(1)} %pad_maximum_fusion.8), channel_id=1, source_target_pairs={{0,16},{1,17},{2,18},{3,19},{4,20},{5,21},{6,22},{7,23},{8,24},{9,... | collective-permute-start | bytes 3538952 | tf_op jit(solution)/shard_map/ppermute | solution.py:91
  356.9 35.8 %collective-permute-start.33 = (bf16[576,512]{1,0:T(8,128)(2,1)}, bf16[576,512]{1,0:T(8,128)(2,1)}, u32[]{:S(2)}, u32[]{:S(2)}) collective-permute-start(bf16[576,512]{1,0:T(8,128)(2,1)} %get-tuple-element.324), channel_id=1, source_target_pairs={{0,16},{1,17},{2,18},{3,19},{4,20},{5,21},{6,22},{7,23},{8,24},{9,... | collective-permute-start | bytes 1769480 | tf_op jit(solution)/shard_map/ppermute | solution.py:91
  358.1 34.6 %collective-permute-start.34 = (bf16[576,512]{1,0:T(8,128)(2,1)S(1)}, bf16[576,512]{1,0:T(8,128)(2,1)}, u32[]{:S(2)}, u32[]{:S(2)}) collective-permute-start(bf16[576,512]{1,0:T(8,128)(2,1)S(1)} %get-tuple-element.323), channel_id=1, source_target_pairs={{0,8},{1,9},{2,10},{3,11},{4,12},{5,13},{6,14},{7,15},{8,0},{9,1},... | collective-permute-start | bytes 1769480 | tf_op jit(solution)/shard_map/ppermute | solution.py:91
  361.9 58.2 %collective-permute-start.36 = (bf16[2,64,4608]{2,1,0:T(8,128)(2,1)}, bf16[2,64,4608]{2,1,0:T(8,128)(2,1)S(1)}, u32[]{:S(2)}, u32[]{:S(2)}) collective-permute-start(bf16[2,64,4608]{2,1,0:T(8,128)(2,1)} %pad_maximum_fusion.9), channel_id=1, source_target_pairs={{0,8},{1,9},{2,10},{3,11},{4,12},{5,13},{6,14},{7,15},{8,0},{9,1},... | collective-permute-start | bytes 3538952 | tf_op jit(solution)/shard_map/ppermute | solution.py:91
  364.0 56.2 %collective-permute-start.37 = (bf16[2,64,4608]{2,1,0:T(8,128)(2,1)}, bf16[2,64,4608]{2,1,0:T(8,128)(2,1)}, u32[]{:S(2)}, u32[]{:S(2)}) collective-permute-start(bf16[2,64,4608]{2,1,0:T(8,128)(2,1)} %pad_maximum_fusion.10), channel_id=1, source_target_pairs={{0,16},{1,17},{2,18},{3,19},{4,20},{5,21},{6,22},{7,23},{8,24},{9,... | collective-permute-start | bytes 3538952 | tf_op jit(solution)/shard_map/ppermute | solution.py:91
  401.9 18.3 %collective-permute-start.35 = (bf16[4,128,1024]{2,1,0:T(8,128)(2,1)S(1)}, bf16[4,128,1024]{2,1,0:T(8,128)(2,1)S(1)}, u32[]{:S(2)}, u32[]{:S(2)}) collective-permute-start(bf16[4,128,1024]{2,1,0:T(8,128)(2,1)S(1)} %bitcast.231), channel_id=1, source_target_pairs={{0,1},{1,0},{2,3},{3,2},{4,5},{5,4},{6,7},{7,6},{8,9},{9,8},{10,11... | collective-permute-start | bytes 3145736 | tf_op jit(solution)/shard_map/ppermute | solution.py:99
  406.9 13.2 %collective-permute-start.38 = (bf16[576,512]{1,0:T(8,128)(2,1)S(1)}, bf16[576,512]{1,0:T(8,128)(2,1)S(1)}, u32[]{:S(2)}, u32[]{:S(2)}) collective-permute-start(bf16[576,512]{1,0:T(8,128)(2,1)S(1)} %get-tuple-element.308), channel_id=1, source_target_pairs={{0,2},{1,3},{2,0},{3,1},{4,6},{5,7},{6,4},{7,5},{8,10},{9,11},{10,... | collective-permute-start | bytes 1769480 | tf_op jit(solution)/shard_map/ppermute | solution.py:99
  424.3 50.1 %collective-permute-start.42 = (bf16[2,64,4608]{2,1,0:T(8,128)(2,1)}, bf16[2,64,4608]{2,1,0:T(8,128)(2,1)}, u32[]{:S(2)}, u32[]{:S(2)}) collective-permute-start(bf16[2,64,4608]{2,1,0:T(8,128)(2,1)} %pad_maximum_fusion.11), channel_id=1, source_target_pairs={{0,8},{1,9},{2,10},{3,11},{4,12},{5,13},{6,14},{7,15},{8,0},{9,1},... | collective-permute-start | bytes 3538952 | tf_op jit(solution)/shard_map/ppermute | solution.py:91
  425.6 48.9 %collective-permute-start.43 = (bf16[2,64,4608]{2,1,0:T(8,128)(2,1)}, bf16[2,64,4608]{2,1,0:T(8,128)(2,1)}, u32[]{:S(2)}, u32[]{:S(2)}) collective-permute-start(bf16[2,64,4608]{2,1,0:T(8,128)(2,1)} %pad_maximum_fusion.12), channel_id=1, source_target_pairs={{0,16},{1,17},{2,18},{3,19},{4,20},{5,21},{6,22},{7,23},{8,24},{9,... | collective-permute-start | bytes 3538952 | tf_op jit(solution)/shard_map/ppermute | solution.py:91
  430.3 44.1 %collective-permute-start.39 = (bf16[64,4608]{1,0:T(8,128)(2,1)}, bf16[64,4608]{1,0:T(8,128)(2,1)}, u32[]{:S(2)}, u32[]{:S(2)}) collective-permute-start(bf16[64,4608]{1,0:T(8,128)(2,1)} %get-tuple-element.318), channel_id=1, source_target_pairs={{0,16},{1,17},{2,18},{3,19},{4,20},{5,21},{6,22},{7,23},{8,24},{9,... | collective-permute-start | bytes 1769480 | tf_op jit(solution)/shard_map/ppermute | solution.py:91
  430.4 44.0 %collective-permute-start.40 = (bf16[64,4608]{1,0:T(8,128)(2,1)}, bf16[64,4608]{1,0:T(8,128)(2,1)}, u32[]{:S(2)}, u32[]{:S(2)}) collective-permute-start(bf16[64,4608]{1,0:T(8,128)(2,1)} %get-tuple-element.317), channel_id=1, source_target_pairs={{0,8},{1,9},{2,10},{3,11},{4,12},{5,13},{6,14},{7,15},{8,0},{9,1},... | collective-permute-start | bytes 1769480 | tf_op jit(solution)/shard_map/ppermute | solution.py:91
  432.0 42.5 %collective-permute-start.41 = (bf16[576,512]{1,0:T(8,128)(2,1)S(1)}, bf16[576,512]{1,0:T(8,128)(2,1)S(1)}, u32[]{:S(2)}, u32[]{:S(2)}) collective-permute-start(bf16[576,512]{1,0:T(8,128)(2,1)S(1)} %add_convert_fusion.22), channel_id=1, source_target_pairs={{0,4},{1,5},{2,6},{3,7},{4,0},{5,1},{6,2},{7,3},{8,12},{9,13},{10,... | collective-permute-start | bytes 1769480 | tf_op jit(solution)/shard_map/ppermute | solution.py:99
  504.9 36.0 %collective-permute-start.44 = (bf16[64,4608]{1,0:T(8,128)(2,1)}, bf16[64,4608]{1,0:T(8,128)(2,1)}, u32[]{:S(2)}, u32[]{:S(2)}) collective-permute-start(bf16[64,4608]{1,0:T(8,128)(2,1)} %get-tuple-element.312), channel_id=1, source_target_pairs={{0,16},{1,17},{2,18},{3,19},{4,20},{5,21},{6,22},{7,23},{8,24},{9,... | collective-permute-start | bytes 1769480 | tf_op jit(solution)/shard_map/ppermute | solution.py:91
  514.7 26.2 %collective-permute-start.45 = (bf16[64,4608]{1,0:T(8,128)(2,1)}, bf16[64,4608]{1,0:T(8,128)(2,1)}, u32[]{:S(2)}, u32[]{:S(2)}) collective-permute-start(bf16[64,4608]{1,0:T(8,128)(2,1)} %get-tuple-element.311), channel_id=1, source_target_pairs={{0,8},{1,9},{2,10},{3,11},{4,12},{5,13},{6,14},{7,15},{8,0},{9,1},... | collective-permute-start | bytes 1769480 | tf_op jit(solution)/shard_map/ppermute | solution.py:91
  518.7 22.2 %collective-permute-start.46 = (bf16[64,4608]{1,0:T(8,128)(2,1)}, bf16[64,4608]{1,0:T(8,128)(2,1)}, u32[]{:S(2)}, u32[]{:S(2)}) collective-permute-start(bf16[64,4608]{1,0:T(8,128)(2,1)} %get-tuple-element.305), channel_id=1, source_target_pairs={{0,2},{1,3},{2,0},{3,1},{4,6},{5,7},{6,4},{7,5},{8,10},{9,11},{10,... | collective-permute-start | bytes 1769480 | tf_op jit(solution)/shard_map/ppermute | solution.py:99
  519.7 14.3 %collective-permute-start.48 = (bf16[2,64,1024]{2,1,0:T(8,128)(2,1)}, bf16[2,64,1024]{2,1,0:T(8,128)(2,1)}, u32[]{:S(2)}, u32[]{:S(2)}) collective-permute-start(bf16[2,64,1024]{2,1,0:T(8,128)(2,1)} %pad_maximum_fusion.24), channel_id=1, source_target_pairs={{0,8},{1,9},{2,10},{3,11},{4,12},{5,13},{6,14},{7,15},{8,0},{9,1},... | collective-permute-start | bytes 786440 | tf_op jit(solution)/shard_map/ppermute | solution.py:91
  522.1 21.2 %collective-permute-start.47 = (bf16[576,512]{1,0:T(8,128)(2,1)}, bf16[576,512]{1,0:T(8,128)(2,1)}, u32[]{:S(2)}, u32[]{:S(2)}) collective-permute-start(bf16[576,512]{1,0:T(8,128)(2,1)} %add_convert_fusion.13), channel_id=1, source_target_pairs={{0,2},{1,3},{2,0},{3,1},{4,6},{5,7},{6,4},{7,5},{8,10},{9,11},{10,... | collective-permute-start | bytes 1769480 | tf_op jit(solution)/shard_map/ppermute | solution.py:99
  558.9 50.1 %collective-permute-start.50 = (bf16[4,128,2176]{2,1,0:T(8,128)(2,1)S(1)}, bf16[4,128,2176]{2,1,0:T(8,128)(2,1)S(1)}, u32[]{:S(2)}, u32[]{:S(2)}) collective-permute-start(bf16[4,128,2176]{2,1,0:T(8,128)(2,1)S(1)} %pad_maximum_fusion.4), channel_id=1, source_target_pairs={{0,1},{1,0},{2,3},{3,2},{4,5},{5,4},{6,7},{7,6},{8,9},{9,8},{10,11... | collective-permute-start | bytes 6684680 | tf_op jit(solution)/shard_map/ppermute | solution.py:99
  565.1 27.9 %collective-permute-start.51 = (bf16[64,1024]{1,0:T(8,128)(2,1)}, bf16[64,1024]{1,0:T(8,128)(2,1)S(1)}, u32[]{:S(2)}, u32[]{:S(2)}) collective-permute-start(bf16[64,1024]{1,0:T(8,128)(2,1)} %get-tuple-element.352), channel_id=1, source_target_pairs={{0,16},{1,17},{2,18},{3,19},{4,20},{5,21},{6,22},{7,23},{8,24},{9,... | collective-permute-start | bytes 393224 | tf_op jit(solution)/shard_map/ppermute | solution.py:91
  565.5 27.4 %collective-permute-start.52 = (bf16[64,1024]{1,0:T(8,128)(2,1)S(1)}, bf16[64,1024]{1,0:T(8,128)(2,1)S(1)}, u32[]{:S(2)}, u32[]{:S(2)}) collective-permute-start(bf16[64,1024]{1,0:T(8,128)(2,1)S(1)} %get-tuple-element.351), channel_id=1, source_target_pairs={{0,8},{1,9},{2,10},{3,11},{4,12},{5,13},{6,14},{7,15},{8,0},{9,1},... | collective-permute-start | bytes 393224 | tf_op jit(solution)/shard_map/ppermute | solution.py:91
  569.6 23.3 %collective-permute-start.53 = (bf16[64,4608]{1,0:T(8,128)(2,1)S(1)}, bf16[64,4608]{1,0:T(8,128)(2,1)S(1)}, u32[]{:S(2)}, u32[]{:S(2)}) collective-permute-start(bf16[64,4608]{1,0:T(8,128)(2,1)S(1)} %get-tuple-element.302), channel_id=1, source_target_pairs={{0,2},{1,3},{2,0},{3,1},{4,6},{5,7},{6,4},{7,5},{8,10},{9,11},{10,... | collective-permute-start | bytes 1769480 | tf_op jit(solution)/shard_map/ppermute | solution.py:99
  571.3 9.8 %collective-permute-start.72 = (bf16[1152,512]{1,0:T(8,128)(2,1)S(1)}, bf16[1152,512]{1,0:T(8,128)(2,1)S(1)}, u32[]{:S(2)}, u32[]{:S(2)}) collective-permute-start(bf16[1152,512]{1,0:T(8,128)(2,1)S(1)} %pad_maximum_fusion.15), channel_id=1, source_target_pairs={{0,1},{1,0},{2,3},{3,2},{4,5},{5,4},{6,7},{7,6},{8,9},{9,8},{10,11... | collective-permute-start | bytes 3538952 | tf_op jit(solution)/shard_map/ppermute | solution.py:99
  581.1 27.9 %collective-permute-start.54 = (bf16[64,4608]{1,0:T(8,128)(2,1)S(1)}, bf16[64,4608]{1,0:T(8,128)(2,1)S(1)}, u32[]{:S(2)}, u32[]{:S(2)}) collective-permute-start(bf16[64,4608]{1,0:T(8,128)(2,1)S(1)} %add_convert_fusion.10), channel_id=1, source_target_pairs={{0,4},{1,5},{2,6},{3,7},{4,0},{5,1},{6,2},{7,3},{8,12},{9,13},{10,... | collective-permute-start | bytes 1769480 | tf_op jit(solution)/shard_map/ppermute | solution.py:99
  609.2 29.2 %collective-permute-start.55 = (bf16[64,4608]{1,0:T(8,128)(2,1)S(1)}, bf16[64,4608]{1,0:T(8,128)(2,1)S(1)}, u32[]{:S(2)}, u32[]{:S(2)}) collective-permute-start(bf16[64,4608]{1,0:T(8,128)(2,1)S(1)} %add_convert_fusion.9), channel_id=1, source_target_pairs={{0,4},{1,5},{2,6},{3,7},{4,0},{5,1},{6,2},{7,3},{8,12},{9,13},{10,... | collective-permute-start | bytes 1769480 | tf_op jit(solution)/shard_map/ppermute | solution.py:99
  609.4 29.0 %collective-permute-start.56 = (bf16[64,4608]{1,0:T(8,128)(2,1)S(1)}, bf16[64,4608]{1,0:T(8,128)(2,1)S(1)}, u32[]{:S(2)}, u32[]{:S(2)}) collective-permute-start(bf16[64,4608]{1,0:T(8,128)(2,1)S(1)} %add_convert_fusion.8), channel_id=1, source_target_pairs={{0,2},{1,3},{2,0},{3,1},{4,6},{5,7},{6,4},{7,5},{8,10},{9,11},{10,... | collective-permute-start | bytes 1769480 | tf_op jit(solution)/shard_map/ppermute | solution.py:99
  612.3 26.1 %collective-permute-start.57 = (bf16[64,1024]{1,0:T(8,128)(2,1)S(1)}, bf16[64,1024]{1,0:T(8,128)(2,1)S(1)}, u32[]{:S(2)}, u32[]{:S(2)}) collective-permute-start(bf16[64,1024]{1,0:T(8,128)(2,1)S(1)} %get-tuple-element.299), channel_id=1, source_target_pairs={{0,2},{1,3},{2,0},{3,1},{4,6},{5,7},{6,4},{7,5},{8,10},{9,11},{10,... | collective-permute-start | bytes 393224 | tf_op jit(solution)/shard_map/ppermute | solution.py:99
  612.8 25.6 %collective-permute-start.58 = (bf16[2,64,2176]{2,1,0:T(8,128)(2,1)S(1)}, bf16[2,64,2176]{2,1,0:T(8,128)(2,1)S(1)}, u32[]{:S(2)}, u32[]{:S(2)}) collective-permute-start(bf16[2,64,2176]{2,1,0:T(8,128)(2,1)S(1)} %pad_maximum_fusion.21), channel_id=1, source_target_pairs={{0,8},{1,9},{2,10},{3,11},{4,12},{5,13},{6,14},{7,15},{8,0},{9,1},... | collective-permute-start | bytes 1671176 | tf_op jit(solution)/shard_map/ppermute | solution.py:91
  614.0 24.4 %collective-permute-start.59 = (bf16[2,64,2176]{2,1,0:T(8,128)(2,1)S(1)}, bf16[2,64,2176]{2,1,0:T(8,128)(2,1)S(1)}, u32[]{:S(2)}, u32[]{:S(2)}) collective-permute-start(bf16[2,64,2176]{2,1,0:T(8,128)(2,1)S(1)} %pad_maximum_fusion.22), channel_id=1, source_target_pairs={{0,16},{1,17},{2,18},{3,19},{4,20},{5,21},{6,22},{7,23},{8,24},{9,... | collective-permute-start | bytes 1671176 | tf_op jit(solution)/shard_map/ppermute | solution.py:91
  638.6 16.9 %collective-permute-start.60 = (bf16[64,2176]{1,0:T(8,128)(2,1)S(1)}, bf16[64,2176]{1,0:T(8,128)(2,1)S(1)}, u32[]{:S(2)}, u32[]{:S(2)}) collective-permute-start(bf16[64,2176]{1,0:T(8,128)(2,1)S(1)} %get-tuple-element.332), channel_id=1, source_target_pairs={{0,8},{1,9},{2,10},{3,11},{4,12},{5,13},{6,14},{7,15},{8,0},{9,1},... | collective-permute-start | bytes 835592 | tf_op jit(solution)/shard_map/ppermute | solution.py:91
  640.2 15.4 %collective-permute-start.61 = (bf16[64,2176]{1,0:T(8,128)(2,1)S(1)}, bf16[64,2176]{1,0:T(8,128)(2,1)S(1)}, u32[]{:S(2)}, u32[]{:S(2)}) collective-permute-start(bf16[64,2176]{1,0:T(8,128)(2,1)S(1)} %get-tuple-element.331), channel_id=1, source_target_pairs={{0,16},{1,17},{2,18},{3,19},{4,20},{5,21},{6,22},{7,23},{8,24},{9,... | collective-permute-start | bytes 835592 | tf_op jit(solution)/shard_map/ppermute | solution.py:91
  649.0 43.3 %collective-permute-start.69 = (bf16[128,4608]{1,0:T(8,128)(2,1)S(1)}, bf16[128,4608]{1,0:T(8,128)(2,1)S(1)}, u32[]{:S(2)}, u32[]{:S(2)}) collective-permute-start(bf16[128,4608]{1,0:T(8,128)(2,1)S(1)} %pad_maximum_fusion.13), channel_id=1, source_target_pairs={{0,1},{1,0},{2,3},{3,2},{4,5},{5,4},{6,7},{7,6},{8,9},{9,8},{10,11... | collective-permute-start | bytes 3538952 | tf_op jit(solution)/shard_map/ppermute | solution.py:99
  655.9 8.3 %collective-permute-start.62 = (bf16[64,2176]{1,0:T(8,128)(2,1)S(1)}, bf16[64,2176]{1,0:T(8,128)(2,1)S(1)}, u32[]{:S(2)}, u32[]{:S(2)}) collective-permute-start(bf16[64,2176]{1,0:T(8,128)(2,1)S(1)} %get-tuple-element.296), channel_id=1, source_target_pairs={{0,2},{1,3},{2,0},{3,1},{4,6},{5,7},{6,4},{7,5},{8,10},{9,11},{10,... | collective-permute-start | bytes 835592 | tf_op jit(solution)/shard_map/ppermute | solution.py:99
  656.1 26.7 %collective-permute-start.70 = (bf16[64,4608]{1,0:T(8,128)(2,1)S(1)}, bf16[64,4608]{1,0:T(8,128)(2,1)S(1)}, u32[]{:S(2)}, u32[]{:S(2)}) collective-permute-start(bf16[64,4608]{1,0:T(8,128)(2,1)S(1)} %add_convert_fusion.7), channel_id=1, source_target_pairs={{0,2},{1,3},{2,0},{3,1},{4,6},{5,7},{6,4},{7,5},{8,10},{9,11},{10,... | collective-permute-start | bytes 1769480 | tf_op jit(solution)/shard_map/ppermute | solution.py:99
  664.3 18.6 %collective-permute-start.63 = (bf16[64,2176]{1,0:T(8,128)(2,1)S(1)}, bf16[64,2176]{1,0:T(8,128)(2,1)S(1)}, u32[]{:S(2)}, u32[]{:S(2)}) collective-permute-start(bf16[64,2176]{1,0:T(8,128)(2,1)S(1)} %add_convert_fusion.41), channel_id=1, source_target_pairs={{0,4},{1,5},{2,6},{3,7},{4,0},{5,1},{6,2},{7,3},{8,12},{9,13},{10,... | collective-permute-start | bytes 835592 | tf_op jit(solution)/shard_map/ppermute | solution.py:99
  683.0 7.4 %collective-permute-start.64 = (bf16[64,2176]{1,0:T(8,128)(2,1)S(1)}, bf16[64,2176]{1,0:T(8,128)(2,1)S(1)}, u32[]{:S(2)}, u32[]{:S(2)}) collective-permute-start(bf16[64,2176]{1,0:T(8,128)(2,1)S(1)} %add_convert_fusion.40), channel_id=1, source_target_pairs={{0,2},{1,3},{2,0},{3,1},{4,6},{5,7},{6,4},{7,5},{8,10},{9,11},{10,... | collective-permute-start | bytes 835592 | tf_op jit(solution)/shard_map/ppermute | solution.py:99
  683.7 14.9 %collective-permute-start.71 = (bf16[128,4608]{1,0:T(8,128)(2,1)S(1)}, bf16[128,4608]{1,0:T(8,128)(2,1)S(1)}, u32[]{:S(2)}, u32[]{:S(2)}) collective-permute-start(bf16[128,4608]{1,0:T(8,128)(2,1)S(1)} %pad_maximum_fusion.14), channel_id=1, source_target_pairs={{0,1},{1,0},{2,3},{3,2},{4,5},{5,4},{6,7},{7,6},{8,9},{9,8},{10,11... | collective-permute-start | bytes 3538952 | tf_op jit(solution)/shard_map/ppermute | solution.py:99
  (130 other events, 1005.5 us)

commit v6 on v5

--- a/solution.py
+++ b/solution.py
@@ -172,12 +172,12 @@
 FF_TILE = 512
 
 
-def block_specs(count, rows, tiles):
+def block_specs(count, rows, tiles, start=0):
     own = [
-        pl.BlockSpec((rows, FF_TILE), lambda i, spot, at=at: (at, i)) for at in (0, 1)
+        pl.BlockSpec((rows, FF_TILE), lambda i, spot, at=at: (at, i + start)) for at in (0, 1)
     ]
-    gate = [pl.BlockSpec((rows, FF_TILE), lambda i, spot: (0, i))] * (count - 2)
-    up = [pl.BlockSpec((rows, FF_TILE), lambda i, spot: (0, i + tiles))] * (count - 2)
+    gate = [pl.BlockSpec((rows, FF_TILE), lambda i, spot: (0, i + start))] * (count - 2)
+    up = [pl.BlockSpec((rows, FF_TILE), lambda i, spot: (0, i + start + tiles))] * (count - 2)
     return own + gate + own + up
 
 
@@ -188,7 +188,8 @@
         whole_ref[pl.ds(begin, rows), :] = ref[...]
 
 
-def ffn_forward_kernel(count, spots_ref, a_ref, *refs):
+def ffn_forward_kernel(count, spare, spots_ref, a_ref, *refs):
+    refs = refs[: 2 * count] + refs[2 * count + spare :]
     gate_refs, up_refs = refs[:count], refs[count : 2 * count]
     z_ref, act_ref, slope_ref, gate_whole, up_whole = refs[2 * count :]
     settle(spots_ref, gate_refs, gate_whole)
@@ -205,28 +206,32 @@
         slope_ref[rows] = (up * (sig + act * (1.0 - sig))).astype(jnp.bfloat16)
 
 
-def ffn_forward(normed, gate, up, gathered):
+def ffn_forward(normed, gate, up, gathered, start, steps, into):
     rows, depth = normed.shape
     blocks, spots = gathered
     count = len(blocks) + 2
     hidden = gate.shape[1]
     part = gate.shape[0] // 2
     out = jax.ShapeDtypeStruct((rows, hidden), jnp.bfloat16)
+    into = [] if into is None else list(into)
+    first = 2 + 2 * count
     return pl.pallas_call(
-        functools.partial(ffn_forward_kernel, count),
+        functools.partial(ffn_forward_kernel, count, len(into)),
         out_shape=(out, out, out),
         grid_spec=pltpu.PrefetchScalarGridSpec(
             num_scalar_prefetch=1,
-            grid=(hidden // FF_TILE,),
+            grid=(steps,),
             in_specs=[pl.BlockSpec((rows, depth), lambda i, spot: (0, 0))]
-            + block_specs(count, part, hidden // FF_TILE),
-            out_specs=[pl.BlockSpec((rows, FF_TILE), lambda i, spot: (0, i))] * 3,
+            + block_specs(count, part, hidden // FF_TILE, start)
+            + [pl.BlockSpec(memory_space=pl.ANY)] * len(into),
+            out_specs=[pl.BlockSpec((rows, FF_TILE), lambda i, spot: (0, i + start))] * 3,
             scratch_shapes=[pltpu.VMEM((depth, FF_TILE), jnp.bfloat16)] * 2,
         ),
+        input_output_aliases={first + at: at for at in range(len(into))},
         cost_estimate=TINY,
         compiler_params=pltpu.CompilerParams(vmem_limit_bytes=60 << 20),
         name="ffn_forward",
-    )(spots, normed, gate, gate, *blocks, up, up, *blocks)
+    )(spots, normed, gate, gate, *blocks, up, up, *blocks, *into)
 
 
 def ffn_inner_kernel(g_ref, down_ref, act_ref, slope_ref, dgate_ref, dup_ref):
@@ -323,8 +328,13 @@
             early, waiting = (rep_swap(pieces[1], 1), rep_swap(pieces[2], 1)), (3,)
             corner_a, corner_b, *early = yield (corner_a, corner_b, *early)
         pieces[3] = jnp.concatenate([corner_a, corner_b], axis=0)
-        rest = yield tuple(rep_swap(pieces[d], 1) for d in waiting)
-        others = dict(zip((1, 2, 3), (*early, *rest)))
+        if late == "joined":
+            joined = jnp.stack([pieces[1], pieces[2], pieces[3]])
+            (got,) = yield (rep_swap(joined, 1),)
+            others = {d: got[d - 1] for d in (1, 2, 3)}
+        else:
+            rest = yield tuple(rep_swap(pieces[d], 1) for d in waiting)
+            others = dict(zip((1, 2, 3), (*early, *rest)))
     else:
         pieces[0] = mine
         bit = 1
@@ -676,13 +686,14 @@
             links,
             jnp.concatenate([core_half(weight) for weight in attn_weights], axis=1),
             jnp.concatenate(attn_weights, axis=1),
+            late="joined",
         )
     )
     w_out, w_gate, w_up, w_down = sync((w_out, w_gate, w_up, w_down), front_flow)
-    out_flow = Flow(gather_steps(links, core_half(w_out), w_out))
-    w_gate, w_up, w_down = sync((w_gate, w_up, w_down), front_flow, out_flow)
     pair = jnp.concatenate([core_half(w_gate), core_half(w_up)], axis=1)
     pair_flow = Flow(gather_steps(links, pair, None, late=True))
+    w_out, w_down = sync((w_out, w_down), front_flow)
+    out_flow = Flow(gather_steps(links, core_half(w_out), w_out, late="joined"))
     w_down = sync(w_down, front_flow)
     front = place_blocks(front_flow.finish())
     full_query = front[:, : HQ * HD]
@@ -722,17 +733,21 @@
     query_rot, key_rot, value_low, w_down = sync(
         (query_rot, key_rot, value_low, w_down), out_flow, pair_flow
     )
+    attn_low = attend(query_rot, key_rot, value_low, segment)
+    attn_low, w_down = sync((attn_low, w_down), out_flow, pair_flow)
     down_flow = Flow(gather_steps(links, core_half(w_down), w_down))
-    attn_low = attend(query_rot, key_rot, value_low, segment)
-    attn_low = sync(attn_low, out_flow)
     full_out = place_blocks(out_flow.finish())
     hidden = inputs + matmul_plain(attn_low, full_out)
     scale_two = inv_rms(hidden)
     normed_ffn = (hidden * scale_two * full_ffn_gain.astype(jnp.float32)).astype(jnp.bfloat16)
     normed_ffn, hidden = sync((normed_ffn, hidden), pair_flow)
-    normed_ffn = sync(normed_ffn, pair_flow, down_flow)
     pair = pair_flow.finish()
-    mixed_act, act_low, slope = ffn_forward(normed_ffn, w_gate, w_up, pair)
+    tiles = w_gate.shape[1] // FF_TILE
+    first = ffn_forward(normed_ffn, w_gate, w_up, pair, 0, tiles // 2, None)
+    normed_ffn, first = sync((normed_ffn, first), down_flow)
+    mixed_act, act_low, slope = ffn_forward(
+        normed_ffn, w_gate, w_up, pair, tiles // 2, tiles - tiles // 2, first
+    )
     mixed_act, slope, act_low = sync((mixed_act, slope, act_low), down_flow)
     mixed_act, slope, act_low = sync((mixed_act, slope, act_low), down_flow)
     full_down = place_blocks(down_flow.finish())
@@ -771,7 +786,6 @@
     gate_back = Flow(scatter_steps(links, gate_given, gate_sent))
     grad_normed_ffn = ffn_input(grad_gate_low, grad_up_low, w_gate, w_up, pair)
     grad_normed_ffn, up_given, up_sent = sync((grad_normed_ffn, up_given, up_sent), down_back)
-    grad_ffn_gain = jnp.sum(grad_normed_ffn * hidden * scale_two, axis=0)
     grad_hidden = out_grad + norm_back(
         grad_normed_ffn, hidden, scale_two, full_ffn_gain.astype(jnp.float32)
     )
@@ -799,6 +813,9 @@
     grad_key_rot = grad_key_rot.reshape(row_count, HK, HD)
     grad_query_norm = rotate_back(grad_query_rot, cosine, sine_table)
     grad_key_norm = rotate_back(grad_key_rot, cosine, sine_table)
+    grad_query_norm, grad_key_norm = sync(
+        (grad_query_norm, grad_key_norm), up_back, gate_back, down_back, out_back
+    )
     back_gains = full_qk_gain.astype(jnp.float32)
     grad_qk_gain = jnp.concatenate(
         [
@@ -820,37 +837,36 @@
     normed_own, normed_other = pick_columns(links, normed)
     grad_front = jnp.concatenate([grad_query_low, grad_key_low, grad_value_low], axis=1)
     grad_front = sync(grad_front, up_back, gate_back, down_back, out_back)
+    front_other = blocked(links, matmul_rows(normed_other, grad_front))
+    front_own = blocked(links, matmul_rows(normed_own, grad_front))
+    front_other, front_own = (part.astype(jnp.bfloat16) for part in (front_other, front_own))
+    grad_front = pin(grad_front, front_other, front_own)
     grad_query_low = grad_front[:, : HQ * HD]
     grad_key_low = grad_front[:, HQ * HD : (HQ + HK) * HD]
     grad_value_low = grad_front[:, (HQ + HK) * HD :]
-    front_other = blocked(links, matmul_rows(normed_other, grad_front))
-    front_own = blocked(links, matmul_rows(normed_own, grad_front))
     grad_normed = (
         matmul_cols(grad_query_low, full_query)
         + matmul_cols(grad_key_low, full_key)
         + matmul_cols(grad_value_low, full_value)
     )
-    grad_attn_gain = jnp.sum(grad_normed * inputs * scale_one, axis=0)
-    grad_inputs = grad_hidden + norm_back(
-        grad_normed, inputs, scale_one, full_attn_gain.astype(jnp.float32)
-    )
     qk_part = jnp.pad(
         grad_qk_gain.reshape(links[0], -1),
         ((0, 0), (0, attn_gain.shape[0] - qk_gain.shape[0])),
     )
-    small = jnp.stack([grad_attn_gain, grad_ffn_gain, qk_part.reshape(-1)], axis=1)
-    small = jnp.pad(small, ((0, 0), (0, 125)))
-    small = small.reshape(links[0], 2, -1, 128)
+    small = jnp.pad(qk_part.reshape(-1, 1), ((0, 0), (0, 127)))
+    small = small.astype(jnp.bfloat16).reshape(links[0], 2, -1, 128)
     own_front = jnp.concatenate([front_own, lax.dynamic_slice_in_dim(small, core, 1, 1)[:, 0]], axis=2)
     other_front = jnp.concatenate(
         [front_other, lax.dynamic_slice_in_dim(small, 1 - core, 1, 1)[:, 0]], axis=2
     )
-    front_sent = rep_swap(other_front.astype(jnp.bfloat16), 1)
-    own_front = own_front.astype(jnp.bfloat16)
-    own_front, front_sent, mixed_act = sync(
-        (own_front, front_sent, mixed_act), out_back, up_back, gate_back
+    front_sent = rep_swap(other_front, 1)
+    own_front, front_sent, mixed_act, grad_normed = sync(
+        (own_front, front_sent, mixed_act, grad_normed), out_back, up_back, gate_back
     )
     front_back = Flow(scatter_steps(links, own_front, front_sent))
+    grad_inputs = grad_hidden + norm_back(
+        grad_normed, inputs, scale_one, full_attn_gain.astype(jnp.float32)
+    )
     result = live_rows * (hidden + matmul_plain(mixed_act, full_down))
     grad_inputs, result = sync((grad_inputs, result), up_back, gate_back, out_back, front_back)
     front_share = join_rows(front_back.finish())
@@ -858,13 +874,21 @@
     share_key = front_share[:, HQ * HD : (HQ + HK) * HD]
     share_value = front_share[:, (HQ + HK) * HD : (HQ + 2 * HK) * HD]
     extras = front_share[:, (HQ + 2 * HK) * HD :]
-    share_again = extras[:, 0]
-    share_fgain = extras[:, 1]
-    share_qk = extras[: qk_gain.shape[0], 2]
+    share_qk = extras[: qk_gain.shape[0], 0]
     share_out = join_rows(out_back.finish())
     share_gate = join_rows(gate_back.finish())
     share_up = join_rows(up_back.finish())
     share_down = join_columns(down_back.finish())
+    def gain_share(gain, *pairs):
+        inner = sum(
+            jnp.sum(weight.astype(jnp.float32) * share, axis=1) for weight, share in pairs
+        )
+        return inner / gain.astype(jnp.float32)
+
+    share_again = gain_share(
+        attn_gain, (w_query, share_query), (w_key, share_key), (w_value, share_value)
+    )
+    share_fgain = gain_share(ffn_gain, (w_gate, share_gate), (w_up, share_up))
     return (
         result.astype(jnp.bfloat16),
         grad_inputs.astype(jnp.bfloat16),

time: 705 us -> 673 us (0.955)
  waiting for transfers between devices: 159 us -> 99 us
  other arithmetic: 119 us -> 137 us
  starting transfers between devices: 82.5 us -> 96.5 us
  local copies, waits for them, and re-layouts: 69.1 us -> 61.6 us
    ppermute x37 -> x33, waiting for transfers between devices: 71.5 us -> 33.4 us  [rep_swap(): return lax.ppermute(value, axes, pairs)]
    ppermute x36, waiting for transfers between devices: 87.5 us -> 65.7 us  [shard_swap(): return lax.ppermute(value, axes, pairs)]
    ppermute x37 -> x33, starting transfers between devices: 37.5 us -> 53.6 us  [rep_swap(): return lax.ppermute(value, axes, pairs)]
    reduce_sum x2 -> x4, other arithmetic: 4.95 us -> 12.2 us  [norm_back(): row_inner = jnp.mean(weighted * inputs, axis=-1, keepdims=True)]
    pallas_call x1 -> x2, Pallas kernels: 28.8 us -> 33.3 us  [ffn_forward(): pl.pallas_call(functools.partial(ffn_forward_kernel, count, len(into)), o...]
    unnamed x247 -> x294, local copies, waits for them, and re-layouts: 14.9 us -> 13.9 us
  transfers between devices with their start and end apart: 73 -> 69, of which waited for: 20 -> 18; matrix products, arithmetic and copies ran while one was open for 30% -> 31% of each run, Pallas kernels for 19% -> 20%
where the time goes in v6:
time: 673 us; the launch traced here: 667 us
  Pallas kernels  169 us (25%)
  other arithmetic  137 us (20%)
  matrix products  101 us (15%)
  waiting for transfers between devices  99 us (15%)
  starting transfers between devices  96.5 us (14%)
  local copies, waits for them, and re-layouts  61.6 us (9%)
    ppermute x36, waiting for transfers between devices, shard_swap(): return lax.ppermute(value, axes, pairs)  65.7 us
    dot_general x10, matrix products, matmul_rows(): lax.dot_general(left_mat, right_mat, (((0,), (0,)), ((), ())), preferred_...  64.7 us
    ppermute x33, starting transfers between devices, rep_swap(): return lax.ppermute(value, axes, pairs)  53.6 us
    ppermute x36, starting transfers between devices, shard_swap(): return lax.ppermute(value, axes, pairs)  43 us
    pallas_call x2, Pallas kernels, attend_back(): pl.pallas_call(attend_back_kernel, out_shape=(jax.ShapeDtypeStruct((rows,...  37.2 us
    ppermute x33, waiting for transfers between devices, rep_swap(): return lax.ppermute(value, axes, pairs)  33.4 us
    pallas_call x2, Pallas kernels, ffn_forward(): pl.pallas_call(functools.partial(ffn_forward_kernel, count, len(into)), o...  33.3 us
    convert_element_type x20, other arithmetic, add_low(): (left.astype(jnp.float32) + right.astype(jnp.float32)).astype(jnp.bfloat16)  30.5 us
  transfers between devices with their start and end apart: 69, of which 18 were waited for; matrix products, arithmetic and copies ran while one was open for 31% of the time, Pallas kernels for 20%

profile of v6, /device:TPU:1, one launch (start us, length us, event | category | flops | bytes accessed | tf_op | source)
XLA Modules:
  0.0 667.3 jit_solution(1733092167127886467)
XLA Ops:
  12.1 8.3 %collective-permute-done.refs_2_ = bf16[128,2176]{1,0:T(8,128)(2,1)S(1)} collective-permute-done((bf16[128,2176]{1,0:T(8,128)(2,1)S(1)}, bf16[128,2176]{1,0:T(8,128)(2,1)S(1)}, u32[]{:S(2)}, u32[]{:S(2)}) %collective-permute-start) | collective-permute-done | bytes 557088 | tf_op jit(solution)/shard_map/ppermute | solution.py:91
  24.9 2.8 collective-permute-done.2
  29.0 3.1 collective-permute-start.4
  38.9 6.8 %place_blocks.3 = bf16[1024,2176]{1,0:T(8,128)(2,1)} custom-call(s32[8]{0:T(128)} %stack.70.spots_ref, bf16[256,2176]{1,0:T(8,128)(2,1)} %pad_maximum_fusion.17.refs_0_.refs_1_, bf16[256,2176]{1,0:T(8,128)(2,1)} %pad_maximum_fusion.17.refs_0_.refs_1_, bf16[128,2176]{1,0:T(8,128)(2,1)} %copy-done.29, bf16[128,2176]{1,0:T(8,128)(2,1)} %get-tuple-element.413.refs_3_, ...), custom_call_target="tpu_custom_call" | custom-call | flops 1 | bytes 1 | tf_op jit(solution)/shard_map/place_blocks/pallas_call | solution.py:154
  49.4 4.5 multiply_reduce_fusion.6
  53.9 2.7 multiply_reduce_fusion.9
  68.0 24.4 %collective-permute-done.5.refs_2_ = bf16[128,1024]{1,0:T(8,128)(2,1)} collective-permute-done((bf16[128,1024]{1,0:T(8,128)(2,1)}, bf16[128,1024]{1,0:T(8,128)(2,1)}, u32[]{:S(2)}, u32[]{:S(2)}) %collective-permute-start.5) | collective-permute-done | bytes 262176 | tf_op jit(solution)/shard_map/ppermute | solution.py:91
  104.1 3.9 copy.103.q_ref
  109.3 23.4 %attend.1 = bf16[1024,1024]{1,0:T(8,128)(2,1)} custom-call(s32[4,4]{1,0:T(4,128)} %fusion.80.live_ref, bf16[1024,1024]{1,0:T(8,128)(2,1)} %copy.103.q_ref, bf16[1024,512]{1,0:T(8,128)(2,1)} %copy.104.k_ref, bf16[1024,512]{1,0:T(8,128)(2,1)} %convolution_convert_fusion.11.v_ref, s32[1024,1]{1,0:T(8,128)} %copy.105.seg_col_ref, s32[1,1024]{1,0:T(1,128)} %bitcast.204), custom_call_target="tpu_custom_call" | custom-call | flops 1 | bytes 1 | tf_op jit(solution)/shard_map/attend/pallas_call | solution.py:600
  144.6 5.9 collective-permute-start.17
  150.5 2.9 collective-permute-start.18
  155.4 5.3 place_blocks.4
  160.7 5.3 multiply_reduce_fusion.5
  168.7 15.3 %ffn_forward.2 = (bf16[1024,4608]{1,0:T(8,128)(2,1)}, bf16[1024,4608]{1,0:T(8,128)(2,1)}, bf16[1024,4608]{1,0:T(8,128)(2,1)}) custom-call(s32[8]{0:T(128)} %stack.70.spots_ref, bf16[1024,1024]{1,0:T(8,128)(2,1)} %multiply_convert_fusion.a_ref, bf16[256,4608]{1,0:T(8,128)(2,1)} %refs_1_.4, bf16[256,4608]{1,0:T(8,128)(2,1)} %refs_1_.4, ...), custom_call_target="tpu_custom_call" | custom-call | flops 1 | bytes 1 | tf_op jit(solution)/shard_map/ffn_forward/pallas_call | solution.py:218
  189.6 18.0 %ffn_forward.3 = (bf16[1024,4608]{1,0:T(8,128)(2,1)}, bf16[1024,4608]{1,0:T(8,128)(2,1)}, bf16[1024,4608]{1,0:T(8,128)(2,1)}) custom-call(s32[8]{0:T(128)} %stack.70.spots_ref, bf16[1024,1024]{1,0:T(8,128)(2,1)} %multiply_convert_fusion.a_ref, bf16[256,4608]{1,0:T(8,128)(2,1)} %refs_1_.4, ...), custom_call_target="tpu_custom_call", output_to_operand_aliasing={{0}: (18, {}), {1}: (19, {}), {2}: (20, {})} | custom-call | flops 1 | bytes 1 | tf_op jit(solution)/shard_map/ffn_forward/pallas_call | solution.py:218
  215.8 9.4 %place_blocks.5.down_ref = bf16[4608,1024]{1,0:T(8,128)(2,1)} custom-call(s32[8]{0:T(128)} %stack.70.spots_ref, bf16[1152,1024]{1,0:T(8,128)(2,1)} %refs_1_.3, bf16[1152,1024]{1,0:T(8,128)(2,1)} %refs_1_.3, bf16[576,1024]{1,0:T(8,128)(2,1)} %copy-done.39, bf16[576,1024]{1,0:T(8,128)(2,1)} %copy-done.56, bf16[576,1024]{1,0:T(8,128)(2,1)} %collective-permute-done.18.refs_4_, ...), custom_call_target="tpu_custom_call" | custom-call | flops 1 | bytes 1 | tf_op jit(solution)/shard_map/place_blocks/pallas_call | solution.py:154
  225.2 24.8 %ffn_inner.1 = (bf16[1024,4608]{1,0:T(8,128)(2,1)}, bf16[1024,4608]{1,0:T(8,128)(2,1)}) custom-call(bf16[1024,1024]{1,0:T(8,128)(2,1)} %copy-done.18, bf16[4608,1024]{1,0:T(8,128)(2,1)} %place_blocks.5.down_ref, bf16[1024,4608]{1,0:T(8,128)(2,1)} %get-tuple-element.218.act_ref, bf16[1024,4608]{1,0:T(8,128)(2,1)} %get-tuple-element.219.slope_ref), custom_call_target="tpu_custom_call" | custom-call | flops 1 | bytes 1 | tf_op jit(solution)/shard_map/ffn_inner/pallas_call | solution.py:251
  250.1 11.1 %convolution_convert_fusion.1 = bf16[4608,512]{1,0:T(8,128)(2,1)} fusion(bf16[1024,4608]{1,0:T(8,128)(2,1)} %get-tuple-element.298, bf16[1024,512]{1,0:T(8,128)(2,1)S(1)} %copy-done.70), kind=kOutput, calls=%fused_computation.6 | convolution fusion | flops 4834197504 | bytes 15204352 | tf_op jit(solution)/shard_map/dot_general | solution.py:70
  262.3 10.9 %convolution_convert_fusion.5 = bf16[512,4608]{1,0:T(8,128)(2,1)} fusion(bf16[1024,4608]{1,0:T(8,128)(2,1)} %get-tuple-element.238.dgate_ref, bf16[1024,128]{1,0:T(8,128)(2,1)S(1)} %get-tuple-element.405, bf16[1024,128]{1,0:T(8,128)(2,1)S(1)} %get-tuple-element.406, bf16[1024,128]{1,0:T(8,128)(2,1)S(1)} %get-tuple-element.407, ...), kind=kOutput, calls=%fused_computation.10 | convolution fusion | flops 4838391808 | bytes 15204352 | tf_op jit(solution)/shard_map/dot_general | solution.py:70
  273.4 6.9 %convolution_convert_fusion = bf16[4608,512]{1,0:T(8,128)(2,1)} fusion(bf16[1024,4608]{1,0:T(8,128)(2,1)S(1)} %bitcast.165, bf16[1024,512]{1,0:T(8,128)(2,1)S(1)} %copy-done.69), kind=kOutput, calls=%fused_computation.5 | convolution fusion | flops 4834197504 | bytes 15204352 | tf_op jit(solution)/shard_map/dot_general | solution.py:70
  280.4 7.1 %convolution_convert_fusion.2 = bf16[512,4608]{1,0:T(8,128)(2,1)} fusion(bf16[1024,512]{1,0:T(8,128)(2,1)S(1)} %pad_maximum_fusion.19, bf16[1024,4608]{1,0:T(8,128)(2,1)S(1)} %bitcast.169), kind=kOutput, calls=%fused_computation.7 | convolution fusion | flops 4834197504 | bytes 15204352 | tf_op jit(solution)/shard_map/dot_general | solution.py:70
  289.4 3.0 add_convert_fusion.34
  294.5 11.2 %convolution_convert_fusion.3 = bf16[512,4608]{1,0:T(8,128)(2,1)} fusion(bf16[1024,512]{1,0:T(8,128)(2,1)S(1)} %pad_maximum_fusion.20, bf16[1024,4608]{1,0:T(8,128)(2,1)} %get-tuple-element.239.dup_ref), kind=kOutput, calls=%fused_computation.8 | convolution fusion | flops 4834197504 | bytes 15204352 | tf_op jit(solution)/shard_map/dot_general | solution.py:70
  305.7 5.4 convolution_convert_fusion.4
  311.2 8.8 %collective-permute-done.27 = bf16[2,576,512]{2,1,0:T(8,128)(2,1)S(1)} collective-permute-done((bf16[2,576,512]{2,1,0:T(8,128)(2,1)S(1)}, bf16[2,576,512]{2,1,0:T(8,128)(2,1)S(1)}, u32[]{:S(2)}, u32[]{:S(2)}) %collective-permute-start.27) | collective-permute-done | bytes 1179680 | tf_op jit(solution)/shard_map/ppermute | solution.py:91
  320.7 3.3 fusion.61
  331.3 28.5 %ffn_input.1 = f32[1024,1024]{1,0:T(8,128)} custom-call(s32[8]{0:T(128)} %stack.70.spots_ref, bf16[1024,4608]{1,0:T(8,128)(2,1)} %get-tuple-element.238.dgate_ref, bf16[1024,4608]{1,0:T(8,128)(2,1)} %get-tuple-element.239.dup_ref, bf16[256,4608]{1,0:T(8,128)(2,1)} %refs_1_.4, bf16[256,4608]{1,0:T(8,128)(2,1)} %refs_1_.4, bf16[128,9216]{1,0:T(8,128)(2,1)} %copy-done.4, ...), custom_call_target="tpu_custom_call" | custom-call | flops 1 | bytes 1 | tf_op jit(solution)/shard_map/ffn_input/pallas_call | solution.py:293
  359.9 4.1 multiply_reduce_fusion.4
  371.1 2.6 broadcast_select_fusion.8
  373.8 2.8 collective-permute-start.34
  378.9 3.7 convolution_convert_fusion.8.do_ref
  382.6 5.9 collective-permute-done.34
  388.6 2.9 add_convert_fusion.19
  395.1 3.0 fusion.63
  402.7 18.5 %attend_back.2 = (f32[1024,512]{1,0:T(8,128)}, f32[1024,256]{1,0:T(8,128)}, f32[1024,256]{1,0:T(8,128)}) custom-call(s32[4,4]{1,0:T(4,128)} %fusion.80.live_ref, bf16[1024,1024]{1,0:T(8,128)(2,1)} %copy.103.q_ref, bf16[1024,1024]{1,0:T(8,128)(2,1)} %convolution_convert_fusion.8.do_ref, bf16[1024,512]{1,0:T(8,128)(2,1)} %copy.104.k_ref, ...), custom_call_target="tpu_custom_call" | custom-call | flops 1 | bytes 1 | tf_op jit(solution)/shard_map/attend_back/pallas_call | solution.py:624
  421.2 18.8 %attend_back.3 = (f32[1024,512]{1,0:T(8,128)}, f32[1024,256]{1,0:T(8,128)}, f32[1024,256]{1,0:T(8,128)}) custom-call(s32[4,4]{1,0:T(4,128)} %fusion.80.live_ref, bf16[1024,1024]{1,0:T(8,128)(2,1)} %copy.103.q_ref, bf16[1024,1024]{1,0:T(8,128)(2,1)} %convolution_convert_fusion.8.do_ref, bf16[1024,512]{1,0:T(8,128)(2,1)} %copy.104.k_ref, ...), custom_call_target="tpu_custom_call" | custom-call | flops 1 | bytes 1 | tf_op jit(solution)/shard_map/attend_back/pallas_call | solution.py:624
  441.9 2.9 copy.113
  446.9 2.7 multiply_add_fusion
  453.2 3.5 fusion.65
  456.7 5.9 collective-permute-start.40
  463.8 3.9 broadcast_select_fusion.5
  467.7 4.3 collective-permute-start.42
  476.1 6.0 collective-permute-done.44
  486.5 5.0 pad_maximum_fusion
  494.2 6.5 multiply_reduce_fusion.3
  500.8 4.0 broadcast_select_fusion.4
  513.7 4.9 collective-permute-start.48
  525.8 2.7 pad_maximum_fusion.1
  529.8 4.8 convolution_convert_fusion.6
  536.2 9.2 %collective-permute-start.51 = (bf16[4,128,2176]{2,1,0:T(8,128)(2,1)}, bf16[4,128,2176]{2,1,0:T(8,128)(2,1)}, u32[]{:S(2)}, u32[]{:S(2)}) collective-permute-start(bf16[4,128,2176]{2,1,0:T(8,128)(2,1)} %pad_maximum_fusion.4), channel_id=1, source_target_pairs={{0,1},{1,0},{2,3},{3,2},{4,5},{5,4},{6,7},{7,6},{8,9},{9,8},{10,11... | collective-permute-start | bytes 6684680 | tf_op jit(solution)/shard_map/ppermute | solution.py:99
  545.4 3.8 convolution_convert_fusion.7
  554.1 3.2 collective-permute-start.53
  562.7 12.8 %fusion.11 = f32[1152,1024]{1,0:T(8,128)} fusion(bf16[1152,512]{1,0:T(8,128)(2,1)} %collective-permute-done.48, bf16[576,512]{1,0:T(8,128)(2,1)S(1)} %get-tuple-element.419, bf16[576,512]{1,0:T(8,128)(2,1)S(1)} %get-tuple-element.418, pred[]{:T(512)S(6)} %eq.38), kind=kLoop, calls=%fused_computation.48 | loop fusion | flops 16515072 | bytes 7077889 | tf_op jit(solution)/shard_map/convert_element_type | solution.py:461
  575.8 7.2 %collective-permute-done.53 = bf16[64,4608]{1,0:T(8,128)(2,1)} collective-permute-done((bf16[64,4608]{1,0:T(8,128)(2,1)S(1)}, bf16[64,4608]{1,0:T(8,128)(2,1)}, u32[]{:S(2)}, u32[]{:S(2)}) %collective-permute-start.53) | collective-permute-done | bytes 589856 | tf_op jit(solution)/shard_map/ppermute | solution.py:99
  584.5 13.1 %add_multiply_fusion = bf16[1024,1024]{1,0:T(8,128)(2,1)} fusion(f32[1024,1024]{1,0:T(8,128)S(1)} %copy-done.10, f32[1024]{0:T(1024)S(1)} %copy-done.114, bf16[1024,4608]{1,0:T(8,128)(2,1)} %get-tuple-element.298, bf16[4608,1024]{1,0:T(8,128)(2,1)S(1)} %bitcast.162), kind=kOutput, calls=%fused_computation.23 | convolution fusion | flops 9666822144 | bytes 25169920 | tf_op jit(solution)/shard_map/dot_general | solution.py:66
  599.4 2.9 collective-permute-start.56
  609.6 2.5 collective-permute-done.57
  612.1 7.7 %collective-permute-done.58 = bf16[2,64,2176]{2,1,0:T(8,128)(2,1)S(1)} collective-permute-done((bf16[2,64,2176]{2,1,0:T(8,128)(2,1)S(1)}, bf16[2,64,2176]{2,1,0:T(8,128)(2,1)S(1)}, u32[]{:S(2)}, u32[]{:S(2)}) %collective-permute-start.58) | collective-permute-done | bytes 557088 | tf_op jit(solution)/shard_map/ppermute | solution.py:91
  623.8 4.2 collective-permute-done.60
  630.3 2.9 multiply_reduce_fusion.1
  636.6 4.2 collective-permute-start.67
  640.8 9.5 %collective-permute-done.63 = bf16[64,2176]{1,0:T(8,128)(2,1)S(1)} collective-permute-done((bf16[64,2176]{1,0:T(8,128)(2,1)S(1)}, bf16[64,2176]{1,0:T(8,128)(2,1)S(1)}, u32[]{:S(2)}, u32[]{:S(2)}) %collective-permute-start.63) | collective-permute-done | bytes 278560 | tf_op jit(solution)/shard_map/ppermute | solution.py:99
  653.2 4.0 collective-permute-done.64
  659.7 2.8 multiply_reduce_fusion
  (564 shorter events, 192.0 us)
Async XLA Ops:
  6.0 14.5 %collective-permute-start = (bf16[128,2176]{1,0:T(8,128)(2,1)S(1)}, bf16[128,2176]{1,0:T(8,128)(2,1)S(1)}, u32[]{:S(2)}, u32[]{:S(2)}) collective-permute-start(bf16[128,2176]{1,0:T(8,128)(2,1)S(1)} %pad_maximum_fusion.22), channel_id=1, source_target_pairs={{0,8},{1,9},{2,10},{3,11},{4,12},{5,13},{6,14},{7,15},{8,0},{9,1},... | collective-permute-start | bytes 1671176 | tf_op jit(solution)/shard_map/ppermute | solution.py:91
  8.1 13.2 %collective-permute-start.1 = (bf16[128,2176]{1,0:T(8,128)(2,1)S(1)}, bf16[128,2176]{1,0:T(8,128)(2,1)S(1)}, u32[]{:S(2)}, u32[]{:S(2)}) collective-permute-start(bf16[128,2176]{1,0:T(8,128)(2,1)S(1)} %pad_maximum_fusion.22), channel_id=1, source_target_pairs={{0,16},{1,17},{2,18},{3,19},{4,20},{5,21},{6,22},{7,23},{8,24},{9,... | collective-permute-start | bytes 1671176 | tf_op jit(solution)/shard_map/ppermute | solution.py:91
  29.0 8.6 %collective-permute-start.4 = (bf16[3,128,2176]{2,1,0:T(8,128)(2,1)S(1)}, bf16[3,128,2176]{2,1,0:T(8,128)(2,1)S(1)}, u32[]{:S(2)}, u32[]{:S(2)}) collective-permute-start(bf16[3,128,2176]{2,1,0:T(8,128)(2,1)S(1)} %pad_maximum_fusion.7), channel_id=1, source_target_pairs={{0,1},{1,0},{2,3},{3,2},{4,5},{5,4},{6,7},{7,6},{8,9},{9,8},{10,11... | collective-permute-start | bytes 5013512 | tf_op jit(solution)/shard_map/ppermute | solution.py:99
  34.0 58.5 %collective-permute-start.7 = (bf16[128,9216]{1,0:T(8,128)(2,1)}, bf16[128,9216]{1,0:T(8,128)(2,1)S(1)}, u32[]{:S(2)}, u32[]{:S(2)}) collective-permute-start(bf16[128,9216]{1,0:T(8,128)(2,1)} %pad_maximum_fusion.2), channel_id=1, source_target_pairs={{0,8},{1,9},{2,10},{3,11},{4,12},{5,13},{6,14},{7,15},{8,0},{9,1},... | collective-permute-start | bytes 7077896 | tf_op jit(solution)/shard_map/ppermute | solution.py:91
  34.3 58.2 %collective-permute-start.8 = (bf16[128,9216]{1,0:T(8,128)(2,1)}, bf16[128,9216]{1,0:T(8,128)(2,1)}, u32[]{:S(2)}, u32[]{:S(2)}) collective-permute-start(bf16[128,9216]{1,0:T(8,128)(2,1)} %pad_maximum_fusion.2), channel_id=1, source_target_pairs={{0,16},{1,17},{2,18},{3,19},{4,20},{5,21},{6,22},{7,23},{8,24},{9,... | collective-permute-start | bytes 7077896 | tf_op jit(solution)/shard_map/ppermute | solution.py:91
  35.3 57.1 %collective-permute-start.5 = (bf16[128,1024]{1,0:T(8,128)(2,1)}, bf16[128,1024]{1,0:T(8,128)(2,1)}, u32[]{:S(2)}, u32[]{:S(2)}) collective-permute-start(bf16[128,1024]{1,0:T(8,128)(2,1)} %constant_dynamic-slice_fusion.31), channel_id=1, source_target_pairs={{0,8},{1,9},{2,10},{3,11},{4,12},{5,13},{6,14},{7,15},{8,0},{9,1},... | collective-permute-start | bytes 786440 | tf_op jit(solution)/shard_map/ppermute | solution.py:91
  36.4 56.0 %collective-permute-start.6 = (bf16[128,1024]{1,0:T(8,128)(2,1)}, bf16[128,1024]{1,0:T(8,128)(2,1)}, u32[]{:S(2)}, u32[]{:S(2)}) collective-permute-start(bf16[128,1024]{1,0:T(8,128)(2,1)} %constant_dynamic-slice_fusion.31), channel_id=1, source_target_pairs={{0,16},{1,17},{2,18},{3,19},{4,20},{5,21},{6,22},{7,23},{8,24},{9,... | collective-permute-start | bytes 786440 | tf_op jit(solution)/shard_map/ppermute | solution.py:91
  93.7 39.0 %collective-permute-start.11 = (bf16[64,9216]{1,0:T(8,128)(2,1)}, bf16[64,9216]{1,0:T(8,128)(2,1)}, u32[]{:S(2)}, u32[]{:S(2)}) collective-permute-start(bf16[64,9216]{1,0:T(8,128)(2,1)} %slice.219), channel_id=1, source_target_pairs={{0,16},{1,17},{2,18},{3,19},{4,20},{5,21},{6,22},{7,23},{8,24},{9,... | collective-permute-start | bytes 3538952 | tf_op jit(solution)/shard_map/ppermute | solution.py:91
  96.4 36.4 %collective-permute-start.12 = (bf16[64,9216]{1,0:T(8,128)(2,1)}, bf16[64,9216]{1,0:T(8,128)(2,1)}, u32[]{:S(2)}, u32[]{:S(2)}) collective-permute-start(bf16[64,9216]{1,0:T(8,128)(2,1)} %slice.220), channel_id=1, source_target_pairs={{0,8},{1,9},{2,10},{3,11},{4,12},{5,13},{6,14},{7,15},{8,0},{9,1},... | collective-permute-start | bytes 3538952 | tf_op jit(solution)/shard_map/ppermute | solution.py:91
  100.2 32.5 %collective-permute-start.9 = (bf16[64,1024]{1,0:T(8,128)(2,1)}, bf16[64,1024]{1,0:T(8,128)(2,1)}, u32[]{:S(2)}, u32[]{:S(2)}) collective-permute-start(bf16[64,1024]{1,0:T(8,128)(2,1)} %slice.217), channel_id=1, source_target_pairs={{0,16},{1,17},{2,18},{3,19},{4,20},{5,21},{6,22},{7,23},{8,24},{9,... | collective-permute-start | bytes 393224 | tf_op jit(solution)/shard_map/ppermute | solution.py:91
  103.1 29.7 %collective-permute-start.10 = (bf16[64,1024]{1,0:T(8,128)(2,1)}, bf16[64,1024]{1,0:T(8,128)(2,1)S(1)}, u32[]{:S(2)}, u32[]{:S(2)}) collective-permute-start(bf16[64,1024]{1,0:T(8,128)(2,1)} %slice.218), channel_id=1, source_target_pairs={{0,8},{1,9},{2,10},{3,11},{4,12},{5,13},{6,14},{7,15},{8,0},{9,1},... | collective-permute-start | bytes 393224 | tf_op jit(solution)/shard_map/ppermute | solution.py:91
  133.7 35.0 %collective-permute-start.14 = (bf16[128,9216]{1,0:T(8,128)(2,1)S(1)}, bf16[128,9216]{1,0:T(8,128)(2,1)}, u32[]{:S(2)}, u32[]{:S(2)}) collective-permute-start(bf16[128,9216]{1,0:T(8,128)(2,1)S(1)} %collective-permute-done.7.refs_2_.refs_10_), channel_id=1, source_target_pairs={{0,1},{1,0},{2,3},{3,2},{4,5},{5,4},{6,7},{7,6},{8,9},{9,8},{10,11... | collective-permute-start | bytes 7077896 | tf_op jit(solution)/shard_map/ppermute | solution.py:99
  133.8 34.9 %collective-permute-start.15 = (bf16[128,9216]{1,0:T(8,128)(2,1)}, bf16[128,9216]{1,0:T(8,128)(2,1)}, u32[]{:S(2)}, u32[]{:S(2)}) collective-permute-start(bf16[128,9216]{1,0:T(8,128)(2,1)} %collective-permute-done.8.refs_4_.refs_12_), channel_id=1, source_target_pairs={{0,1},{1,0},{2,3},{3,2},{4,5},{5,4},{6,7},{7,6},{8,9},{9,8},{10,11... | collective-permute-start | bytes 7077896 | tf_op jit(solution)/shard_map/ppermute | solution.py:99
  139.0 29.7 %collective-permute-start.16 = (bf16[128,9216]{1,0:T(8,128)(2,1)}, bf16[128,9216]{1,0:T(8,128)(2,1)}, u32[]{:S(2)}, u32[]{:S(2)}) collective-permute-start(bf16[128,9216]{1,0:T(8,128)(2,1)} %constant_dynamic-update-slice_fusion.4.refs_6_.refs_14_), channel_id=1, source_target_pairs={{0,1},{1,0},{2,3},{3,2},{4,5},{5,4},{6,7},{7,6},{8,9},{9,8},{10,11... | collective-permute-start | bytes 7077896 | tf_op jit(solution)/shard_map/ppermute | solution.py:99
  141.8 8.7 %collective-permute-start.13 = (bf16[3,128,1024]{2,1,0:T(8,128)(2,1)}, bf16[3,128,1024]{2,1,0:T(8,128)(2,1)}, u32[]{:S(2)}, u32[]{:S(2)}) collective-permute-start(bf16[3,128,1024]{2,1,0:T(8,128)(2,1)} %pad_maximum_fusion.21), channel_id=1, source_target_pairs={{0,1},{1,0},{2,3},{3,2},{4,5},{5,4},{6,7},{7,6},{8,9},{9,8},{10,11... | collective-permute-start | bytes 2359304 | tf_op jit(solution)/shard_map/ppermute | solution.py:99
  144.6 39.4 %collective-permute-start.17 = (bf16[576,1024]{1,0:T(8,128)(2,1)}, bf16[576,1024]{1,0:T(8,128)(2,1)S(1)}, u32[]{:S(2)}, u32[]{:S(2)}) collective-permute-start(bf16[576,1024]{1,0:T(8,128)(2,1)} %constant_dynamic-slice_fusion.28), channel_id=1, source_target_pairs={{0,8},{1,9},{2,10},{3,11},{4,12},{5,13},{6,14},{7,15},{8,0},{9,1},... | collective-permute-start | bytes 3538952 | tf_op jit(solution)/shard_map/ppermute | solution.py:91
  150.5 33.6 %collective-permute-start.18 = (bf16[576,1024]{1,0:T(8,128)(2,1)}, bf16[576,1024]{1,0:T(8,128)(2,1)}, u32[]{:S(2)}, u32[]{:S(2)}) collective-permute-start(bf16[576,1024]{1,0:T(8,128)(2,1)} %constant_dynamic-slice_fusion.28), channel_id=1, source_target_pairs={{0,16},{1,17},{2,18},{3,19},{4,20},{5,21},{6,22},{7,23},{8,24},{9,... | collective-permute-start | bytes 3538952 | tf_op jit(solution)/shard_map/ppermute | solution.py:91
  184.1 23.6 %collective-permute-start.21 = (bf16[576,1024]{1,0:T(8,128)(2,1)S(1)}, bf16[576,1024]{1,0:T(8,128)(2,1)S(1)}, u32[]{:S(2)}, u32[]{:S(2)}) collective-permute-start(bf16[576,1024]{1,0:T(8,128)(2,1)S(1)} %collective-permute-done.17.refs_2_), channel_id=1, source_target_pairs={{0,1},{1,0},{2,3},{3,2},{4,5},{5,4},{6,7},{7,6},{8,9},{9,8},{10,11... | collective-permute-start | bytes 3538952 | tf_op jit(solution)/shard_map/ppermute | solution.py:99
  185.1 22.5 %collective-permute-start.22 = (bf16[576,1024]{1,0:T(8,128)(2,1)}, bf16[576,1024]{1,0:T(8,128)(2,1)S(1)}, u32[]{:S(2)}, u32[]{:S(2)}) collective-permute-start(bf16[576,1024]{1,0:T(8,128)(2,1)} %collective-permute-done.18.refs_4_), channel_id=1, source_target_pairs={{0,1},{1,0},{2,3},{3,2},{4,5},{5,4},{6,7},{7,6},{8,9},{9,8},{10,11... | collective-permute-start | bytes 3538952 | tf_op jit(solution)/shard_map/ppermute | solution.py:99
  188.0 19.7 %collective-permute-start.19 = (bf16[288,1024]{1,0:T(8,128)(2,1)}, bf16[288,1024]{1,0:T(8,128)(2,1)}, u32[]{:S(2)}, u32[]{:S(2)}) collective-permute-start(bf16[288,1024]{1,0:T(8,128)(2,1)} %slice.225), channel_id=1, source_target_pairs={{0,16},{1,17},{2,18},{3,19},{4,20},{5,21},{6,22},{7,23},{8,24},{9,... | collective-permute-start | bytes 1769480 | tf_op jit(solution)/shard_map/ppermute | solution.py:91
  188.0 19.7 %collective-permute-start.20 = (bf16[288,1024]{1,0:T(8,128)(2,1)}, bf16[288,1024]{1,0:T(8,128)(2,1)}, u32[]{:S(2)}, u32[]{:S(2)}) collective-permute-start(bf16[288,1024]{1,0:T(8,128)(2,1)} %slice.226), channel_id=1, source_target_pairs={{0,8},{1,9},{2,10},{3,11},{4,12},{5,13},{6,14},{7,15},{8,0},{9,1},... | collective-permute-start | bytes 1769480 | tf_op jit(solution)/shard_map/ppermute | solution.py:91
  261.1 12.2 %collective-permute-start.24 = (bf16[4,1152,512]{2,1,0:T(8,128)(2,1)}, bf16[4,1152,512]{2,1,0:T(8,128)(2,1)}, u32[]{:S(2)}, u32[]{:S(2)}) collective-permute-start(bf16[4,1152,512]{2,1,0:T(8,128)(2,1)} %bitcast.27), channel_id=1, source_target_pairs={{0,1},{1,0},{2,3},{3,2},{4,5},{5,4},{6,7},{7,6},{8,9},{9,8},{10,11... | collective-permute-start | bytes 14155784 | tf_op jit(solution)/shard_map/ppermute | solution.py:99
  273.2 37.9 %collective-permute-start.25 = (bf16[4,128,4608]{2,1,0:T(8,128)(2,1)}, bf16[4,128,4608]{2,1,0:T(8,128)(2,1)}, u32[]{:S(2)}, u32[]{:S(2)}) collective-permute-start(bf16[4,128,4608]{2,1,0:T(8,128)(2,1)} %bitcast.30), channel_id=1, source_target_pairs={{0,1},{1,0},{2,3},{3,2},{4,5},{5,4},{6,7},{7,6},{8,9},{9,8},{10,11... | collective-permute-start | bytes 14155784 | tf_op jit(solution)/shard_map/ppermute | solution.py:99
  287.4 33.2 %collective-permute-start.26 = (bf16[4,128,4608]{2,1,0:T(8,128)(2,1)}, bf16[4,128,4608]{2,1,0:T(8,128)(2,1)}, u32[]{:S(2)}, u32[]{:S(2)}) collective-permute-start(bf16[4,128,4608]{2,1,0:T(8,128)(2,1)} %bitcast.32), channel_id=1, source_target_pairs={{0,1},{1,0},{2,3},{3,2},{4,5},{5,4},{6,7},{7,6},{8,9},{9,8},{10,11... | collective-permute-start | bytes 14155784 | tf_op jit(solution)/shard_map/ppermute | solution.py:99
  292.5 27.5 %collective-permute-start.27 = (bf16[2,576,512]{2,1,0:T(8,128)(2,1)S(1)}, bf16[2,576,512]{2,1,0:T(8,128)(2,1)S(1)}, u32[]{:S(2)}, u32[]{:S(2)}) collective-permute-start(bf16[2,576,512]{2,1,0:T(8,128)(2,1)S(1)} %pad_maximum_fusion.8), channel_id=1, source_target_pairs={{0,8},{1,9},{2,10},{3,11},{4,12},{5,13},{6,14},{7,15},{8,0},{9,1},... | collective-permute-start | bytes 3538952 | tf_op jit(solution)/shard_map/ppermute | solution.py:91
  292.7 28.0 %collective-permute-start.28 = (bf16[2,576,512]{2,1,0:T(8,128)(2,1)S(1)}, bf16[2,576,512]{2,1,0:T(8,128)(2,1)S(1)}, u32[]{:S(2)}, u32[]{:S(2)}) collective-permute-start(bf16[2,576,512]{2,1,0:T(8,128)(2,1)S(1)} %pad_maximum_fusion.9), channel_id=1, source_target_pairs={{0,16},{1,17},{2,18},{3,19},{4,20},{5,21},{6,22},{7,23},{8,24},{9,... | collective-permute-start | bytes 3538952 | tf_op jit(solution)/shard_map/ppermute | solution.py:91
  324.0 35.9 %collective-permute-start.29 = (bf16[576,512]{1,0:T(8,128)(2,1)}, bf16[576,512]{1,0:T(8,128)(2,1)}, u32[]{:S(2)}, u32[]{:S(2)}) collective-permute-start(bf16[576,512]{1,0:T(8,128)(2,1)} %get-tuple-element.358), channel_id=1, source_target_pairs={{0,16},{1,17},{2,18},{3,19},{4,20},{5,21},{6,22},{7,23},{8,24},{9,... | collective-permute-start | bytes 1769480 | tf_op jit(solution)/shard_map/ppermute | solution.py:91
  325.5 34.4 %collective-permute-start.30 = (bf16[576,512]{1,0:T(8,128)(2,1)S(1)}, bf16[576,512]{1,0:T(8,128)(2,1)}, u32[]{:S(2)}, u32[]{:S(2)}) collective-permute-start(bf16[576,512]{1,0:T(8,128)(2,1)S(1)} %get-tuple-element.357), channel_id=1, source_target_pairs={{0,8},{1,9},{2,10},{3,11},{4,12},{5,13},{6,14},{7,15},{8,0},{9,1},... | collective-permute-start | bytes 1769480 | tf_op jit(solution)/shard_map/ppermute | solution.py:91
  329.7 58.9 %collective-permute-start.32 = (bf16[2,64,4608]{2,1,0:T(8,128)(2,1)}, bf16[2,64,4608]{2,1,0:T(8,128)(2,1)S(1)}, u32[]{:S(2)}, u32[]{:S(2)}) collective-permute-start(bf16[2,64,4608]{2,1,0:T(8,128)(2,1)} %pad_maximum_fusion.10), channel_id=1, source_target_pairs={{0,8},{1,9},{2,10},{3,11},{4,12},{5,13},{6,14},{7,15},{8,0},{9,1},... | collective-permute-start | bytes 3538952 | tf_op jit(solution)/shard_map/ppermute | solution.py:91
  331.3 57.2 %collective-permute-start.33 = (bf16[2,64,4608]{2,1,0:T(8,128)(2,1)}, bf16[2,64,4608]{2,1,0:T(8,128)(2,1)}, u32[]{:S(2)}, u32[]{:S(2)}) collective-permute-start(bf16[2,64,4608]{2,1,0:T(8,128)(2,1)} %pad_maximum_fusion.11), channel_id=1, source_target_pairs={{0,16},{1,17},{2,18},{3,19},{4,20},{5,21},{6,22},{7,23},{8,24},{9,... | collective-permute-start | bytes 3538952 | tf_op jit(solution)/shard_map/ppermute | solution.py:91
  369.2 19.4 %collective-permute-start.31 = (bf16[4,128,1024]{2,1,0:T(8,128)(2,1)S(1)}, bf16[4,128,1024]{2,1,0:T(8,128)(2,1)S(1)}, u32[]{:S(2)}, u32[]{:S(2)}) collective-permute-start(bf16[4,128,1024]{2,1,0:T(8,128)(2,1)S(1)} %bitcast.209), channel_id=1, source_target_pairs={{0,1},{1,0},{2,3},{3,2},{4,5},{5,4},{6,7},{7,6},{8,9},{9,8},{10,11... | collective-permute-start | bytes 3145736 | tf_op jit(solution)/shard_map/ppermute | solution.py:99
  373.8 14.7 %collective-permute-start.34 = (bf16[576,512]{1,0:T(8,128)(2,1)S(1)}, bf16[576,512]{1,0:T(8,128)(2,1)S(1)}, u32[]{:S(2)}, u32[]{:S(2)}) collective-permute-start(bf16[576,512]{1,0:T(8,128)(2,1)S(1)} %get-tuple-element.342), channel_id=1, source_target_pairs={{0,2},{1,3},{2,0},{3,1},{4,6},{5,7},{6,4},{7,5},{8,10},{9,11},{10,... | collective-permute-start | bytes 1769480 | tf_op jit(solution)/shard_map/ppermute | solution.py:99
  392.7 47.3 %collective-permute-start.38 = (bf16[2,64,4608]{2,1,0:T(8,128)(2,1)}, bf16[2,64,4608]{2,1,0:T(8,128)(2,1)}, u32[]{:S(2)}, u32[]{:S(2)}) collective-permute-start(bf16[2,64,4608]{2,1,0:T(8,128)(2,1)} %pad_maximum_fusion.12), channel_id=1, source_target_pairs={{0,8},{1,9},{2,10},{3,11},{4,12},{5,13},{6,14},{7,15},{8,0},{9,1},... | collective-permute-start | bytes 3538952 | tf_op jit(solution)/shard_map/ppermute | solution.py:91
  395.0 44.9 %collective-permute-start.39 = (bf16[2,64,4608]{2,1,0:T(8,128)(2,1)}, bf16[2,64,4608]{2,1,0:T(8,128)(2,1)}, u32[]{:S(2)}, u32[]{:S(2)}) collective-permute-start(bf16[2,64,4608]{2,1,0:T(8,128)(2,1)} %pad_maximum_fusion.13), channel_id=1, source_target_pairs={{0,16},{1,17},{2,18},{3,19},{4,20},{5,21},{6,22},{7,23},{8,24},{9,... | collective-permute-start | bytes 3538952 | tf_op jit(solution)/shard_map/ppermute | solution.py:91
  398.1 41.8 %collective-permute-start.35 = (bf16[64,4608]{1,0:T(8,128)(2,1)}, bf16[64,4608]{1,0:T(8,128)(2,1)}, u32[]{:S(2)}, u32[]{:S(2)}) collective-permute-start(bf16[64,4608]{1,0:T(8,128)(2,1)} %get-tuple-element.352), channel_id=1, source_target_pairs={{0,16},{1,17},{2,18},{3,19},{4,20},{5,21},{6,22},{7,23},{8,24},{9,... | collective-permute-start | bytes 1769480 | tf_op jit(solution)/shard_map/ppermute | solution.py:91
  399.5 40.4 %collective-permute-start.36 = (bf16[64,4608]{1,0:T(8,128)(2,1)S(1)}, bf16[64,4608]{1,0:T(8,128)(2,1)}, u32[]{:S(2)}, u32[]{:S(2)}) collective-permute-start(bf16[64,4608]{1,0:T(8,128)(2,1)S(1)} %get-tuple-element.351), channel_id=1, source_target_pairs={{0,8},{1,9},{2,10},{3,11},{4,12},{5,13},{6,14},{7,15},{8,0},{9,1},... | collective-permute-start | bytes 1769480 | tf_op jit(solution)/shard_map/ppermute | solution.py:91
  400.0 40.0 %collective-permute-start.37 = (bf16[576,512]{1,0:T(8,128)(2,1)S(1)}, bf16[576,512]{1,0:T(8,128)(2,1)}, u32[]{:S(2)}, u32[]{:S(2)}) collective-permute-start(bf16[576,512]{1,0:T(8,128)(2,1)S(1)} %add_convert_fusion.22), channel_id=1, source_target_pairs={{0,4},{1,5},{2,6},{3,7},{4,0},{5,1},{6,2},{7,3},{8,12},{9,13},{10,... | collective-permute-start | bytes 1769480 | tf_op jit(solution)/shard_map/ppermute | solution.py:99
  456.7 34.8 %collective-permute-start.40 = (bf16[64,4608]{1,0:T(8,128)(2,1)}, bf16[64,4608]{1,0:T(8,128)(2,1)}, u32[]{:S(2)}, u32[]{:S(2)}) collective-permute-start(bf16[64,4608]{1,0:T(8,128)(2,1)} %get-tuple-element.346), channel_id=1, source_target_pairs={{0,16},{1,17},{2,18},{3,19},{4,20},{5,21},{6,22},{7,23},{8,24},{9,... | collective-permute-start | bytes 1769480 | tf_op jit(solution)/shard_map/ppermute | solution.py:91
  462.5 28.9 %collective-permute-start.41 = (bf16[64,4608]{1,0:T(8,128)(2,1)}, bf16[64,4608]{1,0:T(8,128)(2,1)}, u32[]{:S(2)}, u32[]{:S(2)}) collective-permute-start(bf16[64,4608]{1,0:T(8,128)(2,1)} %get-tuple-element.345), channel_id=1, source_target_pairs={{0,8},{1,9},{2,10},{3,11},{4,12},{5,13},{6,14},{7,15},{8,0},{9,1},... | collective-permute-start | bytes 1769480 | tf_op jit(solution)/shard_map/ppermute | solution.py:91
  467.7 23.8 %collective-permute-start.42 = (bf16[64,4608]{1,0:T(8,128)(2,1)}, bf16[64,4608]{1,0:T(8,128)(2,1)}, u32[]{:S(2)}, u32[]{:S(2)}) collective-permute-start(bf16[64,4608]{1,0:T(8,128)(2,1)} %get-tuple-element.339), channel_id=1, source_target_pairs={{0,2},{1,3},{2,0},{3,1},{4,6},{5,7},{6,4},{7,5},{8,10},{9,11},{10,... | collective-permute-start | bytes 1769480 | tf_op jit(solution)/shard_map/ppermute | solution.py:99
  473.1 19.9 %collective-permute-start.43 = (bf16[576,512]{1,0:T(8,128)(2,1)S(1)}, bf16[576,512]{1,0:T(8,128)(2,1)}, u32[]{:S(2)}, u32[]{:S(2)}) collective-permute-start(bf16[576,512]{1,0:T(8,128)(2,1)S(1)} %add_convert_fusion.13), channel_id=1, source_target_pairs={{0,2},{1,3},{2,0},{3,1},{4,6},{5,7},{6,4},{7,5},{8,10},{9,11},{10,... | collective-permute-start | bytes 1769480 | tf_op jit(solution)/shard_map/ppermute | solution.py:99
  473.5 8.6 %collective-permute-start.44 = (bf16[2,64,1024]{2,1,0:T(8,128)(2,1)S(1)}, bf16[2,64,1024]{2,1,0:T(8,128)(2,1)S(1)}, u32[]{:S(2)}, u32[]{:S(2)}) collective-permute-start(bf16[2,64,1024]{2,1,0:T(8,128)(2,1)S(1)} %pad_maximum_fusion.26), channel_id=1, source_target_pairs={{0,8},{1,9},{2,10},{3,11},{4,12},{5,13},{6,14},{7,15},{8,0},{9,1},... | collective-permute-start | bytes 786440 | tf_op jit(solution)/shard_map/ppermute | solution.py:91
  482.1 9.3 %collective-permute-start.45 = (bf16[2,64,1024]{2,1,0:T(8,128)(2,1)}, bf16[2,64,1024]{2,1,0:T(8,128)(2,1)}, u32[]{:S(2)}, u32[]{:S(2)}) collective-permute-start(bf16[2,64,1024]{2,1,0:T(8,128)(2,1)} %pad_maximum_fusion.27), channel_id=1, source_target_pairs={{0,16},{1,17},{2,18},{3,19},{4,20},{5,21},{6,22},{7,23},{8,24},{9,... | collective-permute-start | bytes 786440 | tf_op jit(solution)/shard_map/ppermute | solution.py:91
  504.8 24.8 %collective-permute-start.46 = (bf16[64,4608]{1,0:T(8,128)(2,1)}, bf16[64,4608]{1,0:T(8,128)(2,1)}, u32[]{:S(2)}, u32[]{:S(2)}) collective-permute-start(bf16[64,4608]{1,0:T(8,128)(2,1)} %get-tuple-element.336), channel_id=1, source_target_pairs={{0,2},{1,3},{2,0},{3,1},{4,6},{5,7},{6,4},{7,5},{8,10},{9,11},{10,... | collective-permute-start | bytes 1769480 | tf_op jit(solution)/shard_map/ppermute | solution.py:99
  509.3 20.4 %collective-permute-start.47 = (bf16[64,4608]{1,0:T(8,128)(2,1)}, bf16[64,4608]{1,0:T(8,128)(2,1)}, u32[]{:S(2)}, u32[]{:S(2)}) collective-permute-start(bf16[64,4608]{1,0:T(8,128)(2,1)} %add_convert_fusion.10), channel_id=1, source_target_pairs={{0,4},{1,5},{2,6},{3,7},{4,0},{5,1},{6,2},{7,3},{8,12},{9,13},{10,... | collective-permute-start | bytes 1769480 | tf_op jit(solution)/shard_map/ppermute | solution.py:99
  513.7 16.0 %collective-permute-start.48 = (bf16[1152,512]{1,0:T(8,128)(2,1)}, bf16[1152,512]{1,0:T(8,128)(2,1)}, u32[]{:S(2)}, u32[]{:S(2)}) collective-permute-start(bf16[1152,512]{1,0:T(8,128)(2,1)} %pad_maximum_fusion.14), channel_id=1, source_target_pairs={{0,1},{1,0},{2,3},{3,2},{4,5},{5,4},{6,7},{7,6},{8,9},{9,8},{10,11... | collective-permute-start | bytes 3538952 | tf_op jit(solution)/shard_map/ppermute | solution.py:99
  520.6 9.1 %collective-permute-start.49 = (bf16[64,1024]{1,0:T(8,128)(2,1)}, bf16[64,1024]{1,0:T(8,128)(2,1)S(1)}, u32[]{:S(2)}, u32[]{:S(2)}) collective-permute-start(bf16[64,1024]{1,0:T(8,128)(2,1)} %get-tuple-element.388), channel_id=1, source_target_pairs={{0,16},{1,17},{2,18},{3,19},{4,20},{5,21},{6,22},{7,23},{8,24},{9,... | collective-permute-start | bytes 393224 | tf_op jit(solution)/shard_map/ppermute | solution.py:91
  522.0 7.6 %collective-permute-start.50 = (bf16[64,1024]{1,0:T(8,128)(2,1)}, bf16[64,1024]{1,0:T(8,128)(2,1)}, u32[]{:S(2)}, u32[]{:S(2)}) collective-permute-start(bf16[64,1024]{1,0:T(8,128)(2,1)} %get-tuple-element.387), channel_id=1, source_target_pairs={{0,8},{1,9},{2,10},{3,11},{4,12},{5,13},{6,14},{7,15},{8,0},{9,1},... | collective-permute-start | bytes 393224 | tf_op jit(solution)/shard_map/ppermute | solution.py:91
  536.2 47.6 %collective-permute-start.51 = (bf16[4,128,2176]{2,1,0:T(8,128)(2,1)}, bf16[4,128,2176]{2,1,0:T(8,128)(2,1)}, u32[]{:S(2)}, u32[]{:S(2)}) collective-permute-start(bf16[4,128,2176]{2,1,0:T(8,128)(2,1)} %pad_maximum_fusion.4), channel_id=1, source_target_pairs={{0,1},{1,0},{2,3},{3,2},{4,5},{5,4},{6,7},{7,6},{8,9},{9,8},{10,11... | collective-permute-start | bytes 6684680 | tf_op jit(solution)/shard_map/ppermute | solution.py:99
  552.6 23.2 %collective-permute-start.52 = (bf16[64,1024]{1,0:T(8,128)(2,1)S(1)}, bf16[64,1024]{1,0:T(8,128)(2,1)S(1)}, u32[]{:S(2)}, u32[]{:S(2)}) collective-permute-start(bf16[64,1024]{1,0:T(8,128)(2,1)S(1)} %get-tuple-element.333), channel_id=1, source_target_pairs={{0,2},{1,3},{2,0},{3,1},{4,6},{5,7},{6,4},{7,5},{8,10},{9,11},{10,... | collective-permute-start | bytes 393224 | tf_op jit(solution)/shard_map/ppermute | solution.py:99
  554.1 28.8 %collective-permute-start.53 = (bf16[64,4608]{1,0:T(8,128)(2,1)S(1)}, bf16[64,4608]{1,0:T(8,128)(2,1)}, u32[]{:S(2)}, u32[]{:S(2)}) collective-permute-start(bf16[64,4608]{1,0:T(8,128)(2,1)S(1)} %add_convert_fusion.9), channel_id=1, source_target_pairs={{0,4},{1,5},{2,6},{3,7},{4,0},{5,1},{6,2},{7,3},{8,12},{9,13},{10,... | collective-permute-start | bytes 1769480 | tf_op jit(solution)/shard_map/ppermute | solution.py:99
  558.7 24.2 %collective-permute-start.54 = (bf16[64,4608]{1,0:T(8,128)(2,1)S(1)}, bf16[64,4608]{1,0:T(8,128)(2,1)S(1)}, u32[]{:S(2)}, u32[]{:S(2)}) collective-permute-start(bf16[64,4608]{1,0:T(8,128)(2,1)S(1)} %add_convert_fusion.8), channel_id=1, source_target_pairs={{0,2},{1,3},{2,0},{3,1},{4,6},{5,7},{6,4},{7,5},{8,10},{9,11},{10,... | collective-permute-start | bytes 1769480 | tf_op jit(solution)/shard_map/ppermute | solution.py:99
  598.9 20.9 %collective-permute-start.55 = (bf16[64,4608]{1,0:T(8,128)(2,1)S(1)}, bf16[64,4608]{1,0:T(8,128)(2,1)S(1)}, u32[]{:S(2)}, u32[]{:S(2)}) collective-permute-start(bf16[64,4608]{1,0:T(8,128)(2,1)S(1)} %add_convert_fusion.7), channel_id=1, source_target_pairs={{0,2},{1,3},{2,0},{3,1},{4,6},{5,7},{6,4},{7,5},{8,10},{9,11},{10,... | collective-permute-start | bytes 1769480 | tf_op jit(solution)/shard_map/ppermute | solution.py:99
  599.4 20.4 %collective-permute-start.56 = (bf16[128,4608]{1,0:T(8,128)(2,1)S(1)}, bf16[128,4608]{1,0:T(8,128)(2,1)S(1)}, u32[]{:S(2)}, u32[]{:S(2)}) collective-permute-start(bf16[128,4608]{1,0:T(8,128)(2,1)S(1)} %pad_maximum_fusion.15), channel_id=1, source_target_pairs={{0,1},{1,0},{2,3},{3,2},{4,5},{5,4},{6,7},{7,6},{8,9},{9,8},{10,11... | collective-permute-start | bytes 3538952 | tf_op jit(solution)/shard_map/ppermute | solution.py:99
  602.3 9.8 %collective-permute-start.57 = (bf16[64,1024]{1,0:T(8,128)(2,1)S(1)}, bf16[64,1024]{1,0:T(8,128)(2,1)S(1)}, u32[]{:S(2)}, u32[]{:S(2)}) collective-permute-start(bf16[64,1024]{1,0:T(8,128)(2,1)S(1)} %add_convert_fusion.53), channel_id=1, source_target_pairs={{0,4},{1,5},{2,6},{3,7},{4,0},{5,1},{6,2},{7,3},{8,12},{9,13},{10,... | collective-permute-start | bytes 393224 | tf_op jit(solution)/shard_map/ppermute | solution.py:99
  605.8 14.0 %collective-permute-start.58 = (bf16[2,64,2176]{2,1,0:T(8,128)(2,1)S(1)}, bf16[2,64,2176]{2,1,0:T(8,128)(2,1)S(1)}, u32[]{:S(2)}, u32[]{:S(2)}) collective-permute-start(bf16[2,64,2176]{2,1,0:T(8,128)(2,1)S(1)} %pad_maximum_fusion.23), channel_id=1, source_target_pairs={{0,8},{1,9},{2,10},{3,11},{4,12},{5,13},{6,14},{7,15},{8,0},{9,1},... | collective-permute-start | bytes 1671176 | tf_op jit(solution)/shard_map/ppermute | solution.py:91
  606.0 13.8 %collective-permute-start.59 = (bf16[2,64,2176]{2,1,0:T(8,128)(2,1)S(1)}, bf16[2,64,2176]{2,1,0:T(8,128)(2,1)S(1)}, u32[]{:S(2)}, u32[]{:S(2)}) collective-permute-start(bf16[2,64,2176]{2,1,0:T(8,128)(2,1)S(1)} %pad_maximum_fusion.24), channel_id=1, source_target_pairs={{0,16},{1,17},{2,18},{3,19},{4,20},{5,21},{6,22},{7,23},{8,24},{9,... | collective-permute-start | bytes 1671176 | tf_op jit(solution)/shard_map/ppermute | solution.py:91
  621.1 6.9 %collective-permute-start.60 = (bf16[64,2176]{1,0:T(8,128)(2,1)S(1)}, bf16[64,2176]{1,0:T(8,128)(2,1)S(1)}, u32[]{:S(2)}, u32[]{:S(2)}) collective-permute-start(bf16[64,2176]{1,0:T(8,128)(2,1)S(1)} %get-tuple-element.364), channel_id=1, source_target_pairs={{0,8},{1,9},{2,10},{3,11},{4,12},{5,13},{6,14},{7,15},{8,0},{9,1},... | collective-permute-start | bytes 835592 | tf_op jit(solution)/shard_map/ppermute | solution.py:91
  622.4 6.4 collective-permute-start.61
  623.5 13.0 %collective-permute-start.66 = (bf16[64,1024]{1,0:T(8,128)(2,1)S(1)}, bf16[64,1024]{1,0:T(8,128)(2,1)S(1)}, u32[]{:S(2)}, u32[]{:S(2)}) collective-permute-start(bf16[64,1024]{1,0:T(8,128)(2,1)S(1)} %add_convert_fusion.52), channel_id=1, source_target_pairs={{0,2},{1,3},{2,0},{3,1},{4,6},{5,7},{6,4},{7,5},{8,10},{9,11},{10,... | collective-permute-start | bytes 393224 | tf_op jit(solution)/shard_map/ppermute | solution.py:99
  635.8 14.6 %collective-permute-start.63 = (bf16[64,2176]{1,0:T(8,128)(2,1)S(1)}, bf16[64,2176]{1,0:T(8,128)(2,1)S(1)}, u32[]{:S(2)}, u32[]{:S(2)}) collective-permute-start(bf16[64,2176]{1,0:T(8,128)(2,1)S(1)} %add_convert_fusion.41), channel_id=1, source_target_pairs={{0,4},{1,5},{2,6},{3,7},{4,0},{5,1},{6,2},{7,3},{8,12},{9,13},{10,... | collective-permute-start | bytes 835592 | tf_op jit(solution)/shard_map/ppermute | solution.py:99
  636.6 15.5 %collective-permute-start.67 = (bf16[128,1024]{1,0:T(8,128)(2,1)S(1)}, bf16[128,1024]{1,0:T(8,128)(2,1)S(1)}, u32[]{:S(2)}, u32[]{:S(2)}) collective-permute-start(bf16[128,1024]{1,0:T(8,128)(2,1)S(1)} %pad_maximum_fusion.28), channel_id=1, source_target_pairs={{0,1},{1,0},{2,3},{3,2},{4,5},{5,4},{6,7},{7,6},{8,9},{9,8},{10,11... | collective-permute-start | bytes 786440 | tf_op jit(solution)/shard_map/ppermute | solution.py:99
  650.4 6.8 %collective-permute-start.64 = (bf16[64,2176]{1,0:T(8,128)(2,1)S(1)}, bf16[64,2176]{1,0:T(8,128)(2,1)S(1)}, u32[]{:S(2)}, u32[]{:S(2)}) collective-permute-start(bf16[64,2176]{1,0:T(8,128)(2,1)S(1)} %add_convert_fusion.40), channel_id=1, source_target_pairs={{0,2},{1,3},{2,0},{3,1},{4,6},{5,7},{6,4},{7,5},{8,10},{9,11},{10,... | collective-permute-start | bytes 835592 | tf_op jit(solution)/shard_map/ppermute | solution.py:99
  650.6 9.1 %collective-permute-start.68 = (bf16[128,4608]{1,0:T(8,128)(2,1)S(1)}, bf16[128,4608]{1,0:T(8,128)(2,1)S(1)}, u32[]{:S(2)}, u32[]{:S(2)}) collective-permute-start(bf16[128,4608]{1,0:T(8,128)(2,1)S(1)} %pad_maximum_fusion.16), channel_id=1, source_target_pairs={{0,1},{1,0},{2,3},{3,2},{4,5},{5,4},{6,7},{7,6},{8,9},{9,8},{10,11... | collective-permute-start | bytes 3538952 | tf_op jit(solution)/shard_map/ppermute | solution.py:99
  (149 other events, 1165.6 us)

commit v7 on v6

--- a/solution.py
+++ b/solution.py
@@ -38,19 +38,6 @@
         [
             first_half * cosine - second_half * sine_table,
             second_half * cosine + first_half * sine_table,
-        ],
-        axis=-1,
-    )
-
-
-def rotate_back(grad_vals, cosine, sine_table):
-    half_dim = HD // 2
-    first_half = grad_vals[..., :half_dim]
-    second_half = grad_vals[..., half_dim:]
-    return jnp.concatenate(
-        [
-            first_half * cosine + second_half * sine_table,
-            second_half * cosine - first_half * sine_table,
         ],
         axis=-1,
     )
@@ -509,9 +496,32 @@
         o_ref[:, group * 2 * HD : (group + 1) * 2 * HD] = (top / total).astype(o_ref.dtype)
 
 
+def head_norm_back(grad, linear, turn, gain):
+    half = HD // 2
+    cosine, sine = turn[:half], turn[half:]
+    gain_1, gain_2 = gain[:half], gain[half:]
+    parts, sums = [], None
+    for begin in range(0, grad.shape[0], HD):
+        grad_1, grad_2 = grad[begin : begin + half], grad[begin + half : begin + HD]
+        lin_1, lin_2 = linear[begin : begin + half], linear[begin + half : begin + HD]
+        back_1 = grad_1 * cosine + grad_2 * sine
+        back_2 = grad_2 * cosine - grad_1 * sine
+        square = jnp.sum(lin_1 * lin_1 + lin_2 * lin_2, axis=0, keepdims=True)
+        scale = lax.rsqrt(square * (1.0 / HD) + norm_eps)
+        unit_1, unit_2 = lin_1 * scale, lin_2 * scale
+        both = jnp.concatenate([back_1 * unit_1, back_2 * unit_2], axis=0)
+        sums = both if sums is None else sums + both
+        back_1, back_2 = back_1 * gain_1, back_2 * gain_2
+        inner = jnp.sum(back_1 * unit_1 + back_2 * unit_2, axis=0, keepdims=True) * (1.0 / HD)
+        parts += [scale * (back_1 - unit_1 * inner), scale * (back_2 - unit_2 * inner)]
+    return jnp.concatenate(parts, axis=0), sums
+
+
 def attend_back_kernel(
     live_ref, q_ref, do_ref, k_ref, v_ref, seg_col_ref, seg_row_ref,
-    dq_ref, dk_ref, dv_ref, exp_ref, dp_ref, total_ref, inner_ref, dqt_ref,
+    q_lin_ref, k_lin_ref, q_turn_ref, k_turn_ref, gain_ref,
+    dq_out_ref, dk_out_ref, dv_out_ref, q_gain_ref, k_gain_ref,
+    exp_ref, dp_ref, total_ref, inner_ref, dqt_ref, dk_ref, dv_ref,
 ):
     at = pl.program_id(1)
 
@@ -519,6 +529,7 @@
     def _():
         dk_ref[...] = jnp.zeros_like(dk_ref)
         dv_ref[...] = jnp.zeros_like(dv_ref)
+        q_gain_ref[...] = jnp.zeros_like(q_gain_ref)
 
     total_ref[...] = jnp.zeros_like(total_ref)
     inner_ref[...] = jnp.zeros_like(inner_ref)
@@ -582,7 +593,24 @@
 
     each_block(first)
     each_block(second)
-    dq_ref[...] = dqt_ref[...].T
+    grad, gain_sum = head_norm_back(
+        dqt_ref[...] * (1.0 / math.sqrt(HD)), q_lin_ref[...].T, q_turn_ref[...], gain_ref[:HD]
+    )
+    q_gain_ref[0] += gain_sum
+    dq_out_ref[...] = grad.T.astype(jnp.bfloat16)
+
+    @pl.when(at == pl.num_programs(1) - 1)
+    def _():
+        dv_out_ref[...] = dv_ref[...].astype(jnp.bfloat16)
+        key_sum = None
+        for begin in range(0, dk_ref.shape[0], BLOCK):
+            rows = slice(begin, begin + BLOCK)
+            grad, gain_sum = head_norm_back(
+                dk_ref[rows].T, k_lin_ref[rows].T, k_turn_ref[:, rows], gain_ref[HD:]
+            )
+            dk_out_ref[rows] = grad.T.astype(jnp.bfloat16)
+            key_sum = gain_sum if key_sum is None else key_sum + gain_sum
+        k_gain_ref[0] = key_sum
 
 
 def live_blocks(segment):
@@ -618,15 +646,17 @@
     )(live_blocks(segment), query, key, value, segment[:, None], segment[None, :])
 
 
-def attend_back(query, grad_out, key, value, segment, start, panels):
+def attend_back(query, grad_out, key, value, segment, query_lin, key_lin, turn, gain, start, panels):
     rows = query.shape[0]
     count = rows // BLOCK
     return pl.pallas_call(
         attend_back_kernel,
         out_shape=(
-            jax.ShapeDtypeStruct((rows, panels * 4 * HD), jnp.float32),
-            jax.ShapeDtypeStruct((rows, panels * 2 * HD), jnp.float32),
-            jax.ShapeDtypeStruct((rows, panels * 2 * HD), jnp.float32),
+            jax.ShapeDtypeStruct((rows, panels * 4 * HD), jnp.bfloat16),
+            jax.ShapeDtypeStruct((rows, panels * 2 * HD), jnp.bfloat16),
+            jax.ShapeDtypeStruct((rows, panels * 2 * HD), jnp.bfloat16),
+            jax.ShapeDtypeStruct((panels, HD, BLOCK), jnp.float32),
+            jax.ShapeDtypeStruct((panels, HD, BLOCK), jnp.float32),
         ),
         grid_spec=pltpu.PrefetchScalarGridSpec(
             num_scalar_prefetch=1,
@@ -638,11 +668,18 @@
                 pl.BlockSpec((rows, 2 * HD), lambda p, i, live: (0, start + p)),
                 pl.BlockSpec((rows, 1), lambda p, i, live: (0, 0)),
                 pl.BlockSpec((1, BLOCK), lambda p, i, live: (0, i)),
+                pl.BlockSpec((BLOCK, 4 * HD), lambda p, i, live: (i, start + p)),
+                pl.BlockSpec((rows, 2 * HD), lambda p, i, live: (0, start + p)),
+                pl.BlockSpec((HD, BLOCK), lambda p, i, live: (0, i)),
+                pl.BlockSpec((HD, rows), lambda p, i, live: (0, 0)),
+                pl.BlockSpec((2 * HD, 1), lambda p, i, live: (0, 0)),
             ],
             out_specs=[
                 pl.BlockSpec((BLOCK, 4 * HD), lambda p, i, live: (i, p)),
                 pl.BlockSpec((rows, 2 * HD), lambda p, i, live: (0, p)),
                 pl.BlockSpec((rows, 2 * HD), lambda p, i, live: (0, p)),
+                pl.BlockSpec((1, HD, BLOCK), lambda p, i, live: (p, 0, 0)),
+                pl.BlockSpec((1, HD, BLOCK), lambda p, i, live: (p, 0, 0)),
             ],
             scratch_shapes=[
                 pltpu.VMEM((4, LOOK, BLOCK, BLOCK), jnp.float32),
@@ -650,11 +687,14 @@
                 pltpu.VMEM((8, BLOCK), jnp.float32),
                 pltpu.VMEM((8, BLOCK), jnp.float32),
                 pltpu.VMEM((4 * HD, BLOCK), jnp.float32),
+                pltpu.VMEM((rows, 2 * HD), jnp.float32),
+                pltpu.VMEM((rows, 2 * HD), jnp.float32),
             ],
         ),
         cost_estimate=TINY,
         name="attend_back",
-    )(live_blocks(segment), query, grad_out, key, value, segment[:, None], segment[None, :])
+    )(live_blocks(segment), query, grad_out, key, value, segment[:, None], segment[None, :],
+      query_lin, key_lin, turn, turn, gain)
 
 
 def body(
@@ -690,10 +730,10 @@
         )
     )
     w_out, w_gate, w_up, w_down = sync((w_out, w_gate, w_up, w_down), front_flow)
+    out_flow = Flow(gather_steps(links, core_half(w_out), w_out, late="joined"))
+    w_gate, w_up, w_down = sync((w_gate, w_up, w_down), front_flow)
     pair = jnp.concatenate([core_half(w_gate), core_half(w_up)], axis=1)
     pair_flow = Flow(gather_steps(links, pair, None, late=True))
-    w_out, w_down = sync((w_out, w_down), front_flow)
-    out_flow = Flow(gather_steps(links, core_half(w_out), w_out, late="joined"))
     w_down = sync(w_down, front_flow)
     front = place_blocks(front_flow.finish())
     full_query = front[:, : HQ * HD]
@@ -731,7 +771,7 @@
     key_rot = key_rot.reshape(row_count, HK * HD)
     value_low = value_low.reshape(row_count, HK * HD)
     query_rot, key_rot, value_low, w_down = sync(
-        (query_rot, key_rot, value_low, w_down), out_flow, pair_flow
+        (query_rot, key_rot, value_low, w_down), out_flow
     )
     attn_low = attend(query_rot, key_rot, value_low, segment)
     attn_low, w_down = sync((attn_low, w_down), out_flow, pair_flow)
@@ -799,44 +839,20 @@
         (grad_attn_low, out_given, out_sent, up_given, up_sent), gate_back, down_back
     )
     up_back = Flow(scatter_steps(links, up_given, up_sent))
-    lower = attend_back(query_rot, grad_attn_low, key_rot, value_low, segment, 0, panels)
+    turn = jnp.concatenate([cosine[:, 0].T, sine_table[:, 0].T], axis=0)
+    flat = (query_lin.reshape(row_count, -1), key_lin.reshape(row_count, -1), turn, qk_gains[:, None])
+    lower = attend_back(query_rot, grad_attn_low, key_rot, value_low, segment, *flat, 0, panels)
     grad_attn_low, lower = pin((grad_attn_low, lower))
-    upper = attend_back(query_rot, grad_attn_low, key_rot, value_low, segment, panels, panels)
+    upper = attend_back(query_rot, grad_attn_low, key_rot, value_low, segment, *flat, panels, panels)
     lower, upper, out_given, out_sent = sync(
         (lower, upper, out_given, out_sent), gate_back, down_back, up_back
     )
     out_back = Flow(scatter_steps(links, out_given, out_sent))
-    grad_query_rot, grad_key_rot, grad_value = (
-        jnp.concatenate(pair, axis=1) for pair in zip(lower, upper)
-    )
-    grad_query_rot = (score_scale * grad_query_rot).reshape(row_count, HQ, HD)
-    grad_key_rot = grad_key_rot.reshape(row_count, HK, HD)
-    grad_query_norm = rotate_back(grad_query_rot, cosine, sine_table)
-    grad_key_norm = rotate_back(grad_key_rot, cosine, sine_table)
-    grad_query_norm, grad_key_norm = sync(
-        (grad_query_norm, grad_key_norm), up_back, gate_back, down_back, out_back
-    )
-    back_gains = full_qk_gain.astype(jnp.float32)
     grad_qk_gain = jnp.concatenate(
-        [
-            jnp.sum(grad_query_norm * query_lin * query_scale, axis=(0, 1)),
-            jnp.sum(grad_key_norm * key_lin * key_scale, axis=(0, 1)),
-        ]
-    )
-    grad_query_low = (
-        norm_back(grad_query_norm, query_lin, query_scale, back_gains[:HD])
-        .astype(jnp.bfloat16)
-        .reshape(row_count, HQ * HD)
-    )
-    grad_key_low = (
-        norm_back(grad_key_norm, key_lin, key_scale, back_gains[HD:])
-        .astype(jnp.bfloat16)
-        .reshape(row_count, HK * HD)
-    )
-    grad_value_low = grad_value.astype(jnp.bfloat16).reshape(row_count, HK * HD)
+        [jnp.sum(lower[at] + upper[at], axis=(0, 2)) for at in (3, 4)]
+    )
+    grad_front = jnp.concatenate([part for at in range(3) for part in (lower[at], upper[at])], axis=1)
     normed_own, normed_other = pick_columns(links, normed)
-    grad_front = jnp.concatenate([grad_query_low, grad_key_low, grad_value_low], axis=1)
-    grad_front = sync(grad_front, up_back, gate_back, down_back, out_back)
     front_other = blocked(links, matmul_rows(normed_other, grad_front))
     front_own = blocked(links, matmul_rows(normed_own, grad_front))
     front_other, front_own = (part.astype(jnp.bfloat16) for part in (front_other, front_own))

time: 673 us -> 665 us (0.988)
  other arithmetic: 137 us -> 97.9 us
  waiting for transfers between devices: 99 us -> 123 us
  Pallas kernels: 169 us -> 177 us
    ppermute x33, waiting for transfers between devices: 33.4 us -> 72.6 us  [rep_swap(): return lax.ppermute(value, axes, pairs)]
    ppermute x36, waiting for transfers between devices: 65.7 us -> 50.6 us  [shard_swap(): return lax.ppermute(value, axes, pairs)]
    concatenate x4 -> x1, other arithmetic: 10.7 us -> 0.71 us  [body(): turn = jnp.concatenate([cosine[:, 0].T, sine_table[:, 0].T], axis=0)]
    dot_general x0 -> x2, local copies, waits for them, and re-layouts: none -> 8.4 us  [matmul_plain(): return jnp.dot(left_mat, right_mat, preferred_element_type=jnp.float32)]
    pallas_call x2, Pallas kernels: 37.2 us -> 45.1 us  [attend_back(): pl.pallas_call(attend_back_kernel, out_shape=(jax.ShapeDtypeStruct((rows,...]
    reduce_sum x4 -> x2, other arithmetic: 12.2 us -> 4.7 us  [norm_back(): row_inner = jnp.mean(weighted * inputs, axis=-1, keepdims=True)]
    unnamed x294 -> x255, local copies, waits for them, and re-layouts: 13.9 us -> 13.4 us
  transfers between devices with their start and end apart: 69 -> 69, of which waited for: 18 -> 24; matrix products, arithmetic and copies ran while one was open for 31% -> 29% of each run, Pallas kernels for 20% -> 22%
where the time goes in v7:
time: 665 us; the launch traced here: 660 us
  Pallas kernels  177 us (27%)
  waiting for transfers between devices  123 us (18%)
  matrix products  101 us (15%)
  other arithmetic  97.9 us (15%)
  starting transfers between devices  95.8 us (14%)
  local copies, waits for them, and re-layouts  62.2 us (9%)
    ppermute x33, waiting for transfers between devices, rep_swap(): return lax.ppermute(value, axes, pairs)  72.6 us
    dot_general x10, matrix products, matmul_rows(): lax.dot_general(left_mat, right_mat, (((0,), (0,)), ((), ())), preferred_...  62.7 us
    ppermute x33, starting transfers between devices, rep_swap(): return lax.ppermute(value, axes, pairs)  51.2 us
    ppermute x36, waiting for transfers between devices, shard_swap(): return lax.ppermute(value, axes, pairs)  50.6 us
    pallas_call x2, Pallas kernels, attend_back(): pl.pallas_call(attend_back_kernel, out_shape=(jax.ShapeDtypeStruct((rows,...  45.1 us
    ppermute x36, starting transfers between devices, shard_swap(): return lax.ppermute(value, axes, pairs)  44.6 us
    pallas_call x2, Pallas kernels, ffn_forward(): pl.pallas_call(functools.partial(ffn_forward_kernel, count, len(into)), o...  33.2 us
    pallas_call x1, Pallas kernels, ffn_input(): pl.pallas_call(functools.partial(ffn_input_kernel, count), out_shape=jax....  28.5 us
  transfers between devices with their start and end apart: 69, of which 24 were waited for; matrix products, arithmetic and copies ran while one was open for 29% of the time, Pallas kernels for 22%

profile of v7, /device:TPU:1, one launch (start us, length us, event | category | flops | bytes accessed | tf_op | source)
XLA Modules:
  0.0 659.9 jit_solution(2911271017382627889)
XLA Ops:
  12.8 7.7 %collective-permute-done.refs_2_ = bf16[128,2176]{1,0:T(8,128)(2,1)S(1)} collective-permute-done((bf16[128,2176]{1,0:T(8,128)(2,1)S(1)}, bf16[128,2176]{1,0:T(8,128)(2,1)S(1)}, u32[]{:S(2)}, u32[]{:S(2)}) %collective-permute-start) | collective-permute-done | bytes 557088 | tf_op jit(solution)/shard_map/ppermute | solution.py:78
  29.0 5.3 collective-permute-start.4
  38.7 7.0 %place_blocks.3 = bf16[1024,2176]{1,0:T(8,128)(2,1)} custom-call(s32[8]{0:T(128)} %stack.70.spots_ref, bf16[256,2176]{1,0:T(8,128)(2,1)} %pad_maximum_fusion.13.refs_0_.refs_1_, bf16[256,2176]{1,0:T(8,128)(2,1)} %pad_maximum_fusion.13.refs_0_.refs_1_, bf16[128,2176]{1,0:T(8,128)(2,1)} %copy-done.24, bf16[128,2176]{1,0:T(8,128)(2,1)} %get-tuple-element.399.refs_3_, ...), custom_call_target="tpu_custom_call" | custom-call | flops 1 | bytes 1 | tf_op jit(solution)/shard_map/place_blocks/pallas_call | solution.py:141
  49.4 4.4 multiply_reduce_fusion.4
  53.9 2.6 multiply_reduce_fusion.5
  72.1 3.9 copy.106.q_ref
  77.4 23.8 %attend.1 = bf16[1024,1024]{1,0:T(8,128)(2,1)} custom-call(s32[4,4]{1,0:T(4,128)} %fusion.80.live_ref, bf16[1024,1024]{1,0:T(8,128)(2,1)} %copy.106.q_ref, bf16[1024,512]{1,0:T(8,128)(2,1)} %copy.107.k_ref, bf16[1024,512]{1,0:T(8,128)(2,1)} %convolution_convert_fusion.11.v_ref, s32[1024,1]{1,0:T(8,128)} %copy.108.seg_col_ref, s32[1,1024]{1,0:T(1,128)} %bitcast.190), custom_call_target="tpu_custom_call" | custom-call | flops 1 | bytes 1 | tf_op jit(solution)/shard_map/attend/pallas_call | solution.py:628
  104.7 4.1 collective-permute-start.12
  111.2 2.5 collective-permute-start.13
  114.6 5.3 place_blocks.4
  119.9 5.3 multiply_reduce_fusion.3
  128.0 7.5 %collective-permute-done.12 = bf16[64,9216]{1,0:T(8,128)(2,1)S(1)} collective-permute-done((bf16[64,9216]{1,0:T(8,128)(2,1)}, bf16[64,9216]{1,0:T(8,128)(2,1)S(1)}, u32[]{:S(2)}, u32[]{:S(2)}) %collective-permute-start.12) | collective-permute-done | bytes 1179680 | tf_op jit(solution)/shard_map/ppermute | solution.py:78
  135.4 4.1 collective-permute-done.13
  148.8 3.4 collective-permute-done.16.refs_7_.refs_15_
  152.2 15.3 %ffn_forward.2 = (bf16[1024,4608]{1,0:T(8,128)(2,1)}, bf16[1024,4608]{1,0:T(8,128)(2,1)}, bf16[1024,4608]{1,0:T(8,128)(2,1)}) custom-call(s32[8]{0:T(128)} %stack.70.spots_ref, bf16[1024,1024]{1,0:T(8,128)(2,1)} %multiply_convert_fusion.a_ref, bf16[256,4608]{1,0:T(8,128)(2,1)} %refs_1_.4, bf16[256,4608]{1,0:T(8,128)(2,1)} %refs_1_.4, ...), custom_call_target="tpu_custom_call" | custom-call | flops 1 | bytes 1 | tf_op jit(solution)/shard_map/ffn_forward/pallas_call | solution.py:205
  167.4 7.8 %collective-permute-done.17.refs_2_ = bf16[576,1024]{1,0:T(8,128)(2,1)S(1)} collective-permute-done((bf16[576,1024]{1,0:T(8,128)(2,1)}, bf16[576,1024]{1,0:T(8,128)(2,1)S(1)}, u32[]{:S(2)}, u32[]{:S(2)}) %collective-permute-start.17) | collective-permute-done | bytes 1179680 | tf_op jit(solution)/shard_map/ppermute | solution.py:78
  180.3 18.0 %ffn_forward.3 = (bf16[1024,4608]{1,0:T(8,128)(2,1)}, bf16[1024,4608]{1,0:T(8,128)(2,1)}, bf16[1024,4608]{1,0:T(8,128)(2,1)}) custom-call(s32[8]{0:T(128)} %stack.70.spots_ref, bf16[1024,1024]{1,0:T(8,128)(2,1)} %multiply_convert_fusion.a_ref, bf16[256,4608]{1,0:T(8,128)(2,1)} %refs_1_.4, ...), custom_call_target="tpu_custom_call", output_to_operand_aliasing={{0}: (18, {}), {1}: (19, {}), {2}: (20, {})} | custom-call | flops 1 | bytes 1 | tf_op jit(solution)/shard_map/ffn_forward/pallas_call | solution.py:205
  204.5 9.4 %place_blocks.5.down_ref = bf16[4608,1024]{1,0:T(8,128)(2,1)} custom-call(s32[8]{0:T(128)} %stack.70.spots_ref, bf16[1152,1024]{1,0:T(8,128)(2,1)} %refs_1_.3, bf16[1152,1024]{1,0:T(8,128)(2,1)} %refs_1_.3, bf16[576,1024]{1,0:T(8,128)(2,1)} %copy-done.30, bf16[576,1024]{1,0:T(8,128)(2,1)} %collective-permute-done.21.refs_3_, ...), custom_call_target="tpu_custom_call" | custom-call | flops 1 | bytes 1 | tf_op jit(solution)/shard_map/place_blocks/pallas_call | solution.py:141
  213.9 24.8 %ffn_inner.1 = (bf16[1024,4608]{1,0:T(8,128)(2,1)}, bf16[1024,4608]{1,0:T(8,128)(2,1)}) custom-call(bf16[1024,1024]{1,0:T(8,128)(2,1)} %copy-done.12, bf16[4608,1024]{1,0:T(8,128)(2,1)} %place_blocks.5.down_ref, bf16[1024,4608]{1,0:T(8,128)(2,1)} %get-tuple-element.213.act_ref, bf16[1024,4608]{1,0:T(8,128)(2,1)} %get-tuple-element.214.slope_ref), custom_call_target="tpu_custom_call" | custom-call | flops 1 | bytes 1 | tf_op jit(solution)/shard_map/ffn_inner/pallas_call | solution.py:238
  238.7 10.8 %convolution_convert_fusion.1 = bf16[4608,512]{1,0:T(8,128)(2,1)} fusion(bf16[1024,4608]{1,0:T(8,128)(2,1)} %get-tuple-element.289, bf16[1024,512]{1,0:T(8,128)(2,1)S(1)} %copy-done.53), kind=kOutput, calls=%fused_computation.6 | convolution fusion | flops 4834197504 | bytes 15204352 | tf_op jit(solution)/shard_map/dot_general | solution.py:57
  250.6 10.9 %convolution_convert_fusion.5 = bf16[512,4608]{1,0:T(8,128)(2,1)} fusion(bf16[1024,4608]{1,0:T(8,128)(2,1)} %get-tuple-element.233.dgate_ref, bf16[1024,128]{1,0:T(8,128)(2,1)S(1)} %get-tuple-element.391, bf16[1024,128]{1,0:T(8,128)(2,1)S(1)} %get-tuple-element.392, bf16[1024,128]{1,0:T(8,128)(2,1)S(1)} %get-tuple-element.393, ...), kind=kOutput, calls=%fused_computation.10 | convolution fusion | flops 4838391808 | bytes 15204352 | tf_op jit(solution)/shard_map/dot_general | solution.py:57
  261.7 6.9 %convolution_convert_fusion = bf16[4608,512]{1,0:T(8,128)(2,1)} fusion(bf16[1024,4608]{1,0:T(8,128)(2,1)S(1)} %bitcast.156, bf16[1024,512]{1,0:T(8,128)(2,1)S(1)} %copy-done.52), kind=kOutput, calls=%fused_computation.5 | convolution fusion | flops 4834197504 | bytes 15204352 | tf_op jit(solution)/shard_map/dot_general | solution.py:57
  268.7 7.1 %convolution_convert_fusion.2 = bf16[512,4608]{1,0:T(8,128)(2,1)} fusion(bf16[1024,512]{1,0:T(8,128)(2,1)S(1)} %pad_maximum_fusion.15, bf16[1024,4608]{1,0:T(8,128)(2,1)S(1)} %bitcast.160), kind=kOutput, calls=%fused_computation.7 | convolution fusion | flops 4834197504 | bytes 15204352 | tf_op jit(solution)/shard_map/dot_general | solution.py:57
  277.7 3.0 add_convert_fusion.34
  284.0 11.1 %convolution_convert_fusion.3 = bf16[512,4608]{1,0:T(8,128)(2,1)} fusion(bf16[1024,512]{1,0:T(8,128)(2,1)S(1)} %pad_maximum_fusion.16, bf16[1024,4608]{1,0:T(8,128)(2,1)} %get-tuple-element.234.dup_ref), kind=kOutput, calls=%fused_computation.8 | convolution fusion | flops 4834197504 | bytes 15204352 | tf_op jit(solution)/shard_map/dot_general | solution.py:57
  295.1 5.4 convolution_convert_fusion.4
  300.6 7.7 %collective-permute-done.27 = bf16[2,576,512]{2,1,0:T(8,128)(2,1)S(1)} collective-permute-done((bf16[2,576,512]{2,1,0:T(8,128)(2,1)S(1)}, bf16[2,576,512]{2,1,0:T(8,128)(2,1)S(1)}, u32[]{:S(2)}, u32[]{:S(2)}) %collective-permute-start.27) | collective-permute-done | bytes 1179680 | tf_op jit(solution)/shard_map/ppermute | solution.py:78
  309.6 3.3 fusion.61
  320.4 28.5 %ffn_input.1 = f32[1024,1024]{1,0:T(8,128)} custom-call(s32[8]{0:T(128)} %stack.70.spots_ref, bf16[1024,4608]{1,0:T(8,128)(2,1)} %get-tuple-element.233.dgate_ref, bf16[1024,4608]{1,0:T(8,128)(2,1)} %get-tuple-element.234.dup_ref, bf16[256,4608]{1,0:T(8,128)(2,1)} %refs_1_.4, bf16[256,4608]{1,0:T(8,128)(2,1)} %refs_1_.4, bf16[128,9216]{1,0:T(8,128)(2,1)} %copy-done.4, ...), custom_call_target="tpu_custom_call" | custom-call | flops 1 | bytes 1 | tf_op jit(solution)/shard_map/ffn_input/pallas_call | solution.py:280
  349.0 4.1 multiply_reduce_fusion.2
  360.6 2.6 broadcast_select_fusion.8
  367.3 3.7 convolution_convert_fusion.8.do_ref
  371.0 6.0 collective-permute-done.34
  377.1 2.9 add_convert_fusion.19
  385.0 3.0 fusion.63
  388.5 2.9 collective-permute-start.37
  392.7 5.3 copy.113.q_lin_ref
  398.0 3.1 copy.114.k_lin_ref
  403.5 22.4 %attend_back.2 = (bf16[1024,512]{1,0:T(8,128)(2,1)}, bf16[1024,256]{1,0:T(8,128)(2,1)}, bf16[1024,256]{1,0:T(8,128)(2,1)}, f32[2,64,256]{2,1,0:T(8,128)}, f32[2,64,256]{2,1,0:T(8,128)}) custom-call(s32[4,4]{1,0:T(4,128)} %fusion.80.live_ref, bf16[1024,1024]{1,0:T(8,128)(2,1)} %copy.106.q_ref, bf16[1024,1024]{1,0:T(8,128)(2,1)} %convolution_convert_fusion.8.do_ref, ...), custom_call_target="tpu_custom_call" | custom-call | flops 1 | bytes 1 | tf_op jit(solution)/shard_map/attend_back/pallas_call | solution.py:652
  425.9 22.7 %attend_back.3 = (bf16[1024,512]{1,0:T(8,128)(2,1)}, bf16[1024,256]{1,0:T(8,128)(2,1)}, bf16[1024,256]{1,0:T(8,128)(2,1)}, f32[2,64,256]{2,1,0:T(8,128)}, f32[2,64,256]{2,1,0:T(8,128)}) custom-call(s32[4,4]{1,0:T(4,128)} %fusion.80.live_ref, bf16[1024,1024]{1,0:T(8,128)(2,1)} %copy.106.q_ref, bf16[1024,1024]{1,0:T(8,128)(2,1)} %convolution_convert_fusion.8.do_ref, ...), custom_call_target="tpu_custom_call" | custom-call | flops 1 | bytes 1 | tf_op jit(solution)/shard_map/attend_back/pallas_call | solution.py:652
  458.8 4.6 convolution_convert_fusion.6
  466.0 8.0 %collective-permute-start.41 = (bf16[2,64,1024]{2,1,0:T(8,128)(2,1)S(1)}, bf16[2,64,1024]{2,1,0:T(8,128)(2,1)S(1)}, u32[]{:S(2)}, u32[]{:S(2)}) collective-permute-start(bf16[2,64,1024]{2,1,0:T(8,128)(2,1)S(1)} %pad_maximum_fusion.23), channel_id=1, source_target_pairs={{0,8},{1,9},{2,10},{3,11},{4,12},{5,13},{6,14},{7,15},{8,0},{9,1},... | collective-permute-start | bytes 786440 | tf_op jit(solution)/shard_map/ppermute | solution.py:78
  476.1 3.2 fusion.65
  480.7 2.9 collective-permute-start.67
  483.6 3.7 broadcast_select_fusion.5
  487.4 2.4 convolution_convert_fusion.7
  492.3 4.1 collective-permute-done.67
  499.5 2.7 add_add_fusion
  505.8 10.3 %fusion.11 = f32[1152,1024]{1,0:T(8,128)} fusion(bf16[1152,512]{1,0:T(8,128)(2,1)S(1)} %collective-permute-done.68, bf16[576,512]{1,0:T(8,128)(2,1)S(1)} %get-tuple-element.401, bf16[576,512]{1,0:T(8,128)(2,1)S(1)} %get-tuple-element.400, pred[]{:T(512)S(6)} %eq.38), kind=kLoop, calls=%fused_computation.42 | loop fusion | flops 16515072 | bytes 7077889 | tf_op jit(solution)/shard_map/convert_element_type | solution.py:448
  519.9 13.2 %add_multiply_fusion = bf16[1024,1024]{1,0:T(8,128)(2,1)} fusion(f32[1024,1024]{1,0:T(8,128)S(1)} %copy-done.8, f32[1024]{0:T(1024)S(1)} %copy-done.90, bf16[1024,4608]{1,0:T(8,128)(2,1)} %get-tuple-element.289, bf16[4608,1024]{1,0:T(8,128)(2,1)S(1)} %bitcast.154), kind=kOutput, calls=%fused_computation.20 | convolution fusion | flops 9666822144 | bytes 25169920 | tf_op jit(solution)/shard_map/dot_general | solution.py:53
  533.1 2.8 broadcast_select_fusion.4
  545.0 2.5 fusion.5
  547.4 9.4 %collective-permute-done.50 = bf16[2,64,2176]{2,1,0:T(8,128)(2,1)S(1)} collective-permute-done((bf16[2,64,2176]{2,1,0:T(8,128)(2,1)S(1)}, bf16[2,64,2176]{2,1,0:T(8,128)(2,1)S(1)}, u32[]{:S(2)}, u32[]{:S(2)}) %collective-permute-start.50) | collective-permute-done | bytes 557088 | tf_op jit(solution)/shard_map/ppermute | solution.py:78
  556.9 5.1 collective-permute-done.46
  564.2 4.4 collective-permute-start.53
  576.7 9.7 %collective-permute-done.59 = bf16[64,1024]{1,0:T(8,128)(2,1)S(1)} collective-permute-done((bf16[64,1024]{1,0:T(8,128)(2,1)S(1)}, bf16[64,1024]{1,0:T(8,128)(2,1)S(1)}, u32[]{:S(2)}, u32[]{:S(2)}) %collective-permute-start.59) | collective-permute-done | bytes 131104 | tf_op jit(solution)/shard_map/ppermute | solution.py:86
  589.4 12.5 %collective-permute-done.60 = bf16[64,1024]{1,0:T(8,128)(2,1)S(1)} collective-permute-done((bf16[64,1024]{1,0:T(8,128)(2,1)S(1)}, bf16[64,1024]{1,0:T(8,128)(2,1)S(1)}, u32[]{:S(2)}, u32[]{:S(2)}) %collective-permute-start.60) | collective-permute-done | bytes 131104 | tf_op jit(solution)/shard_map/ppermute | solution.py:86
  601.9 10.8 %collective-permute-start.61 = (bf16[128,1024]{1,0:T(8,128)(2,1)S(1)}, bf16[128,1024]{1,0:T(8,128)(2,1)S(1)}, u32[]{:S(2)}, u32[]{:S(2)}) collective-permute-start(bf16[128,1024]{1,0:T(8,128)(2,1)S(1)} %pad_maximum_fusion.25), channel_id=1, source_target_pairs={{0,1},{1,0},{2,3},{3,2},{4,5},{5,4},{6,7},{7,6},{8,9},{9,8},{10,11... | collective-permute-start | bytes 786440 | tf_op jit(solution)/shard_map/ppermute | solution.py:86
  613.2 3.1 collective-permute-start.63
  616.3 11.6 %collective-permute-done.55 = bf16[64,2176]{1,0:T(8,128)(2,1)S(1)} collective-permute-done((bf16[64,2176]{1,0:T(8,128)(2,1)S(1)}, bf16[64,2176]{1,0:T(8,128)(2,1)S(1)}, u32[]{:S(2)}, u32[]{:S(2)}) %collective-permute-start.55) | collective-permute-done | bytes 278560 | tf_op jit(solution)/shard_map/ppermute | solution.py:86
  630.7 5.0 collective-permute-done.56
  638.1 10.2 %collective-permute-done.65 = bf16[64,4608]{1,0:T(8,128)(2,1)S(1)} collective-permute-done((bf16[64,4608]{1,0:T(8,128)(2,1)S(1)}, bf16[64,4608]{1,0:T(8,128)(2,1)S(1)}, u32[]{:S(2)}, u32[]{:S(2)}) %collective-permute-start.65) | collective-permute-done | bytes 589856 | tf_op jit(solution)/shard_map/ppermute | solution.py:86
  653.5 2.8 multiply_reduce_fusion.1
  656.3 2.8 multiply_reduce_fusion
  (513 shorter events, 173.4 us)
Async XLA Ops:
  6.0 14.5 %collective-permute-start = (bf16[128,2176]{1,0:T(8,128)(2,1)S(1)}, bf16[128,2176]{1,0:T(8,128)(2,1)S(1)}, u32[]{:S(2)}, u32[]{:S(2)}) collective-permute-start(bf16[128,2176]{1,0:T(8,128)(2,1)S(1)} %pad_maximum_fusion.18), channel_id=1, source_target_pairs={{0,8},{1,9},{2,10},{3,11},{4,12},{5,13},{6,14},{7,15},{8,0},{9,1},... | collective-permute-start | bytes 1671176 | tf_op jit(solution)/shard_map/ppermute | solution.py:78
  8.1 13.2 %collective-permute-start.1 = (bf16[128,2176]{1,0:T(8,128)(2,1)S(1)}, bf16[128,2176]{1,0:T(8,128)(2,1)S(1)}, u32[]{:S(2)}, u32[]{:S(2)}) collective-permute-start(bf16[128,2176]{1,0:T(8,128)(2,1)S(1)} %pad_maximum_fusion.18), channel_id=1, source_target_pairs={{0,16},{1,17},{2,18},{3,19},{4,20},{5,21},{6,22},{7,23},{8,24},{9,... | collective-permute-start | bytes 1671176 | tf_op jit(solution)/shard_map/ppermute | solution.py:78
  26.2 40.5 %collective-permute-start.5 = (bf16[128,1024]{1,0:T(8,128)(2,1)}, bf16[128,1024]{1,0:T(8,128)(2,1)}, u32[]{:S(2)}, u32[]{:S(2)}) collective-permute-start(bf16[128,1024]{1,0:T(8,128)(2,1)} %constant_dynamic-slice_fusion.31), channel_id=1, source_target_pairs={{0,8},{1,9},{2,10},{3,11},{4,12},{5,13},{6,14},{7,15},{8,0},{9,1},... | collective-permute-start | bytes 786440 | tf_op jit(solution)/shard_map/ppermute | solution.py:78
  27.4 39.4 %collective-permute-start.6 = (bf16[128,1024]{1,0:T(8,128)(2,1)}, bf16[128,1024]{1,0:T(8,128)(2,1)}, u32[]{:S(2)}, u32[]{:S(2)}) collective-permute-start(bf16[128,1024]{1,0:T(8,128)(2,1)} %constant_dynamic-slice_fusion.31), channel_id=1, source_target_pairs={{0,16},{1,17},{2,18},{3,19},{4,20},{5,21},{6,22},{7,23},{8,24},{9,... | collective-permute-start | bytes 786440 | tf_op jit(solution)/shard_map/ppermute | solution.py:78
  29.0 8.5 %collective-permute-start.4 = (bf16[3,128,2176]{2,1,0:T(8,128)(2,1)S(1)}, bf16[3,128,2176]{2,1,0:T(8,128)(2,1)S(1)}, u32[]{:S(2)}, u32[]{:S(2)}) collective-permute-start(bf16[3,128,2176]{2,1,0:T(8,128)(2,1)S(1)} %pad_maximum_fusion.3), channel_id=1, source_target_pairs={{0,1},{1,0},{2,3},{3,2},{4,5},{5,4},{6,7},{7,6},{8,9},{9,8},{10,11... | collective-permute-start | bytes 5013512 | tf_op jit(solution)/shard_map/ppermute | solution.py:86
  36.2 65.0 %collective-permute-start.9 = (bf16[128,9216]{1,0:T(8,128)(2,1)}, bf16[128,9216]{1,0:T(8,128)(2,1)S(1)}, u32[]{:S(2)}, u32[]{:S(2)}) collective-permute-start(bf16[128,9216]{1,0:T(8,128)(2,1)} %pad_maximum_fusion), channel_id=1, source_target_pairs={{0,8},{1,9},{2,10},{3,11},{4,12},{5,13},{6,14},{7,15},{8,0},{9,1},... | collective-permute-start | bytes 7077896 | tf_op jit(solution)/shard_map/ppermute | solution.py:78
  36.2 65.0 %collective-permute-start.10 = (bf16[128,9216]{1,0:T(8,128)(2,1)}, bf16[128,9216]{1,0:T(8,128)(2,1)}, u32[]{:S(2)}, u32[]{:S(2)}) collective-permute-start(bf16[128,9216]{1,0:T(8,128)(2,1)} %pad_maximum_fusion), channel_id=1, source_target_pairs={{0,16},{1,17},{2,18},{3,19},{4,20},{5,21},{6,22},{7,23},{8,24},{9,... | collective-permute-start | bytes 7077896 | tf_op jit(solution)/shard_map/ppermute | solution.py:78
  68.4 32.8 %collective-permute-start.7 = (bf16[64,1024]{1,0:T(8,128)(2,1)}, bf16[64,1024]{1,0:T(8,128)(2,1)S(1)}, u32[]{:S(2)}, u32[]{:S(2)}) collective-permute-start(bf16[64,1024]{1,0:T(8,128)(2,1)} %slice.203), channel_id=1, source_target_pairs={{0,16},{1,17},{2,18},{3,19},{4,20},{5,21},{6,22},{7,23},{8,24},{9,... | collective-permute-start | bytes 393224 | tf_op jit(solution)/shard_map/ppermute | solution.py:78
  70.0 31.2 %collective-permute-start.8 = (bf16[64,1024]{1,0:T(8,128)(2,1)}, bf16[64,1024]{1,0:T(8,128)(2,1)}, u32[]{:S(2)}, u32[]{:S(2)}) collective-permute-start(bf16[64,1024]{1,0:T(8,128)(2,1)} %slice.204), channel_id=1, source_target_pairs={{0,8},{1,9},{2,10},{3,11},{4,12},{5,13},{6,14},{7,15},{8,0},{9,1},... | collective-permute-start | bytes 393224 | tf_op jit(solution)/shard_map/ppermute | solution.py:78
  103.5 10.2 %collective-permute-start.11 = (bf16[3,128,1024]{2,1,0:T(8,128)(2,1)S(1)}, bf16[3,128,1024]{2,1,0:T(8,128)(2,1)S(1)}, u32[]{:S(2)}, u32[]{:S(2)}) collective-permute-start(bf16[3,128,1024]{2,1,0:T(8,128)(2,1)S(1)} %pad_maximum_fusion.17), channel_id=1, source_target_pairs={{0,1},{1,0},{2,3},{3,2},{4,5},{5,4},{6,7},{7,6},{8,9},{9,8},{10,11... | collective-permute-start | bytes 2359304 | tf_op jit(solution)/shard_map/ppermute | solution.py:86
  104.7 30.8 %collective-permute-start.12 = (bf16[64,9216]{1,0:T(8,128)(2,1)}, bf16[64,9216]{1,0:T(8,128)(2,1)S(1)}, u32[]{:S(2)}, u32[]{:S(2)}) collective-permute-start(bf16[64,9216]{1,0:T(8,128)(2,1)} %slice.209), channel_id=1, source_target_pairs={{0,16},{1,17},{2,18},{3,19},{4,20},{5,21},{6,22},{7,23},{8,24},{9,... | collective-permute-start | bytes 3538952 | tf_op jit(solution)/shard_map/ppermute | solution.py:78
  111.2 28.4 %collective-permute-start.13 = (bf16[64,9216]{1,0:T(8,128)(2,1)}, bf16[64,9216]{1,0:T(8,128)(2,1)}, u32[]{:S(2)}, u32[]{:S(2)}) collective-permute-start(bf16[64,9216]{1,0:T(8,128)(2,1)} %slice.210), channel_id=1, source_target_pairs={{0,8},{1,9},{2,10},{3,11},{4,12},{5,13},{6,14},{7,15},{8,0},{9,1},... | collective-permute-start | bytes 3538952 | tf_op jit(solution)/shard_map/ppermute | solution.py:78
  139.6 9.2 %collective-permute-start.14 = (bf16[128,9216]{1,0:T(8,128)(2,1)S(1)}, bf16[128,9216]{1,0:T(8,128)(2,1)}, u32[]{:S(2)}, u32[]{:S(2)}) collective-permute-start(bf16[128,9216]{1,0:T(8,128)(2,1)S(1)} %collective-permute-done.9.refs_2_.refs_10_), channel_id=1, source_target_pairs={{0,1},{1,0},{2,3},{3,2},{4,5},{5,4},{6,7},{7,6},{8,9},{9,8},{10,11... | collective-permute-start | bytes 7077896 | tf_op jit(solution)/shard_map/ppermute | solution.py:86
  140.9 7.9 %collective-permute-start.15 = (bf16[128,9216]{1,0:T(8,128)(2,1)}, bf16[128,9216]{1,0:T(8,128)(2,1)}, u32[]{:S(2)}, u32[]{:S(2)}) collective-permute-start(bf16[128,9216]{1,0:T(8,128)(2,1)} %collective-permute-done.10.refs_4_.refs_12_), channel_id=1, source_target_pairs={{0,1},{1,0},{2,3},{3,2},{4,5},{5,4},{6,7},{7,6},{8,9},{9,8},{10,11... | collective-permute-start | bytes 7077896 | tf_op jit(solution)/shard_map/ppermute | solution.py:86
  144.4 7.7 %collective-permute-start.16 = (bf16[128,9216]{1,0:T(8,128)(2,1)}, bf16[128,9216]{1,0:T(8,128)(2,1)}, u32[]{:S(2)}, u32[]{:S(2)}) collective-permute-start(bf16[128,9216]{1,0:T(8,128)(2,1)} %constant_dynamic-update-slice_fusion.4.refs_6_.refs_14_), channel_id=1, source_target_pairs={{0,1},{1,0},{2,3},{3,2},{4,5},{5,4},{6,7},{7,6},{8,9},{9,8},{10,11... | collective-permute-start | bytes 7077896 | tf_op jit(solution)/shard_map/ppermute | solution.py:86
  147.3 27.9 %collective-permute-start.17 = (bf16[576,1024]{1,0:T(8,128)(2,1)}, bf16[576,1024]{1,0:T(8,128)(2,1)S(1)}, u32[]{:S(2)}, u32[]{:S(2)}) collective-permute-start(bf16[576,1024]{1,0:T(8,128)(2,1)} %constant_dynamic-slice_fusion.28), channel_id=1, source_target_pairs={{0,8},{1,9},{2,10},{3,11},{4,12},{5,13},{6,14},{7,15},{8,0},{9,1},... | collective-permute-start | bytes 3538952 | tf_op jit(solution)/shard_map/ppermute | solution.py:78
  148.8 27.6 %collective-permute-start.18 = (bf16[576,1024]{1,0:T(8,128)(2,1)}, bf16[576,1024]{1,0:T(8,128)(2,1)}, u32[]{:S(2)}, u32[]{:S(2)}) collective-permute-start(bf16[576,1024]{1,0:T(8,128)(2,1)} %constant_dynamic-slice_fusion.28), channel_id=1, source_target_pairs={{0,16},{1,17},{2,18},{3,19},{4,20},{5,21},{6,22},{7,23},{8,24},{9,... | collective-permute-start | bytes 3538952 | tf_op jit(solution)/shard_map/ppermute | solution.py:78
  176.4 22.0 %collective-permute-start.21 = (bf16[576,1024]{1,0:T(8,128)(2,1)S(1)}, bf16[576,1024]{1,0:T(8,128)(2,1)}, u32[]{:S(2)}, u32[]{:S(2)}) collective-permute-start(bf16[576,1024]{1,0:T(8,128)(2,1)S(1)} %collective-permute-done.17.refs_2_), channel_id=1, source_target_pairs={{0,1},{1,0},{2,3},{3,2},{4,5},{5,4},{6,7},{7,6},{8,9},{9,8},{10,11... | collective-permute-start | bytes 3538952 | tf_op jit(solution)/shard_map/ppermute | solution.py:86
  177.5 20.9 %collective-permute-start.22 = (bf16[576,1024]{1,0:T(8,128)(2,1)}, bf16[576,1024]{1,0:T(8,128)(2,1)}, u32[]{:S(2)}, u32[]{:S(2)}) collective-permute-start(bf16[576,1024]{1,0:T(8,128)(2,1)} %collective-permute-done.18.refs_4_), channel_id=1, source_target_pairs={{0,1},{1,0},{2,3},{3,2},{4,5},{5,4},{6,7},{7,6},{8,9},{9,8},{10,11... | collective-permute-start | bytes 3538952 | tf_op jit(solution)/shard_map/ppermute | solution.py:86
  180.3 18.0 %collective-permute-start.19 = (bf16[288,1024]{1,0:T(8,128)(2,1)}, bf16[288,1024]{1,0:T(8,128)(2,1)}, u32[]{:S(2)}, u32[]{:S(2)}) collective-permute-start(bf16[288,1024]{1,0:T(8,128)(2,1)} %slice.211), channel_id=1, source_target_pairs={{0,16},{1,17},{2,18},{3,19},{4,20},{5,21},{6,22},{7,23},{8,24},{9,... | collective-permute-start | bytes 1769480 | tf_op jit(solution)/shard_map/ppermute | solution.py:78
  180.3 18.0 %collective-permute-start.20 = (bf16[288,1024]{1,0:T(8,128)(2,1)}, bf16[288,1024]{1,0:T(8,128)(2,1)}, u32[]{:S(2)}, u32[]{:S(2)}) collective-permute-start(bf16[288,1024]{1,0:T(8,128)(2,1)} %slice.212), channel_id=1, source_target_pairs={{0,8},{1,9},{2,10},{3,11},{4,12},{5,13},{6,14},{7,15},{8,0},{9,1},... | collective-permute-start | bytes 1769480 | tf_op jit(solution)/shard_map/ppermute | solution.py:78
  249.4 12.2 %collective-permute-start.24 = (bf16[4,1152,512]{2,1,0:T(8,128)(2,1)}, bf16[4,1152,512]{2,1,0:T(8,128)(2,1)}, u32[]{:S(2)}, u32[]{:S(2)}) collective-permute-start(bf16[4,1152,512]{2,1,0:T(8,128)(2,1)} %bitcast.27), channel_id=1, source_target_pairs={{0,1},{1,0},{2,3},{3,2},{4,5},{5,4},{6,7},{7,6},{8,9},{9,8},{10,11... | collective-permute-start | bytes 14155784 | tf_op jit(solution)/shard_map/ppermute | solution.py:86
  261.5 39.1 %collective-permute-start.25 = (bf16[4,128,4608]{2,1,0:T(8,128)(2,1)}, bf16[4,128,4608]{2,1,0:T(8,128)(2,1)}, u32[]{:S(2)}, u32[]{:S(2)}) collective-permute-start(bf16[4,128,4608]{2,1,0:T(8,128)(2,1)} %bitcast.30), channel_id=1, source_target_pairs={{0,1},{1,0},{2,3},{3,2},{4,5},{5,4},{6,7},{7,6},{8,9},{9,8},{10,11... | collective-permute-start | bytes 14155784 | tf_op jit(solution)/shard_map/ppermute | solution.py:86
  275.7 33.9 %collective-permute-start.26 = (bf16[4,128,4608]{2,1,0:T(8,128)(2,1)}, bf16[4,128,4608]{2,1,0:T(8,128)(2,1)}, u32[]{:S(2)}, u32[]{:S(2)}) collective-permute-start(bf16[4,128,4608]{2,1,0:T(8,128)(2,1)} %bitcast.32), channel_id=1, source_target_pairs={{0,1},{1,0},{2,3},{3,2},{4,5},{5,4},{6,7},{7,6},{8,9},{9,8},{10,11... | collective-permute-start | bytes 14155784 | tf_op jit(solution)/shard_map/ppermute | solution.py:86
  280.8 27.5 %collective-permute-start.27 = (bf16[2,576,512]{2,1,0:T(8,128)(2,1)S(1)}, bf16[2,576,512]{2,1,0:T(8,128)(2,1)S(1)}, u32[]{:S(2)}, u32[]{:S(2)}) collective-permute-start(bf16[2,576,512]{2,1,0:T(8,128)(2,1)S(1)} %pad_maximum_fusion.4), channel_id=1, source_target_pairs={{0,8},{1,9},{2,10},{3,11},{4,12},{5,13},{6,14},{7,15},{8,0},{9,1},... | collective-permute-start | bytes 3538952 | tf_op jit(solution)/shard_map/ppermute | solution.py:78
  282.4 27.2 %collective-permute-start.28 = (bf16[2,576,512]{2,1,0:T(8,128)(2,1)S(1)}, bf16[2,576,512]{2,1,0:T(8,128)(2,1)S(1)}, u32[]{:S(2)}, u32[]{:S(2)}) collective-permute-start(bf16[2,576,512]{2,1,0:T(8,128)(2,1)S(1)} %pad_maximum_fusion.5), channel_id=1, source_target_pairs={{0,16},{1,17},{2,18},{3,19},{4,20},{5,21},{6,22},{7,23},{8,24},{9,... | collective-permute-start | bytes 3538952 | tf_op jit(solution)/shard_map/ppermute | solution.py:78
  313.0 36.0 %collective-permute-start.29 = (bf16[576,512]{1,0:T(8,128)(2,1)}, bf16[576,512]{1,0:T(8,128)(2,1)}, u32[]{:S(2)}, u32[]{:S(2)}) collective-permute-start(bf16[576,512]{1,0:T(8,128)(2,1)} %get-tuple-element.348), channel_id=1, source_target_pairs={{0,16},{1,17},{2,18},{3,19},{4,20},{5,21},{6,22},{7,23},{8,24},{9,... | collective-permute-start | bytes 1769480 | tf_op jit(solution)/shard_map/ppermute | solution.py:78
  314.5 34.5 %collective-permute-start.30 = (bf16[576,512]{1,0:T(8,128)(2,1)S(1)}, bf16[576,512]{1,0:T(8,128)(2,1)}, u32[]{:S(2)}, u32[]{:S(2)}) collective-permute-start(bf16[576,512]{1,0:T(8,128)(2,1)S(1)} %get-tuple-element.347), channel_id=1, source_target_pairs={{0,8},{1,9},{2,10},{3,11},{4,12},{5,13},{6,14},{7,15},{8,0},{9,1},... | collective-permute-start | bytes 1769480 | tf_op jit(solution)/shard_map/ppermute | solution.py:78
  318.4 58.6 %collective-permute-start.32 = (bf16[2,64,4608]{2,1,0:T(8,128)(2,1)}, bf16[2,64,4608]{2,1,0:T(8,128)(2,1)S(1)}, u32[]{:S(2)}, u32[]{:S(2)}) collective-permute-start(bf16[2,64,4608]{2,1,0:T(8,128)(2,1)} %pad_maximum_fusion.6), channel_id=1, source_target_pairs={{0,8},{1,9},{2,10},{3,11},{4,12},{5,13},{6,14},{7,15},{8,0},{9,1},... | collective-permute-start | bytes 3538952 | tf_op jit(solution)/shard_map/ppermute | solution.py:78
  320.4 56.6 %collective-permute-start.33 = (bf16[2,64,4608]{2,1,0:T(8,128)(2,1)}, bf16[2,64,4608]{2,1,0:T(8,128)(2,1)}, u32[]{:S(2)}, u32[]{:S(2)}) collective-permute-start(bf16[2,64,4608]{2,1,0:T(8,128)(2,1)} %pad_maximum_fusion.7), channel_id=1, source_target_pairs={{0,16},{1,17},{2,18},{3,19},{4,20},{5,21},{6,22},{7,23},{8,24},{9,... | collective-permute-start | bytes 3538952 | tf_op jit(solution)/shard_map/ppermute | solution.py:78
  358.3 18.8 %collective-permute-start.31 = (bf16[4,128,1024]{2,1,0:T(8,128)(2,1)S(1)}, bf16[4,128,1024]{2,1,0:T(8,128)(2,1)S(1)}, u32[]{:S(2)}, u32[]{:S(2)}) collective-permute-start(bf16[4,128,1024]{2,1,0:T(8,128)(2,1)S(1)} %bitcast.195), channel_id=1, source_target_pairs={{0,1},{1,0},{2,3},{3,2},{4,5},{5,4},{6,7},{7,6},{8,9},{9,8},{10,11... | collective-permute-start | bytes 3145736 | tf_op jit(solution)/shard_map/ppermute | solution.py:86
  363.3 13.7 %collective-permute-start.34 = (bf16[576,512]{1,0:T(8,128)(2,1)S(1)}, bf16[576,512]{1,0:T(8,128)(2,1)S(1)}, u32[]{:S(2)}, u32[]{:S(2)}) collective-permute-start(bf16[576,512]{1,0:T(8,128)(2,1)S(1)} %get-tuple-element.332), channel_id=1, source_target_pairs={{0,2},{1,3},{2,0},{3,1},{4,6},{5,7},{6,4},{7,5},{8,10},{9,11},{10,... | collective-permute-start | bytes 1769480 | tf_op jit(solution)/shard_map/ppermute | solution.py:86
  381.1 67.5 %collective-permute-start.38 = (bf16[2,64,4608]{2,1,0:T(8,128)(2,1)}, bf16[2,64,4608]{2,1,0:T(8,128)(2,1)}, u32[]{:S(2)}, u32[]{:S(2)}) collective-permute-start(bf16[2,64,4608]{2,1,0:T(8,128)(2,1)} %pad_maximum_fusion.8), channel_id=1, source_target_pairs={{0,8},{1,9},{2,10},{3,11},{4,12},{5,13},{6,14},{7,15},{8,0},{9,1},... | collective-permute-start | bytes 3538952 | tf_op jit(solution)/shard_map/ppermute | solution.py:78
  383.5 65.1 %collective-permute-start.39 = (bf16[2,64,4608]{2,1,0:T(8,128)(2,1)}, bf16[2,64,4608]{2,1,0:T(8,128)(2,1)}, u32[]{:S(2)}, u32[]{:S(2)}) collective-permute-start(bf16[2,64,4608]{2,1,0:T(8,128)(2,1)} %pad_maximum_fusion.9), channel_id=1, source_target_pairs={{0,16},{1,17},{2,18},{3,19},{4,20},{5,21},{6,22},{7,23},{8,24},{9,... | collective-permute-start | bytes 3538952 | tf_op jit(solution)/shard_map/ppermute | solution.py:78
  388.0 60.6 %collective-permute-start.35 = (bf16[64,4608]{1,0:T(8,128)(2,1)}, bf16[64,4608]{1,0:T(8,128)(2,1)}, u32[]{:S(2)}, u32[]{:S(2)}) collective-permute-start(bf16[64,4608]{1,0:T(8,128)(2,1)} %get-tuple-element.342), channel_id=1, source_target_pairs={{0,16},{1,17},{2,18},{3,19},{4,20},{5,21},{6,22},{7,23},{8,24},{9,... | collective-permute-start | bytes 1769480 | tf_op jit(solution)/shard_map/ppermute | solution.py:78
  388.0 60.6 %collective-permute-start.36 = (bf16[64,4608]{1,0:T(8,128)(2,1)S(1)}, bf16[64,4608]{1,0:T(8,128)(2,1)}, u32[]{:S(2)}, u32[]{:S(2)}) collective-permute-start(bf16[64,4608]{1,0:T(8,128)(2,1)S(1)} %get-tuple-element.341), channel_id=1, source_target_pairs={{0,8},{1,9},{2,10},{3,11},{4,12},{5,13},{6,14},{7,15},{8,0},{9,1},... | collective-permute-start | bytes 1769480 | tf_op jit(solution)/shard_map/ppermute | solution.py:78
  388.5 60.1 %collective-permute-start.37 = (bf16[576,512]{1,0:T(8,128)(2,1)S(1)}, bf16[576,512]{1,0:T(8,128)(2,1)}, u32[]{:S(2)}, u32[]{:S(2)}) collective-permute-start(bf16[576,512]{1,0:T(8,128)(2,1)S(1)} %add_convert_fusion.22), channel_id=1, source_target_pairs={{0,4},{1,5},{2,6},{3,7},{4,0},{5,1},{6,2},{7,3},{8,12},{9,13},{10,... | collective-permute-start | bytes 1769480 | tf_op jit(solution)/shard_map/ppermute | solution.py:86
  465.1 54.1 %collective-permute-start.40 = (bf16[4,128,2176]{2,1,0:T(8,128)(2,1)}, bf16[4,128,2176]{2,1,0:T(8,128)(2,1)}, u32[]{:S(2)}, u32[]{:S(2)}) collective-permute-start(bf16[4,128,2176]{2,1,0:T(8,128)(2,1)} %pad_maximum_fusion.2), channel_id=1, source_target_pairs={{0,1},{1,0},{2,3},{3,2},{4,5},{5,4},{6,7},{7,6},{8,9},{9,8},{10,11... | collective-permute-start | bytes 6684680 | tf_op jit(solution)/shard_map/ppermute | solution.py:86
  466.0 36.7 %collective-permute-start.41 = (bf16[2,64,1024]{2,1,0:T(8,128)(2,1)S(1)}, bf16[2,64,1024]{2,1,0:T(8,128)(2,1)S(1)}, u32[]{:S(2)}, u32[]{:S(2)}) collective-permute-start(bf16[2,64,1024]{2,1,0:T(8,128)(2,1)S(1)} %pad_maximum_fusion.23), channel_id=1, source_target_pairs={{0,8},{1,9},{2,10},{3,11},{4,12},{5,13},{6,14},{7,15},{8,0},{9,1},... | collective-permute-start | bytes 786440 | tf_op jit(solution)/shard_map/ppermute | solution.py:78
  474.7 41.5 %collective-permute-start.42 = (bf16[2,64,1024]{2,1,0:T(8,128)(2,1)}, bf16[2,64,1024]{2,1,0:T(8,128)(2,1)}, u32[]{:S(2)}, u32[]{:S(2)}) collective-permute-start(bf16[2,64,1024]{2,1,0:T(8,128)(2,1)} %pad_maximum_fusion.24), channel_id=1, source_target_pairs={{0,16},{1,17},{2,18},{3,19},{4,20},{5,21},{6,22},{7,23},{8,24},{9,... | collective-permute-start | bytes 786440 | tf_op jit(solution)/shard_map/ppermute | solution.py:78
  479.3 36.9 %collective-permute-start.43 = (bf16[64,4608]{1,0:T(8,128)(2,1)}, bf16[64,4608]{1,0:T(8,128)(2,1)}, u32[]{:S(2)}, u32[]{:S(2)}) collective-permute-start(bf16[64,4608]{1,0:T(8,128)(2,1)} %get-tuple-element.336), channel_id=1, source_target_pairs={{0,16},{1,17},{2,18},{3,19},{4,20},{5,21},{6,22},{7,23},{8,24},{9,... | collective-permute-start | bytes 1769480 | tf_op jit(solution)/shard_map/ppermute | solution.py:78
  480.7 15.6 %collective-permute-start.67 = (bf16[576,512]{1,0:T(8,128)(2,1)S(1)}, bf16[576,512]{1,0:T(8,128)(2,1)S(1)}, u32[]{:S(2)}, u32[]{:S(2)}) collective-permute-start(bf16[576,512]{1,0:T(8,128)(2,1)S(1)} %add_convert_fusion.7), channel_id=1, source_target_pairs={{0,2},{1,3},{2,0},{3,1},{4,6},{5,7},{6,4},{7,5},{8,10},{9,11},{10,... | collective-permute-start | bytes 1769480 | tf_op jit(solution)/shard_map/ppermute | solution.py:86
  496.5 7.8 %collective-permute-start.68 = (bf16[1152,512]{1,0:T(8,128)(2,1)S(1)}, bf16[1152,512]{1,0:T(8,128)(2,1)S(1)}, u32[]{:S(2)}, u32[]{:S(2)}) collective-permute-start(bf16[1152,512]{1,0:T(8,128)(2,1)S(1)} %pad_maximum_fusion.12), channel_id=1, source_target_pairs={{0,1},{1,0},{2,3},{3,2},{4,5},{5,4},{6,7},{7,6},{8,9},{9,8},{10,11... | collective-permute-start | bytes 3538952 | tf_op jit(solution)/shard_map/ppermute | solution.py:86
  502.8 15.0 %collective-permute-start.44 = (bf16[64,4608]{1,0:T(8,128)(2,1)S(1)}, bf16[64,4608]{1,0:T(8,128)(2,1)S(1)}, u32[]{:S(2)}, u32[]{:S(2)}) collective-permute-start(bf16[64,4608]{1,0:T(8,128)(2,1)S(1)} %get-tuple-element.335), channel_id=1, source_target_pairs={{0,8},{1,9},{2,10},{3,11},{4,12},{5,13},{6,14},{7,15},{8,0},{9,1},... | collective-permute-start | bytes 1769480 | tf_op jit(solution)/shard_map/ppermute | solution.py:78
  504.3 14.9 %collective-permute-start.45 = (bf16[64,4608]{1,0:T(8,128)(2,1)}, bf16[64,4608]{1,0:T(8,128)(2,1)S(1)}, u32[]{:S(2)}, u32[]{:S(2)}) collective-permute-start(bf16[64,4608]{1,0:T(8,128)(2,1)} %get-tuple-element.329), channel_id=1, source_target_pairs={{0,2},{1,3},{2,0},{3,1},{4,6},{5,7},{6,4},{7,5},{8,10},{9,11},{10,... | collective-permute-start | bytes 1769480 | tf_op jit(solution)/shard_map/ppermute | solution.py:86
  535.9 26.0 %collective-permute-start.46 = (bf16[64,4608]{1,0:T(8,128)(2,1)S(1)}, bf16[64,4608]{1,0:T(8,128)(2,1)S(1)}, u32[]{:S(2)}, u32[]{:S(2)}) collective-permute-start(bf16[64,4608]{1,0:T(8,128)(2,1)S(1)} %get-tuple-element.326), channel_id=1, source_target_pairs={{0,2},{1,3},{2,0},{3,1},{4,6},{5,7},{6,4},{7,5},{8,10},{9,11},{10,... | collective-permute-start | bytes 1769480 | tf_op jit(solution)/shard_map/ppermute | solution.py:86
  537.6 24.3 %collective-permute-start.47 = (bf16[64,4608]{1,0:T(8,128)(2,1)S(1)}, bf16[64,4608]{1,0:T(8,128)(2,1)S(1)}, u32[]{:S(2)}, u32[]{:S(2)}) collective-permute-start(bf16[64,4608]{1,0:T(8,128)(2,1)S(1)} %add_convert_fusion.11), channel_id=1, source_target_pairs={{0,4},{1,5},{2,6},{3,7},{4,0},{5,1},{6,2},{7,3},{8,12},{9,13},{10,... | collective-permute-start | bytes 1769480 | tf_op jit(solution)/shard_map/ppermute | solution.py:86
  540.2 7.2 %collective-permute-start.49 = (bf16[64,1024]{1,0:T(8,128)(2,1)S(1)}, bf16[64,1024]{1,0:T(8,128)(2,1)S(1)}, u32[]{:S(2)}, u32[]{:S(2)}) collective-permute-start(bf16[64,1024]{1,0:T(8,128)(2,1)S(1)} %get-tuple-element.365), channel_id=1, source_target_pairs={{0,8},{1,9},{2,10},{3,11},{4,12},{5,13},{6,14},{7,15},{8,0},{9,1},... | collective-permute-start | bytes 393224 | tf_op jit(solution)/shard_map/ppermute | solution.py:78
  543.0 13.8 %collective-permute-start.50 = (bf16[2,64,2176]{2,1,0:T(8,128)(2,1)S(1)}, bf16[2,64,2176]{2,1,0:T(8,128)(2,1)S(1)}, u32[]{:S(2)}, u32[]{:S(2)}) collective-permute-start(bf16[2,64,2176]{2,1,0:T(8,128)(2,1)S(1)} %pad_maximum_fusion.19), channel_id=1, source_target_pairs={{0,8},{1,9},{2,10},{3,11},{4,12},{5,13},{6,14},{7,15},{8,0},{9,1},... | collective-permute-start | bytes 1671176 | tf_op jit(solution)/shard_map/ppermute | solution.py:78
  544.0 12.9 %collective-permute-start.51 = (bf16[2,64,2176]{2,1,0:T(8,128)(2,1)S(1)}, bf16[2,64,2176]{2,1,0:T(8,128)(2,1)S(1)}, u32[]{:S(2)}, u32[]{:S(2)}) collective-permute-start(bf16[2,64,2176]{2,1,0:T(8,128)(2,1)S(1)} %pad_maximum_fusion.20), channel_id=1, source_target_pairs={{0,16},{1,17},{2,18},{3,19},{4,20},{5,21},{6,22},{7,23},{8,24},{9,... | collective-permute-start | bytes 1671176 | tf_op jit(solution)/shard_map/ppermute | solution.py:78
  563.2 24.5 %collective-permute-start.52 = (bf16[64,2176]{1,0:T(8,128)(2,1)S(1)}, bf16[64,2176]{1,0:T(8,128)(2,1)S(1)}, u32[]{:S(2)}, u32[]{:S(2)}) collective-permute-start(bf16[64,2176]{1,0:T(8,128)(2,1)S(1)} %get-tuple-element.354), channel_id=1, source_target_pairs={{0,8},{1,9},{2,10},{3,11},{4,12},{5,13},{6,14},{7,15},{8,0},{9,1},... | collective-permute-start | bytes 835592 | tf_op jit(solution)/shard_map/ppermute | solution.py:78
  564.2 23.5 %collective-permute-start.53 = (bf16[64,2176]{1,0:T(8,128)(2,1)S(1)}, bf16[64,2176]{1,0:T(8,128)(2,1)S(1)}, u32[]{:S(2)}, u32[]{:S(2)}) collective-permute-start(bf16[64,2176]{1,0:T(8,128)(2,1)S(1)} %get-tuple-element.353), channel_id=1, source_target_pairs={{0,16},{1,17},{2,18},{3,19},{4,20},{5,21},{6,22},{7,23},{8,24},{9,... | collective-permute-start | bytes 835592 | tf_op jit(solution)/shard_map/ppermute | solution.py:78
  569.9 43.0 %collective-permute-start.62 = (bf16[64,4608]{1,0:T(8,128)(2,1)S(1)}, bf16[64,4608]{1,0:T(8,128)(2,1)S(1)}, u32[]{:S(2)}, u32[]{:S(2)}) collective-permute-start(bf16[64,4608]{1,0:T(8,128)(2,1)S(1)} %add_convert_fusion.10), channel_id=1, source_target_pairs={{0,2},{1,3},{2,0},{3,1},{4,6},{5,7},{6,4},{7,5},{8,10},{9,11},{10,... | collective-permute-start | bytes 1769480 | tf_op jit(solution)/shard_map/ppermute | solution.py:86
  574.0 12.4 %collective-permute-start.59 = (bf16[64,1024]{1,0:T(8,128)(2,1)S(1)}, bf16[64,1024]{1,0:T(8,128)(2,1)S(1)}, u32[]{:S(2)}, u32[]{:S(2)}) collective-permute-start(bf16[64,1024]{1,0:T(8,128)(2,1)S(1)} %add_convert_fusion.53), channel_id=1, source_target_pairs={{0,4},{1,5},{2,6},{3,7},{4,0},{5,1},{6,2},{7,3},{8,12},{9,13},{10,... | collective-permute-start | bytes 393224 | tf_op jit(solution)/shard_map/ppermute | solution.py:86
  574.3 53.7 %collective-permute-start.64 = (bf16[64,4608]{1,0:T(8,128)(2,1)S(1)}, bf16[64,4608]{1,0:T(8,128)(2,1)S(1)}, u32[]{:S(2)}, u32[]{:S(2)}) collective-permute-start(bf16[64,4608]{1,0:T(8,128)(2,1)S(1)} %add_convert_fusion.9), channel_id=1, source_target_pairs={{0,4},{1,5},{2,6},{3,7},{4,0},{5,1},{6,2},{7,3},{8,12},{9,13},{10,... | collective-permute-start | bytes 1769480 | tf_op jit(solution)/shard_map/ppermute | solution.py:86
  586.4 15.5 %collective-permute-start.60 = (bf16[64,1024]{1,0:T(8,128)(2,1)S(1)}, bf16[64,1024]{1,0:T(8,128)(2,1)S(1)}, u32[]{:S(2)}, u32[]{:S(2)}) collective-permute-start(bf16[64,1024]{1,0:T(8,128)(2,1)S(1)} %add_convert_fusion.52), channel_id=1, source_target_pairs={{0,2},{1,3},{2,0},{3,1},{4,6},{5,7},{6,4},{7,5},{8,10},{9,11},{10,... | collective-permute-start | bytes 393224 | tf_op jit(solution)/shard_map/ppermute | solution.py:86
  589.1 23.6 %collective-permute-start.54 = (bf16[64,2176]{1,0:T(8,128)(2,1)S(1)}, bf16[64,2176]{1,0:T(8,128)(2,1)S(1)}, u32[]{:S(2)}, u32[]{:S(2)}) collective-permute-start(bf16[64,2176]{1,0:T(8,128)(2,1)S(1)} %get-tuple-element.323), channel_id=1, source_target_pairs={{0,2},{1,3},{2,0},{3,1},{4,6},{5,7},{6,4},{7,5},{8,10},{9,11},{10,... | collective-permute-start | bytes 835592 | tf_op jit(solution)/shard_map/ppermute | solution.py:86
  601.9 27.7 %collective-permute-start.61 = (bf16[128,1024]{1,0:T(8,128)(2,1)S(1)}, bf16[128,1024]{1,0:T(8,128)(2,1)S(1)}, u32[]{:S(2)}, u32[]{:S(2)}) collective-permute-start(bf16[128,1024]{1,0:T(8,128)(2,1)S(1)} %pad_maximum_fusion.25), channel_id=1, source_target_pairs={{0,1},{1,0},{2,3},{3,2},{4,5},{5,4},{6,7},{7,6},{8,9},{9,8},{10,11... | collective-permute-start | bytes 786440 | tf_op jit(solution)/shard_map/ppermute | solution.py:86
  612.9 15.0 %collective-permute-start.55 = (bf16[64,2176]{1,0:T(8,128)(2,1)S(1)}, bf16[64,2176]{1,0:T(8,128)(2,1)S(1)}, u32[]{:S(2)}, u32[]{:S(2)}) collective-permute-start(bf16[64,2176]{1,0:T(8,128)(2,1)S(1)} %add_convert_fusion.41), channel_id=1, source_target_pairs={{0,4},{1,5},{2,6},{3,7},{4,0},{5,1},{6,2},{7,3},{8,12},{9,13},{10,... | collective-permute-start | bytes 835592 | tf_op jit(solution)/shard_map/ppermute | solution.py:86
  613.2 40.3 %collective-permute-start.63 = (bf16[128,4608]{1,0:T(8,128)(2,1)S(1)}, bf16[128,4608]{1,0:T(8,128)(2,1)S(1)}, u32[]{:S(2)}, u32[]{:S(2)}) collective-permute-start(bf16[128,4608]{1,0:T(8,128)(2,1)S(1)} %pad_maximum_fusion.10), channel_id=1, source_target_pairs={{0,1},{1,0},{2,3},{3,2},{4,5},{5,4},{6,7},{7,6},{8,9},{9,8},{10,11... | collective-permute-start | bytes 3538952 | tf_op jit(solution)/shard_map/ppermute | solution.py:86
  627.9 7.8 %collective-permute-start.56 = (bf16[64,2176]{1,0:T(8,128)(2,1)S(1)}, bf16[64,2176]{1,0:T(8,128)(2,1)S(1)}, u32[]{:S(2)}, u32[]{:S(2)}) collective-permute-start(bf16[64,2176]{1,0:T(8,128)(2,1)S(1)} %add_convert_fusion.40), channel_id=1, source_target_pairs={{0,2},{1,3},{2,0},{3,1},{4,6},{5,7},{6,4},{7,5},{8,10},{9,11},{10,... | collective-permute-start | bytes 835592 | tf_op jit(solution)/shard_map/ppermute | solution.py:86
  628.1 20.2 %collective-permute-start.65 = (bf16[64,4608]{1,0:T(8,128)(2,1)S(1)}, bf16[64,4608]{1,0:T(8,128)(2,1)S(1)}, u32[]{:S(2)}, u32[]{:S(2)}) collective-permute-start(bf16[64,4608]{1,0:T(8,128)(2,1)S(1)} %add_convert_fusion.8), channel_id=1, source_target_pairs={{0,2},{1,3},{2,0},{3,1},{4,6},{5,7},{6,4},{7,5},{8,10},{9,11},{10,... | collective-permute-start | bytes 1769480 | tf_op jit(solution)/shard_map/ppermute | solution.py:86
  635.8 14.1 %collective-permute-start.57 = (bf16[128,2176]{1,0:T(8,128)(2,1)S(1)}, bf16[128,2176]{1,0:T(8,128)(2,1)S(1)}, u32[]{:S(2)}, u32[]{:S(2)}) collective-permute-start(bf16[128,2176]{1,0:T(8,128)(2,1)S(1)} %pad_maximum_fusion.21), channel_id=1, source_target_pairs={{0,1},{1,0},{2,3},{3,2},{4,5},{5,4},{6,7},{7,6},{8,9},{9,8},{10,11... | collective-permute-start | bytes 1671176 | tf_op jit(solution)/shard_map/ppermute | solution.py:86
  648.5 7.8 %collective-permute-start.66 = (bf16[128,4608]{1,0:T(8,128)(2,1)S(1)}, bf16[128,4608]{1,0:T(8,128)(2,1)S(1)}, u32[]{:S(2)}, u32[]{:S(2)}) collective-permute-start(bf16[128,4608]{1,0:T(8,128)(2,1)S(1)} %pad_maximum_fusion.11), channel_id=1, source_target_pairs={{0,1},{1,0},{2,3},{3,2},{4,5},{5,4},{6,7},{7,6},{8,9},{9,8},{10,11... | collective-permute-start | bytes 3538952 | tf_op jit(solution)/shard_map/ppermute | solution.py:86
  (127 other events, 970.9 us)

commit v8 on v7

--- a/solution.py
+++ b/solution.py
@@ -842,10 +842,10 @@
     turn = jnp.concatenate([cosine[:, 0].T, sine_table[:, 0].T], axis=0)
     flat = (query_lin.reshape(row_count, -1), key_lin.reshape(row_count, -1), turn, qk_gains[:, None])
     lower = attend_back(query_rot, grad_attn_low, key_rot, value_low, segment, *flat, 0, panels)
-    grad_attn_low, lower = pin((grad_attn_low, lower))
+    grad_attn_low, lower = sync((grad_attn_low, lower), up_back, gate_back, down_back)
     upper = attend_back(query_rot, grad_attn_low, key_rot, value_low, segment, *flat, panels, panels)
     lower, upper, out_given, out_sent = sync(
-        (lower, upper, out_given, out_sent), gate_back, down_back, up_back
+        (lower, upper, out_given, out_sent), up_back, gate_back, down_back
     )
     out_back = Flow(scatter_steps(links, out_given, out_sent))
     grad_qk_gain = jnp.concatenate(
@@ -877,14 +877,17 @@
     )
     front_sent = rep_swap(other_front, 1)
     own_front, front_sent, mixed_act, grad_normed = sync(
-        (own_front, front_sent, mixed_act, grad_normed), out_back, up_back, gate_back
+        (own_front, front_sent, mixed_act, grad_normed), up_back, gate_back
     )
     front_back = Flow(scatter_steps(links, own_front, front_sent))
     grad_inputs = grad_hidden + norm_back(
         grad_normed, inputs, scale_one, full_attn_gain.astype(jnp.float32)
     )
     result = live_rows * (hidden + matmul_plain(mixed_act, full_down))
-    grad_inputs, result = sync((grad_inputs, result), up_back, gate_back, out_back, front_back)
+    grad_inputs, result = sync((grad_inputs, result), gate_back, front_back, out_back)
+    sync((), up_back, front_back, out_back)
+    sync((), up_back, front_back, out_back)
+    sync((), front_back, out_back)
     front_share = join_rows(front_back.finish())
     share_query = front_share[:, : HQ * HD]
     share_key = front_share[:, HQ * HD : (HQ + HK) * HD]

time: 665 us -> 653 us (0.982)
  waiting for transfers between devices: 123 us -> 107 us
  starting transfers between devices: 95.8 us -> 83.1 us
  other arithmetic: 97.9 us -> 108 us
    ppermute x33, waiting for transfers between devices: 72.6 us -> 60.6 us  [rep_swap(): return lax.ppermute(value, axes, pairs)]
    unnamed x255 -> x263, local copies, waits for them, and re-layouts: 13.4 us -> 16 us
  transfers between devices with their start and end apart: 69 -> 69, of which waited for: 24 -> 21; matrix products, arithmetic and copies ran while one was open for 29% -> 34% of each run, Pallas kernels for 22% -> 22%
where the time goes in v8:
time: 653 us; the launch traced here: 647 us
  Pallas kernels  177 us (27%)
  other arithmetic  108 us (17%)
  waiting for transfers between devices  107 us (16%)
  matrix products  106 us (16%)
  starting transfers between devices  83.1 us (13%)
  local copies, waits for them, and re-layouts  63.7 us (10%)
    dot_general x10, matrix products, matmul_rows(): lax.dot_general(left_mat, right_mat, (((0,), (0,)), ((), ())), preferred_...  64.2 us
    ppermute x33, waiting for transfers between devices, rep_swap(): return lax.ppermute(value, axes, pairs)  60.6 us
    ppermute x36, waiting for transfers between devices, shard_swap(): return lax.ppermute(value, axes, pairs)  46.9 us
    pallas_call x2, Pallas kernels, attend_back(): pl.pallas_call(attend_back_kernel, out_shape=(jax.ShapeDtypeStruct((rows,...  45 us
    ppermute x33, starting transfers between devices, rep_swap(): return lax.ppermute(value, axes, pairs)  44.7 us
    ppermute x36, starting transfers between devices, shard_swap(): return lax.ppermute(value, axes, pairs)  38.4 us
    pallas_call x2, Pallas kernels, ffn_forward(): pl.pallas_call(functools.partial(ffn_forward_kernel, count, len(into)), o...  33.3 us
    pallas_call x1, Pallas kernels, ffn_input(): pl.pallas_call(functools.partial(ffn_input_kernel, count), out_shape=jax....  28.5 us
  transfers between devices with their start and end apart: 69, of which 21 were waited for; matrix products, arithmetic and copies ran while one was open for 34% of the time, Pallas kernels for 22%

profile of v8, /device:TPU:1, one launch (start us, length us, event | category | flops | bytes accessed | tf_op | source)
XLA Modules:
  0.0 647.4 jit_solution(6444610242343846958)
XLA Ops:
  12.8 7.7 %collective-permute-done.refs_2_ = bf16[128,2176]{1,0:T(8,128)(2,1)S(1)} collective-permute-done((bf16[128,2176]{1,0:T(8,128)(2,1)S(1)}, bf16[128,2176]{1,0:T(8,128)(2,1)S(1)}, u32[]{:S(2)}, u32[]{:S(2)}) %collective-permute-start) | collective-permute-done | bytes 557088 | tf_op jit(solution)/shard_map/ppermute | solution.py:78
  29.0 5.4 collective-permute-start.4
  38.8 6.9 %place_blocks.3 = bf16[1024,2176]{1,0:T(8,128)(2,1)} custom-call(s32[8]{0:T(128)} %stack.70.spots_ref, bf16[256,2176]{1,0:T(8,128)(2,1)} %pad_maximum_fusion.13.refs_0_.refs_1_, bf16[256,2176]{1,0:T(8,128)(2,1)} %pad_maximum_fusion.13.refs_0_.refs_1_, bf16[128,2176]{1,0:T(8,128)(2,1)} %copy-done.26, bf16[128,2176]{1,0:T(8,128)(2,1)} %get-tuple-element.419.refs_3_, ...), custom_call_target="tpu_custom_call" | custom-call | flops 1 | bytes 1 | tf_op jit(solution)/shard_map/place_blocks/pallas_call | solution.py:141
  49.4 4.4 multiply_reduce_fusion.4
  53.8 2.6 multiply_reduce_fusion.5
  72.1 3.9 copy.106.q_ref
  77.4 23.8 %attend.1 = bf16[1024,1024]{1,0:T(8,128)(2,1)} custom-call(s32[4,4]{1,0:T(4,128)} %fusion.80.live_ref, bf16[1024,1024]{1,0:T(8,128)(2,1)} %copy.106.q_ref, bf16[1024,512]{1,0:T(8,128)(2,1)} %copy.107.k_ref, bf16[1024,512]{1,0:T(8,128)(2,1)} %convolution_convert_fusion.11.v_ref, s32[1024,1]{1,0:T(8,128)} %copy.108.seg_col_ref, s32[1,1024]{1,0:T(1,128)} %bitcast.190), custom_call_target="tpu_custom_call" | custom-call | flops 1 | bytes 1 | tf_op jit(solution)/shard_map/attend/pallas_call | solution.py:628
  104.6 6.8 %collective-permute-start.12 = (bf16[64,9216]{1,0:T(8,128)(2,1)}, bf16[64,9216]{1,0:T(8,128)(2,1)S(1)}, u32[]{:S(2)}, u32[]{:S(2)}) collective-permute-start(bf16[64,9216]{1,0:T(8,128)(2,1)} %slice.209), channel_id=1, source_target_pairs={{0,16},{1,17},{2,18},{3,19},{4,20},{5,21},{6,22},{7,23},{8,24},{9,... | collective-permute-start | bytes 3538952 | tf_op jit(solution)/shard_map/ppermute | solution.py:78
  114.7 5.4 place_blocks.4
  120.1 5.3 multiply_reduce_fusion.3
  128.1 10.0 %collective-permute-done.12 = bf16[64,9216]{1,0:T(8,128)(2,1)S(1)} collective-permute-done((bf16[64,9216]{1,0:T(8,128)(2,1)}, bf16[64,9216]{1,0:T(8,128)(2,1)S(1)}, u32[]{:S(2)}, u32[]{:S(2)}) %collective-permute-start.12) | collective-permute-done | bytes 1179680 | tf_op jit(solution)/shard_map/ppermute | solution.py:78
  138.1 3.3 collective-permute-done.13
  143.6 2.4 constant_dynamic-update-slice_fusion.4.refs_6_.refs_14_
  146.5 2.4 constant_dynamic-slice_fusion.28
  150.4 3.4 collective-permute-done.16.refs_7_.refs_15_
  153.8 15.3 %ffn_forward.2 = (bf16[1024,4608]{1,0:T(8,128)(2,1)}, bf16[1024,4608]{1,0:T(8,128)(2,1)}, bf16[1024,4608]{1,0:T(8,128)(2,1)}) custom-call(s32[8]{0:T(128)} %stack.70.spots_ref, bf16[1024,1024]{1,0:T(8,128)(2,1)} %multiply_convert_fusion.a_ref, bf16[256,4608]{1,0:T(8,128)(2,1)} %refs_1_.4, bf16[256,4608]{1,0:T(8,128)(2,1)} %refs_1_.4, ...), custom_call_target="tpu_custom_call" | custom-call | flops 1 | bytes 1 | tf_op jit(solution)/shard_map/ffn_forward/pallas_call | solution.py:205
  169.1 7.7 %collective-permute-done.17.refs_2_ = bf16[576,1024]{1,0:T(8,128)(2,1)S(1)} collective-permute-done((bf16[576,1024]{1,0:T(8,128)(2,1)}, bf16[576,1024]{1,0:T(8,128)(2,1)S(1)}, u32[]{:S(2)}, u32[]{:S(2)}) %collective-permute-start.17) | collective-permute-done | bytes 1179680 | tf_op jit(solution)/shard_map/ppermute | solution.py:78
  181.9 18.0 %ffn_forward.3 = (bf16[1024,4608]{1,0:T(8,128)(2,1)}, bf16[1024,4608]{1,0:T(8,128)(2,1)}, bf16[1024,4608]{1,0:T(8,128)(2,1)}) custom-call(s32[8]{0:T(128)} %stack.70.spots_ref, bf16[1024,1024]{1,0:T(8,128)(2,1)} %multiply_convert_fusion.a_ref, bf16[256,4608]{1,0:T(8,128)(2,1)} %refs_1_.4, ...), custom_call_target="tpu_custom_call", output_to_operand_aliasing={{0}: (18, {}), {1}: (19, {}), {2}: (20, {})} | custom-call | flops 1 | bytes 1 | tf_op jit(solution)/shard_map/ffn_forward/pallas_call | solution.py:205
  206.0 9.4 %place_blocks.5.down_ref = bf16[4608,1024]{1,0:T(8,128)(2,1)} custom-call(s32[8]{0:T(128)} %stack.70.spots_ref, bf16[1152,1024]{1,0:T(8,128)(2,1)} %refs_1_.3, bf16[1152,1024]{1,0:T(8,128)(2,1)} %refs_1_.3, bf16[576,1024]{1,0:T(8,128)(2,1)} %copy-done.32, bf16[576,1024]{1,0:T(8,128)(2,1)} %collective-permute-done.21.refs_3_, ...), custom_call_target="tpu_custom_call" | custom-call | flops 1 | bytes 1 | tf_op jit(solution)/shard_map/place_blocks/pallas_call | solution.py:141
  215.4 24.8 %ffn_inner.1 = (bf16[1024,4608]{1,0:T(8,128)(2,1)}, bf16[1024,4608]{1,0:T(8,128)(2,1)}) custom-call(bf16[1024,1024]{1,0:T(8,128)(2,1)} %copy-done.12, bf16[4608,1024]{1,0:T(8,128)(2,1)} %place_blocks.5.down_ref, bf16[1024,4608]{1,0:T(8,128)(2,1)} %get-tuple-element.223.act_ref, bf16[1024,4608]{1,0:T(8,128)(2,1)} %get-tuple-element.224.slope_ref), custom_call_target="tpu_custom_call" | custom-call | flops 1 | bytes 1 | tf_op jit(solution)/shard_map/ffn_inner/pallas_call | solution.py:238
  240.2 10.8 %convolution_convert_fusion.1 = bf16[4608,512]{1,0:T(8,128)(2,1)} fusion(bf16[1024,4608]{1,0:T(8,128)(2,1)} %get-tuple-element.301, bf16[1024,512]{1,0:T(8,128)(2,1)S(1)} %copy-done.59), kind=kOutput, calls=%fused_computation.6 | convolution fusion | flops 4834197504 | bytes 15204352 | tf_op jit(solution)/shard_map/dot_general | solution.py:57
  252.2 10.9 %convolution_convert_fusion.5 = bf16[512,4608]{1,0:T(8,128)(2,1)} fusion(bf16[1024,4608]{1,0:T(8,128)(2,1)} %get-tuple-element.243.dgate_ref, bf16[1024,128]{1,0:T(8,128)(2,1)S(1)} %get-tuple-element.411, bf16[1024,128]{1,0:T(8,128)(2,1)S(1)} %get-tuple-element.412, bf16[1024,128]{1,0:T(8,128)(2,1)S(1)} %get-tuple-element.413, ...), kind=kOutput, calls=%fused_computation.10 | convolution fusion | flops 4838391808 | bytes 15204352 | tf_op jit(solution)/shard_map/dot_general | solution.py:57
  263.2 6.9 %convolution_convert_fusion = bf16[4608,512]{1,0:T(8,128)(2,1)} fusion(bf16[1024,4608]{1,0:T(8,128)(2,1)S(1)} %bitcast.156, bf16[1024,512]{1,0:T(8,128)(2,1)S(1)} %copy-done.58), kind=kOutput, calls=%fused_computation.5 | convolution fusion | flops 4834197504 | bytes 15204352 | tf_op jit(solution)/shard_map/dot_general | solution.py:57
  270.2 7.1 %convolution_convert_fusion.2 = bf16[512,4608]{1,0:T(8,128)(2,1)} fusion(bf16[1024,512]{1,0:T(8,128)(2,1)S(1)} %pad_maximum_fusion.15, bf16[1024,4608]{1,0:T(8,128)(2,1)S(1)} %bitcast.160), kind=kOutput, calls=%fused_computation.7 | convolution fusion | flops 4834197504 | bytes 15204352 | tf_op jit(solution)/shard_map/dot_general | solution.py:57
  279.3 3.0 add_convert_fusion.34
  284.1 11.1 %convolution_convert_fusion.3 = bf16[512,4608]{1,0:T(8,128)(2,1)} fusion(bf16[1024,512]{1,0:T(8,128)(2,1)S(1)} %pad_maximum_fusion.16, bf16[1024,4608]{1,0:T(8,128)(2,1)} %get-tuple-element.244.dup_ref), kind=kOutput, calls=%fused_computation.8 | convolution fusion | flops 4834197504 | bytes 15204352 | tf_op jit(solution)/shard_map/dot_general | solution.py:57
  295.2 5.4 convolution_convert_fusion.4
  300.7 9.2 %collective-permute-done.27 = bf16[2,576,512]{2,1,0:T(8,128)(2,1)S(1)} collective-permute-done((bf16[2,576,512]{2,1,0:T(8,128)(2,1)S(1)}, bf16[2,576,512]{2,1,0:T(8,128)(2,1)S(1)}, u32[]{:S(2)}, u32[]{:S(2)}) %collective-permute-start.27) | collective-permute-done | bytes 1179680 | tf_op jit(solution)/shard_map/ppermute | solution.py:78
  309.9 3.8 fusion.61
  321.0 28.5 %ffn_input.1 = f32[1024,1024]{1,0:T(8,128)} custom-call(s32[8]{0:T(128)} %stack.70.spots_ref, bf16[1024,4608]{1,0:T(8,128)(2,1)} %get-tuple-element.243.dgate_ref, bf16[1024,4608]{1,0:T(8,128)(2,1)} %get-tuple-element.244.dup_ref, bf16[256,4608]{1,0:T(8,128)(2,1)} %refs_1_.4, bf16[256,4608]{1,0:T(8,128)(2,1)} %refs_1_.4, bf16[128,9216]{1,0:T(8,128)(2,1)} %copy-done.4, ...), custom_call_target="tpu_custom_call" | custom-call | flops 1 | bytes 1 | tf_op jit(solution)/shard_map/ffn_input/pallas_call | solution.py:280
  349.6 4.1 multiply_reduce_fusion.2
  360.9 2.6 broadcast_select_fusion.8
  365.9 3.7 convolution_convert_fusion.8.do_ref
  369.6 7.1 %collective-permute-done.34 = bf16[576,512]{1,0:T(8,128)(2,1)S(1)} collective-permute-done((bf16[576,512]{1,0:T(8,128)(2,1)S(1)}, bf16[576,512]{1,0:T(8,128)(2,1)S(1)}, u32[]{:S(2)}, u32[]{:S(2)}) %collective-permute-start.34) | collective-permute-done | bytes 589856 | tf_op jit(solution)/shard_map/ppermute | solution.py:86
  376.8 2.9 add_convert_fusion.22
  384.7 3.3 fusion.63
  388.5 2.4 collective-permute-start.39
  392.2 5.5 copy.113.q_lin_ref
  400.3 22.4 %attend_back.2 = (bf16[1024,512]{1,0:T(8,128)(2,1)}, bf16[1024,256]{1,0:T(8,128)(2,1)}, bf16[1024,256]{1,0:T(8,128)(2,1)}, f32[2,64,256]{2,1,0:T(8,128)}, f32[2,64,256]{2,1,0:T(8,128)}) custom-call(s32[4,4]{1,0:T(4,128)} %fusion.80.live_ref, bf16[1024,1024]{1,0:T(8,128)(2,1)} %copy.106.q_ref, bf16[1024,1024]{1,0:T(8,128)(2,1)} %convolution_convert_fusion.8.do_ref, ...), custom_call_target="tpu_custom_call" | custom-call | flops 1 | bytes 1 | tf_op jit(solution)/shard_map/attend_back/pallas_call | solution.py:652
  422.7 3.6 fusion.65
  426.4 5.8 collective-permute-start.40
  433.4 4.0 broadcast_select_fusion.5
  440.6 22.6 %attend_back.3 = (bf16[1024,512]{1,0:T(8,128)(2,1)}, bf16[1024,256]{1,0:T(8,128)(2,1)}, bf16[1024,256]{1,0:T(8,128)(2,1)}, f32[2,64,256]{2,1,0:T(8,128)}, f32[2,64,256]{2,1,0:T(8,128)}) custom-call(s32[4,4]{1,0:T(4,128)} %fusion.80.live_ref, bf16[1024,1024]{1,0:T(8,128)(2,1)} %copy.106.q_ref, bf16[1024,1024]{1,0:T(8,128)(2,1)} %convolution_convert_fusion.8.do_ref, ...), custom_call_target="tpu_custom_call" | custom-call | flops 1 | bytes 1 | tf_op jit(solution)/shard_map/attend_back/pallas_call | solution.py:652
  474.5 4.7 convolution_convert_fusion.6
  480.9 2.6 collective-permute-start.44
  483.5 3.8 convolution_convert_fusion.7
  487.3 3.3 fusion.53
  490.6 4.0 broadcast_select_fusion.4
  496.9 2.6 collective-permute-start.46
  508.8 4.1 fusion.12
  513.0 2.7 add_add_fusion
  515.7 12.3 %fusion.11 = f32[1152,1024]{1,0:T(8,128)} fusion(bf16[1152,512]{1,0:T(8,128)(2,1)} %collective-permute-done.68, bf16[576,512]{1,0:T(8,128)(2,1)S(1)} %get-tuple-element.421, bf16[576,512]{1,0:T(8,128)(2,1)S(1)} %get-tuple-element.420, pred[]{:T(512)S(6)} %eq.38), kind=kLoop, calls=%fused_computation.42 | loop fusion | flops 16515072 | bytes 7077889 | tf_op jit(solution)/shard_map/convert_element_type | solution.py:448
  530.2 13.1 %add_multiply_fusion = bf16[1024,1024]{1,0:T(8,128)(2,1)} fusion(f32[1024,1024]{1,0:T(8,128)S(1)} %copy-done.8, f32[1024]{0:T(1024)S(1)} %copy-done.94, bf16[1024,4608]{1,0:T(8,128)(2,1)} %get-tuple-element.301, bf16[4608,1024]{1,0:T(8,128)(2,1)S(1)} %bitcast.154), kind=kOutput, calls=%fused_computation.20 | convolution fusion | flops 9666822144 | bytes 25169920 | tf_op jit(solution)/shard_map/dot_general | solution.py:53
  551.0 2.5 fusion.5
  553.5 2.4 collective-permute-start.52
  556.0 6.0 collective-permute-done.48
  570.7 10.5 %collective-permute-done.52 = bf16[64,4608]{1,0:T(8,128)(2,1)S(1)} collective-permute-done((bf16[64,4608]{1,0:T(8,128)(2,1)S(1)}, bf16[64,4608]{1,0:T(8,128)(2,1)S(1)}, u32[]{:S(2)}, u32[]{:S(2)}) %collective-permute-start.52) | collective-permute-done | bytes 589856 | tf_op jit(solution)/shard_map/ppermute | solution.py:86
  587.9 15.5 %collective-permute-done.59 = bf16[64,1024]{1,0:T(8,128)(2,1)S(1)} collective-permute-done((bf16[64,1024]{1,0:T(8,128)(2,1)S(1)}, bf16[64,1024]{1,0:T(8,128)(2,1)S(1)}, u32[]{:S(2)}, u32[]{:S(2)}) %collective-permute-start.59) | collective-permute-done | bytes 131104 | tf_op jit(solution)/shard_map/ppermute | solution.py:86
  606.2 3.2 collective-permute-start.67
  609.5 14.8 %collective-permute-done.61 = bf16[64,1024]{1,0:T(8,128)(2,1)S(1)} collective-permute-done((bf16[64,1024]{1,0:T(8,128)(2,1)S(1)}, bf16[64,1024]{1,0:T(8,128)(2,1)S(1)}, u32[]{:S(2)}, u32[]{:S(2)}) %collective-permute-start.61) | collective-permute-done | bytes 131104 | tf_op jit(solution)/shard_map/ppermute | solution.py:86
  628.2 3.6 collective-permute-start.65
  631.8 2.7 collective-permute-done.62
  636.4 2.8 multiply_reduce_fusion.1
  643.9 2.8 multiply_reduce_fusion
  (521 shorter events, 169.4 us)
Async XLA Ops:
  6.0 14.5 %collective-permute-start = (bf16[128,2176]{1,0:T(8,128)(2,1)S(1)}, bf16[128,2176]{1,0:T(8,128)(2,1)S(1)}, u32[]{:S(2)}, u32[]{:S(2)}) collective-permute-start(bf16[128,2176]{1,0:T(8,128)(2,1)S(1)} %pad_maximum_fusion.18), channel_id=1, source_target_pairs={{0,8},{1,9},{2,10},{3,11},{4,12},{5,13},{6,14},{7,15},{8,0},{9,1},... | collective-permute-start | bytes 1671176 | tf_op jit(solution)/shard_map/ppermute | solution.py:78
  8.1 13.2 %collective-permute-start.1 = (bf16[128,2176]{1,0:T(8,128)(2,1)S(1)}, bf16[128,2176]{1,0:T(8,128)(2,1)S(1)}, u32[]{:S(2)}, u32[]{:S(2)}) collective-permute-start(bf16[128,2176]{1,0:T(8,128)(2,1)S(1)} %pad_maximum_fusion.18), channel_id=1, source_target_pairs={{0,16},{1,17},{2,18},{3,19},{4,20},{5,21},{6,22},{7,23},{8,24},{9,... | collective-permute-start | bytes 1671176 | tf_op jit(solution)/shard_map/ppermute | solution.py:78
  26.2 40.5 %collective-permute-start.5 = (bf16[128,1024]{1,0:T(8,128)(2,1)}, bf16[128,1024]{1,0:T(8,128)(2,1)}, u32[]{:S(2)}, u32[]{:S(2)}) collective-permute-start(bf16[128,1024]{1,0:T(8,128)(2,1)} %constant_dynamic-slice_fusion.31), channel_id=1, source_target_pairs={{0,8},{1,9},{2,10},{3,11},{4,12},{5,13},{6,14},{7,15},{8,0},{9,1},... | collective-permute-start | bytes 786440 | tf_op jit(solution)/shard_map/ppermute | solution.py:78
  27.4 39.4 %collective-permute-start.6 = (bf16[128,1024]{1,0:T(8,128)(2,1)}, bf16[128,1024]{1,0:T(8,128)(2,1)}, u32[]{:S(2)}, u32[]{:S(2)}) collective-permute-start(bf16[128,1024]{1,0:T(8,128)(2,1)} %constant_dynamic-slice_fusion.31), channel_id=1, source_target_pairs={{0,16},{1,17},{2,18},{3,19},{4,20},{5,21},{6,22},{7,23},{8,24},{9,... | collective-permute-start | bytes 786440 | tf_op jit(solution)/shard_map/ppermute | solution.py:78
  29.0 8.5 %collective-permute-start.4 = (bf16[3,128,2176]{2,1,0:T(8,128)(2,1)S(1)}, bf16[3,128,2176]{2,1,0:T(8,128)(2,1)S(1)}, u32[]{:S(2)}, u32[]{:S(2)}) collective-permute-start(bf16[3,128,2176]{2,1,0:T(8,128)(2,1)S(1)} %pad_maximum_fusion.3), channel_id=1, source_target_pairs={{0,1},{1,0},{2,3},{3,2},{4,5},{5,4},{6,7},{7,6},{8,9},{9,8},{10,11... | collective-permute-start | bytes 5013512 | tf_op jit(solution)/shard_map/ppermute | solution.py:86
  36.2 64.9 %collective-permute-start.9 = (bf16[128,9216]{1,0:T(8,128)(2,1)}, bf16[128,9216]{1,0:T(8,128)(2,1)S(1)}, u32[]{:S(2)}, u32[]{:S(2)}) collective-permute-start(bf16[128,9216]{1,0:T(8,128)(2,1)} %pad_maximum_fusion), channel_id=1, source_target_pairs={{0,8},{1,9},{2,10},{3,11},{4,12},{5,13},{6,14},{7,15},{8,0},{9,1},... | collective-permute-start | bytes 7077896 | tf_op jit(solution)/shard_map/ppermute | solution.py:78
  36.2 64.9 %collective-permute-start.10 = (bf16[128,9216]{1,0:T(8,128)(2,1)}, bf16[128,9216]{1,0:T(8,128)(2,1)}, u32[]{:S(2)}, u32[]{:S(2)}) collective-permute-start(bf16[128,9216]{1,0:T(8,128)(2,1)} %pad_maximum_fusion), channel_id=1, source_target_pairs={{0,16},{1,17},{2,18},{3,19},{4,20},{5,21},{6,22},{7,23},{8,24},{9,... | collective-permute-start | bytes 7077896 | tf_op jit(solution)/shard_map/ppermute | solution.py:78
  68.3 32.8 %collective-permute-start.7 = (bf16[64,1024]{1,0:T(8,128)(2,1)}, bf16[64,1024]{1,0:T(8,128)(2,1)S(1)}, u32[]{:S(2)}, u32[]{:S(2)}) collective-permute-start(bf16[64,1024]{1,0:T(8,128)(2,1)} %slice.203), channel_id=1, source_target_pairs={{0,16},{1,17},{2,18},{3,19},{4,20},{5,21},{6,22},{7,23},{8,24},{9,... | collective-permute-start | bytes 393224 | tf_op jit(solution)/shard_map/ppermute | solution.py:78
  70.0 31.2 %collective-permute-start.8 = (bf16[64,1024]{1,0:T(8,128)(2,1)}, bf16[64,1024]{1,0:T(8,128)(2,1)}, u32[]{:S(2)}, u32[]{:S(2)}) collective-permute-start(bf16[64,1024]{1,0:T(8,128)(2,1)} %slice.204), channel_id=1, source_target_pairs={{0,8},{1,9},{2,10},{3,11},{4,12},{5,13},{6,14},{7,15},{8,0},{9,1},... | collective-permute-start | bytes 393224 | tf_op jit(solution)/shard_map/ppermute | solution.py:78
  103.5 10.4 %collective-permute-start.11 = (bf16[3,128,1024]{2,1,0:T(8,128)(2,1)S(1)}, bf16[3,128,1024]{2,1,0:T(8,128)(2,1)S(1)}, u32[]{:S(2)}, u32[]{:S(2)}) collective-permute-start(bf16[3,128,1024]{2,1,0:T(8,128)(2,1)S(1)} %pad_maximum_fusion.17), channel_id=1, source_target_pairs={{0,1},{1,0},{2,3},{3,2},{4,5},{5,4},{6,7},{7,6},{8,9},{9,8},{10,11... | collective-permute-start | bytes 2359304 | tf_op jit(solution)/shard_map/ppermute | solution.py:86
  104.6 33.5 %collective-permute-start.12 = (bf16[64,9216]{1,0:T(8,128)(2,1)}, bf16[64,9216]{1,0:T(8,128)(2,1)S(1)}, u32[]{:S(2)}, u32[]{:S(2)}) collective-permute-start(bf16[64,9216]{1,0:T(8,128)(2,1)} %slice.209), channel_id=1, source_target_pairs={{0,16},{1,17},{2,18},{3,19},{4,20},{5,21},{6,22},{7,23},{8,24},{9,... | collective-permute-start | bytes 3538952 | tf_op jit(solution)/shard_map/ppermute | solution.py:78
  113.8 27.6 %collective-permute-start.13 = (bf16[64,9216]{1,0:T(8,128)(2,1)}, bf16[64,9216]{1,0:T(8,128)(2,1)}, u32[]{:S(2)}, u32[]{:S(2)}) collective-permute-start(bf16[64,9216]{1,0:T(8,128)(2,1)} %slice.210), channel_id=1, source_target_pairs={{0,8},{1,9},{2,10},{3,11},{4,12},{5,13},{6,14},{7,15},{8,0},{9,1},... | collective-permute-start | bytes 3538952 | tf_op jit(solution)/shard_map/ppermute | solution.py:78
  141.4 8.7 %collective-permute-start.14 = (bf16[128,9216]{1,0:T(8,128)(2,1)S(1)}, bf16[128,9216]{1,0:T(8,128)(2,1)}, u32[]{:S(2)}, u32[]{:S(2)}) collective-permute-start(bf16[128,9216]{1,0:T(8,128)(2,1)S(1)} %collective-permute-done.9.refs_2_.refs_10_), channel_id=1, source_target_pairs={{0,1},{1,0},{2,3},{3,2},{4,5},{5,4},{6,7},{7,6},{8,9},{9,8},{10,11... | collective-permute-start | bytes 7077896 | tf_op jit(solution)/shard_map/ppermute | solution.py:86
  142.5 7.9 %collective-permute-start.15 = (bf16[128,9216]{1,0:T(8,128)(2,1)}, bf16[128,9216]{1,0:T(8,128)(2,1)}, u32[]{:S(2)}, u32[]{:S(2)}) collective-permute-start(bf16[128,9216]{1,0:T(8,128)(2,1)} %collective-permute-done.10.refs_4_.refs_12_), channel_id=1, source_target_pairs={{0,1},{1,0},{2,3},{3,2},{4,5},{5,4},{6,7},{7,6},{8,9},{9,8},{10,11... | collective-permute-start | bytes 7077896 | tf_op jit(solution)/shard_map/ppermute | solution.py:86
  146.0 7.8 %collective-permute-start.16 = (bf16[128,9216]{1,0:T(8,128)(2,1)}, bf16[128,9216]{1,0:T(8,128)(2,1)}, u32[]{:S(2)}, u32[]{:S(2)}) collective-permute-start(bf16[128,9216]{1,0:T(8,128)(2,1)} %constant_dynamic-update-slice_fusion.4.refs_6_.refs_14_), channel_id=1, source_target_pairs={{0,1},{1,0},{2,3},{3,2},{4,5},{5,4},{6,7},{7,6},{8,9},{9,8},{10,11... | collective-permute-start | bytes 7077896 | tf_op jit(solution)/shard_map/ppermute | solution.py:86
  148.9 27.9 %collective-permute-start.17 = (bf16[576,1024]{1,0:T(8,128)(2,1)}, bf16[576,1024]{1,0:T(8,128)(2,1)S(1)}, u32[]{:S(2)}, u32[]{:S(2)}) collective-permute-start(bf16[576,1024]{1,0:T(8,128)(2,1)} %constant_dynamic-slice_fusion.28), channel_id=1, source_target_pairs={{0,8},{1,9},{2,10},{3,11},{4,12},{5,13},{6,14},{7,15},{8,0},{9,1},... | collective-permute-start | bytes 3538952 | tf_op jit(solution)/shard_map/ppermute | solution.py:78
  148.9 27.9 %collective-permute-start.18 = (bf16[576,1024]{1,0:T(8,128)(2,1)}, bf16[576,1024]{1,0:T(8,128)(2,1)}, u32[]{:S(2)}, u32[]{:S(2)}) collective-permute-start(bf16[576,1024]{1,0:T(8,128)(2,1)} %constant_dynamic-slice_fusion.28), channel_id=1, source_target_pairs={{0,16},{1,17},{2,18},{3,19},{4,20},{5,21},{6,22},{7,23},{8,24},{9,... | collective-permute-start | bytes 3538952 | tf_op jit(solution)/shard_map/ppermute | solution.py:78
  176.8 23.1 %collective-permute-start.21 = (bf16[576,1024]{1,0:T(8,128)(2,1)S(1)}, bf16[576,1024]{1,0:T(8,128)(2,1)}, u32[]{:S(2)}, u32[]{:S(2)}) collective-permute-start(bf16[576,1024]{1,0:T(8,128)(2,1)S(1)} %collective-permute-done.17.refs_2_), channel_id=1, source_target_pairs={{0,1},{1,0},{2,3},{3,2},{4,5},{5,4},{6,7},{7,6},{8,9},{9,8},{10,11... | collective-permute-start | bytes 3538952 | tf_op jit(solution)/shard_map/ppermute | solution.py:86
  177.6 22.3 %collective-permute-start.22 = (bf16[576,1024]{1,0:T(8,128)(2,1)}, bf16[576,1024]{1,0:T(8,128)(2,1)}, u32[]{:S(2)}, u32[]{:S(2)}) collective-permute-start(bf16[576,1024]{1,0:T(8,128)(2,1)} %collective-permute-done.18.refs_4_), channel_id=1, source_target_pairs={{0,1},{1,0},{2,3},{3,2},{4,5},{5,4},{6,7},{7,6},{8,9},{9,8},{10,11... | collective-permute-start | bytes 3538952 | tf_op jit(solution)/shard_map/ppermute | solution.py:86
  180.4 19.5 %collective-permute-start.19 = (bf16[288,1024]{1,0:T(8,128)(2,1)}, bf16[288,1024]{1,0:T(8,128)(2,1)}, u32[]{:S(2)}, u32[]{:S(2)}) collective-permute-start(bf16[288,1024]{1,0:T(8,128)(2,1)} %slice.211), channel_id=1, source_target_pairs={{0,16},{1,17},{2,18},{3,19},{4,20},{5,21},{6,22},{7,23},{8,24},{9,... | collective-permute-start | bytes 1769480 | tf_op jit(solution)/shard_map/ppermute | solution.py:78
  180.4 19.5 %collective-permute-start.20 = (bf16[288,1024]{1,0:T(8,128)(2,1)}, bf16[288,1024]{1,0:T(8,128)(2,1)}, u32[]{:S(2)}, u32[]{:S(2)}) collective-permute-start(bf16[288,1024]{1,0:T(8,128)(2,1)} %slice.212), channel_id=1, source_target_pairs={{0,8},{1,9},{2,10},{3,11},{4,12},{5,13},{6,14},{7,15},{8,0},{9,1},... | collective-permute-start | bytes 1769480 | tf_op jit(solution)/shard_map/ppermute | solution.py:78
  251.0 12.2 %collective-permute-start.24 = (bf16[4,1152,512]{2,1,0:T(8,128)(2,1)}, bf16[4,1152,512]{2,1,0:T(8,128)(2,1)}, u32[]{:S(2)}, u32[]{:S(2)}) collective-permute-start(bf16[4,1152,512]{2,1,0:T(8,128)(2,1)} %bitcast.27), channel_id=1, source_target_pairs={{0,1},{1,0},{2,3},{3,2},{4,5},{5,4},{6,7},{7,6},{8,9},{9,8},{10,11... | collective-permute-start | bytes 14155784 | tf_op jit(solution)/shard_map/ppermute | solution.py:86
  263.1 37.6 %collective-permute-start.25 = (bf16[4,128,4608]{2,1,0:T(8,128)(2,1)}, bf16[4,128,4608]{2,1,0:T(8,128)(2,1)}, u32[]{:S(2)}, u32[]{:S(2)}) collective-permute-start(bf16[4,128,4608]{2,1,0:T(8,128)(2,1)} %bitcast.30), channel_id=1, source_target_pairs={{0,1},{1,0},{2,3},{3,2},{4,5},{5,4},{6,7},{7,6},{8,9},{9,8},{10,11... | collective-permute-start | bytes 14155784 | tf_op jit(solution)/shard_map/ppermute | solution.py:86
  277.3 32.6 %collective-permute-start.26 = (bf16[4,128,4608]{2,1,0:T(8,128)(2,1)}, bf16[4,128,4608]{2,1,0:T(8,128)(2,1)}, u32[]{:S(2)}, u32[]{:S(2)}) collective-permute-start(bf16[4,128,4608]{2,1,0:T(8,128)(2,1)} %bitcast.32), channel_id=1, source_target_pairs={{0,1},{1,0},{2,3},{3,2},{4,5},{5,4},{6,7},{7,6},{8,9},{9,8},{10,11... | collective-permute-start | bytes 14155784 | tf_op jit(solution)/shard_map/ppermute | solution.py:86
  282.4 27.5 %collective-permute-start.27 = (bf16[2,576,512]{2,1,0:T(8,128)(2,1)S(1)}, bf16[2,576,512]{2,1,0:T(8,128)(2,1)S(1)}, u32[]{:S(2)}, u32[]{:S(2)}) collective-permute-start(bf16[2,576,512]{2,1,0:T(8,128)(2,1)S(1)} %pad_maximum_fusion.4), channel_id=1, source_target_pairs={{0,8},{1,9},{2,10},{3,11},{4,12},{5,13},{6,14},{7,15},{8,0},{9,1},... | collective-permute-start | bytes 3538952 | tf_op jit(solution)/shard_map/ppermute | solution.py:78
  282.6 27.3 %collective-permute-start.28 = (bf16[2,576,512]{2,1,0:T(8,128)(2,1)S(1)}, bf16[2,576,512]{2,1,0:T(8,128)(2,1)S(1)}, u32[]{:S(2)}, u32[]{:S(2)}) collective-permute-start(bf16[2,576,512]{2,1,0:T(8,128)(2,1)S(1)} %pad_maximum_fusion.5), channel_id=1, source_target_pairs={{0,16},{1,17},{2,18},{3,19},{4,20},{5,21},{6,22},{7,23},{8,24},{9,... | collective-permute-start | bytes 3538952 | tf_op jit(solution)/shard_map/ppermute | solution.py:78
  313.6 35.9 %collective-permute-start.29 = (bf16[576,512]{1,0:T(8,128)(2,1)}, bf16[576,512]{1,0:T(8,128)(2,1)}, u32[]{:S(2)}, u32[]{:S(2)}) collective-permute-start(bf16[576,512]{1,0:T(8,128)(2,1)} %get-tuple-element.368), channel_id=1, source_target_pairs={{0,16},{1,17},{2,18},{3,19},{4,20},{5,21},{6,22},{7,23},{8,24},{9,... | collective-permute-start | bytes 1769480 | tf_op jit(solution)/shard_map/ppermute | solution.py:78
  315.0 34.5 %collective-permute-start.30 = (bf16[576,512]{1,0:T(8,128)(2,1)S(1)}, bf16[576,512]{1,0:T(8,128)(2,1)}, u32[]{:S(2)}, u32[]{:S(2)}) collective-permute-start(bf16[576,512]{1,0:T(8,128)(2,1)S(1)} %get-tuple-element.367), channel_id=1, source_target_pairs={{0,8},{1,9},{2,10},{3,11},{4,12},{5,13},{6,14},{7,15},{8,0},{9,1},... | collective-permute-start | bytes 1769480 | tf_op jit(solution)/shard_map/ppermute | solution.py:78
  319.2 57.5 %collective-permute-start.32 = (bf16[2,64,4608]{2,1,0:T(8,128)(2,1)}, bf16[2,64,4608]{2,1,0:T(8,128)(2,1)S(1)}, u32[]{:S(2)}, u32[]{:S(2)}) collective-permute-start(bf16[2,64,4608]{2,1,0:T(8,128)(2,1)} %pad_maximum_fusion.6), channel_id=1, source_target_pairs={{0,8},{1,9},{2,10},{3,11},{4,12},{5,13},{6,14},{7,15},{8,0},{9,1},... | collective-permute-start | bytes 3538952 | tf_op jit(solution)/shard_map/ppermute | solution.py:78
  320.9 55.8 %collective-permute-start.33 = (bf16[2,64,4608]{2,1,0:T(8,128)(2,1)}, bf16[2,64,4608]{2,1,0:T(8,128)(2,1)}, u32[]{:S(2)}, u32[]{:S(2)}) collective-permute-start(bf16[2,64,4608]{2,1,0:T(8,128)(2,1)} %pad_maximum_fusion.7), channel_id=1, source_target_pairs={{0,16},{1,17},{2,18},{3,19},{4,20},{5,21},{6,22},{7,23},{8,24},{9,... | collective-permute-start | bytes 3538952 | tf_op jit(solution)/shard_map/ppermute | solution.py:78
  358.8 18.0 %collective-permute-start.31 = (bf16[4,128,1024]{2,1,0:T(8,128)(2,1)S(1)}, bf16[4,128,1024]{2,1,0:T(8,128)(2,1)S(1)}, u32[]{:S(2)}, u32[]{:S(2)}) collective-permute-start(bf16[4,128,1024]{2,1,0:T(8,128)(2,1)S(1)} %bitcast.195), channel_id=1, source_target_pairs={{0,1},{1,0},{2,3},{3,2},{4,5},{5,4},{6,7},{7,6},{8,9},{9,8},{10,11... | collective-permute-start | bytes 3145736 | tf_op jit(solution)/shard_map/ppermute | solution.py:86
  363.6 13.2 %collective-permute-start.34 = (bf16[576,512]{1,0:T(8,128)(2,1)S(1)}, bf16[576,512]{1,0:T(8,128)(2,1)S(1)}, u32[]{:S(2)}, u32[]{:S(2)}) collective-permute-start(bf16[576,512]{1,0:T(8,128)(2,1)S(1)} %get-tuple-element.352), channel_id=1, source_target_pairs={{0,2},{1,3},{2,0},{3,1},{4,6},{5,7},{6,4},{7,5},{8,10},{9,11},{10,... | collective-permute-start | bytes 1769480 | tf_op jit(solution)/shard_map/ppermute | solution.py:86
  380.9 41.8 %collective-permute-start.35 = (bf16[2,64,4608]{2,1,0:T(8,128)(2,1)}, bf16[2,64,4608]{2,1,0:T(8,128)(2,1)}, u32[]{:S(2)}, u32[]{:S(2)}) collective-permute-start(bf16[2,64,4608]{2,1,0:T(8,128)(2,1)} %pad_maximum_fusion.8), channel_id=1, source_target_pairs={{0,8},{1,9},{2,10},{3,11},{4,12},{5,13},{6,14},{7,15},{8,0},{9,1},... | collective-permute-start | bytes 3538952 | tf_op jit(solution)/shard_map/ppermute | solution.py:78
  383.2 39.5 %collective-permute-start.36 = (bf16[2,64,4608]{2,1,0:T(8,128)(2,1)}, bf16[2,64,4608]{2,1,0:T(8,128)(2,1)}, u32[]{:S(2)}, u32[]{:S(2)}) collective-permute-start(bf16[2,64,4608]{2,1,0:T(8,128)(2,1)} %pad_maximum_fusion.9), channel_id=1, source_target_pairs={{0,16},{1,17},{2,18},{3,19},{4,20},{5,21},{6,22},{7,23},{8,24},{9,... | collective-permute-start | bytes 3538952 | tf_op jit(solution)/shard_map/ppermute | solution.py:78
  388.0 34.7 %collective-permute-start.37 = (bf16[64,4608]{1,0:T(8,128)(2,1)}, bf16[64,4608]{1,0:T(8,128)(2,1)}, u32[]{:S(2)}, u32[]{:S(2)}) collective-permute-start(bf16[64,4608]{1,0:T(8,128)(2,1)} %get-tuple-element.358), channel_id=1, source_target_pairs={{0,16},{1,17},{2,18},{3,19},{4,20},{5,21},{6,22},{7,23},{8,24},{9,... | collective-permute-start | bytes 1769480 | tf_op jit(solution)/shard_map/ppermute | solution.py:78
  388.0 34.6 %collective-permute-start.38 = (bf16[64,4608]{1,0:T(8,128)(2,1)}, bf16[64,4608]{1,0:T(8,128)(2,1)}, u32[]{:S(2)}, u32[]{:S(2)}) collective-permute-start(bf16[64,4608]{1,0:T(8,128)(2,1)} %get-tuple-element.357), channel_id=1, source_target_pairs={{0,8},{1,9},{2,10},{3,11},{4,12},{5,13},{6,14},{7,15},{8,0},{9,1},... | collective-permute-start | bytes 1769480 | tf_op jit(solution)/shard_map/ppermute | solution.py:78
  388.5 34.2 %collective-permute-start.39 = (bf16[576,512]{1,0:T(8,128)(2,1)S(1)}, bf16[576,512]{1,0:T(8,128)(2,1)S(1)}, u32[]{:S(2)}, u32[]{:S(2)}) collective-permute-start(bf16[576,512]{1,0:T(8,128)(2,1)S(1)} %add_convert_fusion.18), channel_id=1, source_target_pairs={{0,4},{1,5},{2,6},{3,7},{4,0},{5,1},{6,2},{7,3},{8,12},{9,13},{10,... | collective-permute-start | bytes 1769480 | tf_op jit(solution)/shard_map/ppermute | solution.py:86
  426.4 36.9 %collective-permute-start.40 = (bf16[64,4608]{1,0:T(8,128)(2,1)}, bf16[64,4608]{1,0:T(8,128)(2,1)}, u32[]{:S(2)}, u32[]{:S(2)}) collective-permute-start(bf16[64,4608]{1,0:T(8,128)(2,1)} %get-tuple-element.356), channel_id=1, source_target_pairs={{0,16},{1,17},{2,18},{3,19},{4,20},{5,21},{6,22},{7,23},{8,24},{9,... | collective-permute-start | bytes 1769480 | tf_op jit(solution)/shard_map/ppermute | solution.py:78
  432.1 31.1 %collective-permute-start.41 = (bf16[64,4608]{1,0:T(8,128)(2,1)}, bf16[64,4608]{1,0:T(8,128)(2,1)}, u32[]{:S(2)}, u32[]{:S(2)}) collective-permute-start(bf16[64,4608]{1,0:T(8,128)(2,1)} %get-tuple-element.355), channel_id=1, source_target_pairs={{0,8},{1,9},{2,10},{3,11},{4,12},{5,13},{6,14},{7,15},{8,0},{9,1},... | collective-permute-start | bytes 1769480 | tf_op jit(solution)/shard_map/ppermute | solution.py:78
  437.3 25.9 %collective-permute-start.42 = (bf16[64,4608]{1,0:T(8,128)(2,1)}, bf16[64,4608]{1,0:T(8,128)(2,1)}, u32[]{:S(2)}, u32[]{:S(2)}) collective-permute-start(bf16[64,4608]{1,0:T(8,128)(2,1)} %get-tuple-element.349), channel_id=1, source_target_pairs={{0,2},{1,3},{2,0},{3,1},{4,6},{5,7},{6,4},{7,5},{8,10},{9,11},{10,... | collective-permute-start | bytes 1769480 | tf_op jit(solution)/shard_map/ppermute | solution.py:86
  437.5 25.8 %collective-permute-start.43 = (bf16[576,512]{1,0:T(8,128)(2,1)S(1)}, bf16[576,512]{1,0:T(8,128)(2,1)S(1)}, u32[]{:S(2)}, u32[]{:S(2)}) collective-permute-start(bf16[576,512]{1,0:T(8,128)(2,1)S(1)} %add_convert_fusion.13), channel_id=1, source_target_pairs={{0,2},{1,3},{2,0},{3,1},{4,6},{5,7},{6,4},{7,5},{8,10},{9,11},{10,... | collective-permute-start | bytes 1769480 | tf_op jit(solution)/shard_map/ppermute | solution.py:86
  480.9 47.1 %collective-permute-start.44 = (bf16[4,128,2176]{2,1,0:T(8,128)(2,1)}, bf16[4,128,2176]{2,1,0:T(8,128)(2,1)}, u32[]{:S(2)}, u32[]{:S(2)}) collective-permute-start(bf16[4,128,2176]{2,1,0:T(8,128)(2,1)} %pad_maximum_fusion.2), channel_id=1, source_target_pairs={{0,1},{1,0},{2,3},{3,2},{4,5},{5,4},{6,7},{7,6},{8,9},{9,8},{10,11... | collective-permute-start | bytes 6684680 | tf_op jit(solution)/shard_map/ppermute | solution.py:86
  494.6 33.4 %collective-permute-start.45 = (bf16[64,4608]{1,0:T(8,128)(2,1)}, bf16[64,4608]{1,0:T(8,128)(2,1)}, u32[]{:S(2)}, u32[]{:S(2)}) collective-permute-start(bf16[64,4608]{1,0:T(8,128)(2,1)} %get-tuple-element.346), channel_id=1, source_target_pairs={{0,2},{1,3},{2,0},{3,1},{4,6},{5,7},{6,4},{7,5},{8,10},{9,11},{10,... | collective-permute-start | bytes 1769480 | tf_op jit(solution)/shard_map/ppermute | solution.py:86
  496.9 31.1 %collective-permute-start.46 = (bf16[64,4608]{1,0:T(8,128)(2,1)S(1)}, bf16[64,4608]{1,0:T(8,128)(2,1)}, u32[]{:S(2)}, u32[]{:S(2)}) collective-permute-start(bf16[64,4608]{1,0:T(8,128)(2,1)S(1)} %add_convert_fusion.10), channel_id=1, source_target_pairs={{0,4},{1,5},{2,6},{3,7},{4,0},{5,1},{6,2},{7,3},{8,12},{9,13},{10,... | collective-permute-start | bytes 1769480 | tf_op jit(solution)/shard_map/ppermute | solution.py:86
  500.4 53.1 %collective-permute-start.50 = (bf16[2,64,1024]{2,1,0:T(8,128)(2,1)}, bf16[2,64,1024]{2,1,0:T(8,128)(2,1)S(1)}, u32[]{:S(2)}, u32[]{:S(2)}) collective-permute-start(bf16[2,64,1024]{2,1,0:T(8,128)(2,1)} %pad_maximum_fusion.23), channel_id=1, source_target_pairs={{0,8},{1,9},{2,10},{3,11},{4,12},{5,13},{6,14},{7,15},{8,0},{9,1},... | collective-permute-start | bytes 786440 | tf_op jit(solution)/shard_map/ppermute | solution.py:78
  503.4 12.3 %collective-permute-start.68 = (bf16[1152,512]{1,0:T(8,128)(2,1)}, bf16[1152,512]{1,0:T(8,128)(2,1)}, u32[]{:S(2)}, u32[]{:S(2)}) collective-permute-start(bf16[1152,512]{1,0:T(8,128)(2,1)} %pad_maximum_fusion.12), channel_id=1, source_target_pairs={{0,1},{1,0},{2,3},{3,2},{4,5},{5,4},{6,7},{7,6},{8,9},{9,8},{10,11... | collective-permute-start | bytes 3538952 | tf_op jit(solution)/shard_map/ppermute | solution.py:86
  515.7 40.3 %collective-permute-start.51 = (bf16[2,64,1024]{2,1,0:T(8,128)(2,1)}, bf16[2,64,1024]{2,1,0:T(8,128)(2,1)}, u32[]{:S(2)}, u32[]{:S(2)}) collective-permute-start(bf16[2,64,1024]{2,1,0:T(8,128)(2,1)} %pad_maximum_fusion.24), channel_id=1, source_target_pairs={{0,16},{1,17},{2,18},{3,19},{4,20},{5,21},{6,22},{7,23},{8,24},{9,... | collective-permute-start | bytes 786440 | tf_op jit(solution)/shard_map/ppermute | solution.py:78
  544.5 20.1 %collective-permute-start.47 = (bf16[64,4608]{1,0:T(8,128)(2,1)S(1)}, bf16[64,4608]{1,0:T(8,128)(2,1)S(1)}, u32[]{:S(2)}, u32[]{:S(2)}) collective-permute-start(bf16[64,4608]{1,0:T(8,128)(2,1)S(1)} %add_convert_fusion.9), channel_id=1, source_target_pairs={{0,2},{1,3},{2,0},{3,1},{4,6},{5,7},{6,4},{7,5},{8,10},{9,11},{10,... | collective-permute-start | bytes 1769480 | tf_op jit(solution)/shard_map/ppermute | solution.py:86
  547.8 14.2 %collective-permute-start.48 = (bf16[2,64,2176]{2,1,0:T(8,128)(2,1)S(1)}, bf16[2,64,2176]{2,1,0:T(8,128)(2,1)S(1)}, u32[]{:S(2)}, u32[]{:S(2)}) collective-permute-start(bf16[2,64,2176]{2,1,0:T(8,128)(2,1)S(1)} %pad_maximum_fusion.19), channel_id=1, source_target_pairs={{0,8},{1,9},{2,10},{3,11},{4,12},{5,13},{6,14},{7,15},{8,0},{9,1},... | collective-permute-start | bytes 1671176 | tf_op jit(solution)/shard_map/ppermute | solution.py:78
  549.6 13.4 %collective-permute-start.49 = (bf16[2,64,2176]{2,1,0:T(8,128)(2,1)S(1)}, bf16[2,64,2176]{2,1,0:T(8,128)(2,1)S(1)}, u32[]{:S(2)}, u32[]{:S(2)}) collective-permute-start(bf16[2,64,2176]{2,1,0:T(8,128)(2,1)S(1)} %pad_maximum_fusion.20), channel_id=1, source_target_pairs={{0,16},{1,17},{2,18},{3,19},{4,20},{5,21},{6,22},{7,23},{8,24},{9,... | collective-permute-start | bytes 1671176 | tf_op jit(solution)/shard_map/ppermute | solution.py:78
  553.5 27.7 %collective-permute-start.52 = (bf16[64,4608]{1,0:T(8,128)(2,1)S(1)}, bf16[64,4608]{1,0:T(8,128)(2,1)S(1)}, u32[]{:S(2)}, u32[]{:S(2)}) collective-permute-start(bf16[64,4608]{1,0:T(8,128)(2,1)S(1)} %add_convert_fusion.8), channel_id=1, source_target_pairs={{0,4},{1,5},{2,6},{3,7},{4,0},{5,1},{6,2},{7,3},{8,12},{9,13},{10,... | collective-permute-start | bytes 1769480 | tf_op jit(solution)/shard_map/ppermute | solution.py:86
  565.8 15.4 %collective-permute-start.53 = (bf16[64,2176]{1,0:T(8,128)(2,1)S(1)}, bf16[64,2176]{1,0:T(8,128)(2,1)S(1)}, u32[]{:S(2)}, u32[]{:S(2)}) collective-permute-start(bf16[64,2176]{1,0:T(8,128)(2,1)S(1)} %get-tuple-element.374), channel_id=1, source_target_pairs={{0,16},{1,17},{2,18},{3,19},{4,20},{5,21},{6,22},{7,23},{8,24},{9,... | collective-permute-start | bytes 835592 | tf_op jit(solution)/shard_map/ppermute | solution.py:78
  567.2 14.0 %collective-permute-start.54 = (bf16[64,2176]{1,0:T(8,128)(2,1)S(1)}, bf16[64,2176]{1,0:T(8,128)(2,1)S(1)}, u32[]{:S(2)}, u32[]{:S(2)}) collective-permute-start(bf16[64,2176]{1,0:T(8,128)(2,1)S(1)} %get-tuple-element.373), channel_id=1, source_target_pairs={{0,8},{1,9},{2,10},{3,11},{4,12},{5,13},{6,14},{7,15},{8,0},{9,1},... | collective-permute-start | bytes 835592 | tf_op jit(solution)/shard_map/ppermute | solution.py:78
  569.2 12.1 %collective-permute-start.55 = (bf16[64,1024]{1,0:T(8,128)(2,1)S(1)}, bf16[64,1024]{1,0:T(8,128)(2,1)S(1)}, u32[]{:S(2)}, u32[]{:S(2)}) collective-permute-start(bf16[64,1024]{1,0:T(8,128)(2,1)S(1)} %get-tuple-element.386), channel_id=1, source_target_pairs={{0,16},{1,17},{2,18},{3,19},{4,20},{5,21},{6,22},{7,23},{8,24},{9,... | collective-permute-start | bytes 393224 | tf_op jit(solution)/shard_map/ppermute | solution.py:78
  570.6 10.6 %collective-permute-start.56 = (bf16[64,1024]{1,0:T(8,128)(2,1)S(1)}, bf16[64,1024]{1,0:T(8,128)(2,1)S(1)}, u32[]{:S(2)}, u32[]{:S(2)}) collective-permute-start(bf16[64,1024]{1,0:T(8,128)(2,1)S(1)} %get-tuple-element.385), channel_id=1, source_target_pairs={{0,8},{1,9},{2,10},{3,11},{4,12},{5,13},{6,14},{7,15},{8,0},{9,1},... | collective-permute-start | bytes 393224 | tf_op jit(solution)/shard_map/ppermute | solution.py:78
  581.4 22.0 %collective-permute-start.57 = (bf16[64,4608]{1,0:T(8,128)(2,1)S(1)}, bf16[64,4608]{1,0:T(8,128)(2,1)S(1)}, u32[]{:S(2)}, u32[]{:S(2)}) collective-permute-start(bf16[64,4608]{1,0:T(8,128)(2,1)S(1)} %add_convert_fusion.7), channel_id=1, source_target_pairs={{0,2},{1,3},{2,0},{3,1},{4,6},{5,7},{6,4},{7,5},{8,10},{9,11},{10,... | collective-permute-start | bytes 1769480 | tf_op jit(solution)/shard_map/ppermute | solution.py:86
  582.8 20.5 %collective-permute-start.58 = (bf16[64,2176]{1,0:T(8,128)(2,1)S(1)}, bf16[64,2176]{1,0:T(8,128)(2,1)S(1)}, u32[]{:S(2)}, u32[]{:S(2)}) collective-permute-start(bf16[64,2176]{1,0:T(8,128)(2,1)S(1)} %get-tuple-element.343), channel_id=1, source_target_pairs={{0,2},{1,3},{2,0},{3,1},{4,6},{5,7},{6,4},{7,5},{8,10},{9,11},{10,... | collective-permute-start | bytes 835592 | tf_op jit(solution)/shard_map/ppermute | solution.py:86
  585.4 17.9 %collective-permute-start.59 = (bf16[64,1024]{1,0:T(8,128)(2,1)S(1)}, bf16[64,1024]{1,0:T(8,128)(2,1)S(1)}, u32[]{:S(2)}, u32[]{:S(2)}) collective-permute-start(bf16[64,1024]{1,0:T(8,128)(2,1)S(1)} %get-tuple-element.340), channel_id=1, source_target_pairs={{0,2},{1,3},{2,0},{3,1},{4,6},{5,7},{6,4},{7,5},{8,10},{9,11},{10,... | collective-permute-start | bytes 393224 | tf_op jit(solution)/shard_map/ppermute | solution.py:86
  585.6 50.8 %collective-permute-start.66 = (bf16[128,4608]{1,0:T(8,128)(2,1)S(1)}, bf16[128,4608]{1,0:T(8,128)(2,1)S(1)}, u32[]{:S(2)}, u32[]{:S(2)}) collective-permute-start(bf16[128,4608]{1,0:T(8,128)(2,1)S(1)} %pad_maximum_fusion.10), channel_id=1, source_target_pairs={{0,1},{1,0},{2,3},{3,2},{4,5},{5,4},{6,7},{7,6},{8,9},{9,8},{10,11... | collective-permute-start | bytes 3538952 | tf_op jit(solution)/shard_map/ppermute | solution.py:86
  603.5 20.7 %collective-permute-start.60 = (bf16[64,2176]{1,0:T(8,128)(2,1)S(1)}, bf16[64,2176]{1,0:T(8,128)(2,1)S(1)}, u32[]{:S(2)}, u32[]{:S(2)}) collective-permute-start(bf16[64,2176]{1,0:T(8,128)(2,1)S(1)} %add_convert_fusion.41), channel_id=1, source_target_pairs={{0,4},{1,5},{2,6},{3,7},{4,0},{5,1},{6,2},{7,3},{8,12},{9,13},{10,... | collective-permute-start | bytes 835592 | tf_op jit(solution)/shard_map/ppermute | solution.py:86
  605.4 18.8 %collective-permute-start.61 = (bf16[64,1024]{1,0:T(8,128)(2,1)S(1)}, bf16[64,1024]{1,0:T(8,128)(2,1)S(1)}, u32[]{:S(2)}, u32[]{:S(2)}) collective-permute-start(bf16[64,1024]{1,0:T(8,128)(2,1)S(1)} %add_convert_fusion.53), channel_id=1, source_target_pairs={{0,4},{1,5},{2,6},{3,7},{4,0},{5,1},{6,2},{7,3},{8,12},{9,13},{10,... | collective-permute-start | bytes 393224 | tf_op jit(solution)/shard_map/ppermute | solution.py:86
  606.2 37.7 %collective-permute-start.67 = (bf16[128,4608]{1,0:T(8,128)(2,1)S(1)}, bf16[128,4608]{1,0:T(8,128)(2,1)S(1)}, u32[]{:S(2)}, u32[]{:S(2)}) collective-permute-start(bf16[128,4608]{1,0:T(8,128)(2,1)S(1)} %pad_maximum_fusion.11), channel_id=1, source_target_pairs={{0,1},{1,0},{2,3},{3,2},{4,5},{5,4},{6,7},{7,6},{8,9},{9,8},{10,11... | collective-permute-start | bytes 3538952 | tf_op jit(solution)/shard_map/ppermute | solution.py:86
  624.7 9.7 %collective-permute-start.62 = (bf16[64,2176]{1,0:T(8,128)(2,1)S(1)}, bf16[64,2176]{1,0:T(8,128)(2,1)S(1)}, u32[]{:S(2)}, u32[]{:S(2)}) collective-permute-start(bf16[64,2176]{1,0:T(8,128)(2,1)S(1)} %add_convert_fusion.40), channel_id=1, source_target_pairs={{0,2},{1,3},{2,0},{3,1},{4,6},{5,7},{6,4},{7,5},{8,10},{9,11},{10,... | collective-permute-start | bytes 835592 | tf_op jit(solution)/shard_map/ppermute | solution.py:86
  628.2 11.0 %collective-permute-start.65 = (bf16[128,1024]{1,0:T(8,128)(2,1)S(1)}, bf16[128,1024]{1,0:T(8,128)(2,1)S(1)}, u32[]{:S(2)}, u32[]{:S(2)}) collective-permute-start(bf16[128,1024]{1,0:T(8,128)(2,1)S(1)} %pad_maximum_fusion.25), channel_id=1, source_target_pairs={{0,1},{1,0},{2,3},{3,2},{4,5},{5,4},{6,7},{7,6},{8,9},{9,8},{10,11... | collective-permute-start | bytes 786440 | tf_op jit(solution)/shard_map/ppermute | solution.py:86
  (131 other events, 1048.1 us)

commit v9 on v7

--- a/solution.py
+++ b/solution.py
@@ -842,12 +842,12 @@
     turn = jnp.concatenate([cosine[:, 0].T, sine_table[:, 0].T], axis=0)
     flat = (query_lin.reshape(row_count, -1), key_lin.reshape(row_count, -1), turn, qk_gains[:, None])
     lower = attend_back(query_rot, grad_attn_low, key_rot, value_low, segment, *flat, 0, panels)
-    grad_attn_low, lower = pin((grad_attn_low, lower))
+    grad_attn_low, lower, out_given, out_sent = sync(
+        (grad_attn_low, lower, out_given, out_sent), up_back, gate_back
+    )
+    out_back = Flow(scatter_steps(links, out_given, out_sent))
     upper = attend_back(query_rot, grad_attn_low, key_rot, value_low, segment, *flat, panels, panels)
-    lower, upper, out_given, out_sent = sync(
-        (lower, upper, out_given, out_sent), gate_back, down_back, up_back
-    )
-    out_back = Flow(scatter_steps(links, out_given, out_sent))
+    lower, upper = sync((lower, upper), up_back, gate_back, out_back, down_back)
     grad_qk_gain = jnp.concatenate(
         [jnp.sum(lower[at] + upper[at], axis=(0, 2)) for at in (3, 4)]
     )
@@ -877,14 +877,17 @@
     )
     front_sent = rep_swap(other_front, 1)
     own_front, front_sent, mixed_act, grad_normed = sync(
-        (own_front, front_sent, mixed_act, grad_normed), out_back, up_back, gate_back
+        (own_front, front_sent, mixed_act, grad_normed), out_back
     )
     front_back = Flow(scatter_steps(links, own_front, front_sent))
     grad_inputs = grad_hidden + norm_back(
         grad_normed, inputs, scale_one, full_attn_gain.astype(jnp.float32)
     )
     result = live_rows * (hidden + matmul_plain(mixed_act, full_down))
-    grad_inputs, result = sync((grad_inputs, result), up_back, gate_back, out_back, front_back)
+    grad_inputs, result = sync((grad_inputs, result), up_back, gate_back, front_back, out_back)
+    sync((), front_back, out_back, gate_back)
+    sync((), front_back, up_back, out_back)
+    sync((), front_back, up_back)
     front_share = join_rows(front_back.finish())
     share_query = front_share[:, : HQ * HD]
     share_key = front_share[:, HQ * HD : (HQ + HK) * HD]

time: 665 us -> 674 us (1.014)
  starting transfers between devices: 95.8 us -> 79.6 us
  waiting for transfers between devices: 123 us -> 136 us
  other arithmetic: 97.9 us -> 107 us
    ppermute x33, starting transfers between devices: 51.2 us -> 33.7 us  [rep_swap(): return lax.ppermute(value, axes, pairs)]
    ppermute x33, waiting for transfers between devices: 72.6 us -> 86.8 us  [rep_swap(): return lax.ppermute(value, axes, pairs)]
  transfers between devices with their start and end apart: 69 -> 69, of which waited for: 24 -> 26; matrix products, arithmetic and copies ran while one was open for 29% -> 31% of each run, Pallas kernels for 22% -> 21%
where the time goes in v9:
time: 674 us; the launch traced here: 667 us
  Pallas kernels  177 us (26%)
  waiting for transfers between devices  136 us (20%)
  other arithmetic  107 us (16%)
  matrix products  104 us (15%)
  starting transfers between devices  79.6 us (12%)
  local copies, waits for them, and re-layouts  59.7 us (9%)
    ppermute x33, waiting for transfers between devices, rep_swap(): return lax.ppermute(value, axes, pairs)  86.8 us
    dot_general x10, matrix products, matmul_rows(): lax.dot_general(left_mat, right_mat, (((0,), (0,)), ((), ())), preferred_...  62.7 us
    ppermute x36, waiting for transfers between devices, shard_swap(): return lax.ppermute(value, axes, pairs)  49.6 us
    ppermute x36, starting transfers between devices, shard_swap(): return lax.ppermute(value, axes, pairs)  45.9 us
    pallas_call x2, Pallas kernels, attend_back(): pl.pallas_call(attend_back_kernel, out_shape=(jax.ShapeDtypeStruct((rows,...  45 us
    ppermute x33, starting transfers between devices, rep_swap(): return lax.ppermute(value, axes, pairs)  33.7 us
    pallas_call x2, Pallas kernels, ffn_forward(): pl.pallas_call(functools.partial(ffn_forward_kernel, count, len(into)), o...  33.2 us
    convert_element_type x20, other arithmetic, add_low(): (left.astype(jnp.float32) + right.astype(jnp.float32)).astype(jnp.bfloat16)  28.7 us
  transfers between devices with their start and end apart: 69, of which 26 were waited for; matrix products, arithmetic and copies ran while one was open for 31% of the time, Pallas kernels for 21%

profile of v9, /device:TPU:1, one launch (start us, length us, event | category | flops | bytes accessed | tf_op | source)
XLA Modules:
  0.0 667.1 jit_solution(8093240803498463406)
XLA Ops:
  12.8 7.7 %collective-permute-done.refs_2_ = bf16[128,2176]{1,0:T(8,128)(2,1)S(1)} collective-permute-done((bf16[128,2176]{1,0:T(8,128)(2,1)S(1)}, bf16[128,2176]{1,0:T(8,128)(2,1)S(1)}, u32[]{:S(2)}, u32[]{:S(2)}) %collective-permute-start) | collective-permute-done | bytes 557088 | tf_op jit(solution)/shard_map/ppermute | solution.py:78
  29.0 5.4 collective-permute-start.4
  38.8 6.9 %place_blocks.3 = bf16[1024,2176]{1,0:T(8,128)(2,1)} custom-call(s32[8]{0:T(128)} %stack.70.spots_ref, bf16[256,2176]{1,0:T(8,128)(2,1)} %pad_maximum_fusion.13.refs_0_.refs_1_, bf16[256,2176]{1,0:T(8,128)(2,1)} %pad_maximum_fusion.13.refs_0_.refs_1_, bf16[128,2176]{1,0:T(8,128)(2,1)} %copy-done.27, bf16[128,2176]{1,0:T(8,128)(2,1)} %get-tuple-element.419.refs_3_, ...), custom_call_target="tpu_custom_call" | custom-call | flops 1 | bytes 1 | tf_op jit(solution)/shard_map/place_blocks/pallas_call | solution.py:141
  49.4 4.4 multiply_reduce_fusion.4
  53.9 2.6 multiply_reduce_fusion.5
  72.0 3.9 copy.106.q_ref
  77.3 23.7 %attend.1 = bf16[1024,1024]{1,0:T(8,128)(2,1)} custom-call(s32[4,4]{1,0:T(4,128)} %fusion.80.live_ref, bf16[1024,1024]{1,0:T(8,128)(2,1)} %copy.106.q_ref, bf16[1024,512]{1,0:T(8,128)(2,1)} %copy.107.k_ref, bf16[1024,512]{1,0:T(8,128)(2,1)} %convolution_convert_fusion.11.v_ref, s32[1024,1]{1,0:T(8,128)} %copy.108.seg_col_ref, s32[1,1024]{1,0:T(1,128)} %bitcast.192), custom_call_target="tpu_custom_call" | custom-call | flops 1 | bytes 1 | tf_op jit(solution)/shard_map/attend/pallas_call | solution.py:628
  104.6 4.2 collective-permute-start.12
  114.3 5.3 place_blocks.4
  119.6 5.3 multiply_reduce_fusion.3
  127.6 7.8 %collective-permute-done.12 = bf16[64,9216]{1,0:T(8,128)(2,1)S(1)} collective-permute-done((bf16[64,9216]{1,0:T(8,128)(2,1)}, bf16[64,9216]{1,0:T(8,128)(2,1)S(1)}, u32[]{:S(2)}, u32[]{:S(2)}) %collective-permute-start.12) | collective-permute-done | bytes 1179680 | tf_op jit(solution)/shard_map/ppermute | solution.py:78
  135.4 4.6 collective-permute-done.13
  141.8 2.4 constant_dynamic-update-slice_fusion.4.refs_6_.refs_14_
  144.6 2.4 constant_dynamic-slice_fusion.28
  151.9 15.2 %ffn_forward.2 = (bf16[1024,4608]{1,0:T(8,128)(2,1)}, bf16[1024,4608]{1,0:T(8,128)(2,1)}, bf16[1024,4608]{1,0:T(8,128)(2,1)}) custom-call(s32[8]{0:T(128)} %stack.70.spots_ref, bf16[1024,1024]{1,0:T(8,128)(2,1)} %multiply_convert_fusion.a_ref, bf16[256,4608]{1,0:T(8,128)(2,1)} %refs_1_.4, bf16[256,4608]{1,0:T(8,128)(2,1)} %refs_1_.4, ...), custom_call_target="tpu_custom_call" | custom-call | flops 1 | bytes 1 | tf_op jit(solution)/shard_map/ffn_forward/pallas_call | solution.py:205
  167.1 7.8 %collective-permute-done.17.refs_2_ = bf16[576,1024]{1,0:T(8,128)(2,1)S(1)} collective-permute-done((bf16[576,1024]{1,0:T(8,128)(2,1)}, bf16[576,1024]{1,0:T(8,128)(2,1)S(1)}, u32[]{:S(2)}, u32[]{:S(2)}) %collective-permute-start.17) | collective-permute-done | bytes 1179680 | tf_op jit(solution)/shard_map/ppermute | solution.py:78
  181.4 18.0 %ffn_forward.3 = (bf16[1024,4608]{1,0:T(8,128)(2,1)}, bf16[1024,4608]{1,0:T(8,128)(2,1)}, bf16[1024,4608]{1,0:T(8,128)(2,1)}) custom-call(s32[8]{0:T(128)} %stack.70.spots_ref, bf16[1024,1024]{1,0:T(8,128)(2,1)} %multiply_convert_fusion.a_ref, bf16[256,4608]{1,0:T(8,128)(2,1)} %refs_1_.4, ...), custom_call_target="tpu_custom_call", output_to_operand_aliasing={{0}: (18, {}), {1}: (19, {}), {2}: (20, {})} | custom-call | flops 1 | bytes 1 | tf_op jit(solution)/shard_map/ffn_forward/pallas_call | solution.py:205
  205.6 9.4 %place_blocks.5.down_ref = bf16[4608,1024]{1,0:T(8,128)(2,1)} custom-call(s32[8]{0:T(128)} %stack.70.spots_ref, bf16[1152,1024]{1,0:T(8,128)(2,1)} %refs_1_.3, bf16[1152,1024]{1,0:T(8,128)(2,1)} %refs_1_.3, bf16[576,1024]{1,0:T(8,128)(2,1)} %copy-done.33, bf16[576,1024]{1,0:T(8,128)(2,1)} %collective-permute-done.21.refs_3_, ...), custom_call_target="tpu_custom_call" | custom-call | flops 1 | bytes 1 | tf_op jit(solution)/shard_map/place_blocks/pallas_call | solution.py:141
  215.0 24.8 %ffn_inner.1 = (bf16[1024,4608]{1,0:T(8,128)(2,1)}, bf16[1024,4608]{1,0:T(8,128)(2,1)}) custom-call(bf16[1024,1024]{1,0:T(8,128)(2,1)} %copy-done.12, bf16[4608,1024]{1,0:T(8,128)(2,1)} %place_blocks.5.down_ref, bf16[1024,4608]{1,0:T(8,128)(2,1)} %get-tuple-element.223.act_ref, bf16[1024,4608]{1,0:T(8,128)(2,1)} %get-tuple-element.224.slope_ref), custom_call_target="tpu_custom_call" | custom-call | flops 1 | bytes 1 | tf_op jit(solution)/shard_map/ffn_inner/pallas_call | solution.py:238
  239.8 10.8 %convolution_convert_fusion.1 = bf16[4608,512]{1,0:T(8,128)(2,1)} fusion(bf16[1024,4608]{1,0:T(8,128)(2,1)} %get-tuple-element.301, bf16[1024,512]{1,0:T(8,128)(2,1)S(1)} %copy-done.56), kind=kOutput, calls=%fused_computation.6 | convolution fusion | flops 4834197504 | bytes 15204352 | tf_op jit(solution)/shard_map/dot_general | solution.py:57
  251.7 10.9 %convolution_convert_fusion.5 = bf16[512,4608]{1,0:T(8,128)(2,1)} fusion(bf16[1024,4608]{1,0:T(8,128)(2,1)} %get-tuple-element.243.dgate_ref, bf16[1024,128]{1,0:T(8,128)(2,1)S(1)} %get-tuple-element.411, bf16[1024,128]{1,0:T(8,128)(2,1)S(1)} %get-tuple-element.412, bf16[1024,128]{1,0:T(8,128)(2,1)S(1)} %get-tuple-element.413, ...), kind=kOutput, calls=%fused_computation.10 | convolution fusion | flops 4838391808 | bytes 15204352 | tf_op jit(solution)/shard_map/dot_general | solution.py:57
  262.8 6.9 %convolution_convert_fusion = bf16[4608,512]{1,0:T(8,128)(2,1)} fusion(bf16[1024,4608]{1,0:T(8,128)(2,1)S(1)} %bitcast.156, bf16[1024,512]{1,0:T(8,128)(2,1)S(1)} %copy-done.55), kind=kOutput, calls=%fused_computation.5 | convolution fusion | flops 4834197504 | bytes 15204352 | tf_op jit(solution)/shard_map/dot_general | solution.py:57
  269.8 7.1 %convolution_convert_fusion.2 = bf16[512,4608]{1,0:T(8,128)(2,1)} fusion(bf16[1024,512]{1,0:T(8,128)(2,1)S(1)} %pad_maximum_fusion.15, bf16[1024,4608]{1,0:T(8,128)(2,1)S(1)} %bitcast.160), kind=kOutput, calls=%fused_computation.7 | convolution fusion | flops 4834197504 | bytes 15204352 | tf_op jit(solution)/shard_map/dot_general | solution.py:57
  278.8 3.0 add_convert_fusion.34
  283.7 10.5 %convolution_convert_fusion.3 = bf16[512,4608]{1,0:T(8,128)(2,1)} fusion(bf16[1024,512]{1,0:T(8,128)(2,1)S(1)} %pad_maximum_fusion.16, bf16[1024,4608]{1,0:T(8,128)(2,1)} %get-tuple-element.244.dup_ref), kind=kOutput, calls=%fused_computation.8 | convolution fusion | flops 4834197504 | bytes 15204352 | tf_op jit(solution)/shard_map/dot_general | solution.py:57
  294.3 5.4 convolution_convert_fusion.4
  299.7 9.6 %collective-permute-done.27 = bf16[2,576,512]{2,1,0:T(8,128)(2,1)S(1)} collective-permute-done((bf16[2,576,512]{2,1,0:T(8,128)(2,1)S(1)}, bf16[2,576,512]{2,1,0:T(8,128)(2,1)S(1)}, u32[]{:S(2)}, u32[]{:S(2)}) %collective-permute-start.27) | collective-permute-done | bytes 1179680 | tf_op jit(solution)/shard_map/ppermute | solution.py:78
  310.7 3.3 fusion.61
  321.4 28.5 %ffn_input.1 = f32[1024,1024]{1,0:T(8,128)} custom-call(s32[8]{0:T(128)} %stack.70.spots_ref, bf16[1024,4608]{1,0:T(8,128)(2,1)} %get-tuple-element.243.dgate_ref, bf16[1024,4608]{1,0:T(8,128)(2,1)} %get-tuple-element.244.dup_ref, bf16[256,4608]{1,0:T(8,128)(2,1)} %refs_1_.4, bf16[256,4608]{1,0:T(8,128)(2,1)} %refs_1_.4, bf16[128,9216]{1,0:T(8,128)(2,1)} %copy-done.4, ...), custom_call_target="tpu_custom_call" | custom-call | flops 1 | bytes 1 | tf_op jit(solution)/shard_map/ffn_input/pallas_call | solution.py:280
  349.9 4.1 multiply_reduce_fusion.2
  359.1 2.5 collective-permute-start.31
  361.6 3.4 broadcast_select_fusion.8
  368.4 3.7 convolution_convert_fusion.8.do_ref
  372.1 6.1 collective-permute-done.34
  378.3 3.1 add_convert_fusion.22
  385.8 3.3 fusion.63
  391.2 5.5 copy.113.q_lin_ref
  402.4 22.4 %attend_back.2 = (bf16[1024,512]{1,0:T(8,128)(2,1)}, bf16[1024,256]{1,0:T(8,128)(2,1)}, bf16[1024,256]{1,0:T(8,128)(2,1)}, f32[2,64,256]{2,1,0:T(8,128)}, f32[2,64,256]{2,1,0:T(8,128)}) custom-call(s32[4,4]{1,0:T(4,128)} %fusion.80.live_ref, bf16[1024,1024]{1,0:T(8,128)(2,1)} %copy.106.q_ref, bf16[1024,1024]{1,0:T(8,128)(2,1)} %convolution_convert_fusion.8.do_ref, ...), custom_call_target="tpu_custom_call" | custom-call | flops 1 | bytes 1 | tf_op jit(solution)/shard_map/attend_back/pallas_call | solution.py:652
  424.8 3.6 fusion.65
  428.4 3.6 collective-permute-start.39
  433.3 3.8 broadcast_select_fusion.5
  443.0 22.6 %attend_back.3 = (bf16[1024,512]{1,0:T(8,128)(2,1)}, bf16[1024,256]{1,0:T(8,128)(2,1)}, bf16[1024,256]{1,0:T(8,128)(2,1)}, f32[2,64,256]{2,1,0:T(8,128)}, f32[2,64,256]{2,1,0:T(8,128)}) custom-call(s32[4,4]{1,0:T(4,128)} %fusion.80.live_ref, bf16[1024,1024]{1,0:T(8,128)(2,1)} %copy.106.q_ref, bf16[1024,1024]{1,0:T(8,128)(2,1)} %convolution_convert_fusion.8.do_ref, ...), custom_call_target="tpu_custom_call" | custom-call | flops 1 | bytes 1 | tf_op jit(solution)/shard_map/attend_back/pallas_call | solution.py:652
  468.6 3.8 convolution_convert_fusion.7
  472.3 3.8 convolution_convert_fusion.6
  476.1 4.4 fusion.12
  480.5 3.3 fusion.53
  488.8 3.4 pad_maximum_fusion.2
  494.2 8.3 %collective-permute-start.46 = (bf16[64,1024]{1,0:T(8,128)(2,1)S(1)}, bf16[64,1024]{1,0:T(8,128)(2,1)S(1)}, u32[]{:S(2)}, u32[]{:S(2)}) collective-permute-start(bf16[64,1024]{1,0:T(8,128)(2,1)S(1)} %get-tuple-element.386), channel_id=1, source_target_pairs={{0,16},{1,17},{2,18},{3,19},{4,20},{5,21},{6,22},{7,23},{8,24},{9,... | collective-permute-start | bytes 393224 | tf_op jit(solution)/shard_map/ppermute | solution.py:78
  504.4 4.1 broadcast_select_fusion.4
  511.3 2.7 add_add_fusion
  513.9 22.0 %collective-permute-done.67 = bf16[576,512]{1,0:T(8,128)(2,1)S(1)} collective-permute-done((bf16[576,512]{1,0:T(8,128)(2,1)S(1)}, bf16[576,512]{1,0:T(8,128)(2,1)S(1)}, u32[]{:S(2)}, u32[]{:S(2)}) %collective-permute-start.67) | collective-permute-done | bytes 589856 | tf_op jit(solution)/shard_map/ppermute | solution.py:86
  540.2 10.7 %fusion.11 = f32[1152,1024]{1,0:T(8,128)} fusion(bf16[1152,512]{1,0:T(8,128)(2,1)S(1)} %collective-permute-done.68, bf16[576,512]{1,0:T(8,128)(2,1)S(1)} %get-tuple-element.421, bf16[576,512]{1,0:T(8,128)(2,1)S(1)} %get-tuple-element.420, pred[]{:T(512)S(6)} %eq.38), kind=kLoop, calls=%fused_computation.42 | loop fusion | flops 16515072 | bytes 7077889 | tf_op jit(solution)/shard_map/convert_element_type | solution.py:448
  553.2 13.1 %add_multiply_fusion = bf16[1024,1024]{1,0:T(8,128)(2,1)} fusion(f32[1024,1024]{1,0:T(8,128)S(1)} %copy-done.8, f32[1024]{0:T(1024)S(1)} %copy-done.93, bf16[1024,4608]{1,0:T(8,128)(2,1)} %get-tuple-element.301, bf16[4608,1024]{1,0:T(8,128)(2,1)S(1)} %bitcast.154), kind=kOutput, calls=%fused_computation.20 | convolution fusion | flops 9666822144 | bytes 25169920 | tf_op jit(solution)/shard_map/dot_general | solution.py:53
  571.2 2.5 fusion.5
  575.3 6.3 collective-permute-done.50
  589.6 2.7 collective-permute-done.55
  592.3 22.5 %collective-permute-done.56 = bf16[64,4608]{1,0:T(8,128)(2,1)S(1)} collective-permute-done((bf16[64,4608]{1,0:T(8,128)(2,1)S(1)}, bf16[64,4608]{1,0:T(8,128)(2,1)S(1)}, u32[]{:S(2)}, u32[]{:S(2)}) %collective-permute-start.56) | collective-permute-done | bytes 589856 | tf_op jit(solution)/shard_map/ppermute | solution.py:86
  618.1 9.4 %collective-permute-done.59 = bf16[64,1024]{1,0:T(8,128)(2,1)S(1)} collective-permute-done((bf16[64,1024]{1,0:T(8,128)(2,1)S(1)}, bf16[64,1024]{1,0:T(8,128)(2,1)S(1)}, u32[]{:S(2)}, u32[]{:S(2)}) %collective-permute-start.59) | collective-permute-done | bytes 131104 | tf_op jit(solution)/shard_map/ppermute | solution.py:86
  633.9 8.3 %collective-permute-done.60 = bf16[64,2176]{1,0:T(8,128)(2,1)S(1)} collective-permute-done((bf16[64,2176]{1,0:T(8,128)(2,1)S(1)}, bf16[64,2176]{1,0:T(8,128)(2,1)S(1)}, u32[]{:S(2)}, u32[]{:S(2)}) %collective-permute-start.60) | collective-permute-done | bytes 278560 | tf_op jit(solution)/shard_map/ppermute | solution.py:86
  642.2 5.3 collective-permute-done.61
  650.2 3.4 collective-permute-done.62
  653.7 3.2 collective-permute-start.63
  656.9 2.8 multiply_reduce_fusion.1
  663.5 2.8 multiply_reduce_fusion
  (524 shorter events, 170.1 us)
Async XLA Ops:
  6.0 14.5 %collective-permute-start = (bf16[128,2176]{1,0:T(8,128)(2,1)S(1)}, bf16[128,2176]{1,0:T(8,128)(2,1)S(1)}, u32[]{:S(2)}, u32[]{:S(2)}) collective-permute-start(bf16[128,2176]{1,0:T(8,128)(2,1)S(1)} %pad_maximum_fusion.18), channel_id=1, source_target_pairs={{0,8},{1,9},{2,10},{3,11},{4,12},{5,13},{6,14},{7,15},{8,0},{9,1},... | collective-permute-start | bytes 1671176 | tf_op jit(solution)/shard_map/ppermute | solution.py:78
  8.1 13.2 %collective-permute-start.1 = (bf16[128,2176]{1,0:T(8,128)(2,1)S(1)}, bf16[128,2176]{1,0:T(8,128)(2,1)S(1)}, u32[]{:S(2)}, u32[]{:S(2)}) collective-permute-start(bf16[128,2176]{1,0:T(8,128)(2,1)S(1)} %pad_maximum_fusion.18), channel_id=1, source_target_pairs={{0,16},{1,17},{2,18},{3,19},{4,20},{5,21},{6,22},{7,23},{8,24},{9,... | collective-permute-start | bytes 1671176 | tf_op jit(solution)/shard_map/ppermute | solution.py:78
  21.3 6.4 collective-permute-start.2
  22.6 6.1 collective-permute-start.3
  26.2 40.5 %collective-permute-start.5 = (bf16[128,1024]{1,0:T(8,128)(2,1)}, bf16[128,1024]{1,0:T(8,128)(2,1)}, u32[]{:S(2)}, u32[]{:S(2)}) collective-permute-start(bf16[128,1024]{1,0:T(8,128)(2,1)} %constant_dynamic-slice_fusion.31), channel_id=1, source_target_pairs={{0,8},{1,9},{2,10},{3,11},{4,12},{5,13},{6,14},{7,15},{8,0},{9,1},... | collective-permute-start | bytes 786440 | tf_op jit(solution)/shard_map/ppermute | solution.py:78
  27.3 39.4 %collective-permute-start.6 = (bf16[128,1024]{1,0:T(8,128)(2,1)}, bf16[128,1024]{1,0:T(8,128)(2,1)}, u32[]{:S(2)}, u32[]{:S(2)}) collective-permute-start(bf16[128,1024]{1,0:T(8,128)(2,1)} %constant_dynamic-slice_fusion.31), channel_id=1, source_target_pairs={{0,16},{1,17},{2,18},{3,19},{4,20},{5,21},{6,22},{7,23},{8,24},{9,... | collective-permute-start | bytes 786440 | tf_op jit(solution)/shard_map/ppermute | solution.py:78
  29.0 8.6 %collective-permute-start.4 = (bf16[3,128,2176]{2,1,0:T(8,128)(2,1)S(1)}, bf16[3,128,2176]{2,1,0:T(8,128)(2,1)S(1)}, u32[]{:S(2)}, u32[]{:S(2)}) collective-permute-start(bf16[3,128,2176]{2,1,0:T(8,128)(2,1)S(1)} %pad_maximum_fusion.3), channel_id=1, source_target_pairs={{0,1},{1,0},{2,3},{3,2},{4,5},{5,4},{6,7},{7,6},{8,9},{9,8},{10,11... | collective-permute-start | bytes 5013512 | tf_op jit(solution)/shard_map/ppermute | solution.py:86
  36.2 64.8 %collective-permute-start.9 = (bf16[128,9216]{1,0:T(8,128)(2,1)}, bf16[128,9216]{1,0:T(8,128)(2,1)S(1)}, u32[]{:S(2)}, u32[]{:S(2)}) collective-permute-start(bf16[128,9216]{1,0:T(8,128)(2,1)} %pad_maximum_fusion), channel_id=1, source_target_pairs={{0,8},{1,9},{2,10},{3,11},{4,12},{5,13},{6,14},{7,15},{8,0},{9,1},... | collective-permute-start | bytes 7077896 | tf_op jit(solution)/shard_map/ppermute | solution.py:78
  36.2 64.8 %collective-permute-start.10 = (bf16[128,9216]{1,0:T(8,128)(2,1)}, bf16[128,9216]{1,0:T(8,128)(2,1)}, u32[]{:S(2)}, u32[]{:S(2)}) collective-permute-start(bf16[128,9216]{1,0:T(8,128)(2,1)} %pad_maximum_fusion), channel_id=1, source_target_pairs={{0,16},{1,17},{2,18},{3,19},{4,20},{5,21},{6,22},{7,23},{8,24},{9,... | collective-permute-start | bytes 7077896 | tf_op jit(solution)/shard_map/ppermute | solution.py:78
  68.3 32.7 %collective-permute-start.7 = (bf16[64,1024]{1,0:T(8,128)(2,1)}, bf16[64,1024]{1,0:T(8,128)(2,1)S(1)}, u32[]{:S(2)}, u32[]{:S(2)}) collective-permute-start(bf16[64,1024]{1,0:T(8,128)(2,1)} %slice.203), channel_id=1, source_target_pairs={{0,16},{1,17},{2,18},{3,19},{4,20},{5,21},{6,22},{7,23},{8,24},{9,... | collective-permute-start | bytes 393224 | tf_op jit(solution)/shard_map/ppermute | solution.py:78
  70.0 31.1 %collective-permute-start.8 = (bf16[64,1024]{1,0:T(8,128)(2,1)}, bf16[64,1024]{1,0:T(8,128)(2,1)}, u32[]{:S(2)}, u32[]{:S(2)}) collective-permute-start(bf16[64,1024]{1,0:T(8,128)(2,1)} %slice.204), channel_id=1, source_target_pairs={{0,8},{1,9},{2,10},{3,11},{4,12},{5,13},{6,14},{7,15},{8,0},{9,1},... | collective-permute-start | bytes 393224 | tf_op jit(solution)/shard_map/ppermute | solution.py:78
  103.4 10.0 %collective-permute-start.11 = (bf16[3,128,1024]{2,1,0:T(8,128)(2,1)S(1)}, bf16[3,128,1024]{2,1,0:T(8,128)(2,1)S(1)}, u32[]{:S(2)}, u32[]{:S(2)}) collective-permute-start(bf16[3,128,1024]{2,1,0:T(8,128)(2,1)S(1)} %pad_maximum_fusion.17), channel_id=1, source_target_pairs={{0,1},{1,0},{2,3},{3,2},{4,5},{5,4},{6,7},{7,6},{8,9},{9,8},{10,11... | collective-permute-start | bytes 2359304 | tf_op jit(solution)/shard_map/ppermute | solution.py:86
  104.6 30.8 %collective-permute-start.12 = (bf16[64,9216]{1,0:T(8,128)(2,1)}, bf16[64,9216]{1,0:T(8,128)(2,1)S(1)}, u32[]{:S(2)}, u32[]{:S(2)}) collective-permute-start(bf16[64,9216]{1,0:T(8,128)(2,1)} %slice.209), channel_id=1, source_target_pairs={{0,16},{1,17},{2,18},{3,19},{4,20},{5,21},{6,22},{7,23},{8,24},{9,... | collective-permute-start | bytes 3538952 | tf_op jit(solution)/shard_map/ppermute | solution.py:78
  111.1 28.9 %collective-permute-start.13 = (bf16[64,9216]{1,0:T(8,128)(2,1)}, bf16[64,9216]{1,0:T(8,128)(2,1)}, u32[]{:S(2)}, u32[]{:S(2)}) collective-permute-start(bf16[64,9216]{1,0:T(8,128)(2,1)} %slice.210), channel_id=1, source_target_pairs={{0,8},{1,9},{2,10},{3,11},{4,12},{5,13},{6,14},{7,15},{8,0},{9,1},... | collective-permute-start | bytes 3538952 | tf_op jit(solution)/shard_map/ppermute | solution.py:78
  140.0 9.9 %collective-permute-start.14 = (bf16[128,9216]{1,0:T(8,128)(2,1)S(1)}, bf16[128,9216]{1,0:T(8,128)(2,1)}, u32[]{:S(2)}, u32[]{:S(2)}) collective-permute-start(bf16[128,9216]{1,0:T(8,128)(2,1)S(1)} %collective-permute-done.9.refs_2_.refs_10_), channel_id=1, source_target_pairs={{0,1},{1,0},{2,3},{3,2},{4,5},{5,4},{6,7},{7,6},{8,9},{9,8},{10,11... | collective-permute-start | bytes 7077896 | tf_op jit(solution)/shard_map/ppermute | solution.py:86
  140.6 9.3 %collective-permute-start.15 = (bf16[128,9216]{1,0:T(8,128)(2,1)}, bf16[128,9216]{1,0:T(8,128)(2,1)}, u32[]{:S(2)}, u32[]{:S(2)}) collective-permute-start(bf16[128,9216]{1,0:T(8,128)(2,1)} %collective-permute-done.10.refs_4_.refs_12_), channel_id=1, source_target_pairs={{0,1},{1,0},{2,3},{3,2},{4,5},{5,4},{6,7},{7,6},{8,9},{9,8},{10,11... | collective-permute-start | bytes 7077896 | tf_op jit(solution)/shard_map/ppermute | solution.py:86
  144.1 7.8 %collective-permute-start.16 = (bf16[128,9216]{1,0:T(8,128)(2,1)}, bf16[128,9216]{1,0:T(8,128)(2,1)}, u32[]{:S(2)}, u32[]{:S(2)}) collective-permute-start(bf16[128,9216]{1,0:T(8,128)(2,1)} %constant_dynamic-update-slice_fusion.4.refs_6_.refs_14_), channel_id=1, source_target_pairs={{0,1},{1,0},{2,3},{3,2},{4,5},{5,4},{6,7},{7,6},{8,9},{9,8},{10,11... | collective-permute-start | bytes 7077896 | tf_op jit(solution)/shard_map/ppermute | solution.py:86
  147.0 27.9 %collective-permute-start.17 = (bf16[576,1024]{1,0:T(8,128)(2,1)}, bf16[576,1024]{1,0:T(8,128)(2,1)S(1)}, u32[]{:S(2)}, u32[]{:S(2)}) collective-permute-start(bf16[576,1024]{1,0:T(8,128)(2,1)} %constant_dynamic-slice_fusion.28), channel_id=1, source_target_pairs={{0,8},{1,9},{2,10},{3,11},{4,12},{5,13},{6,14},{7,15},{8,0},{9,1},... | collective-permute-start | bytes 3538952 | tf_op jit(solution)/shard_map/ppermute | solution.py:78
  148.5 27.7 %collective-permute-start.18 = (bf16[576,1024]{1,0:T(8,128)(2,1)}, bf16[576,1024]{1,0:T(8,128)(2,1)}, u32[]{:S(2)}, u32[]{:S(2)}) collective-permute-start(bf16[576,1024]{1,0:T(8,128)(2,1)} %constant_dynamic-slice_fusion.28), channel_id=1, source_target_pairs={{0,16},{1,17},{2,18},{3,19},{4,20},{5,21},{6,22},{7,23},{8,24},{9,... | collective-permute-start | bytes 3538952 | tf_op jit(solution)/shard_map/ppermute | solution.py:78
  176.1 23.3 %collective-permute-start.21 = (bf16[576,1024]{1,0:T(8,128)(2,1)S(1)}, bf16[576,1024]{1,0:T(8,128)(2,1)}, u32[]{:S(2)}, u32[]{:S(2)}) collective-permute-start(bf16[576,1024]{1,0:T(8,128)(2,1)S(1)} %collective-permute-done.17.refs_2_), channel_id=1, source_target_pairs={{0,1},{1,0},{2,3},{3,2},{4,5},{5,4},{6,7},{7,6},{8,9},{9,8},{10,11... | collective-permute-start | bytes 3538952 | tf_op jit(solution)/shard_map/ppermute | solution.py:86
  177.2 22.3 %collective-permute-start.22 = (bf16[576,1024]{1,0:T(8,128)(2,1)}, bf16[576,1024]{1,0:T(8,128)(2,1)}, u32[]{:S(2)}, u32[]{:S(2)}) collective-permute-start(bf16[576,1024]{1,0:T(8,128)(2,1)} %collective-permute-done.18.refs_4_), channel_id=1, source_target_pairs={{0,1},{1,0},{2,3},{3,2},{4,5},{5,4},{6,7},{7,6},{8,9},{9,8},{10,11... | collective-permute-start | bytes 3538952 | tf_op jit(solution)/shard_map/ppermute | solution.py:86
  180.0 19.5 %collective-permute-start.19 = (bf16[288,1024]{1,0:T(8,128)(2,1)}, bf16[288,1024]{1,0:T(8,128)(2,1)}, u32[]{:S(2)}, u32[]{:S(2)}) collective-permute-start(bf16[288,1024]{1,0:T(8,128)(2,1)} %slice.211), channel_id=1, source_target_pairs={{0,16},{1,17},{2,18},{3,19},{4,20},{5,21},{6,22},{7,23},{8,24},{9,... | collective-permute-start | bytes 1769480 | tf_op jit(solution)/shard_map/ppermute | solution.py:78
  181.4 18.0 %collective-permute-start.20 = (bf16[288,1024]{1,0:T(8,128)(2,1)}, bf16[288,1024]{1,0:T(8,128)(2,1)}, u32[]{:S(2)}, u32[]{:S(2)}) collective-permute-start(bf16[288,1024]{1,0:T(8,128)(2,1)} %slice.212), channel_id=1, source_target_pairs={{0,8},{1,9},{2,10},{3,11},{4,12},{5,13},{6,14},{7,15},{8,0},{9,1},... | collective-permute-start | bytes 1769480 | tf_op jit(solution)/shard_map/ppermute | solution.py:78
  250.5 12.2 %collective-permute-start.24 = (bf16[4,1152,512]{2,1,0:T(8,128)(2,1)}, bf16[4,1152,512]{2,1,0:T(8,128)(2,1)}, u32[]{:S(2)}, u32[]{:S(2)}) collective-permute-start(bf16[4,1152,512]{2,1,0:T(8,128)(2,1)} %bitcast.27), channel_id=1, source_target_pairs={{0,1},{1,0},{2,3},{3,2},{4,5},{5,4},{6,7},{7,6},{8,9},{9,8},{10,11... | collective-permute-start | bytes 14155784 | tf_op jit(solution)/shard_map/ppermute | solution.py:86
  262.6 37.1 %collective-permute-start.25 = (bf16[4,128,4608]{2,1,0:T(8,128)(2,1)}, bf16[4,128,4608]{2,1,0:T(8,128)(2,1)}, u32[]{:S(2)}, u32[]{:S(2)}) collective-permute-start(bf16[4,128,4608]{2,1,0:T(8,128)(2,1)} %bitcast.30), channel_id=1, source_target_pairs={{0,1},{1,0},{2,3},{3,2},{4,5},{5,4},{6,7},{7,6},{8,9},{9,8},{10,11... | collective-permute-start | bytes 14155784 | tf_op jit(solution)/shard_map/ppermute | solution.py:86
  276.9 33.8 %collective-permute-start.26 = (bf16[4,128,4608]{2,1,0:T(8,128)(2,1)}, bf16[4,128,4608]{2,1,0:T(8,128)(2,1)}, u32[]{:S(2)}, u32[]{:S(2)}) collective-permute-start(bf16[4,128,4608]{2,1,0:T(8,128)(2,1)} %bitcast.32), channel_id=1, source_target_pairs={{0,1},{1,0},{2,3},{3,2},{4,5},{5,4},{6,7},{7,6},{8,9},{9,8},{10,11... | collective-permute-start | bytes 14155784 | tf_op jit(solution)/shard_map/ppermute | solution.py:86
  281.9 27.5 %collective-permute-start.27 = (bf16[2,576,512]{2,1,0:T(8,128)(2,1)S(1)}, bf16[2,576,512]{2,1,0:T(8,128)(2,1)S(1)}, u32[]{:S(2)}, u32[]{:S(2)}) collective-permute-start(bf16[2,576,512]{2,1,0:T(8,128)(2,1)S(1)} %pad_maximum_fusion.4), channel_id=1, source_target_pairs={{0,8},{1,9},{2,10},{3,11},{4,12},{5,13},{6,14},{7,15},{8,0},{9,1},... | collective-permute-start | bytes 3538952 | tf_op jit(solution)/shard_map/ppermute | solution.py:78
  283.6 27.1 %collective-permute-start.28 = (bf16[2,576,512]{2,1,0:T(8,128)(2,1)S(1)}, bf16[2,576,512]{2,1,0:T(8,128)(2,1)S(1)}, u32[]{:S(2)}, u32[]{:S(2)}) collective-permute-start(bf16[2,576,512]{2,1,0:T(8,128)(2,1)S(1)} %pad_maximum_fusion.5), channel_id=1, source_target_pairs={{0,16},{1,17},{2,18},{3,19},{4,20},{5,21},{6,22},{7,23},{8,24},{9,... | collective-permute-start | bytes 3538952 | tf_op jit(solution)/shard_map/ppermute | solution.py:78
  314.0 35.9 %collective-permute-start.29 = (bf16[576,512]{1,0:T(8,128)(2,1)}, bf16[576,512]{1,0:T(8,128)(2,1)}, u32[]{:S(2)}, u32[]{:S(2)}) collective-permute-start(bf16[576,512]{1,0:T(8,128)(2,1)} %get-tuple-element.368), channel_id=1, source_target_pairs={{0,16},{1,17},{2,18},{3,19},{4,20},{5,21},{6,22},{7,23},{8,24},{9,... | collective-permute-start | bytes 1769480 | tf_op jit(solution)/shard_map/ppermute | solution.py:78
  314.2 35.7 %collective-permute-start.30 = (bf16[576,512]{1,0:T(8,128)(2,1)S(1)}, bf16[576,512]{1,0:T(8,128)(2,1)}, u32[]{:S(2)}, u32[]{:S(2)}) collective-permute-start(bf16[576,512]{1,0:T(8,128)(2,1)S(1)} %get-tuple-element.367), channel_id=1, source_target_pairs={{0,8},{1,9},{2,10},{3,11},{4,12},{5,13},{6,14},{7,15},{8,0},{9,1},... | collective-permute-start | bytes 1769480 | tf_op jit(solution)/shard_map/ppermute | solution.py:78
  318.1 60.1 %collective-permute-start.32 = (bf16[2,64,4608]{2,1,0:T(8,128)(2,1)}, bf16[2,64,4608]{2,1,0:T(8,128)(2,1)S(1)}, u32[]{:S(2)}, u32[]{:S(2)}) collective-permute-start(bf16[2,64,4608]{2,1,0:T(8,128)(2,1)} %pad_maximum_fusion.6), channel_id=1, source_target_pairs={{0,8},{1,9},{2,10},{3,11},{4,12},{5,13},{6,14},{7,15},{8,0},{9,1},... | collective-permute-start | bytes 3538952 | tf_op jit(solution)/shard_map/ppermute | solution.py:78
  320.1 58.1 %collective-permute-start.33 = (bf16[2,64,4608]{2,1,0:T(8,128)(2,1)}, bf16[2,64,4608]{2,1,0:T(8,128)(2,1)}, u32[]{:S(2)}, u32[]{:S(2)}) collective-permute-start(bf16[2,64,4608]{2,1,0:T(8,128)(2,1)} %pad_maximum_fusion.7), channel_id=1, source_target_pairs={{0,16},{1,17},{2,18},{3,19},{4,20},{5,21},{6,22},{7,23},{8,24},{9,... | collective-permute-start | bytes 3538952 | tf_op jit(solution)/shard_map/ppermute | solution.py:78
  359.1 19.1 %collective-permute-start.31 = (bf16[4,128,1024]{2,1,0:T(8,128)(2,1)S(1)}, bf16[4,128,1024]{2,1,0:T(8,128)(2,1)S(1)}, u32[]{:S(2)}, u32[]{:S(2)}) collective-permute-start(bf16[4,128,1024]{2,1,0:T(8,128)(2,1)S(1)} %bitcast.197), channel_id=1, source_target_pairs={{0,1},{1,0},{2,3},{3,2},{4,5},{5,4},{6,7},{7,6},{8,9},{9,8},{10,11... | collective-permute-start | bytes 3145736 | tf_op jit(solution)/shard_map/ppermute | solution.py:86
  365.1 13.1 %collective-permute-start.34 = (bf16[576,512]{1,0:T(8,128)(2,1)S(1)}, bf16[576,512]{1,0:T(8,128)(2,1)S(1)}, u32[]{:S(2)}, u32[]{:S(2)}) collective-permute-start(bf16[576,512]{1,0:T(8,128)(2,1)S(1)} %get-tuple-element.352), channel_id=1, source_target_pairs={{0,2},{1,3},{2,0},{3,1},{4,6},{5,7},{6,4},{7,5},{8,10},{9,11},{10,... | collective-permute-start | bytes 1769480 | tf_op jit(solution)/shard_map/ppermute | solution.py:86
  382.6 42.2 %collective-permute-start.35 = (bf16[2,64,4608]{2,1,0:T(8,128)(2,1)}, bf16[2,64,4608]{2,1,0:T(8,128)(2,1)}, u32[]{:S(2)}, u32[]{:S(2)}) collective-permute-start(bf16[2,64,4608]{2,1,0:T(8,128)(2,1)} %pad_maximum_fusion.8), channel_id=1, source_target_pairs={{0,8},{1,9},{2,10},{3,11},{4,12},{5,13},{6,14},{7,15},{8,0},{9,1},... | collective-permute-start | bytes 3538952 | tf_op jit(solution)/shard_map/ppermute | solution.py:78
  384.2 40.6 %collective-permute-start.36 = (bf16[2,64,4608]{2,1,0:T(8,128)(2,1)}, bf16[2,64,4608]{2,1,0:T(8,128)(2,1)}, u32[]{:S(2)}, u32[]{:S(2)}) collective-permute-start(bf16[2,64,4608]{2,1,0:T(8,128)(2,1)} %pad_maximum_fusion.9), channel_id=1, source_target_pairs={{0,16},{1,17},{2,18},{3,19},{4,20},{5,21},{6,22},{7,23},{8,24},{9,... | collective-permute-start | bytes 3538952 | tf_op jit(solution)/shard_map/ppermute | solution.py:78
  389.1 35.7 %collective-permute-start.37 = (bf16[64,4608]{1,0:T(8,128)(2,1)}, bf16[64,4608]{1,0:T(8,128)(2,1)}, u32[]{:S(2)}, u32[]{:S(2)}) collective-permute-start(bf16[64,4608]{1,0:T(8,128)(2,1)} %get-tuple-element.358), channel_id=1, source_target_pairs={{0,16},{1,17},{2,18},{3,19},{4,20},{5,21},{6,22},{7,23},{8,24},{9,... | collective-permute-start | bytes 1769480 | tf_op jit(solution)/shard_map/ppermute | solution.py:78
  389.1 35.7 %collective-permute-start.38 = (bf16[64,4608]{1,0:T(8,128)(2,1)}, bf16[64,4608]{1,0:T(8,128)(2,1)}, u32[]{:S(2)}, u32[]{:S(2)}) collective-permute-start(bf16[64,4608]{1,0:T(8,128)(2,1)} %get-tuple-element.357), channel_id=1, source_target_pairs={{0,8},{1,9},{2,10},{3,11},{4,12},{5,13},{6,14},{7,15},{8,0},{9,1},... | collective-permute-start | bytes 1769480 | tf_op jit(solution)/shard_map/ppermute | solution.py:78
  400.7 40.5 %collective-permute-start.44 = (bf16[576,512]{1,0:T(8,128)(2,1)S(1)}, bf16[576,512]{1,0:T(8,128)(2,1)}, u32[]{:S(2)}, u32[]{:S(2)}) collective-permute-start(bf16[576,512]{1,0:T(8,128)(2,1)S(1)} %add_convert_fusion.14), channel_id=1, source_target_pairs={{0,4},{1,5},{2,6},{3,7},{4,0},{5,1},{6,2},{7,3},{8,12},{9,13},{10,... | collective-permute-start | bytes 1769480 | tf_op jit(solution)/shard_map/ppermute | solution.py:86
  428.4 37.3 %collective-permute-start.39 = (bf16[64,4608]{1,0:T(8,128)(2,1)}, bf16[64,4608]{1,0:T(8,128)(2,1)}, u32[]{:S(2)}, u32[]{:S(2)}) collective-permute-start(bf16[64,4608]{1,0:T(8,128)(2,1)} %get-tuple-element.356), channel_id=1, source_target_pairs={{0,16},{1,17},{2,18},{3,19},{4,20},{5,21},{6,22},{7,23},{8,24},{9,... | collective-permute-start | bytes 1769480 | tf_op jit(solution)/shard_map/ppermute | solution.py:78
  432.0 33.7 %collective-permute-start.40 = (bf16[64,4608]{1,0:T(8,128)(2,1)}, bf16[64,4608]{1,0:T(8,128)(2,1)}, u32[]{:S(2)}, u32[]{:S(2)}) collective-permute-start(bf16[64,4608]{1,0:T(8,128)(2,1)} %get-tuple-element.355), channel_id=1, source_target_pairs={{0,8},{1,9},{2,10},{3,11},{4,12},{5,13},{6,14},{7,15},{8,0},{9,1},... | collective-permute-start | bytes 1769480 | tf_op jit(solution)/shard_map/ppermute | solution.py:78
  437.1 28.6 %collective-permute-start.41 = (bf16[64,4608]{1,0:T(8,128)(2,1)}, bf16[64,4608]{1,0:T(8,128)(2,1)}, u32[]{:S(2)}, u32[]{:S(2)}) collective-permute-start(bf16[64,4608]{1,0:T(8,128)(2,1)} %get-tuple-element.349), channel_id=1, source_target_pairs={{0,2},{1,3},{2,0},{3,1},{4,6},{5,7},{6,4},{7,5},{8,10},{9,11},{10,... | collective-permute-start | bytes 1769480 | tf_op jit(solution)/shard_map/ppermute | solution.py:86
  439.2 26.4 %collective-permute-start.42 = (bf16[2,64,1024]{2,1,0:T(8,128)(2,1)}, bf16[2,64,1024]{2,1,0:T(8,128)(2,1)}, u32[]{:S(2)}, u32[]{:S(2)}) collective-permute-start(bf16[2,64,1024]{2,1,0:T(8,128)(2,1)} %pad_maximum_fusion.23), channel_id=1, source_target_pairs={{0,8},{1,9},{2,10},{3,11},{4,12},{5,13},{6,14},{7,15},{8,0},{9,1},... | collective-permute-start | bytes 786440 | tf_op jit(solution)/shard_map/ppermute | solution.py:78
  441.2 24.4 %collective-permute-start.43 = (bf16[2,64,1024]{2,1,0:T(8,128)(2,1)}, bf16[2,64,1024]{2,1,0:T(8,128)(2,1)}, u32[]{:S(2)}, u32[]{:S(2)}) collective-permute-start(bf16[2,64,1024]{2,1,0:T(8,128)(2,1)} %pad_maximum_fusion.24), channel_id=1, source_target_pairs={{0,16},{1,17},{2,18},{3,19},{4,20},{5,21},{6,22},{7,23},{8,24},{9,... | collective-permute-start | bytes 786440 | tf_op jit(solution)/shard_map/ppermute | solution.py:78
  492.2 58.8 %collective-permute-start.45 = (bf16[4,128,2176]{2,1,0:T(8,128)(2,1)}, bf16[4,128,2176]{2,1,0:T(8,128)(2,1)}, u32[]{:S(2)}, u32[]{:S(2)}) collective-permute-start(bf16[4,128,2176]{2,1,0:T(8,128)(2,1)} %pad_maximum_fusion.2), channel_id=1, source_target_pairs={{0,1},{1,0},{2,3},{3,2},{4,5},{5,4},{6,7},{7,6},{8,9},{9,8},{10,11... | collective-permute-start | bytes 6684680 | tf_op jit(solution)/shard_map/ppermute | solution.py:86
  494.2 56.7 %collective-permute-start.46 = (bf16[64,1024]{1,0:T(8,128)(2,1)S(1)}, bf16[64,1024]{1,0:T(8,128)(2,1)S(1)}, u32[]{:S(2)}, u32[]{:S(2)}) collective-permute-start(bf16[64,1024]{1,0:T(8,128)(2,1)S(1)} %get-tuple-element.386), channel_id=1, source_target_pairs={{0,16},{1,17},{2,18},{3,19},{4,20},{5,21},{6,22},{7,23},{8,24},{9,... | collective-permute-start | bytes 393224 | tf_op jit(solution)/shard_map/ppermute | solution.py:78
  502.5 48.5 %collective-permute-start.47 = (bf16[64,1024]{1,0:T(8,128)(2,1)S(1)}, bf16[64,1024]{1,0:T(8,128)(2,1)S(1)}, u32[]{:S(2)}, u32[]{:S(2)}) collective-permute-start(bf16[64,1024]{1,0:T(8,128)(2,1)S(1)} %get-tuple-element.385), channel_id=1, source_target_pairs={{0,8},{1,9},{2,10},{3,11},{4,12},{5,13},{6,14},{7,15},{8,0},{9,1},... | collective-permute-start | bytes 393224 | tf_op jit(solution)/shard_map/ppermute | solution.py:78
  508.5 65.3 %collective-permute-start.48 = (bf16[64,4608]{1,0:T(8,128)(2,1)}, bf16[64,4608]{1,0:T(8,128)(2,1)}, u32[]{:S(2)}, u32[]{:S(2)}) collective-permute-start(bf16[64,4608]{1,0:T(8,128)(2,1)} %get-tuple-element.346), channel_id=1, source_target_pairs={{0,2},{1,3},{2,0},{3,1},{4,6},{5,7},{6,4},{7,5},{8,10},{9,11},{10,... | collective-permute-start | bytes 1769480 | tf_op jit(solution)/shard_map/ppermute | solution.py:86
  511.1 24.9 %collective-permute-start.67 = (bf16[576,512]{1,0:T(8,128)(2,1)S(1)}, bf16[576,512]{1,0:T(8,128)(2,1)S(1)}, u32[]{:S(2)}, u32[]{:S(2)}) collective-permute-start(bf16[576,512]{1,0:T(8,128)(2,1)S(1)} %add_convert_fusion.7), channel_id=1, source_target_pairs={{0,2},{1,3},{2,0},{3,1},{4,6},{5,7},{6,4},{7,5},{8,10},{9,11},{10,... | collective-permute-start | bytes 1769480 | tf_op jit(solution)/shard_map/ppermute | solution.py:86
  539.8 34.0 %collective-permute-start.49 = (bf16[64,4608]{1,0:T(8,128)(2,1)S(1)}, bf16[64,4608]{1,0:T(8,128)(2,1)S(1)}, u32[]{:S(2)}, u32[]{:S(2)}) collective-permute-start(bf16[64,4608]{1,0:T(8,128)(2,1)S(1)} %add_convert_fusion.11), channel_id=1, source_target_pairs={{0,4},{1,5},{2,6},{3,7},{4,0},{5,1},{6,2},{7,3},{8,12},{9,13},{10,... | collective-permute-start | bytes 1769480 | tf_op jit(solution)/shard_map/ppermute | solution.py:86
  568.0 13.6 %collective-permute-start.50 = (bf16[2,64,2176]{2,1,0:T(8,128)(2,1)S(1)}, bf16[2,64,2176]{2,1,0:T(8,128)(2,1)S(1)}, u32[]{:S(2)}, u32[]{:S(2)}) collective-permute-start(bf16[2,64,2176]{2,1,0:T(8,128)(2,1)S(1)} %pad_maximum_fusion.19), channel_id=1, source_target_pairs={{0,8},{1,9},{2,10},{3,11},{4,12},{5,13},{6,14},{7,15},{8,0},{9,1},... | collective-permute-start | bytes 1671176 | tf_op jit(solution)/shard_map/ppermute | solution.py:78
  569.6 13.3 %collective-permute-start.51 = (bf16[2,64,2176]{2,1,0:T(8,128)(2,1)S(1)}, bf16[2,64,2176]{2,1,0:T(8,128)(2,1)S(1)}, u32[]{:S(2)}, u32[]{:S(2)}) collective-permute-start(bf16[2,64,2176]{2,1,0:T(8,128)(2,1)S(1)} %pad_maximum_fusion.20), channel_id=1, source_target_pairs={{0,16},{1,17},{2,18},{3,19},{4,20},{5,21},{6,22},{7,23},{8,24},{9,... | collective-permute-start | bytes 1671176 | tf_op jit(solution)/shard_map/ppermute | solution.py:78
  584.1 8.2 %collective-permute-start.53 = (bf16[64,2176]{1,0:T(8,128)(2,1)S(1)}, bf16[64,2176]{1,0:T(8,128)(2,1)S(1)}, u32[]{:S(2)}, u32[]{:S(2)}) collective-permute-start(bf16[64,2176]{1,0:T(8,128)(2,1)S(1)} %get-tuple-element.374), channel_id=1, source_target_pairs={{0,16},{1,17},{2,18},{3,19},{4,20},{5,21},{6,22},{7,23},{8,24},{9,... | collective-permute-start | bytes 835592 | tf_op jit(solution)/shard_map/ppermute | solution.py:78
  584.3 8.0 %collective-permute-start.54 = (bf16[64,2176]{1,0:T(8,128)(2,1)S(1)}, bf16[64,2176]{1,0:T(8,128)(2,1)S(1)}, u32[]{:S(2)}, u32[]{:S(2)}) collective-permute-start(bf16[64,2176]{1,0:T(8,128)(2,1)S(1)} %get-tuple-element.373), channel_id=1, source_target_pairs={{0,8},{1,9},{2,10},{3,11},{4,12},{5,13},{6,14},{7,15},{8,0},{9,1},... | collective-permute-start | bytes 835592 | tf_op jit(solution)/shard_map/ppermute | solution.py:78
  585.5 6.8 %collective-permute-start.55 = (bf16[64,1024]{1,0:T(8,128)(2,1)S(1)}, bf16[64,1024]{1,0:T(8,128)(2,1)S(1)}, u32[]{:S(2)}, u32[]{:S(2)}) collective-permute-start(bf16[64,1024]{1,0:T(8,128)(2,1)S(1)} %add_convert_fusion.53), channel_id=1, source_target_pairs={{0,4},{1,5},{2,6},{3,7},{4,0},{5,1},{6,2},{7,3},{8,12},{9,13},{10,... | collective-permute-start | bytes 393224 | tf_op jit(solution)/shard_map/ppermute | solution.py:86
  587.7 27.1 %collective-permute-start.56 = (bf16[64,4608]{1,0:T(8,128)(2,1)S(1)}, bf16[64,4608]{1,0:T(8,128)(2,1)S(1)}, u32[]{:S(2)}, u32[]{:S(2)}) collective-permute-start(bf16[64,4608]{1,0:T(8,128)(2,1)S(1)} %add_convert_fusion.10), channel_id=1, source_target_pairs={{0,2},{1,3},{2,0},{3,1},{4,6},{5,7},{6,4},{7,5},{8,10},{9,11},{10,... | collective-permute-start | bytes 1769480 | tf_op jit(solution)/shard_map/ppermute | solution.py:86
  589.2 28.9 %collective-permute-start.58 = (bf16[64,4608]{1,0:T(8,128)(2,1)S(1)}, bf16[64,4608]{1,0:T(8,128)(2,1)S(1)}, u32[]{:S(2)}, u32[]{:S(2)}) collective-permute-start(bf16[64,4608]{1,0:T(8,128)(2,1)S(1)} %add_convert_fusion.9), channel_id=1, source_target_pairs={{0,4},{1,5},{2,6},{3,7},{4,0},{5,1},{6,2},{7,3},{8,12},{9,13},{10,... | collective-permute-start | bytes 1769480 | tf_op jit(solution)/shard_map/ppermute | solution.py:86
  616.2 11.4 %collective-permute-start.57 = (bf16[64,2176]{1,0:T(8,128)(2,1)S(1)}, bf16[64,2176]{1,0:T(8,128)(2,1)S(1)}, u32[]{:S(2)}, u32[]{:S(2)}) collective-permute-start(bf16[64,2176]{1,0:T(8,128)(2,1)S(1)} %get-tuple-element.340), channel_id=1, source_target_pairs={{0,2},{1,3},{2,0},{3,1},{4,6},{5,7},{6,4},{7,5},{8,10},{9,11},{10,... | collective-permute-start | bytes 835592 | tf_op jit(solution)/shard_map/ppermute | solution.py:86
  616.3 11.2 %collective-permute-start.59 = (bf16[64,1024]{1,0:T(8,128)(2,1)S(1)}, bf16[64,1024]{1,0:T(8,128)(2,1)S(1)}, u32[]{:S(2)}, u32[]{:S(2)}) collective-permute-start(bf16[64,1024]{1,0:T(8,128)(2,1)S(1)} %add_convert_fusion.52), channel_id=1, source_target_pairs={{0,2},{1,3},{2,0},{3,1},{4,6},{5,7},{6,4},{7,5},{8,10},{9,11},{10,... | collective-permute-start | bytes 393224 | tf_op jit(solution)/shard_map/ppermute | solution.py:86
  627.7 14.5 %collective-permute-start.60 = (bf16[64,2176]{1,0:T(8,128)(2,1)S(1)}, bf16[64,2176]{1,0:T(8,128)(2,1)S(1)}, u32[]{:S(2)}, u32[]{:S(2)}) collective-permute-start(bf16[64,2176]{1,0:T(8,128)(2,1)S(1)} %add_convert_fusion.41), channel_id=1, source_target_pairs={{0,4},{1,5},{2,6},{3,7},{4,0},{5,1},{6,2},{7,3},{8,12},{9,13},{10,... | collective-permute-start | bytes 835592 | tf_op jit(solution)/shard_map/ppermute | solution.py:86
  627.9 19.6 %collective-permute-start.61 = (bf16[64,4608]{1,0:T(8,128)(2,1)S(1)}, bf16[64,4608]{1,0:T(8,128)(2,1)S(1)}, u32[]{:S(2)}, u32[]{:S(2)}) collective-permute-start(bf16[64,4608]{1,0:T(8,128)(2,1)S(1)} %add_convert_fusion.8), channel_id=1, source_target_pairs={{0,2},{1,3},{2,0},{3,1},{4,6},{5,7},{6,4},{7,5},{8,10},{9,11},{10,... | collective-permute-start | bytes 1769480 | tf_op jit(solution)/shard_map/ppermute | solution.py:86
  631.8 25.2 %collective-permute-start.65 = (bf16[128,4608]{1,0:T(8,128)(2,1)S(1)}, bf16[128,4608]{1,0:T(8,128)(2,1)S(1)}, u32[]{:S(2)}, u32[]{:S(2)}) collective-permute-start(bf16[128,4608]{1,0:T(8,128)(2,1)S(1)} %pad_maximum_fusion.10), channel_id=1, source_target_pairs={{0,1},{1,0},{2,3},{3,2},{4,5},{5,4},{6,7},{7,6},{8,9},{9,8},{10,11... | collective-permute-start | bytes 3538952 | tf_op jit(solution)/shard_map/ppermute | solution.py:86
  647.9 15.6 %collective-permute-start.66 = (bf16[128,4608]{1,0:T(8,128)(2,1)S(1)}, bf16[128,4608]{1,0:T(8,128)(2,1)S(1)}, u32[]{:S(2)}, u32[]{:S(2)}) collective-permute-start(bf16[128,4608]{1,0:T(8,128)(2,1)S(1)} %pad_maximum_fusion.11), channel_id=1, source_target_pairs={{0,1},{1,0},{2,3},{3,2},{4,5},{5,4},{6,7},{7,6},{8,9},{9,8},{10,11... | collective-permute-start | bytes 3538952 | tf_op jit(solution)/shard_map/ppermute | solution.py:86
  653.7 6.1 collective-permute-start.63
  (132 other events, 1054.2 us)

commit v10 on v9

--- a/solution.py
+++ b/solution.py
@@ -842,12 +842,12 @@
     turn = jnp.concatenate([cosine[:, 0].T, sine_table[:, 0].T], axis=0)
     flat = (query_lin.reshape(row_count, -1), key_lin.reshape(row_count, -1), turn, qk_gains[:, None])
     lower = attend_back(query_rot, grad_attn_low, key_rot, value_low, segment, *flat, 0, panels)
-    grad_attn_low, lower, out_given, out_sent = sync(
-        (grad_attn_low, lower, out_given, out_sent), up_back, gate_back
+    grad_attn_low, lower = sync((grad_attn_low, lower), up_back, gate_back, down_back)
+    upper = attend_back(query_rot, grad_attn_low, key_rot, value_low, segment, *flat, panels, panels)
+    lower, upper, out_given, out_sent = sync(
+        (lower, upper, out_given, out_sent), up_back, gate_back, down_back
     )
     out_back = Flow(scatter_steps(links, out_given, out_sent))
-    upper = attend_back(query_rot, grad_attn_low, key_rot, value_low, segment, *flat, panels, panels)
-    lower, upper = sync((lower, upper), up_back, gate_back, out_back, down_back)
     grad_qk_gain = jnp.concatenate(
         [jnp.sum(lower[at] + upper[at], axis=(0, 2)) for at in (3, 4)]
     )
@@ -876,8 +876,8 @@
         [front_other, lax.dynamic_slice_in_dim(small, 1 - core, 1, 1)[:, 0]], axis=2
     )
     front_sent = rep_swap(other_front, 1)
-    own_front, front_sent, mixed_act, grad_normed = sync(
-        (own_front, front_sent, mixed_act, grad_normed), out_back
+    own_front, front_sent, mixed_act, grad_normed = pin(
+        (own_front, front_sent, mixed_act, grad_normed)
     )
     front_back = Flow(scatter_steps(links, own_front, front_sent))
     grad_inputs = grad_hidden + norm_back(

time: 674 us -> 666 us (0.988)
  waiting for transfers between devices: 136 us -> 127 us
    ppermute x33, waiting for transfers between devices: 86.8 us -> 73.5 us  [rep_swap(): return lax.ppermute(value, axes, pairs)]
    ppermute x36, starting transfers between devices: 45.9 us -> 39.1 us  [shard_swap(): return lax.ppermute(value, axes, pairs)]
    unnamed x265 -> x263, local copies, waits for them, and re-layouts: 12.1 us -> 16.2 us
  transfers between devices with their start and end apart: 69 -> 69, of which waited for: 26 -> 24; matrix products, arithmetic and copies ran while one was open for 31% -> 33% of each run, Pallas kernels for 21% -> 22%
where the time goes in v10:
time: 666 us; the launch traced here: 661 us
  Pallas kernels  177 us (27%)
  waiting for transfers between devices  127 us (19%)
  other arithmetic  108 us (16%)
  matrix products  106 us (16%)
  starting transfers between devices  76.8 us (12%)
  local copies, waits for them, and re-layouts  63.9 us (10%)
    ppermute x33, waiting for transfers between devices, rep_swap(): return lax.ppermute(value, axes, pairs)  73.5 us
    dot_general x10, matrix products, matmul_rows(): lax.dot_general(left_mat, right_mat, (((0,), (0,)), ((), ())), preferred_...  64.1 us
    ppermute x36, waiting for transfers between devices, shard_swap(): return lax.ppermute(value, axes, pairs)  54 us
    pallas_call x2, Pallas kernels, attend_back(): pl.pallas_call(attend_back_kernel, out_shape=(jax.ShapeDtypeStruct((rows,...  45 us
    ppermute x36, starting transfers between devices, shard_swap(): return lax.ppermute(value, axes, pairs)  39.1 us
    ppermute x33, starting transfers between devices, rep_swap(): return lax.ppermute(value, axes, pairs)  37.7 us
    pallas_call x2, Pallas kernels, ffn_forward(): pl.pallas_call(functools.partial(ffn_forward_kernel, count, len(into)), o...  33.3 us
    pallas_call x1, Pallas kernels, ffn_input(): pl.pallas_call(functools.partial(ffn_input_kernel, count), out_shape=jax....  28.5 us
  transfers between devices with their start and end apart: 69, of which 24 were waited for; matrix products, arithmetic and copies ran while one was open for 33% of the time, Pallas kernels for 22%

profile of v10, /device:TPU:1, one launch (start us, length us, event | category | flops | bytes accessed | tf_op | source)
XLA Modules:
  0.0 661.0 jit_solution(6348861662636205280)
XLA Ops:
  12.8 7.7 %collective-permute-done.refs_2_ = bf16[128,2176]{1,0:T(8,128)(2,1)S(1)} collective-permute-done((bf16[128,2176]{1,0:T(8,128)(2,1)S(1)}, bf16[128,2176]{1,0:T(8,128)(2,1)S(1)}, u32[]{:S(2)}, u32[]{:S(2)}) %collective-permute-start) | collective-permute-done | bytes 557088 | tf_op jit(solution)/shard_map/ppermute | solution.py:78
  29.0 5.4 collective-permute-start.4
  38.8 6.9 %place_blocks.3 = bf16[1024,2176]{1,0:T(8,128)(2,1)} custom-call(s32[8]{0:T(128)} %stack.70.spots_ref, bf16[256,2176]{1,0:T(8,128)(2,1)} %pad_maximum_fusion.13.refs_0_.refs_1_, bf16[256,2176]{1,0:T(8,128)(2,1)} %pad_maximum_fusion.13.refs_0_.refs_1_, bf16[128,2176]{1,0:T(8,128)(2,1)} %copy-done.26, bf16[128,2176]{1,0:T(8,128)(2,1)} %get-tuple-element.417.refs_3_, ...), custom_call_target="tpu_custom_call" | custom-call | flops 1 | bytes 1 | tf_op jit(solution)/shard_map/place_blocks/pallas_call | solution.py:141
  49.4 4.4 multiply_reduce_fusion.4
  53.8 2.6 multiply_reduce_fusion.5
  72.1 3.9 copy.106.q_ref
  77.4 23.8 %attend.1 = bf16[1024,1024]{1,0:T(8,128)(2,1)} custom-call(s32[4,4]{1,0:T(4,128)} %fusion.80.live_ref, bf16[1024,1024]{1,0:T(8,128)(2,1)} %copy.106.q_ref, bf16[1024,512]{1,0:T(8,128)(2,1)} %copy.107.k_ref, bf16[1024,512]{1,0:T(8,128)(2,1)} %convolution_convert_fusion.11.v_ref, s32[1024,1]{1,0:T(8,128)} %copy.108.seg_col_ref, s32[1,1024]{1,0:T(1,128)} %bitcast.190), custom_call_target="tpu_custom_call" | custom-call | flops 1 | bytes 1 | tf_op jit(solution)/shard_map/attend/pallas_call | solution.py:628
  104.6 4.1 collective-permute-start.12
  111.2 3.4 collective-permute-start.13
  115.4 5.4 place_blocks.4
  120.8 5.3 multiply_reduce_fusion.3
  128.8 6.6 collective-permute-done.12
  135.4 5.6 collective-permute-done.13
  150.0 3.1 collective-permute-done.16.refs_7_.refs_15_
  153.0 15.3 %ffn_forward.2 = (bf16[1024,4608]{1,0:T(8,128)(2,1)}, bf16[1024,4608]{1,0:T(8,128)(2,1)}, bf16[1024,4608]{1,0:T(8,128)(2,1)}) custom-call(s32[8]{0:T(128)} %stack.70.spots_ref, bf16[1024,1024]{1,0:T(8,128)(2,1)} %multiply_convert_fusion.a_ref, bf16[256,4608]{1,0:T(8,128)(2,1)} %refs_1_.4, bf16[256,4608]{1,0:T(8,128)(2,1)} %refs_1_.4, ...), custom_call_target="tpu_custom_call" | custom-call | flops 1 | bytes 1 | tf_op jit(solution)/shard_map/ffn_forward/pallas_call | solution.py:205
  168.3 7.7 %collective-permute-done.17.refs_2_ = bf16[576,1024]{1,0:T(8,128)(2,1)S(1)} collective-permute-done((bf16[576,1024]{1,0:T(8,128)(2,1)}, bf16[576,1024]{1,0:T(8,128)(2,1)S(1)}, u32[]{:S(2)}, u32[]{:S(2)}) %collective-permute-start.17) | collective-permute-done | bytes 1179680 | tf_op jit(solution)/shard_map/ppermute | solution.py:78
  181.5 18.0 %ffn_forward.3 = (bf16[1024,4608]{1,0:T(8,128)(2,1)}, bf16[1024,4608]{1,0:T(8,128)(2,1)}, bf16[1024,4608]{1,0:T(8,128)(2,1)}) custom-call(s32[8]{0:T(128)} %stack.70.spots_ref, bf16[1024,1024]{1,0:T(8,128)(2,1)} %multiply_convert_fusion.a_ref, bf16[256,4608]{1,0:T(8,128)(2,1)} %refs_1_.4, ...), custom_call_target="tpu_custom_call", output_to_operand_aliasing={{0}: (18, {}), {1}: (19, {}), {2}: (20, {})} | custom-call | flops 1 | bytes 1 | tf_op jit(solution)/shard_map/ffn_forward/pallas_call | solution.py:205
  205.6 9.4 %place_blocks.5.down_ref = bf16[4608,1024]{1,0:T(8,128)(2,1)} custom-call(s32[8]{0:T(128)} %stack.70.spots_ref, bf16[1152,1024]{1,0:T(8,128)(2,1)} %refs_1_.3, bf16[1152,1024]{1,0:T(8,128)(2,1)} %refs_1_.3, bf16[576,1024]{1,0:T(8,128)(2,1)} %copy-done.32, bf16[576,1024]{1,0:T(8,128)(2,1)} %collective-permute-done.21.refs_3_, ...), custom_call_target="tpu_custom_call" | custom-call | flops 1 | bytes 1 | tf_op jit(solution)/shard_map/place_blocks/pallas_call | solution.py:141
  215.0 24.8 %ffn_inner.1 = (bf16[1024,4608]{1,0:T(8,128)(2,1)}, bf16[1024,4608]{1,0:T(8,128)(2,1)}) custom-call(bf16[1024,1024]{1,0:T(8,128)(2,1)} %copy-done.12, bf16[4608,1024]{1,0:T(8,128)(2,1)} %place_blocks.5.down_ref, bf16[1024,4608]{1,0:T(8,128)(2,1)} %get-tuple-element.222.act_ref, bf16[1024,4608]{1,0:T(8,128)(2,1)} %get-tuple-element.223.slope_ref), custom_call_target="tpu_custom_call" | custom-call | flops 1 | bytes 1 | tf_op jit(solution)/shard_map/ffn_inner/pallas_call | solution.py:238
  239.8 10.8 %convolution_convert_fusion.1 = bf16[4608,512]{1,0:T(8,128)(2,1)} fusion(bf16[1024,4608]{1,0:T(8,128)(2,1)} %get-tuple-element.297, bf16[1024,512]{1,0:T(8,128)(2,1)S(1)} %copy-done.59), kind=kOutput, calls=%fused_computation.6 | convolution fusion | flops 4834197504 | bytes 15204352 | tf_op jit(solution)/shard_map/dot_general | solution.py:57
  251.8 10.9 %convolution_convert_fusion.5 = bf16[512,4608]{1,0:T(8,128)(2,1)} fusion(bf16[1024,4608]{1,0:T(8,128)(2,1)} %get-tuple-element.242.dgate_ref, bf16[1024,128]{1,0:T(8,128)(2,1)S(1)} %get-tuple-element.409, bf16[1024,128]{1,0:T(8,128)(2,1)S(1)} %get-tuple-element.410, bf16[1024,128]{1,0:T(8,128)(2,1)S(1)} %get-tuple-element.411, ...), kind=kOutput, calls=%fused_computation.10 | convolution fusion | flops 4838391808 | bytes 15204352 | tf_op jit(solution)/shard_map/dot_general | solution.py:57
  262.8 6.9 %convolution_convert_fusion = bf16[4608,512]{1,0:T(8,128)(2,1)} fusion(bf16[1024,4608]{1,0:T(8,128)(2,1)S(1)} %bitcast.156, bf16[1024,512]{1,0:T(8,128)(2,1)S(1)} %copy-done.58), kind=kOutput, calls=%fused_computation.5 | convolution fusion | flops 4834197504 | bytes 15204352 | tf_op jit(solution)/shard_map/dot_general | solution.py:57
  269.7 7.1 %convolution_convert_fusion.2 = bf16[512,4608]{1,0:T(8,128)(2,1)} fusion(bf16[1024,512]{1,0:T(8,128)(2,1)S(1)} %pad_maximum_fusion.15, bf16[1024,4608]{1,0:T(8,128)(2,1)S(1)} %bitcast.160), kind=kOutput, calls=%fused_computation.7 | convolution fusion | flops 4834197504 | bytes 15204352 | tf_op jit(solution)/shard_map/dot_general | solution.py:57
  278.8 3.0 add_convert_fusion.34
  284.8 11.0 %convolution_convert_fusion.3 = bf16[512,4608]{1,0:T(8,128)(2,1)} fusion(bf16[1024,512]{1,0:T(8,128)(2,1)S(1)} %pad_maximum_fusion.16, bf16[1024,4608]{1,0:T(8,128)(2,1)} %get-tuple-element.243.dup_ref), kind=kOutput, calls=%fused_computation.8 | convolution fusion | flops 4834197504 | bytes 15204352 | tf_op jit(solution)/shard_map/dot_general | solution.py:57
  295.8 5.4 convolution_convert_fusion.4
  301.2 8.3 %collective-permute-done.27 = bf16[2,576,512]{2,1,0:T(8,128)(2,1)S(1)} collective-permute-done((bf16[2,576,512]{2,1,0:T(8,128)(2,1)S(1)}, bf16[2,576,512]{2,1,0:T(8,128)(2,1)S(1)}, u32[]{:S(2)}, u32[]{:S(2)}) %collective-permute-start.27) | collective-permute-done | bytes 1179680 | tf_op jit(solution)/shard_map/ppermute | solution.py:78
  310.7 3.3 fusion.61
  321.4 28.5 %ffn_input.1 = f32[1024,1024]{1,0:T(8,128)} custom-call(s32[8]{0:T(128)} %stack.70.spots_ref, bf16[1024,4608]{1,0:T(8,128)(2,1)} %get-tuple-element.242.dgate_ref, bf16[1024,4608]{1,0:T(8,128)(2,1)} %get-tuple-element.243.dup_ref, bf16[256,4608]{1,0:T(8,128)(2,1)} %refs_1_.4, bf16[256,4608]{1,0:T(8,128)(2,1)} %refs_1_.4, bf16[128,9216]{1,0:T(8,128)(2,1)} %copy-done.4, ...), custom_call_target="tpu_custom_call" | custom-call | flops 1 | bytes 1 | tf_op jit(solution)/shard_map/ffn_input/pallas_call | solution.py:280
  350.0 4.1 multiply_reduce_fusion.2
  361.7 2.6 broadcast_select_fusion.8
  367.3 3.7 convolution_convert_fusion.8.do_ref
  370.9 6.6 collective-permute-done.34
  377.6 2.9 add_convert_fusion.22
  384.9 3.3 fusion.63
  392.9 5.5 copy.113.q_lin_ref
  401.0 22.4 %attend_back.2 = (bf16[1024,512]{1,0:T(8,128)(2,1)}, bf16[1024,256]{1,0:T(8,128)(2,1)}, bf16[1024,256]{1,0:T(8,128)(2,1)}, f32[2,64,256]{2,1,0:T(8,128)}, f32[2,64,256]{2,1,0:T(8,128)}) custom-call(s32[4,4]{1,0:T(4,128)} %fusion.80.live_ref, bf16[1024,1024]{1,0:T(8,128)(2,1)} %copy.106.q_ref, bf16[1024,1024]{1,0:T(8,128)(2,1)} %convolution_convert_fusion.8.do_ref, ...), custom_call_target="tpu_custom_call" | custom-call | flops 1 | bytes 1 | tf_op jit(solution)/shard_map/attend_back/pallas_call | solution.py:652
  423.4 3.6 fusion.65
  427.1 3.3 collective-permute-start.40
  431.3 4.0 broadcast_select_fusion.5
  435.3 3.4 collective-permute-start.42
  440.5 22.6 %attend_back.3 = (bf16[1024,512]{1,0:T(8,128)(2,1)}, bf16[1024,256]{1,0:T(8,128)(2,1)}, bf16[1024,256]{1,0:T(8,128)(2,1)}, f32[2,64,256]{2,1,0:T(8,128)}, f32[2,64,256]{2,1,0:T(8,128)}) custom-call(s32[4,4]{1,0:T(4,128)} %fusion.80.live_ref, bf16[1024,1024]{1,0:T(8,128)(2,1)} %copy.106.q_ref, bf16[1024,1024]{1,0:T(8,128)(2,1)} %convolution_convert_fusion.8.do_ref, ...), custom_call_target="tpu_custom_call" | custom-call | flops 1 | bytes 1 | tf_op jit(solution)/shard_map/attend_back/pallas_call | solution.py:652
  474.4 4.7 convolution_convert_fusion.6
  480.8 2.5 collective-permute-start.44
  483.3 3.8 convolution_convert_fusion.7
  487.1 3.3 fusion.53
  490.4 4.0 broadcast_select_fusion.4
  498.3 2.5 collective-permute-start.46
  501.7 3.7 collective-permute-start.49
  512.5 4.1 fusion.12
  516.6 2.7 add_add_fusion
  519.4 12.3 %fusion.11 = f32[1152,1024]{1,0:T(8,128)} fusion(bf16[1152,512]{1,0:T(8,128)(2,1)} %collective-permute-done.68, bf16[576,512]{1,0:T(8,128)(2,1)S(1)} %get-tuple-element.419, bf16[576,512]{1,0:T(8,128)(2,1)S(1)} %get-tuple-element.418, pred[]{:T(512)S(6)} %eq.38), kind=kLoop, calls=%fused_computation.42 | loop fusion | flops 16515072 | bytes 7077889 | tf_op jit(solution)/shard_map/convert_element_type | solution.py:448
  533.9 13.1 %add_multiply_fusion = bf16[1024,1024]{1,0:T(8,128)(2,1)} fusion(f32[1024,1024]{1,0:T(8,128)S(1)} %copy-done.8, f32[1024]{0:T(1024)S(1)} %copy-done.94, bf16[1024,4608]{1,0:T(8,128)(2,1)} %get-tuple-element.297, bf16[4608,1024]{1,0:T(8,128)(2,1)S(1)} %bitcast.154), kind=kOutput, calls=%fused_computation.20 | convolution fusion | flops 9666822144 | bytes 25169920 | tf_op jit(solution)/shard_map/dot_general | solution.py:53
  552.9 10.1 %collective-permute-done.47 = bf16[2,64,2176]{2,1,0:T(8,128)(2,1)S(1)} collective-permute-done((bf16[2,64,2176]{2,1,0:T(8,128)(2,1)S(1)}, bf16[2,64,2176]{2,1,0:T(8,128)(2,1)S(1)}, u32[]{:S(2)}, u32[]{:S(2)}) %collective-permute-start.47) | collective-permute-done | bytes 557088 | tf_op jit(solution)/shard_map/ppermute | solution.py:78
  571.7 2.9 collective-permute-done.53
  575.2 15.3 %collective-permute-done.55 = bf16[64,4608]{1,0:T(8,128)(2,1)S(1)} collective-permute-done((bf16[64,4608]{1,0:T(8,128)(2,1)S(1)}, bf16[64,4608]{1,0:T(8,128)(2,1)S(1)}, u32[]{:S(2)}, u32[]{:S(2)}) %collective-permute-start.55) | collective-permute-done | bytes 589856 | tf_op jit(solution)/shard_map/ppermute | solution.py:86
  594.7 4.9 collective-permute-done.57
  599.6 6.0 collective-permute-done.58
  608.4 10.5 %collective-permute-done.63 = bf16[64,1024]{1,0:T(8,128)(2,1)S(1)} collective-permute-done((bf16[64,1024]{1,0:T(8,128)(2,1)S(1)}, bf16[64,1024]{1,0:T(8,128)(2,1)S(1)}, u32[]{:S(2)}, u32[]{:S(2)}) %collective-permute-start.63) | collective-permute-done | bytes 131104 | tf_op jit(solution)/shard_map/ppermute | solution.py:86
  620.6 8.2 %collective-permute-done.64 = bf16[64,1024]{1,0:T(8,128)(2,1)S(1)} collective-permute-done((bf16[64,1024]{1,0:T(8,128)(2,1)S(1)}, bf16[64,1024]{1,0:T(8,128)(2,1)S(1)}, u32[]{:S(2)}, u32[]{:S(2)}) %collective-permute-start.64) | collective-permute-done | bytes 131104 | tf_op jit(solution)/shard_map/ppermute | solution.py:86
  631.8 9.7 %collective-permute-done.60 = bf16[64,4608]{1,0:T(8,128)(2,1)S(1)} collective-permute-done((bf16[64,4608]{1,0:T(8,128)(2,1)S(1)}, bf16[64,4608]{1,0:T(8,128)(2,1)S(1)}, u32[]{:S(2)}, u32[]{:S(2)}) %collective-permute-start.60) | collective-permute-done | bytes 589856 | tf_op jit(solution)/shard_map/ppermute | solution.py:86
  642.3 7.0 %collective-permute-done.61 = bf16[64,2176]{1,0:T(8,128)(2,1)S(1)} collective-permute-done((bf16[64,2176]{1,0:T(8,128)(2,1)S(1)}, bf16[64,2176]{1,0:T(8,128)(2,1)S(1)}, u32[]{:S(2)}, u32[]{:S(2)}) %collective-permute-start.61) | collective-permute-done | bytes 278560 | tf_op jit(solution)/shard_map/ppermute | solution.py:86
  650.8 2.8 multiply_reduce_fusion.1
  657.4 2.8 multiply_reduce_fusion
  (521 shorter events, 174.8 us)
Async XLA Ops:
  6.0 14.5 %collective-permute-start = (bf16[128,2176]{1,0:T(8,128)(2,1)S(1)}, bf16[128,2176]{1,0:T(8,128)(2,1)S(1)}, u32[]{:S(2)}, u32[]{:S(2)}) collective-permute-start(bf16[128,2176]{1,0:T(8,128)(2,1)S(1)} %pad_maximum_fusion.18), channel_id=1, source_target_pairs={{0,8},{1,9},{2,10},{3,11},{4,12},{5,13},{6,14},{7,15},{8,0},{9,1},... | collective-permute-start | bytes 1671176 | tf_op jit(solution)/shard_map/ppermute | solution.py:78
  8.1 13.2 %collective-permute-start.1 = (bf16[128,2176]{1,0:T(8,128)(2,1)S(1)}, bf16[128,2176]{1,0:T(8,128)(2,1)S(1)}, u32[]{:S(2)}, u32[]{:S(2)}) collective-permute-start(bf16[128,2176]{1,0:T(8,128)(2,1)S(1)} %pad_maximum_fusion.18), channel_id=1, source_target_pairs={{0,16},{1,17},{2,18},{3,19},{4,20},{5,21},{6,22},{7,23},{8,24},{9,... | collective-permute-start | bytes 1671176 | tf_op jit(solution)/shard_map/ppermute | solution.py:78
  26.2 40.5 %collective-permute-start.5 = (bf16[128,1024]{1,0:T(8,128)(2,1)}, bf16[128,1024]{1,0:T(8,128)(2,1)}, u32[]{:S(2)}, u32[]{:S(2)}) collective-permute-start(bf16[128,1024]{1,0:T(8,128)(2,1)} %constant_dynamic-slice_fusion.31), channel_id=1, source_target_pairs={{0,8},{1,9},{2,10},{3,11},{4,12},{5,13},{6,14},{7,15},{8,0},{9,1},... | collective-permute-start | bytes 786440 | tf_op jit(solution)/shard_map/ppermute | solution.py:78
  27.4 39.4 %collective-permute-start.6 = (bf16[128,1024]{1,0:T(8,128)(2,1)}, bf16[128,1024]{1,0:T(8,128)(2,1)}, u32[]{:S(2)}, u32[]{:S(2)}) collective-permute-start(bf16[128,1024]{1,0:T(8,128)(2,1)} %constant_dynamic-slice_fusion.31), channel_id=1, source_target_pairs={{0,16},{1,17},{2,18},{3,19},{4,20},{5,21},{6,22},{7,23},{8,24},{9,... | collective-permute-start | bytes 786440 | tf_op jit(solution)/shard_map/ppermute | solution.py:78
  29.0 8.5 %collective-permute-start.4 = (bf16[3,128,2176]{2,1,0:T(8,128)(2,1)S(1)}, bf16[3,128,2176]{2,1,0:T(8,128)(2,1)S(1)}, u32[]{:S(2)}, u32[]{:S(2)}) collective-permute-start(bf16[3,128,2176]{2,1,0:T(8,128)(2,1)S(1)} %pad_maximum_fusion.3), channel_id=1, source_target_pairs={{0,1},{1,0},{2,3},{3,2},{4,5},{5,4},{6,7},{7,6},{8,9},{9,8},{10,11... | collective-permute-start | bytes 5013512 | tf_op jit(solution)/shard_map/ppermute | solution.py:86
  36.2 64.9 %collective-permute-start.9 = (bf16[128,9216]{1,0:T(8,128)(2,1)}, bf16[128,9216]{1,0:T(8,128)(2,1)S(1)}, u32[]{:S(2)}, u32[]{:S(2)}) collective-permute-start(bf16[128,9216]{1,0:T(8,128)(2,1)} %pad_maximum_fusion), channel_id=1, source_target_pairs={{0,8},{1,9},{2,10},{3,11},{4,12},{5,13},{6,14},{7,15},{8,0},{9,1},... | collective-permute-start | bytes 7077896 | tf_op jit(solution)/shard_map/ppermute | solution.py:78
  36.2 64.9 %collective-permute-start.10 = (bf16[128,9216]{1,0:T(8,128)(2,1)}, bf16[128,9216]{1,0:T(8,128)(2,1)}, u32[]{:S(2)}, u32[]{:S(2)}) collective-permute-start(bf16[128,9216]{1,0:T(8,128)(2,1)} %pad_maximum_fusion), channel_id=1, source_target_pairs={{0,16},{1,17},{2,18},{3,19},{4,20},{5,21},{6,22},{7,23},{8,24},{9,... | collective-permute-start | bytes 7077896 | tf_op jit(solution)/shard_map/ppermute | solution.py:78
  68.3 32.8 %collective-permute-start.7 = (bf16[64,1024]{1,0:T(8,128)(2,1)}, bf16[64,1024]{1,0:T(8,128)(2,1)S(1)}, u32[]{:S(2)}, u32[]{:S(2)}) collective-permute-start(bf16[64,1024]{1,0:T(8,128)(2,1)} %slice.203), channel_id=1, source_target_pairs={{0,16},{1,17},{2,18},{3,19},{4,20},{5,21},{6,22},{7,23},{8,24},{9,... | collective-permute-start | bytes 393224 | tf_op jit(solution)/shard_map/ppermute | solution.py:78
  70.0 31.2 %collective-permute-start.8 = (bf16[64,1024]{1,0:T(8,128)(2,1)}, bf16[64,1024]{1,0:T(8,128)(2,1)}, u32[]{:S(2)}, u32[]{:S(2)}) collective-permute-start(bf16[64,1024]{1,0:T(8,128)(2,1)} %slice.204), channel_id=1, source_target_pairs={{0,8},{1,9},{2,10},{3,11},{4,12},{5,13},{6,14},{7,15},{8,0},{9,1},... | collective-permute-start | bytes 393224 | tf_op jit(solution)/shard_map/ppermute | solution.py:78
  103.5 11.1 %collective-permute-start.11 = (bf16[3,128,1024]{2,1,0:T(8,128)(2,1)S(1)}, bf16[3,128,1024]{2,1,0:T(8,128)(2,1)S(1)}, u32[]{:S(2)}, u32[]{:S(2)}) collective-permute-start(bf16[3,128,1024]{2,1,0:T(8,128)(2,1)S(1)} %pad_maximum_fusion.17), channel_id=1, source_target_pairs={{0,1},{1,0},{2,3},{3,2},{4,5},{5,4},{6,7},{7,6},{8,9},{9,8},{10,11... | collective-permute-start | bytes 2359304 | tf_op jit(solution)/shard_map/ppermute | solution.py:86
  104.6 30.8 %collective-permute-start.12 = (bf16[64,9216]{1,0:T(8,128)(2,1)}, bf16[64,9216]{1,0:T(8,128)(2,1)S(1)}, u32[]{:S(2)}, u32[]{:S(2)}) collective-permute-start(bf16[64,9216]{1,0:T(8,128)(2,1)} %slice.209), channel_id=1, source_target_pairs={{0,16},{1,17},{2,18},{3,19},{4,20},{5,21},{6,22},{7,23},{8,24},{9,... | collective-permute-start | bytes 3538952 | tf_op jit(solution)/shard_map/ppermute | solution.py:78
  111.2 29.8 %collective-permute-start.13 = (bf16[64,9216]{1,0:T(8,128)(2,1)}, bf16[64,9216]{1,0:T(8,128)(2,1)}, u32[]{:S(2)}, u32[]{:S(2)}) collective-permute-start(bf16[64,9216]{1,0:T(8,128)(2,1)} %slice.210), channel_id=1, source_target_pairs={{0,8},{1,9},{2,10},{3,11},{4,12},{5,13},{6,14},{7,15},{8,0},{9,1},... | collective-permute-start | bytes 3538952 | tf_op jit(solution)/shard_map/ppermute | solution.py:78
  141.0 9.0 %collective-permute-start.14 = (bf16[128,9216]{1,0:T(8,128)(2,1)S(1)}, bf16[128,9216]{1,0:T(8,128)(2,1)}, u32[]{:S(2)}, u32[]{:S(2)}) collective-permute-start(bf16[128,9216]{1,0:T(8,128)(2,1)S(1)} %collective-permute-done.9.refs_2_.refs_10_), channel_id=1, source_target_pairs={{0,1},{1,0},{2,3},{3,2},{4,5},{5,4},{6,7},{7,6},{8,9},{9,8},{10,11... | collective-permute-start | bytes 7077896 | tf_op jit(solution)/shard_map/ppermute | solution.py:86
  141.8 8.2 %collective-permute-start.15 = (bf16[128,9216]{1,0:T(8,128)(2,1)}, bf16[128,9216]{1,0:T(8,128)(2,1)}, u32[]{:S(2)}, u32[]{:S(2)}) collective-permute-start(bf16[128,9216]{1,0:T(8,128)(2,1)} %collective-permute-done.10.refs_4_.refs_12_), channel_id=1, source_target_pairs={{0,1},{1,0},{2,3},{3,2},{4,5},{5,4},{6,7},{7,6},{8,9},{9,8},{10,11... | collective-permute-start | bytes 7077896 | tf_op jit(solution)/shard_map/ppermute | solution.py:86
  145.3 7.8 %collective-permute-start.16 = (bf16[128,9216]{1,0:T(8,128)(2,1)}, bf16[128,9216]{1,0:T(8,128)(2,1)}, u32[]{:S(2)}, u32[]{:S(2)}) collective-permute-start(bf16[128,9216]{1,0:T(8,128)(2,1)} %constant_dynamic-update-slice_fusion.4.refs_6_.refs_14_), channel_id=1, source_target_pairs={{0,1},{1,0},{2,3},{3,2},{4,5},{5,4},{6,7},{7,6},{8,9},{9,8},{10,11... | collective-permute-start | bytes 7077896 | tf_op jit(solution)/shard_map/ppermute | solution.py:86
  148.1 27.9 %collective-permute-start.17 = (bf16[576,1024]{1,0:T(8,128)(2,1)}, bf16[576,1024]{1,0:T(8,128)(2,1)S(1)}, u32[]{:S(2)}, u32[]{:S(2)}) collective-permute-start(bf16[576,1024]{1,0:T(8,128)(2,1)} %constant_dynamic-slice_fusion.28), channel_id=1, source_target_pairs={{0,8},{1,9},{2,10},{3,11},{4,12},{5,13},{6,14},{7,15},{8,0},{9,1},... | collective-permute-start | bytes 3538952 | tf_op jit(solution)/shard_map/ppermute | solution.py:78
  149.6 27.6 %collective-permute-start.18 = (bf16[576,1024]{1,0:T(8,128)(2,1)}, bf16[576,1024]{1,0:T(8,128)(2,1)}, u32[]{:S(2)}, u32[]{:S(2)}) collective-permute-start(bf16[576,1024]{1,0:T(8,128)(2,1)} %constant_dynamic-slice_fusion.28), channel_id=1, source_target_pairs={{0,16},{1,17},{2,18},{3,19},{4,20},{5,21},{6,22},{7,23},{8,24},{9,... | collective-permute-start | bytes 3538952 | tf_op jit(solution)/shard_map/ppermute | solution.py:78
  177.2 22.3 %collective-permute-start.21 = (bf16[576,1024]{1,0:T(8,128)(2,1)S(1)}, bf16[576,1024]{1,0:T(8,128)(2,1)}, u32[]{:S(2)}, u32[]{:S(2)}) collective-permute-start(bf16[576,1024]{1,0:T(8,128)(2,1)S(1)} %collective-permute-done.17.refs_2_), channel_id=1, source_target_pairs={{0,1},{1,0},{2,3},{3,2},{4,5},{5,4},{6,7},{7,6},{8,9},{9,8},{10,11... | collective-permute-start | bytes 3538952 | tf_op jit(solution)/shard_map/ppermute | solution.py:86
  178.3 21.2 %collective-permute-start.22 = (bf16[576,1024]{1,0:T(8,128)(2,1)}, bf16[576,1024]{1,0:T(8,128)(2,1)}, u32[]{:S(2)}, u32[]{:S(2)}) collective-permute-start(bf16[576,1024]{1,0:T(8,128)(2,1)} %collective-permute-done.18.refs_4_), channel_id=1, source_target_pairs={{0,1},{1,0},{2,3},{3,2},{4,5},{5,4},{6,7},{7,6},{8,9},{9,8},{10,11... | collective-permute-start | bytes 3538952 | tf_op jit(solution)/shard_map/ppermute | solution.py:86
  181.1 18.4 %collective-permute-start.19 = (bf16[288,1024]{1,0:T(8,128)(2,1)}, bf16[288,1024]{1,0:T(8,128)(2,1)}, u32[]{:S(2)}, u32[]{:S(2)}) collective-permute-start(bf16[288,1024]{1,0:T(8,128)(2,1)} %slice.211), channel_id=1, source_target_pairs={{0,16},{1,17},{2,18},{3,19},{4,20},{5,21},{6,22},{7,23},{8,24},{9,... | collective-permute-start | bytes 1769480 | tf_op jit(solution)/shard_map/ppermute | solution.py:78
  181.4 18.0 %collective-permute-start.20 = (bf16[288,1024]{1,0:T(8,128)(2,1)}, bf16[288,1024]{1,0:T(8,128)(2,1)}, u32[]{:S(2)}, u32[]{:S(2)}) collective-permute-start(bf16[288,1024]{1,0:T(8,128)(2,1)} %slice.212), channel_id=1, source_target_pairs={{0,8},{1,9},{2,10},{3,11},{4,12},{5,13},{6,14},{7,15},{8,0},{9,1},... | collective-permute-start | bytes 1769480 | tf_op jit(solution)/shard_map/ppermute | solution.py:78
  250.5 12.2 %collective-permute-start.24 = (bf16[4,1152,512]{2,1,0:T(8,128)(2,1)}, bf16[4,1152,512]{2,1,0:T(8,128)(2,1)}, u32[]{:S(2)}, u32[]{:S(2)}) collective-permute-start(bf16[4,1152,512]{2,1,0:T(8,128)(2,1)} %bitcast.27), channel_id=1, source_target_pairs={{0,1},{1,0},{2,3},{3,2},{4,5},{5,4},{6,7},{7,6},{8,9},{9,8},{10,11... | collective-permute-start | bytes 14155784 | tf_op jit(solution)/shard_map/ppermute | solution.py:86
  262.6 38.6 %collective-permute-start.25 = (bf16[4,128,4608]{2,1,0:T(8,128)(2,1)}, bf16[4,128,4608]{2,1,0:T(8,128)(2,1)}, u32[]{:S(2)}, u32[]{:S(2)}) collective-permute-start(bf16[4,128,4608]{2,1,0:T(8,128)(2,1)} %bitcast.30), channel_id=1, source_target_pairs={{0,1},{1,0},{2,3},{3,2},{4,5},{5,4},{6,7},{7,6},{8,9},{9,8},{10,11... | collective-permute-start | bytes 14155784 | tf_op jit(solution)/shard_map/ppermute | solution.py:86
  276.8 33.9 %collective-permute-start.26 = (bf16[4,128,4608]{2,1,0:T(8,128)(2,1)}, bf16[4,128,4608]{2,1,0:T(8,128)(2,1)}, u32[]{:S(2)}, u32[]{:S(2)}) collective-permute-start(bf16[4,128,4608]{2,1,0:T(8,128)(2,1)} %bitcast.32), channel_id=1, source_target_pairs={{0,1},{1,0},{2,3},{3,2},{4,5},{5,4},{6,7},{7,6},{8,9},{9,8},{10,11... | collective-permute-start | bytes 14155784 | tf_op jit(solution)/shard_map/ppermute | solution.py:86
  281.9 27.6 %collective-permute-start.27 = (bf16[2,576,512]{2,1,0:T(8,128)(2,1)S(1)}, bf16[2,576,512]{2,1,0:T(8,128)(2,1)S(1)}, u32[]{:S(2)}, u32[]{:S(2)}) collective-permute-start(bf16[2,576,512]{2,1,0:T(8,128)(2,1)S(1)} %pad_maximum_fusion.4), channel_id=1, source_target_pairs={{0,8},{1,9},{2,10},{3,11},{4,12},{5,13},{6,14},{7,15},{8,0},{9,1},... | collective-permute-start | bytes 3538952 | tf_op jit(solution)/shard_map/ppermute | solution.py:78
  283.6 27.2 %collective-permute-start.28 = (bf16[2,576,512]{2,1,0:T(8,128)(2,1)S(1)}, bf16[2,576,512]{2,1,0:T(8,128)(2,1)S(1)}, u32[]{:S(2)}, u32[]{:S(2)}) collective-permute-start(bf16[2,576,512]{2,1,0:T(8,128)(2,1)S(1)} %pad_maximum_fusion.5), channel_id=1, source_target_pairs={{0,16},{1,17},{2,18},{3,19},{4,20},{5,21},{6,22},{7,23},{8,24},{9,... | collective-permute-start | bytes 3538952 | tf_op jit(solution)/shard_map/ppermute | solution.py:78
  314.1 35.9 %collective-permute-start.29 = (bf16[576,512]{1,0:T(8,128)(2,1)}, bf16[576,512]{1,0:T(8,128)(2,1)}, u32[]{:S(2)}, u32[]{:S(2)}) collective-permute-start(bf16[576,512]{1,0:T(8,128)(2,1)} %get-tuple-element.366), channel_id=1, source_target_pairs={{0,16},{1,17},{2,18},{3,19},{4,20},{5,21},{6,22},{7,23},{8,24},{9,... | collective-permute-start | bytes 1769480 | tf_op jit(solution)/shard_map/ppermute | solution.py:78
  315.3 34.7 %collective-permute-start.30 = (bf16[576,512]{1,0:T(8,128)(2,1)S(1)}, bf16[576,512]{1,0:T(8,128)(2,1)}, u32[]{:S(2)}, u32[]{:S(2)}) collective-permute-start(bf16[576,512]{1,0:T(8,128)(2,1)S(1)} %get-tuple-element.365), channel_id=1, source_target_pairs={{0,8},{1,9},{2,10},{3,11},{4,12},{5,13},{6,14},{7,15},{8,0},{9,1},... | collective-permute-start | bytes 1769480 | tf_op jit(solution)/shard_map/ppermute | solution.py:78
  319.2 58.4 %collective-permute-start.32 = (bf16[2,64,4608]{2,1,0:T(8,128)(2,1)}, bf16[2,64,4608]{2,1,0:T(8,128)(2,1)S(1)}, u32[]{:S(2)}, u32[]{:S(2)}) collective-permute-start(bf16[2,64,4608]{2,1,0:T(8,128)(2,1)} %pad_maximum_fusion.6), channel_id=1, source_target_pairs={{0,8},{1,9},{2,10},{3,11},{4,12},{5,13},{6,14},{7,15},{8,0},{9,1},... | collective-permute-start | bytes 3538952 | tf_op jit(solution)/shard_map/ppermute | solution.py:78
  321.2 56.3 %collective-permute-start.33 = (bf16[2,64,4608]{2,1,0:T(8,128)(2,1)}, bf16[2,64,4608]{2,1,0:T(8,128)(2,1)}, u32[]{:S(2)}, u32[]{:S(2)}) collective-permute-start(bf16[2,64,4608]{2,1,0:T(8,128)(2,1)} %pad_maximum_fusion.7), channel_id=1, source_target_pairs={{0,16},{1,17},{2,18},{3,19},{4,20},{5,21},{6,22},{7,23},{8,24},{9,... | collective-permute-start | bytes 3538952 | tf_op jit(solution)/shard_map/ppermute | solution.py:78
  359.2 18.3 %collective-permute-start.31 = (bf16[4,128,1024]{2,1,0:T(8,128)(2,1)S(1)}, bf16[4,128,1024]{2,1,0:T(8,128)(2,1)S(1)}, u32[]{:S(2)}, u32[]{:S(2)}) collective-permute-start(bf16[4,128,1024]{2,1,0:T(8,128)(2,1)S(1)} %bitcast.195), channel_id=1, source_target_pairs={{0,1},{1,0},{2,3},{3,2},{4,5},{5,4},{6,7},{7,6},{8,9},{9,8},{10,11... | collective-permute-start | bytes 3145736 | tf_op jit(solution)/shard_map/ppermute | solution.py:86
  364.3 13.2 %collective-permute-start.34 = (bf16[576,512]{1,0:T(8,128)(2,1)S(1)}, bf16[576,512]{1,0:T(8,128)(2,1)S(1)}, u32[]{:S(2)}, u32[]{:S(2)}) collective-permute-start(bf16[576,512]{1,0:T(8,128)(2,1)S(1)} %get-tuple-element.350), channel_id=1, source_target_pairs={{0,2},{1,3},{2,0},{3,1},{4,6},{5,7},{6,4},{7,5},{8,10},{9,11},{10,... | collective-permute-start | bytes 1769480 | tf_op jit(solution)/shard_map/ppermute | solution.py:86
  381.7 41.7 %collective-permute-start.35 = (bf16[2,64,4608]{2,1,0:T(8,128)(2,1)}, bf16[2,64,4608]{2,1,0:T(8,128)(2,1)}, u32[]{:S(2)}, u32[]{:S(2)}) collective-permute-start(bf16[2,64,4608]{2,1,0:T(8,128)(2,1)} %pad_maximum_fusion.8), channel_id=1, source_target_pairs={{0,8},{1,9},{2,10},{3,11},{4,12},{5,13},{6,14},{7,15},{8,0},{9,1},... | collective-permute-start | bytes 3538952 | tf_op jit(solution)/shard_map/ppermute | solution.py:78
  383.3 40.1 %collective-permute-start.36 = (bf16[2,64,4608]{2,1,0:T(8,128)(2,1)}, bf16[2,64,4608]{2,1,0:T(8,128)(2,1)}, u32[]{:S(2)}, u32[]{:S(2)}) collective-permute-start(bf16[2,64,4608]{2,1,0:T(8,128)(2,1)} %pad_maximum_fusion.9), channel_id=1, source_target_pairs={{0,16},{1,17},{2,18},{3,19},{4,20},{5,21},{6,22},{7,23},{8,24},{9,... | collective-permute-start | bytes 3538952 | tf_op jit(solution)/shard_map/ppermute | solution.py:78
  388.2 35.2 %collective-permute-start.37 = (bf16[64,4608]{1,0:T(8,128)(2,1)}, bf16[64,4608]{1,0:T(8,128)(2,1)}, u32[]{:S(2)}, u32[]{:S(2)}) collective-permute-start(bf16[64,4608]{1,0:T(8,128)(2,1)} %get-tuple-element.356), channel_id=1, source_target_pairs={{0,16},{1,17},{2,18},{3,19},{4,20},{5,21},{6,22},{7,23},{8,24},{9,... | collective-permute-start | bytes 1769480 | tf_op jit(solution)/shard_map/ppermute | solution.py:78
  388.2 35.2 %collective-permute-start.38 = (bf16[64,4608]{1,0:T(8,128)(2,1)}, bf16[64,4608]{1,0:T(8,128)(2,1)}, u32[]{:S(2)}, u32[]{:S(2)}) collective-permute-start(bf16[64,4608]{1,0:T(8,128)(2,1)} %get-tuple-element.355), channel_id=1, source_target_pairs={{0,8},{1,9},{2,10},{3,11},{4,12},{5,13},{6,14},{7,15},{8,0},{9,1},... | collective-permute-start | bytes 1769480 | tf_op jit(solution)/shard_map/ppermute | solution.py:78
  389.3 34.1 %collective-permute-start.39 = (bf16[576,512]{1,0:T(8,128)(2,1)S(1)}, bf16[576,512]{1,0:T(8,128)(2,1)S(1)}, u32[]{:S(2)}, u32[]{:S(2)}) collective-permute-start(bf16[576,512]{1,0:T(8,128)(2,1)S(1)} %add_convert_fusion.18), channel_id=1, source_target_pairs={{0,4},{1,5},{2,6},{3,7},{4,0},{5,1},{6,2},{7,3},{8,12},{9,13},{10,... | collective-permute-start | bytes 1769480 | tf_op jit(solution)/shard_map/ppermute | solution.py:86
  427.1 36.1 %collective-permute-start.40 = (bf16[64,4608]{1,0:T(8,128)(2,1)}, bf16[64,4608]{1,0:T(8,128)(2,1)}, u32[]{:S(2)}, u32[]{:S(2)}) collective-permute-start(bf16[64,4608]{1,0:T(8,128)(2,1)} %get-tuple-element.354), channel_id=1, source_target_pairs={{0,16},{1,17},{2,18},{3,19},{4,20},{5,21},{6,22},{7,23},{8,24},{9,... | collective-permute-start | bytes 1769480 | tf_op jit(solution)/shard_map/ppermute | solution.py:78
  430.4 32.7 %collective-permute-start.41 = (bf16[64,4608]{1,0:T(8,128)(2,1)}, bf16[64,4608]{1,0:T(8,128)(2,1)}, u32[]{:S(2)}, u32[]{:S(2)}) collective-permute-start(bf16[64,4608]{1,0:T(8,128)(2,1)} %get-tuple-element.353), channel_id=1, source_target_pairs={{0,8},{1,9},{2,10},{3,11},{4,12},{5,13},{6,14},{7,15},{8,0},{9,1},... | collective-permute-start | bytes 1769480 | tf_op jit(solution)/shard_map/ppermute | solution.py:78
  435.3 27.9 %collective-permute-start.42 = (bf16[64,4608]{1,0:T(8,128)(2,1)}, bf16[64,4608]{1,0:T(8,128)(2,1)}, u32[]{:S(2)}, u32[]{:S(2)}) collective-permute-start(bf16[64,4608]{1,0:T(8,128)(2,1)} %get-tuple-element.347), channel_id=1, source_target_pairs={{0,2},{1,3},{2,0},{3,1},{4,6},{5,7},{6,4},{7,5},{8,10},{9,11},{10,... | collective-permute-start | bytes 1769480 | tf_op jit(solution)/shard_map/ppermute | solution.py:86
  438.8 24.3 %collective-permute-start.43 = (bf16[576,512]{1,0:T(8,128)(2,1)S(1)}, bf16[576,512]{1,0:T(8,128)(2,1)S(1)}, u32[]{:S(2)}, u32[]{:S(2)}) collective-permute-start(bf16[576,512]{1,0:T(8,128)(2,1)S(1)} %add_convert_fusion.13), channel_id=1, source_target_pairs={{0,2},{1,3},{2,0},{3,1},{4,6},{5,7},{6,4},{7,5},{8,10},{9,11},{10,... | collective-permute-start | bytes 1769480 | tf_op jit(solution)/shard_map/ppermute | solution.py:86
  480.8 50.9 %collective-permute-start.44 = (bf16[4,128,2176]{2,1,0:T(8,128)(2,1)}, bf16[4,128,2176]{2,1,0:T(8,128)(2,1)}, u32[]{:S(2)}, u32[]{:S(2)}) collective-permute-start(bf16[4,128,2176]{2,1,0:T(8,128)(2,1)} %pad_maximum_fusion.2), channel_id=1, source_target_pairs={{0,1},{1,0},{2,3},{3,2},{4,5},{5,4},{6,7},{7,6},{8,9},{9,8},{10,11... | collective-permute-start | bytes 6684680 | tf_op jit(solution)/shard_map/ppermute | solution.py:86
  494.5 58.4 %collective-permute-start.45 = (bf16[64,4608]{1,0:T(8,128)(2,1)}, bf16[64,4608]{1,0:T(8,128)(2,1)}, u32[]{:S(2)}, u32[]{:S(2)}) collective-permute-start(bf16[64,4608]{1,0:T(8,128)(2,1)} %get-tuple-element.344), channel_id=1, source_target_pairs={{0,2},{1,3},{2,0},{3,1},{4,6},{5,7},{6,4},{7,5},{8,10},{9,11},{10,... | collective-permute-start | bytes 1769480 | tf_op jit(solution)/shard_map/ppermute | solution.py:86
  498.3 54.6 %collective-permute-start.46 = (bf16[64,4608]{1,0:T(8,128)(2,1)S(1)}, bf16[64,4608]{1,0:T(8,128)(2,1)}, u32[]{:S(2)}, u32[]{:S(2)}) collective-permute-start(bf16[64,4608]{1,0:T(8,128)(2,1)S(1)} %add_convert_fusion.10), channel_id=1, source_target_pairs={{0,4},{1,5},{2,6},{3,7},{4,0},{5,1},{6,2},{7,3},{8,12},{9,13},{10,... | collective-permute-start | bytes 1769480 | tf_op jit(solution)/shard_map/ppermute | solution.py:86
  501.7 48.4 %collective-permute-start.49 = (bf16[2,64,1024]{2,1,0:T(8,128)(2,1)}, bf16[2,64,1024]{2,1,0:T(8,128)(2,1)S(1)}, u32[]{:S(2)}, u32[]{:S(2)}) collective-permute-start(bf16[2,64,1024]{2,1,0:T(8,128)(2,1)} %pad_maximum_fusion.23), channel_id=1, source_target_pairs={{0,8},{1,9},{2,10},{3,11},{4,12},{5,13},{6,14},{7,15},{8,0},{9,1},... | collective-permute-start | bytes 786440 | tf_op jit(solution)/shard_map/ppermute | solution.py:78
  506.6 12.7 %collective-permute-start.68 = (bf16[1152,512]{1,0:T(8,128)(2,1)}, bf16[1152,512]{1,0:T(8,128)(2,1)}, u32[]{:S(2)}, u32[]{:S(2)}) collective-permute-start(bf16[1152,512]{1,0:T(8,128)(2,1)} %pad_maximum_fusion.12), channel_id=1, source_target_pairs={{0,1},{1,0},{2,3},{3,2},{4,5},{5,4},{6,7},{7,6},{8,9},{9,8},{10,11... | collective-permute-start | bytes 3538952 | tf_op jit(solution)/shard_map/ppermute | solution.py:86
  519.3 33.5 %collective-permute-start.50 = (bf16[2,64,1024]{2,1,0:T(8,128)(2,1)}, bf16[2,64,1024]{2,1,0:T(8,128)(2,1)}, u32[]{:S(2)}, u32[]{:S(2)}) collective-permute-start(bf16[2,64,1024]{2,1,0:T(8,128)(2,1)} %pad_maximum_fusion.24), channel_id=1, source_target_pairs={{0,16},{1,17},{2,18},{3,19},{4,20},{5,21},{6,22},{7,23},{8,24},{9,... | collective-permute-start | bytes 786440 | tf_op jit(solution)/shard_map/ppermute | solution.py:78
  548.7 14.3 %collective-permute-start.47 = (bf16[2,64,2176]{2,1,0:T(8,128)(2,1)S(1)}, bf16[2,64,2176]{2,1,0:T(8,128)(2,1)S(1)}, u32[]{:S(2)}, u32[]{:S(2)}) collective-permute-start(bf16[2,64,2176]{2,1,0:T(8,128)(2,1)S(1)} %pad_maximum_fusion.19), channel_id=1, source_target_pairs={{0,8},{1,9},{2,10},{3,11},{4,12},{5,13},{6,14},{7,15},{8,0},{9,1},... | collective-permute-start | bytes 1671176 | tf_op jit(solution)/shard_map/ppermute | solution.py:78
  550.1 13.7 %collective-permute-start.48 = (bf16[2,64,2176]{2,1,0:T(8,128)(2,1)S(1)}, bf16[2,64,2176]{2,1,0:T(8,128)(2,1)S(1)}, u32[]{:S(2)}, u32[]{:S(2)}) collective-permute-start(bf16[2,64,2176]{2,1,0:T(8,128)(2,1)S(1)} %pad_maximum_fusion.20), channel_id=1, source_target_pairs={{0,16},{1,17},{2,18},{3,19},{4,20},{5,21},{6,22},{7,23},{8,24},{9,... | collective-permute-start | bytes 1671176 | tf_op jit(solution)/shard_map/ppermute | solution.py:78
  565.0 10.2 %collective-permute-start.51 = (bf16[64,2176]{1,0:T(8,128)(2,1)S(1)}, bf16[64,2176]{1,0:T(8,128)(2,1)S(1)}, u32[]{:S(2)}, u32[]{:S(2)}) collective-permute-start(bf16[64,2176]{1,0:T(8,128)(2,1)S(1)} %get-tuple-element.372), channel_id=1, source_target_pairs={{0,16},{1,17},{2,18},{3,19},{4,20},{5,21},{6,22},{7,23},{8,24},{9,... | collective-permute-start | bytes 835592 | tf_op jit(solution)/shard_map/ppermute | solution.py:78
  565.6 9.6 %collective-permute-start.52 = (bf16[64,2176]{1,0:T(8,128)(2,1)S(1)}, bf16[64,2176]{1,0:T(8,128)(2,1)S(1)}, u32[]{:S(2)}, u32[]{:S(2)}) collective-permute-start(bf16[64,2176]{1,0:T(8,128)(2,1)S(1)} %get-tuple-element.371), channel_id=1, source_target_pairs={{0,8},{1,9},{2,10},{3,11},{4,12},{5,13},{6,14},{7,15},{8,0},{9,1},... | collective-permute-start | bytes 835592 | tf_op jit(solution)/shard_map/ppermute | solution.py:78
  567.8 6.9 %collective-permute-start.53 = (bf16[64,1024]{1,0:T(8,128)(2,1)S(1)}, bf16[64,1024]{1,0:T(8,128)(2,1)S(1)}, u32[]{:S(2)}, u32[]{:S(2)}) collective-permute-start(bf16[64,1024]{1,0:T(8,128)(2,1)S(1)} %get-tuple-element.384), channel_id=1, source_target_pairs={{0,16},{1,17},{2,18},{3,19},{4,20},{5,21},{6,22},{7,23},{8,24},{9,... | collective-permute-start | bytes 393224 | tf_op jit(solution)/shard_map/ppermute | solution.py:78
  568.2 7.0 %collective-permute-start.54 = (bf16[64,1024]{1,0:T(8,128)(2,1)S(1)}, bf16[64,1024]{1,0:T(8,128)(2,1)S(1)}, u32[]{:S(2)}, u32[]{:S(2)}) collective-permute-start(bf16[64,1024]{1,0:T(8,128)(2,1)S(1)} %get-tuple-element.383), channel_id=1, source_target_pairs={{0,8},{1,9},{2,10},{3,11},{4,12},{5,13},{6,14},{7,15},{8,0},{9,1},... | collective-permute-start | bytes 393224 | tf_op jit(solution)/shard_map/ppermute | solution.py:78
  570.4 20.2 %collective-permute-start.55 = (bf16[64,4608]{1,0:T(8,128)(2,1)S(1)}, bf16[64,4608]{1,0:T(8,128)(2,1)S(1)}, u32[]{:S(2)}, u32[]{:S(2)}) collective-permute-start(bf16[64,4608]{1,0:T(8,128)(2,1)S(1)} %add_convert_fusion.9), channel_id=1, source_target_pairs={{0,2},{1,3},{2,0},{3,1},{4,6},{5,7},{6,4},{7,5},{8,10},{9,11},{10,... | collective-permute-start | bytes 1769480 | tf_op jit(solution)/shard_map/ppermute | solution.py:86
  574.6 25.0 %collective-permute-start.57 = (bf16[64,4608]{1,0:T(8,128)(2,1)S(1)}, bf16[64,4608]{1,0:T(8,128)(2,1)S(1)}, u32[]{:S(2)}, u32[]{:S(2)}) collective-permute-start(bf16[64,4608]{1,0:T(8,128)(2,1)S(1)} %add_convert_fusion.8), channel_id=1, source_target_pairs={{0,4},{1,5},{2,6},{3,7},{4,0},{5,1},{6,2},{7,3},{8,12},{9,13},{10,... | collective-permute-start | bytes 1769480 | tf_op jit(solution)/shard_map/ppermute | solution.py:86
  591.9 13.7 %collective-permute-start.56 = (bf16[64,2176]{1,0:T(8,128)(2,1)S(1)}, bf16[64,2176]{1,0:T(8,128)(2,1)S(1)}, u32[]{:S(2)}, u32[]{:S(2)}) collective-permute-start(bf16[64,2176]{1,0:T(8,128)(2,1)S(1)} %get-tuple-element.341), channel_id=1, source_target_pairs={{0,2},{1,3},{2,0},{3,1},{4,6},{5,7},{6,4},{7,5},{8,10},{9,11},{10,... | collective-permute-start | bytes 835592 | tf_op jit(solution)/shard_map/ppermute | solution.py:86
  593.1 12.6 %collective-permute-start.58 = (bf16[64,1024]{1,0:T(8,128)(2,1)S(1)}, bf16[64,1024]{1,0:T(8,128)(2,1)S(1)}, u32[]{:S(2)}, u32[]{:S(2)}) collective-permute-start(bf16[64,1024]{1,0:T(8,128)(2,1)S(1)} %get-tuple-element.338), channel_id=1, source_target_pairs={{0,2},{1,3},{2,0},{3,1},{4,6},{5,7},{6,4},{7,5},{8,10},{9,11},{10,... | collective-permute-start | bytes 393224 | tf_op jit(solution)/shard_map/ppermute | solution.py:86
  605.7 13.1 %collective-permute-start.63 = (bf16[64,1024]{1,0:T(8,128)(2,1)S(1)}, bf16[64,1024]{1,0:T(8,128)(2,1)S(1)}, u32[]{:S(2)}, u32[]{:S(2)}) collective-permute-start(bf16[64,1024]{1,0:T(8,128)(2,1)S(1)} %add_convert_fusion.53), channel_id=1, source_target_pairs={{0,4},{1,5},{2,6},{3,7},{4,0},{5,1},{6,2},{7,3},{8,12},{9,13},{10,... | collective-permute-start | bytes 393224 | tf_op jit(solution)/shard_map/ppermute | solution.py:86
  605.9 25.8 %collective-permute-start.59 = (bf16[64,2176]{1,0:T(8,128)(2,1)S(1)}, bf16[64,2176]{1,0:T(8,128)(2,1)S(1)}, u32[]{:S(2)}, u32[]{:S(2)}) collective-permute-start(bf16[64,2176]{1,0:T(8,128)(2,1)S(1)} %add_convert_fusion.41), channel_id=1, source_target_pairs={{0,4},{1,5},{2,6},{3,7},{4,0},{5,1},{6,2},{7,3},{8,12},{9,13},{10,... | collective-permute-start | bytes 835592 | tf_op jit(solution)/shard_map/ppermute | solution.py:86
  618.9 10.0 %collective-permute-start.64 = (bf16[64,1024]{1,0:T(8,128)(2,1)S(1)}, bf16[64,1024]{1,0:T(8,128)(2,1)S(1)}, u32[]{:S(2)}, u32[]{:S(2)}) collective-permute-start(bf16[64,1024]{1,0:T(8,128)(2,1)S(1)} %add_convert_fusion.52), channel_id=1, source_target_pairs={{0,2},{1,3},{2,0},{3,1},{4,6},{5,7},{6,4},{7,5},{8,10},{9,11},{10,... | collective-permute-start | bytes 393224 | tf_op jit(solution)/shard_map/ppermute | solution.py:86
  619.1 22.4 %collective-permute-start.60 = (bf16[64,4608]{1,0:T(8,128)(2,1)S(1)}, bf16[64,4608]{1,0:T(8,128)(2,1)S(1)}, u32[]{:S(2)}, u32[]{:S(2)}) collective-permute-start(bf16[64,4608]{1,0:T(8,128)(2,1)S(1)} %add_convert_fusion.7), channel_id=1, source_target_pairs={{0,2},{1,3},{2,0},{3,1},{4,6},{5,7},{6,4},{7,5},{8,10},{9,11},{10,... | collective-permute-start | bytes 1769480 | tf_op jit(solution)/shard_map/ppermute | solution.py:86
  629.6 21.2 %collective-permute-start.66 = (bf16[128,4608]{1,0:T(8,128)(2,1)S(1)}, bf16[128,4608]{1,0:T(8,128)(2,1)S(1)}, u32[]{:S(2)}, u32[]{:S(2)}) collective-permute-start(bf16[128,4608]{1,0:T(8,128)(2,1)S(1)} %pad_maximum_fusion.10), channel_id=1, source_target_pairs={{0,1},{1,0},{2,3},{3,2},{4,5},{5,4},{6,7},{7,6},{8,9},{9,8},{10,11... | collective-permute-start | bytes 3538952 | tf_op jit(solution)/shard_map/ppermute | solution.py:86
  641.5 7.8 %collective-permute-start.61 = (bf16[64,2176]{1,0:T(8,128)(2,1)S(1)}, bf16[64,2176]{1,0:T(8,128)(2,1)S(1)}, u32[]{:S(2)}, u32[]{:S(2)}) collective-permute-start(bf16[64,2176]{1,0:T(8,128)(2,1)S(1)} %add_convert_fusion.40), channel_id=1, source_target_pairs={{0,2},{1,3},{2,0},{3,1},{4,6},{5,7},{6,4},{7,5},{8,10},{9,11},{10,... | collective-permute-start | bytes 835592 | tf_op jit(solution)/shard_map/ppermute | solution.py:86
  641.8 15.6 %collective-permute-start.67 = (bf16[128,4608]{1,0:T(8,128)(2,1)S(1)}, bf16[128,4608]{1,0:T(8,128)(2,1)S(1)}, u32[]{:S(2)}, u32[]{:S(2)}) collective-permute-start(bf16[128,4608]{1,0:T(8,128)(2,1)S(1)} %pad_maximum_fusion.11), channel_id=1, source_target_pairs={{0,1},{1,0},{2,3},{3,2},{4,5},{5,4},{6,7},{7,6},{8,9},{9,8},{10,11... | collective-permute-start | bytes 3538952 | tf_op jit(solution)/shard_map/ppermute | solution.py:86
  (131 other events, 1062.1 us)
